TPU v7x, 32 devices: a whole 2x2x4 slice. The times are simulated.
32 devices in a mesh: grp: 2 (over y), seq: 4 (over z), head: 2 (over x), sub: 2 (over core).
Axes of the slice: x: 2, y: 2, z: 4, core: 2. Of those that a mesh axis runs over, the one named last changes fastest.
Arguments:
- tokens: bfloat16 [4096, 3584], P(('grp', 'seq', 'sub')), parts along dimension 0, may hold values from -12 to 12, as said below
- norm_gain: float32 [2, 3584], replicated, may hold values from 0.1 to 1.9
- w_query: bfloat16 [2, 3584, 2048], P(None, ('seq', 'sub'), 'head'), may hold values from -1 to 1
- w_key: bfloat16 [2, 3584, 512], P(None, ('seq', 'sub')), may hold values from -4 to 4
- w_value: bfloat16 [2, 3584, 512], P(None, ('seq', 'sub')), may hold values from -0.09375 to 0.09375
- w_out: bfloat16 [2, 2048, 3584], P(None, 'head', ('seq', 'sub')), may hold values from -0.125 to 0.125
- modality: int32 [4096], P('grp'), parts along dimension 0, may hold values from 0 to 1, as said below
- doc_ids: int32 [4096], P('grp'), parts along dimension 0, may hold values from 0 to 3, never falling along the last dimension, each value on 1 to 1536 neighbouring positions
Outputs:
- mixed: bfloat16 [4096, 3584], P(('grp', 'seq', 'sub'), 'head'), parts along dimension 0
There are 2 independent parts, one for each index of `grp`. A program takes and returns all parts, laid end to end along the dimension named above; an argument that names none is the same for every part. Nothing has to cross between parts.
Inputs may be any that keep to these rules, and one draw needn't show every extreme that they name: `tokens`: rows carry their own scale. `modality`: positions below 512 are 0; after that, each aligned run of 64 positions is all 0 or all 1. `doc_ids`: never falling along the positions; a document holds at most 1536 positions, and one holds exactly that many.
All inputs are finite; a program needn't handle non-finite values.
Results may differ from a plain program's by a relative error of at most 0.015.
Values may be sent and summed in bfloat16 or wider, within the bound.
No kernel may reach another device: no remote copies, remote signals or barrier semaphores. Data moves between devices by JAX's collectives and lax.ppermute only.
A program may use at most 128 MiB of HBM per device.

v0:
```python
import math

import jax
import jax.numpy as jnp
from jax import lax
from jax.experimental import pallas as pl
from jax.experimental.pallas import tpu as pltpu
from jax.sharding import PartitionSpec as P


HEAD_DIM = 128
KV_HEADS = 4
EPS = 1e-06
LOW = -1e30


def swap(x, axis):
    return lax.ppermute(x, axis, [(0, 1), (1, 0)])


def from_ahead(x, axis, offset):
    size = lax.axis_size(axis)
    return lax.ppermute(x, axis, [((i + offset) % size, i) for i in range(size)])


def after(value, *done):
    return lax.optimization_barrier((value, *done))[0]


def spans(modality, doc_ids, own_mod, own_doc, own_pos):
    changed = (modality[1:] != modality[:-1]) | (doc_ids[1:] != doc_ids[:-1])
    begins = jnp.concatenate([jnp.ones((1,), jnp.int32), changed.astype(jnp.int32)])
    blocks = jnp.cumsum(begins)
    own_block = lax.dynamic_slice_in_dim(blocks, own_pos[0], own_pos.shape[0])
    low = jnp.sum((doc_ids[None, :] < own_doc[:, None]).astype(jnp.int32), axis=1)
    end = jnp.sum((blocks[None, :] <= own_block[:, None]).astype(jnp.int32), axis=1) - 1
    return low, jnp.where(own_mod == 1, end, own_pos)


def attention_kernel(starts, limits, q_ref, kv_ref, low_ref, high_ref, o_ref, top, total, acc):
    count, size, _ = kv_ref.shape
    rows = q_ref.shape[0]
    heads = q_ref.shape[1] // HEAD_DIM
    kv_local = kv_ref.shape[2] // (2 * HEAD_DIM)
    repeat = heads // kv_local
    scale = 1.0 / math.sqrt(HEAD_DIM)
    top[...] = jnp.full_like(top, LOW)
    total[...] = jnp.zeros_like(total)
    acc[...] = jnp.zeros_like(acc)

    def visit(number, _):
        start = starts[number]

        @pl.when((start <= limits[1]) & (start + size > limits[0]))
        def _():
            key_pos = start + lax.broadcasted_iota(jnp.int32, (rows, size), 1)
            seen = (key_pos >= low_ref[...]) & (key_pos <= high_ref[...])
            for head in range(heads):
                g = head // repeat
                keys = kv_ref[number, :, g * HEAD_DIM : (g + 1) * HEAD_DIM]
                values = kv_ref[number, :, (kv_local + g) * HEAD_DIM : (kv_local + g + 1) * HEAD_DIM]
                query = q_ref[:, head * HEAD_DIM : (head + 1) * HEAD_DIM]
                scores = lax.dot_general(
                    query, keys, (((1,), (1,)), ((), ())), preferred_element_type=jnp.float32
                )
                scores = jnp.where(seen, scores * scale, LOW)
                old = top[head][:, :1]
                new = jnp.maximum(old, jnp.max(scores, axis=1, keepdims=True))
                weights = jnp.where(seen, jnp.exp(scores - new), 0.0)
                shrink = jnp.exp(old - new)
                total[head] = jnp.broadcast_to(
                    total[head][:, :1] * shrink + jnp.sum(weights, axis=1, keepdims=True),
                    (rows, HEAD_DIM),
                )
                top[head] = jnp.broadcast_to(new, (rows, HEAD_DIM))
                acc[head] = acc[head] * shrink + jnp.dot(
                    weights.astype(jnp.bfloat16), values, preferred_element_type=jnp.float32
                )

        return 0

    lax.fori_loop(0, count, visit, 0)
    for head in range(heads):
        o_ref[:, head * HEAD_DIM : (head + 1) * HEAD_DIM] = (acc[head] / total[head]).astype(
            jnp.bfloat16
        )


def attend(query, kv, starts, low, high):
    rows, width = query.shape
    heads = width // HEAD_DIM
    count, size, _ = kv.shape
    vmem = pl.BlockSpec(memory_space=pltpu.VMEM)
    smem = pl.BlockSpec(memory_space=pltpu.SMEM)
    limits = jnp.stack([low[0], high[-1]])
    return pl.pallas_call(
        attention_kernel,
        out_shape=jax.ShapeDtypeStruct((rows, width), jnp.bfloat16),
        in_specs=[smem, smem, vmem, vmem, vmem, vmem],
        out_specs=vmem,
        scratch_shapes=[
            pltpu.VMEM((heads, rows, HEAD_DIM), jnp.float32),
            pltpu.VMEM((heads, rows, HEAD_DIM), jnp.float32),
            pltpu.VMEM((heads, rows, HEAD_DIM), jnp.float32),
        ],
        cost_estimate=pl.CostEstimate(
            flops=4 * rows * count * size * width,
            bytes_accessed=2 * (2 * rows * width + kv.size),
            transcendentals=rows * count * size * heads,
        ),
        compiler_params=pltpu.CompilerParams(vmem_limit_bytes=32 * 1024 * 1024),
        name="attend",
    )(starts, limits, query, kv, low[:, None], high[:, None])


def project_kernel(turns, places, ours_ref, beside_ref, ours_near, beside_near, own_ref, *rest):
    steps = (len(rest) - 4) // 4
    near = rest[: 2 * steps]
    far = rest[2 * steps : 4 * steps]
    o_ours, o_beside, held, arrived = rest[4 * steps :]
    count = turns.shape[0]
    size = steps + 1
    place, first = places[0], places[1]

    def wanted(turn):
        slot = jnp.int32(-1)
        for i in range(count):
            slot = jnp.where(turns[i] == turn, i, slot)
        return slot

    def fetch(source, kind, turn, valid):
        slot = wanted(turn)

        @pl.when(valid & (slot >= 0))
        def _():
            at = jnp.maximum(slot, 0)
            pltpu.make_async_copy(source, held.at[kind, at], arrived.at[kind, at]).start()

    fetch(own_ref.at[first], 0, 0, True)
    fetch(own_ref.at[1 - first], 1, 0, True)
    for k in range(steps):
        for kind, refs in ((0, near), (1, far)):
            fetch(refs[k], kind, k + 1, place + k + 1 < size)
            fetch(refs[steps + k], kind, size - 1 - k, place >= k + 1)

    contract = (((1,), (1,)), ((), ()))
    halves = []
    for a_ref, near_ref, o_ref in ((ours_ref, ours_near, o_ours), (beside_ref, beside_near, o_beside)):
        a = a_ref[...]
        mine = near_ref[...] != 0
        zero = jnp.zeros_like(a)
        halves.append((jnp.where(mine, a, zero), jnp.where(mine, zero, a), o_ref))
    for i in range(count):
        for kind in range(2):
            pltpu.make_async_copy(own_ref.at[0], held.at[kind, i], arrived.at[kind, i]).wait()
        for a_near, a_far, o_ref in halves:
            o_ref[i] = (
                lax.dot_general(a_near, held[0, i], contract, preferred_element_type=jnp.float32)
                + lax.dot_general(a_far, held[1, i], contract, preferred_element_type=jnp.float32)
            ).astype(jnp.bfloat16)


def project(ours, beside, ours_near, beside_near, weights, turns, places):
    rows, depth = ours.shape
    count = turns.shape[0]
    width = weights[0].shape[1]
    vmem = pl.BlockSpec(memory_space=pltpu.VMEM)
    smem = pl.BlockSpec(memory_space=pltpu.SMEM)
    shape = jax.ShapeDtypeStruct((count, rows, width), jnp.bfloat16)
    return pl.pallas_call(
        project_kernel,
        out_shape=(shape, shape),
        in_specs=[smem, smem] + [vmem] * 4 + [pl.BlockSpec(memory_space=pl.ANY)] * len(weights),
        out_specs=(vmem, vmem),
        scratch_shapes=[
            pltpu.VMEM((2, count, width, depth), jnp.bfloat16),
            pltpu.SemaphoreType.DMA((2, count)),
        ],
        cost_estimate=pl.CostEstimate(
            flops=8 * count * rows * depth * width,
            bytes_accessed=4 * count * depth * width + 4 * count * rows * width,
            transcendentals=0,
        ),
        compiler_params=pltpu.CompilerParams(vmem_limit_bytes=32 * 1024 * 1024),
        name="project",
    )(turns, places, ours, beside, ours_near[:, None], beside_near[:, None], *weights)


def body(tokens, norm_gain, w_query, w_key, w_value, w_out, modality, doc_ids):
    length, depth = tokens.shape
    n = lax.axis_size("seq")
    subs = lax.axis_size("sub")
    heads_over = lax.axis_size("head")
    z, s = lax.axis_index("seq"), lax.axis_index("sub")
    x, y = lax.axis_index("head"), lax.axis_index("grp")
    width = depth // n
    steps = range(n - 1)

    kv_local = max(KV_HEADS // heads_over, 1)
    kv_first = x * KV_HEADS // heads_over
    key_cols = lax.dynamic_slice_in_dim(w_key, kv_first * HEAD_DIM, kv_local * HEAD_DIM, 2)
    value_cols = lax.dynamic_slice_in_dim(w_value, kv_first * HEAD_DIM, kv_local * HEAD_DIM, 2)
    w_out = jnp.swapaxes(w_out, 1, 2)

    def turned(r):
        return (z + r) % n

    def part_of(array, place, core):
        return lax.dynamic_slice_in_dim(array, (place * subs + core) * length, length)

    first_pos = (z * subs + s) * length
    own_mod, own_doc = part_of(modality, z, s), part_of(doc_ids, z, s)
    own_pos = first_pos + jnp.arange(length, dtype=jnp.int32)
    values32 = tokens.astype(jnp.float32)
    factor = lax.rsqrt(jnp.mean(values32 * values32, axis=1, keepdims=True) + EPS)
    gain = jnp.where((own_mod == 1)[:, None], norm_gain[1][None, :], norm_gain[0][None, :])
    normed = (values32 * factor * gain).astype(jnp.bfloat16)

    mine = lax.dynamic_index_in_dim(w_out, y, 0, keepdims=False)
    right, left = [], []

    def step_out(k, *done):
        send_right, send_left = (right[-1], left[-1]) if k else (mine, mine)
        if done:
            send_right, send_left = after((send_right, send_left), *done)
        right.append(lax.ppermute(send_right, "seq", [(i, i + 1) for i in range(k, n - 1)]))
        left.append(lax.ppermute(send_left, "seq", [(i, i - 1) for i in range(1, n - k)]))

    step_out(0)

    order = sorted(range(1, n), key=lambda r: -max(r, n - r)) + [0]
    share_rows = heads_over == 2
    rows = length // 2 if share_rows else length

    def columns(r, first=0, count=length):
        return lax.dynamic_slice(normed, (first, turned(r) * width), (count, width))

    blocks = {0: columns(0)}
    for r in order[:-1]:
        blocks[r] = from_ahead(columns(n - r, x * rows if share_rows else 0, rows), "seq", r)
    if share_rows:
        for group in (order[:2], order[2:-1]):
            if group:
                held = jnp.stack([blocks[r] for r in group])
                other = swap(held, "head")
                for i, r in enumerate(group):
                    blocks[r] = jnp.where(
                        x == 0,
                        jnp.concatenate([held[i], other[i]]),
                        jnp.concatenate([other[i], held[i]]),
                    )

    def share(weight):
        other = swap(weight, "sub")
        both = jnp.where(
            s == 0,
            jnp.concatenate([weight, other], axis=1),
            jnp.concatenate([other, weight], axis=1),
        )
        return both.reshape(2 * width, weight.shape[2])

    w_kv_all = share(jnp.concatenate([key_cols, value_cols], axis=2))
    w_q_all = share(w_query)

    def split(block, mod):
        generate = (mod == 1)[:, None]
        zero = jnp.zeros_like(block)
        return jnp.concatenate(
            [jnp.where(generate, zero, block), jnp.where(generate, block, zero)], axis=1
        )

    modality, doc_ids = after((modality, doc_ids), normed)
    doubled = {r: split(blocks[r], part_of(modality, turned(r), s)) for r in order}
    low, high = spans(modality, doc_ids, own_mod, own_doc, own_pos)
    w_kv_all, w_q_all, low, high = lax.optimization_barrier((w_kv_all, w_q_all, low, high))

    class Scatter:
        def __init__(self, weight):
            self.parts = {
                r: jnp.dot(doubled[r], weight, preferred_element_type=jnp.float32) for r in order
            }
            self.got = None

        def sends(self, k):
            pair = self.parts[n - 1 - k], self.parts[k + 1]
            if k:
                pair = tuple(a + b.astype(jnp.float32) for a, b in zip(pair, self.got))
            return tuple(a.astype(jnp.bfloat16) for a in pair)

        def step(self, k, pair):
            to_right = lax.ppermute(pair[0], "seq", [(i, i + 1) for i in range(min(k + 1, n - 1))])
            to_left = lax.ppermute(
                pair[1], "seq", [(i, i - 1) for i in range(max(n - 1 - k, 1), n)]
            )
            self.got = lax.optimization_barrier((to_right, to_left))

        def result(self):
            total = self.parts[0] + self.got[0].astype(jnp.float32) + self.got[1].astype(jnp.float32)
            return total.astype(jnp.bfloat16)

    kv_sum, q_sum = Scatter(w_kv_all), Scatter(w_q_all)
    kv_pair, q_pair = lax.optimization_barrier((kv_sum.sends(0), q_sum.sends(0)))
    kv_sum.step(0, kv_pair)
    q_sum.step(0, q_pair)
    if n > 2:
        step_out(1, q_pair)
    for k in range(1, n - 1):
        kv_pair = lax.optimization_barrier(kv_sum.sends(k))
        kv_sum.step(k, kv_pair)
        q_pair = after(q_sum.sends(k), kv_sum.got if k < n - 2 else kv_pair)
        q_sum.step(k, q_pair)
        if k + 1 < n - 1:
            step_out(k + 1, q_pair)
    kv = kv_sum.result()

    same = [kv]
    for r in range(1, n):
        same.append(from_ahead(kv, "seq", r))
    beside_0 = swap(kv, "sub")
    others = swap(jnp.stack(same[1:]), "sub")
    kv_all = jnp.concatenate([jnp.stack(same), beside_0[None], others])
    query = q_sum.result()

    pairs = []
    for k in steps:
        for received, there in ((left[k], range(n - 1 - k)), (right[k], range(k + 1, n))):
            hops = [(i, i + n) for i in there] + [(i + n, i) for i in there]
            pairs.append(lax.ppermute(received, ("grp", "seq"), hops))
    weights = [w_out] + left + right + pairs[0::2] + pairs[1::2]

    starts = jnp.stack(
        [(turned(r) * subs + s) * length for r in range(n)]
        + [(turned(r) * subs + (1 - s)) * length for r in range(n)]
    ).astype(jnp.int32)
    attended = attend(query, kv_all, starts, low, high)

    beside = swap(attended, "sub")
    ours_near = (own_mod == y).astype(jnp.bfloat16)
    beside_near = (part_of(modality, z, 1 - s) == y).astype(jnp.bfloat16)
    places = jnp.stack([z, y]).astype(jnp.int32)

    def out(columns):
        turns = ((columns - z + n) % n).astype(jnp.int32)
        return project(attended, beside, ours_near, beside_near, weights, turns, places)

    def placed(ours, theirs):
        sibling = swap(theirs, "sub")
        pair = jnp.where(s == 0, jnp.stack([ours, sibling], 1), jnp.stack([sibling, ours], 1))
        return jnp.transpose(pair, (2, 0, 1, 3)).reshape(length, -1)

    if heads_over != 2:
        wide = placed(*out(jnp.arange(n)))
        return lax.psum_scatter(wide, "head", scatter_dimension=1, tiled=True)

    half = jnp.arange(n // 2)

    def add(a, b):
        return (a.astype(jnp.float32) + b.astype(jnp.float32)).astype(jnp.bfloat16)

    send_ours, send_beside = out((1 - x) * (n // 2) + half)
    got_beside = swap(send_beside, "head")
    got_ours = swap(send_ours, "head")
    keep_ours, keep_beside = out(x * (n // 2) + half)
    return placed(add(keep_ours, got_ours), add(keep_beside, got_beside))


def solution(mesh):
    placed = (
        P(("grp", "seq", "sub"), None),
        P(),
        P(None, ("seq", "sub"), "head"),
        P(None, ("seq", "sub"), None),
        P(None, ("seq", "sub"), None),
        P(None, "head", ("seq", "sub")),
        P("grp"),
        P("grp"),
    )
    return jax.shard_map(
        body,
        mesh=mesh,
        in_specs=placed,
        out_specs=P(("grp", "seq", "sub"), "head"),
        check_vma=False,
    )
```

profile of v0, /device:TPU:0, one launch (start us, length us, event | category | flops | bytes accessed | tf_op | source)
XLA Modules:
  0.0 266.3 jit_solution(5892776441042808789)
XLA Ops:
  3.6 2.4 fusion.2
  8.1 3.1 %collective-permute-start.3 = (bf16[128,896]{1,0:T(8,128)(2,1)S(1)}, bf16[128,896]{1,0:T(8,128)(2,1)S(1)}, u32[]{:S(2)}, u32[]{:S(2)}) collective-permute-start(bf16[128,896]{1,0:T(8,128)(2,1)S(1)} %get-tuple-element.88), channel_id=1, source_target_pairs={{12,0},{0,4},{4,8},{8,12},{13,1},{1,5},{5,9},{9,13},{14,2},{2,6},{... | collective-permute-start | bytes 688136 | tf_op jit(solution)/shard_map/ppermute | solution.py:23
  21.0 3.1 %collective-permute-done.2 = bf16[128,896]{1,0:T(8,128)(2,1)} collective-permute-done((bf16[128,896]{1,0:T(8,128)(2,1)}, bf16[128,896]{1,0:T(8,128)(2,1)}, u32[]{:S(2)}, u32[]{:S(2)}) %collective-permute-start.2) | collective-permute-done | bytes 229408 | tf_op jit(solution)/shard_map/ppermute | solution.py:23
  28.4 5.5 %collective-permute-done.5 = bf16[128,896]{1,0:T(8,128)(2,1)} collective-permute-done((bf16[128,896]{1,0:T(8,128)(2,1)}, bf16[128,896]{1,0:T(8,128)(2,1)}, u32[]{:S(2)}, u32[]{:S(2)}) %collective-permute-start.5) | collective-permute-done | bytes 229408 | tf_op jit(solution)/shard_map/ppermute | solution.py:23
  33.9 3.9 %collective-permute-start.26 = (bf16[448,1024]{1,0:T(8,128)(2,1)}, bf16[448,1024]{1,0:T(8,128)(2,1)}, u32[]{:S(2)}, u32[]{:S(2)}) collective-permute-start(bf16[448,1024]{1,0:T(8,128)(2,1)} %dynamic-slice_bitcast_fusion), channel_id=1, source_target_pairs={{0,4},{4,8},{8,12},{1,5},{5,9},{9,13},{2,6},{6,10},{10,14},{3,7},{... | collective-permute-start | bytes 2752520 | tf_op jit(solution)/shard_map/ppermute | solution.py:226
  43.8 5.1 %maximum_select_fusion = bf16[2,896,1024]{2,1,0:T(8,128)(2,1)S(1)} fusion(bf16[2,448,1024]{2,1,0:T(8,128)(2,1)} %collective-permute-done.1, bf16[2,448,1024]{2,1,0:T(8,128)(2,1)} %param.10, pred[]{:T(512)S(6)} %eq.56), kind=kLoop, calls=%fused_computation.5 | loop fusion | flops 16515072 | bytes 7340033 | tf_op jit(solution)/shard_map/jit(_where)/select_n | solution.py:255
  48.9 2.3 fusion.28
  51.2 2.3 fusion.27
  55.6 7.6 %collective-permute-start.9 = (bf16[256,512]{1,0:T(8,128)(2,1)S(1)}, bf16[256,512]{1,0:T(8,128)(2,1)S(1)}, u32[]{:S(2)}, u32[]{:S(2)}) collective-permute-start(bf16[256,512]{1,0:T(8,128)(2,1)S(1)} %get-tuple-element.53), channel_id=1, source_target_pairs={{0,4},{1,5},{2,6},{3,7},{16,20},{17,21},{18,22},{19,23}} | collective-permute-start | bytes 786440 | tf_op jit(solution)/shard_map/ppermute | solution.py:291
  65.2 4.7 %collective-permute-done.9 = bf16[256,512]{1,0:T(8,128)(2,1)S(1)} collective-permute-done((bf16[256,512]{1,0:T(8,128)(2,1)S(1)}, bf16[256,512]{1,0:T(8,128)(2,1)S(1)}, u32[]{:S(2)}, u32[]{:S(2)}) %collective-permute-start.9) | collective-permute-done | bytes 262176 | tf_op jit(solution)/shard_map/ppermute | solution.py:291
  71.4 4.4 %collective-permute-start.11 = (bf16[256,512]{1,0:T(8,128)(2,1)}, bf16[256,512]{1,0:T(8,128)(2,1)S(1)}, u32[]{:S(2)}, u32[]{:S(2)}) collective-permute-start(bf16[256,512]{1,0:T(8,128)(2,1)} %get-tuple-element.57), channel_id=1, source_target_pairs={{0,4},{4,8},{1,5},{5,9},{2,6},{6,10},{3,7},{7,11},{16,20},{20,24},... | collective-permute-start | bytes 786440 | tf_op jit(solution)/shard_map/ppermute | solution.py:291
  77.1 5.5 %collective-permute-start.7 = (bf16[256,1024]{1,0:T(8,128)(2,1)}, bf16[256,1024]{1,0:T(8,128)(2,1)}, u32[]{:S(2)}, u32[]{:S(2)}) collective-permute-start(bf16[256,1024]{1,0:T(8,128)(2,1)} %get-tuple-element.49), channel_id=1, source_target_pairs={{0,4},{1,5},{2,6},{3,7},{16,20},{17,21},{18,22},{19,23}} | collective-permute-start | bytes 1572872 | tf_op jit(solution)/shard_map/ppermute | solution.py:291
  84.1 2.2 broadcast_select_fusion.7
  91.6 5.6 %collective-permute-start.17 = (bf16[256,512]{1,0:T(8,128)(2,1)S(1)}, bf16[256,512]{1,0:T(8,128)(2,1)S(1)}, u32[]{:S(2)}, u32[]{:S(2)}) collective-permute-start(bf16[256,512]{1,0:T(8,128)(2,1)S(1)} %add_convert_fusion.9), channel_id=1, source_target_pairs={{0,4},{4,8},{8,12},{1,5},{5,9},{9,13},{2,6},{6,10},{10,14},{3,7},{... | collective-permute-start | bytes 786440 | tf_op jit(solution)/shard_map/ppermute | solution.py:291
  98.6 3.5 %add_convert_fusion.5 = (bf16[256,1024]{1,0:T(8,128)(2,1)S(1)}, bf16[256,1024]{1,0:T(8,128)(2,1)S(1)}) fusion(bf16[256,1024]{1,0:T(8,128)(2,1)} %collective-permute-done.8, bf16[256,1024]{1,0:T(8,128)(2,1)} %collective-permute-done.7, bf16[1792,1024]{1,0:T(8,128)(2,1)} %bitcast.61, bf16[256,896]{1,0:T(8,128)(2,1)S(1)} %copy-done.24, ...), kind=kOutput, calls=%fused_computation.16 | convolution fusion | flops 942931968 | bytes 6684672 | tf_op jit(solution)/shard_map/dot_general | solution.py:280
  102.1 4.6 %collective-permute-start.13 = (bf16[256,1024]{1,0:T(8,128)(2,1)S(1)}, bf16[256,1024]{1,0:T(8,128)(2,1)S(1)}, u32[]{:S(2)}, u32[]{:S(2)}) collective-permute-start(bf16[256,1024]{1,0:T(8,128)(2,1)S(1)} %get-tuple-element.61), channel_id=1, source_target_pairs={{0,4},{4,8},{1,5},{5,9},{2,6},{6,10},{3,7},{7,11},{16,20},{20,24},... | collective-permute-start | bytes 1572872 | tf_op jit(solution)/shard_map/ppermute | solution.py:291
  109.0 21.3 %collective-permute-start.19 = (bf16[256,512]{1,0:T(8,128)(2,1)}, bf16[256,512]{1,0:T(8,128)(2,1)S(1)}, u32[]{:S(2)}, u32[]{:S(2)}) collective-permute-start(bf16[256,512]{1,0:T(8,128)(2,1)} %get-tuple-element.84), channel_id=1, source_target_pairs={{4,0},{8,4},{12,8},{0,12},{5,1},{9,5},{13,9},{1,13},{6,2},{10,6},{... | collective-permute-start | bytes 786440 | tf_op jit(solution)/shard_map/ppermute | solution.py:23
  131.6 3.3 %collective-permute-start.21 = (bf16[256,512]{1,0:T(8,128)(2,1)}, bf16[256,512]{1,0:T(8,128)(2,1)S(1)}, u32[]{:S(2)}, u32[]{:S(2)}) collective-permute-start(bf16[256,512]{1,0:T(8,128)(2,1)} %get-tuple-element.84), channel_id=1, source_target_pairs={{12,0},{0,4},{4,8},{8,12},{13,1},{1,5},{5,9},{9,13},{14,2},{2,6},{... | collective-permute-start | bytes 786440 | tf_op jit(solution)/shard_map/ppermute | solution.py:23
  136.8 4.7 %collective-permute-start.15 = (bf16[256,1024]{1,0:T(8,128)(2,1)}, bf16[256,1024]{1,0:T(8,128)(2,1)}, u32[]{:S(2)}, u32[]{:S(2)}) collective-permute-start(bf16[256,1024]{1,0:T(8,128)(2,1)} %add_convert_fusion.4), channel_id=1, source_target_pairs={{0,4},{4,8},{8,12},{1,5},{5,9},{9,13},{2,6},{6,10},{10,14},{3,7},{... | collective-permute-start | bytes 1572872 | tf_op jit(solution)/shard_map/ppermute | solution.py:291
  141.6 2.2 fusion.11
  146.6 3.4 %collective-permute-start.31 = (bf16[448,1024]{1,0:T(8,128)(2,1)S(1)}, bf16[448,1024]{1,0:T(8,128)(2,1)S(1)}, u32[]{:S(2)}, u32[]{:S(2)}) collective-permute-start(bf16[448,1024]{1,0:T(8,128)(2,1)S(1)} %collective-permute-done.25.rest_0_), channel_id=1, source_target_pairs={{0,16},{4,20},{8,24},{16,0},{20,4},{24,8},{1,17},{5,21},{9,25},{17... | collective-permute-start | bytes 2752520 | tf_op jit(solution)/shard_map/ppermute | solution.py:328
  157.7 27.9 %collective-permute-done.16 = bf16[256,1024]{1,0:T(8,128)(2,1)S(1)} collective-permute-done((bf16[256,1024]{1,0:T(8,128)(2,1)}, bf16[256,1024]{1,0:T(8,128)(2,1)S(1)}, u32[]{:S(2)}, u32[]{:S(2)}) %collective-permute-start.16) | collective-permute-done | bytes 524320 | tf_op jit(solution)/shard_map/ppermute | solution.py:292
  189.7 2.5 collective-permute-start.32
  193.8 3.4 %collective-permute-start.33 = (bf16[448,1024]{1,0:T(8,128)(2,1)}, bf16[448,1024]{1,0:T(8,128)(2,1)}, u32[]{:S(2)}, u32[]{:S(2)}) collective-permute-start(bf16[448,1024]{1,0:T(8,128)(2,1)} %collective-permute-done.29.rest_2_), channel_id=1, source_target_pairs={{0,16},{16,0},{1,17},{17,1},{2,18},{18,2},{3,19},{19,3}} | collective-permute-start | bytes 2752520 | tf_op jit(solution)/shard_map/ppermute | solution.py:328
  200.2 5.0 %attend.1.ours_ref = bf16[256,1024]{1,0:T(8,128)(2,1)S(1)} custom-call(s32[8]{0:T(128)S(1)} %stack.94.starts, s32[2]{0:T(128)S(1)} %pad_add_fusion.1.limits, bf16[256,1024]{1,0:T(8,128)(2,1)S(1)} %add_convert_fusion.2.q_ref, bf16[8,256,512]{2,1,0:T(8,128)(2,1)S(1)} %constant_dynamic-update-slice_fusion.kv_ref, s32[256,1]{1,0:T(8,128)S(1)} %copy.17.low_ref, ...), custom_call_target="tpu_custom_call" | custom-call | flops 2147483648 | bytes 3145728 | tf_op jit(solution)/shard_map/attend/pallas_call | solution.py:96
  206.3 2.5 collective-permute-start.24
  209.1 6.1 %collective-permute-done.32.rest_7_ = bf16[448,1024]{1,0:T(8,128)(2,1)} collective-permute-done((bf16[448,1024]{1,0:T(8,128)(2,1)}, bf16[448,1024]{1,0:T(8,128)(2,1)}, u32[]{:S(2)}, u32[]{:S(2)}) %collective-permute-start.32) | collective-permute-done | bytes 917536 | tf_op jit(solution)/shard_map/ppermute | solution.py:328
  215.2 17.8 %collective-permute-done.33.rest_8_ = bf16[448,1024]{1,0:T(8,128)(2,1)} collective-permute-done((bf16[448,1024]{1,0:T(8,128)(2,1)}, bf16[448,1024]{1,0:T(8,128)(2,1)}, u32[]{:S(2)}, u32[]{:S(2)}) %collective-permute-start.33) | collective-permute-done | bytes 917536 | tf_op jit(solution)/shard_map/ppermute | solution.py:328
  235.3 5.3 %project.3 = (bf16[2,256,448]{2,1,0:T(8,128)(2,1)S(1)}, bf16[2,256,448]{2,1,0:T(8,128)(2,1)S(1)}) custom-call(s32[2]{0:T(128)S(1)} %get-tuple-element.117.turns, s32[2]{0:T(128)S(1)} %pad_add_fusion.places, bf16[256,1024]{1,0:T(8,128)(2,1)S(1)} %attend.1.ours_ref, bf16[256,1024]{1,0:T(8,128)(2,1)} %collective-permute-done.24.beside_ref, ...), custom_call_target="tpu_custom_call" | custom-call | flops 1879048192 | bytes 4587520 | tf_op jit(solution)/shard_map/project/pallas_call | solution.py:170
  242.8 5.1 %project.2 = (bf16[2,256,448]{2,1,0:T(8,128)(2,1)S(1)}, bf16[2,256,448]{2,1,0:T(8,128)(2,1)S(1)}) custom-call(s32[2]{0:T(128)S(1)} %get-tuple-element.118.turns, s32[2]{0:T(128)S(1)} %pad_add_fusion.places, bf16[256,1024]{1,0:T(8,128)(2,1)S(1)} %attend.1.ours_ref, bf16[256,1024]{1,0:T(8,128)(2,1)} %collective-permute-done.24.beside_ref, ...), custom_call_target="tpu_custom_call" | custom-call | flops 1879048192 | bytes 4587520 | tf_op jit(solution)/shard_map/project/pallas_call | solution.py:170
  247.8 7.7 %collective-permute-done.38 = bf16[2,256,448]{2,1,0:T(8,128)(2,1)S(1)} collective-permute-done((bf16[2,256,448]{2,1,0:T(8,128)(2,1)S(1)}, bf16[2,256,448]{2,1,0:T(8,128)(2,1)S(1)}, u32[]{:S(2)}, u32[]{:S(2)}) %collective-permute-start.38) | collective-permute-done | bytes 458784 | tf_op jit(solution)/shard_map/ppermute | solution.py:18
  255.8 8.3 %collective-permute-done.37 = bf16[2,256,448]{2,1,0:T(8,128)(2,1)S(1)} collective-permute-done((bf16[2,256,448]{2,1,0:T(8,128)(2,1)S(1)}, bf16[2,256,448]{2,1,0:T(8,128)(2,1)S(1)}, u32[]{:S(2)}, u32[]{:S(2)}) %collective-permute-start.37) | collective-permute-done | bytes 458784 | tf_op jit(solution)/shard_map/ppermute | solution.py:18
  (177 shorter events, 71.4 us)
Async XLA Ops:
  2.4 39.4 %collective-permute-start = (bf16[2,448,512]{2,1,0:T(8,128)(2,1)}, bf16[2,448,512]{2,1,0:T(8,128)(2,1)}, u32[]{:S(2)}, u32[]{:S(2)}) collective-permute-start(bf16[2,448,512]{2,1,0:T(8,128)(2,1)} %pad_maximum_fusion), channel_id=1, source_target_pairs={{0,1},{1,0},{2,3},{3,2},{4,5},{5,4},{6,7},{7,6},{8,9},{9,8},{10,11... | collective-permute-start | bytes 2752520 | tf_op jit(solution)/shard_map/ppermute | solution.py:18
  2.9 40.9 %collective-permute-start.1 = (bf16[2,448,1024]{2,1,0:T(8,128)(2,1)}, bf16[2,448,1024]{2,1,0:T(8,128)(2,1)}, u32[]{:S(2)}, u32[]{:S(2)}) collective-permute-start(bf16[2,448,1024]{2,1,0:T(8,128)(2,1)} %param.10), channel_id=1, source_target_pairs={{0,1},{1,0},{2,3},{3,2},{4,5},{5,4},{6,7},{7,6},{8,9},{9,8},{10,11... | collective-permute-start | bytes 5505032 | tf_op jit(solution)/shard_map/ppermute | solution.py:18
  13.2 20.8 %collective-permute-start.5 = (bf16[128,896]{1,0:T(8,128)(2,1)}, bf16[128,896]{1,0:T(8,128)(2,1)}, u32[]{:S(2)}, u32[]{:S(2)}) collective-permute-start(bf16[128,896]{1,0:T(8,128)(2,1)} %get-tuple-element.87), channel_id=1, source_target_pairs={{8,0},{12,4},{0,8},{4,12},{9,1},{13,5},{1,9},{5,13},{10,2},{14,6},... | collective-permute-start | bytes 688136 | tf_op jit(solution)/shard_map/ppermute | solution.py:23
  19.7 63.0 %collective-permute-start.25 = (bf16[448,1024]{1,0:T(8,128)(2,1)}, bf16[448,1024]{1,0:T(8,128)(2,1)S(1)}, u32[]{:S(2)}, u32[]{:S(2)}) collective-permute-start(bf16[448,1024]{1,0:T(8,128)(2,1)} %dynamic-slice_bitcast_fusion), channel_id=1, source_target_pairs={{4,0},{8,4},{12,8},{5,1},{9,5},{13,9},{6,2},{10,6},{14,10},{7,3},{... | collective-permute-start | bytes 2752520 | tf_op jit(solution)/shard_map/ppermute | solution.py:227
  33.9 52.5 %collective-permute-start.26 = (bf16[448,1024]{1,0:T(8,128)(2,1)}, bf16[448,1024]{1,0:T(8,128)(2,1)}, u32[]{:S(2)}, u32[]{:S(2)}) collective-permute-start(bf16[448,1024]{1,0:T(8,128)(2,1)} %dynamic-slice_bitcast_fusion), channel_id=1, source_target_pairs={{0,4},{4,8},{8,12},{1,5},{5,9},{9,13},{2,6},{6,10},{10,14},{3,7},{... | collective-permute-start | bytes 2752520 | tf_op jit(solution)/shard_map/ppermute | solution.py:226
  37.8 26.1 %collective-permute-start.6 = (bf16[1,128,896]{2,1,0:T(8,128)(2,1)}, bf16[1,128,896]{2,1,0:T(8,128)(2,1)S(1)}, u32[]{:S(2)}, u32[]{:S(2)}) collective-permute-start(bf16[1,128,896]{2,1,0:T(8,128)(2,1)} %bitcast.18), channel_id=1, source_target_pairs={{0,2},{2,0},{1,3},{3,1},{4,6},{6,4},{5,7},{7,5},{8,10},{10,8},{9,1... | collective-permute-start | bytes 688136 | tf_op jit(solution)/shard_map/ppermute | solution.py:18
  55.6 14.3 %collective-permute-start.9 = (bf16[256,512]{1,0:T(8,128)(2,1)S(1)}, bf16[256,512]{1,0:T(8,128)(2,1)S(1)}, u32[]{:S(2)}, u32[]{:S(2)}) collective-permute-start(bf16[256,512]{1,0:T(8,128)(2,1)S(1)} %get-tuple-element.53), channel_id=1, source_target_pairs={{0,4},{1,5},{2,6},{3,7},{16,20},{17,21},{18,22},{19,23}} | collective-permute-start | bytes 786440 | tf_op jit(solution)/shard_map/ppermute | solution.py:291
  71.4 16.5 %collective-permute-start.11 = (bf16[256,512]{1,0:T(8,128)(2,1)}, bf16[256,512]{1,0:T(8,128)(2,1)S(1)}, u32[]{:S(2)}, u32[]{:S(2)}) collective-permute-start(bf16[256,512]{1,0:T(8,128)(2,1)} %get-tuple-element.57), channel_id=1, source_target_pairs={{0,4},{4,8},{1,5},{5,9},{2,6},{6,10},{3,7},{7,11},{16,20},{20,24},... | collective-permute-start | bytes 786440 | tf_op jit(solution)/shard_map/ppermute | solution.py:291
  77.1 20.1 %collective-permute-start.7 = (bf16[256,1024]{1,0:T(8,128)(2,1)}, bf16[256,1024]{1,0:T(8,128)(2,1)}, u32[]{:S(2)}, u32[]{:S(2)}) collective-permute-start(bf16[256,1024]{1,0:T(8,128)(2,1)} %get-tuple-element.49), channel_id=1, source_target_pairs={{0,4},{1,5},{2,6},{3,7},{16,20},{17,21},{18,22},{19,23}} | collective-permute-start | bytes 1572872 | tf_op jit(solution)/shard_map/ppermute | solution.py:291
  82.7 15.9 %collective-permute-start.8 = (bf16[256,1024]{1,0:T(8,128)(2,1)}, bf16[256,1024]{1,0:T(8,128)(2,1)}, u32[]{:S(2)}, u32[]{:S(2)}) collective-permute-start(bf16[256,1024]{1,0:T(8,128)(2,1)} %get-tuple-element.50), channel_id=1, source_target_pairs={{12,8},{13,9},{14,10},{15,11},{28,24},{29,25},{30,26},{31,27}} | collective-permute-start | bytes 1572872 | tf_op jit(solution)/shard_map/ppermute | solution.py:292
  86.4 50.4 %collective-permute-start.27 = (bf16[448,1024]{1,0:T(8,128)(2,1)S(1)}, bf16[448,1024]{1,0:T(8,128)(2,1)}, u32[]{:S(2)}, u32[]{:S(2)}) collective-permute-start(bf16[448,1024]{1,0:T(8,128)(2,1)S(1)} %collective-permute-done.25.rest_0_), channel_id=1, source_target_pairs={{4,0},{8,4},{5,1},{9,5},{6,2},{10,6},{7,3},{11,7},{20,16},{24,20},... | collective-permute-start | bytes 2752520 | tf_op jit(solution)/shard_map/ppermute | solution.py:227
  87.9 49.0 %collective-permute-start.28 = (bf16[448,1024]{1,0:T(8,128)(2,1)}, bf16[448,1024]{1,0:T(8,128)(2,1)}, u32[]{:S(2)}, u32[]{:S(2)}) collective-permute-start(bf16[448,1024]{1,0:T(8,128)(2,1)} %collective-permute-done.26.rest_3_), channel_id=1, source_target_pairs={{4,8},{8,12},{5,9},{9,13},{6,10},{10,14},{7,11},{11,15},{20,24},{2... | collective-permute-start | bytes 2752520 | tf_op jit(solution)/shard_map/ppermute | solution.py:226
  91.6 15.0 %collective-permute-start.17 = (bf16[256,512]{1,0:T(8,128)(2,1)S(1)}, bf16[256,512]{1,0:T(8,128)(2,1)S(1)}, u32[]{:S(2)}, u32[]{:S(2)}) collective-permute-start(bf16[256,512]{1,0:T(8,128)(2,1)S(1)} %add_convert_fusion.9), channel_id=1, source_target_pairs={{0,4},{4,8},{8,12},{1,5},{5,9},{9,13},{2,6},{6,10},{10,14},{3,7},{... | collective-permute-start | bytes 786440 | tf_op jit(solution)/shard_map/ppermute | solution.py:291
  102.1 28.2 %collective-permute-start.13 = (bf16[256,1024]{1,0:T(8,128)(2,1)S(1)}, bf16[256,1024]{1,0:T(8,128)(2,1)S(1)}, u32[]{:S(2)}, u32[]{:S(2)}) collective-permute-start(bf16[256,1024]{1,0:T(8,128)(2,1)S(1)} %get-tuple-element.61), channel_id=1, source_target_pairs={{0,4},{4,8},{1,5},{5,9},{2,6},{6,10},{3,7},{7,11},{16,20},{20,24},... | collective-permute-start | bytes 1572872 | tf_op jit(solution)/shard_map/ppermute | solution.py:291
  106.7 24.9 %collective-permute-start.14 = (bf16[256,1024]{1,0:T(8,128)(2,1)S(1)}, bf16[256,1024]{1,0:T(8,128)(2,1)S(1)}, u32[]{:S(2)}, u32[]{:S(2)}) collective-permute-start(bf16[256,1024]{1,0:T(8,128)(2,1)S(1)} %get-tuple-element.62), channel_id=1, source_target_pairs={{8,4},{12,8},{9,5},{13,9},{10,6},{14,10},{11,7},{15,11},{24,20},{2... | collective-permute-start | bytes 1572872 | tf_op jit(solution)/shard_map/ppermute | solution.py:292
  109.0 37.6 %collective-permute-start.19 = (bf16[256,512]{1,0:T(8,128)(2,1)}, bf16[256,512]{1,0:T(8,128)(2,1)S(1)}, u32[]{:S(2)}, u32[]{:S(2)}) collective-permute-start(bf16[256,512]{1,0:T(8,128)(2,1)} %get-tuple-element.84), channel_id=1, source_target_pairs={{4,0},{8,4},{12,8},{0,12},{5,1},{9,5},{13,9},{1,13},{6,2},{10,6},{... | collective-permute-start | bytes 786440 | tf_op jit(solution)/shard_map/ppermute | solution.py:23
  130.3 19.8 %collective-permute-start.20 = (bf16[256,512]{1,0:T(8,128)(2,1)}, bf16[256,512]{1,0:T(8,128)(2,1)}, u32[]{:S(2)}, u32[]{:S(2)}) collective-permute-start(bf16[256,512]{1,0:T(8,128)(2,1)} %get-tuple-element.84), channel_id=1, source_target_pairs={{8,0},{12,4},{0,8},{4,12},{9,1},{13,5},{1,9},{5,13},{10,2},{14,6},... | collective-permute-start | bytes 786440 | tf_op jit(solution)/shard_map/ppermute | solution.py:23
  131.6 19.8 %collective-permute-start.21 = (bf16[256,512]{1,0:T(8,128)(2,1)}, bf16[256,512]{1,0:T(8,128)(2,1)S(1)}, u32[]{:S(2)}, u32[]{:S(2)}) collective-permute-start(bf16[256,512]{1,0:T(8,128)(2,1)} %get-tuple-element.84), channel_id=1, source_target_pairs={{12,0},{0,4},{4,8},{8,12},{13,1},{1,5},{5,9},{9,13},{14,2},{2,6},{... | collective-permute-start | bytes 786440 | tf_op jit(solution)/shard_map/ppermute | solution.py:23
  136.8 16.9 %collective-permute-start.22 = (bf16[256,512]{1,0:T(8,128)(2,1)}, bf16[256,512]{1,0:T(8,128)(2,1)}, u32[]{:S(2)}, u32[]{:S(2)}) collective-permute-start(bf16[256,512]{1,0:T(8,128)(2,1)} %get-tuple-element.84), channel_id=1, source_target_pairs={{0,1},{1,0},{2,3},{3,2},{4,5},{5,4},{6,7},{7,6},{8,9},{9,8},{10,11... | collective-permute-start | bytes 786440 | tf_op jit(solution)/shard_map/ppermute | solution.py:18
  136.8 18.5 %collective-permute-start.15 = (bf16[256,1024]{1,0:T(8,128)(2,1)}, bf16[256,1024]{1,0:T(8,128)(2,1)}, u32[]{:S(2)}, u32[]{:S(2)}) collective-permute-start(bf16[256,1024]{1,0:T(8,128)(2,1)} %add_convert_fusion.4), channel_id=1, source_target_pairs={{0,4},{4,8},{8,12},{1,5},{5,9},{9,13},{2,6},{6,10},{10,14},{3,7},{... | collective-permute-start | bytes 1572872 | tf_op jit(solution)/shard_map/ppermute | solution.py:291
  146.6 42.1 %collective-permute-start.31 = (bf16[448,1024]{1,0:T(8,128)(2,1)S(1)}, bf16[448,1024]{1,0:T(8,128)(2,1)S(1)}, u32[]{:S(2)}, u32[]{:S(2)}) collective-permute-start(bf16[448,1024]{1,0:T(8,128)(2,1)S(1)} %collective-permute-done.25.rest_0_), channel_id=1, source_target_pairs={{0,16},{4,20},{8,24},{16,0},{20,4},{24,8},{1,17},{5,21},{9,25},{17... | collective-permute-start | bytes 2752520 | tf_op jit(solution)/shard_map/ppermute | solution.py:328
  150.1 43.7 %collective-permute-start.29 = (bf16[448,1024]{1,0:T(8,128)(2,1)}, bf16[448,1024]{1,0:T(8,128)(2,1)}, u32[]{:S(2)}, u32[]{:S(2)}) collective-permute-start(bf16[448,1024]{1,0:T(8,128)(2,1)} %collective-permute-done.27.rest_1_), channel_id=1, source_target_pairs={{4,0},{5,1},{6,2},{7,3},{20,16},{21,17},{22,18},{23,19}} | collective-permute-start | bytes 2752520 | tf_op jit(solution)/shard_map/ppermute | solution.py:227
  151.4 34.2 %collective-permute-start.16 = (bf16[256,1024]{1,0:T(8,128)(2,1)}, bf16[256,1024]{1,0:T(8,128)(2,1)S(1)}, u32[]{:S(2)}, u32[]{:S(2)}) collective-permute-start(bf16[256,1024]{1,0:T(8,128)(2,1)} %add_convert_fusion.3), channel_id=1, source_target_pairs={{4,0},{8,4},{12,8},{5,1},{9,5},{13,9},{6,2},{10,6},{14,10},{7,3},{... | collective-permute-start | bytes 1572872 | tf_op jit(solution)/shard_map/ppermute | solution.py:292
  153.7 43.5 %collective-permute-start.30 = (bf16[448,1024]{1,0:T(8,128)(2,1)}, bf16[448,1024]{1,0:T(8,128)(2,1)}, u32[]{:S(2)}, u32[]{:S(2)}) collective-permute-start(bf16[448,1024]{1,0:T(8,128)(2,1)} %collective-permute-done.28.rest_4_), channel_id=1, source_target_pairs={{8,12},{9,13},{10,14},{11,15},{24,28},{25,29},{26,30},{27,31}} | collective-permute-start | bytes 2752520 | tf_op jit(solution)/shard_map/ppermute | solution.py:226
  155.3 36.9 %collective-permute-start.23 = (bf16[3,256,512]{2,1,0:T(8,128)(2,1)S(1)}, bf16[3,256,512]{2,1,0:T(8,128)(2,1)S(1)}, u32[]{:S(2)}, u32[]{:S(2)}) collective-permute-start(bf16[3,256,512]{2,1,0:T(8,128)(2,1)S(1)} %pad_maximum_fusion.5), channel_id=1, source_target_pairs={{0,1},{1,0},{2,3},{3,2},{4,5},{5,4},{6,7},{7,6},{8,9},{9,8},{10,11... | collective-permute-start | bytes 2359304 | tf_op jit(solution)/shard_map/ppermute | solution.py:18
  185.6 19.7 %collective-permute-start.34 = (bf16[448,1024]{1,0:T(8,128)(2,1)}, bf16[448,1024]{1,0:T(8,128)(2,1)S(1)}, u32[]{:S(2)}, u32[]{:S(2)}) collective-permute-start(bf16[448,1024]{1,0:T(8,128)(2,1)} %collective-permute-done.26.rest_3_), channel_id=1, source_target_pairs={{4,20},{8,24},{12,28},{20,4},{24,8},{28,12},{5,21},{9,25},{13,29},... | collective-permute-start | bytes 2752520 | tf_op jit(solution)/shard_map/ppermute | solution.py:328
  189.7 25.6 %collective-permute-start.32 = (bf16[448,1024]{1,0:T(8,128)(2,1)}, bf16[448,1024]{1,0:T(8,128)(2,1)}, u32[]{:S(2)}, u32[]{:S(2)}) collective-permute-start(bf16[448,1024]{1,0:T(8,128)(2,1)} %collective-permute-done.27.rest_1_), channel_id=1, source_target_pairs={{0,16},{4,20},{16,0},{20,4},{1,17},{5,21},{17,1},{21,5},{2,18},{6,... | collective-permute-start | bytes 2752520 | tf_op jit(solution)/shard_map/ppermute | solution.py:328
  192.2 23.0 %collective-permute-start.35 = (bf16[448,1024]{1,0:T(8,128)(2,1)}, bf16[448,1024]{1,0:T(8,128)(2,1)}, u32[]{:S(2)}, u32[]{:S(2)}) collective-permute-start(bf16[448,1024]{1,0:T(8,128)(2,1)} %collective-permute-done.28.rest_4_), channel_id=1, source_target_pairs={{8,24},{12,28},{24,8},{28,12},{9,25},{13,29},{25,9},{29,13},{10,26... | collective-permute-start | bytes 2752520 | tf_op jit(solution)/shard_map/ppermute | solution.py:328
  193.8 39.2 %collective-permute-start.33 = (bf16[448,1024]{1,0:T(8,128)(2,1)}, bf16[448,1024]{1,0:T(8,128)(2,1)}, u32[]{:S(2)}, u32[]{:S(2)}) collective-permute-start(bf16[448,1024]{1,0:T(8,128)(2,1)} %collective-permute-done.29.rest_2_), channel_id=1, source_target_pairs={{0,16},{16,0},{1,17},{17,1},{2,18},{18,2},{3,19},{19,3}} | collective-permute-start | bytes 2752520 | tf_op jit(solution)/shard_map/ppermute | solution.py:328
  197.3 35.7 %collective-permute-start.36 = (bf16[448,1024]{1,0:T(8,128)(2,1)}, bf16[448,1024]{1,0:T(8,128)(2,1)}, u32[]{:S(2)}, u32[]{:S(2)}) collective-permute-start(bf16[448,1024]{1,0:T(8,128)(2,1)} %collective-permute-done.30.rest_5_), channel_id=1, source_target_pairs={{12,28},{28,12},{13,29},{29,13},{14,30},{30,14},{15,31},{31,15}} | collective-permute-start | bytes 2752520 | tf_op jit(solution)/shard_map/ppermute | solution.py:328
  240.7 14.9 %collective-permute-start.38 = (bf16[2,256,448]{2,1,0:T(8,128)(2,1)S(1)}, bf16[2,256,448]{2,1,0:T(8,128)(2,1)S(1)}, u32[]{:S(2)}, u32[]{:S(2)}) collective-permute-start(bf16[2,256,448]{2,1,0:T(8,128)(2,1)S(1)} %get-tuple-element.80), channel_id=1, source_target_pairs={{0,2},{2,0},{1,3},{3,1},{4,6},{6,4},{5,7},{7,5},{8,10},{10,8},{9,1... | collective-permute-start | bytes 1376264 | tf_op jit(solution)/shard_map/ppermute | solution.py:18
  240.9 23.1 %collective-permute-start.37 = (bf16[2,256,448]{2,1,0:T(8,128)(2,1)S(1)}, bf16[2,256,448]{2,1,0:T(8,128)(2,1)S(1)}, u32[]{:S(2)}, u32[]{:S(2)}) collective-permute-start(bf16[2,256,448]{2,1,0:T(8,128)(2,1)S(1)} %get-tuple-element.78), channel_id=1, source_target_pairs={{0,2},{2,0},{1,3},{3,1},{4,6},{6,4},{5,7},{7,5},{8,10},{10,8},{9,1... | collective-permute-start | bytes 1376264 | tf_op jit(solution)/shard_map/ppermute | solution.py:18
  (38 other events, 418.7 us)
where the time goes:
time: 268 us; the launch traced here: 266 us
  starting transfers between devices  104 us (39%)
  waiting for transfers between devices  81.7 us (30%)
  other arithmetic  28.8 us (11%)
  local copies, waits for them, and re-layouts  19.3 us (7%)
  Pallas kernels  15.4 us (6%)
  matrix products  14.5 us (5%)
  between operations  2.79 us (1%)
    ppermute x6, starting transfers between devices, step(): lax.ppermute(pair[0], 'seq', [(i, i + 1) for i in range(min(k + 1, n - 1))])  32.5 us
    ppermute x6, starting transfers between devices, from_ahead(): lax.ppermute(x, axis, [((i + offset) % size, i) for i in range(size)])  32 us
    ppermute x6, waiting for transfers between devices, step(): lax.ppermute(pair[1], 'seq', [(i, i - 1) for i in range(max(n - 1 - k, 1)...  27.9 us
    ppermute x6, waiting for transfers between devices, body(): pairs.append(lax.ppermute(received, ('grp', 'seq'), hops))  23.9 us
    ppermute x10, waiting for transfers between devices, swap(): return lax.ppermute(x, axis, [(0, 1), (1, 0)])  16 us
    dot_general x8, matrix products, __init__(): jnp.dot(doubled[r], weight, preferred_element_type=jnp.float32)  14.5 us
    ppermute x6, starting transfers between devices, body(): pairs.append(lax.ppermute(received, ('grp', 'seq'), hops))  13.3 us
    unnamed x64, local copies, waits for them, and re-layouts  10.4 us
  transfers between devices with their start and end apart: 40, of which 9 were waited for; matrix products, arithmetic and copies ran while one was open for 20% of the time, Pallas kernels for 4%

commit v1 on v0

v1 whole, which is shorter than its diff:
```python
import functools
import math

import jax
import jax.numpy as jnp
from jax import lax
from jax.experimental import pallas as pl
from jax.experimental.pallas import tpu as pltpu
from jax.sharding import PartitionSpec as P


HEAD_DIM = 128
KV_HEADS = 4
EPS = 1e-06
LOW = -1e30


def swap(x, axis):
    return lax.ppermute(x, axis, [(0, 1), (1, 0)])


def cross(x, axis, bit, among=None):
    size = lax.axis_size(axis)
    return lax.ppermute(x, axis, [(i ^ bit, i) for i in (among or range(size))])


def after(value, *done):
    return lax.optimization_barrier((value, *done))[0]


def add(a, b):
    return (a.astype(jnp.float32) + b.astype(jnp.float32)).astype(jnp.bfloat16)


VMEM = pl.BlockSpec(memory_space=pltpu.VMEM)
SMEM = pl.BlockSpec(memory_space=pltpu.SMEM)
ANY = pl.BlockSpec(memory_space=pl.ANY)


def norm_kernel(place, tokens_ref, gain_ref, mod_ref, own_ref, *rest):
    send_refs, scratch = rest[:-1], rest[-1]
    width = own_ref.shape[1]
    values = tokens_ref[...].astype(jnp.float32)
    factor = lax.rsqrt(jnp.mean(values * values, axis=1, keepdims=True) + EPS)
    gain = jnp.where(mod_ref[...] == 1, gain_ref[1:2, :], gain_ref[0:1, :])
    scratch[...] = (values * factor * gain).astype(jnp.bfloat16)

    def columns(d):
        return pl.ds(pl.multiple_of((place[0] ^ d) * width, width), width)

    own_ref[...] = scratch[:, columns(0)]
    for d, ref in enumerate(send_refs, 1):
        rows = ref.shape[0]
        ref[...] = scratch[pl.ds(pl.multiple_of(place[1] * rows, rows), rows), columns(d)]


def norm_columns(tokens, norm_gain, mod, place, n, rows):
    length, depth = tokens.shape
    width = depth // n
    if width % 128:
        values32 = tokens.astype(jnp.float32)
        factor = lax.rsqrt(jnp.mean(values32 * values32, axis=1, keepdims=True) + EPS)
        gain = jnp.where((mod == 1)[:, None], norm_gain[1][None, :], norm_gain[0][None, :])
        normed = (values32 * factor * gain).astype(jnp.bfloat16)
        first = [0] + [place[1] * rows] * (n - 1)
        count = [length] + [rows] * (n - 1)
        return [
            lax.dynamic_slice(normed, (first[d], (place[0] ^ d) * width), (count[d], width))
            for d in range(n)
        ]
    shapes = [jax.ShapeDtypeStruct((length, width), jnp.bfloat16)]
    shapes += [jax.ShapeDtypeStruct((rows, width), jnp.bfloat16)] * (n - 1)
    return pl.pallas_call(
        norm_kernel,
        out_shape=shapes,
        in_specs=[SMEM, VMEM, VMEM, VMEM],
        out_specs=[VMEM] * n,
        scratch_shapes=[pltpu.VMEM((length, depth), jnp.bfloat16)],
        cost_estimate=pl.CostEstimate(
            flops=6 * length * depth, bytes_accessed=4 * length * depth, transcendentals=length
        ),
        compiler_params=pltpu.CompilerParams(vmem_limit_bytes=32 * 1024 * 1024),
        name="norm",
    )(place, tokens, norm_gain, mod[:, None])


def partial_kernel(counts, place, mod_ref, w_kv, w_q, *rest):
    total = sum(counts)
    refs, kv_ref, q_ref, both = rest[:total], rest[total], rest[total + 1], rest[total + 2]
    length, width = both.shape[0] // len(counts), both.shape[1]
    at = 0
    for number, count in enumerate(counts):
        base = number * length
        if count == 1:
            both[base : base + length] = refs[at][...]
        else:
            half = length // 2
            both[pl.ds(pl.multiple_of(base + place[1] * half, half), half)] = refs[at][...]
            both[pl.ds(pl.multiple_of(base + (1 - place[1]) * half, half), half)] = refs[at + 1][...]
        at += count
    block = both[...]
    generate = mod_ref[...] == 1
    zero = jnp.zeros_like(block)
    first, second = jnp.where(generate, zero, block), jnp.where(generate, block, zero)
    for weight, out in ((w_kv, kv_ref), (w_q, q_ref)):
        out[...] = jnp.dot(first, weight[:width], preferred_element_type=jnp.float32) + jnp.dot(
            second, weight[width:], preferred_element_type=jnp.float32
        )


def partial(blocks, mods, w_kv, w_q, place):
    counts = tuple(len(block) for block in blocks)
    arrays = [array for block in blocks for array in block]
    length = mods[0].shape[0]
    rows, width = length * len(blocks), arrays[0].shape[1]
    kv_cols, q_cols = w_kv.shape[1], w_q.shape[1]
    kv, q = pl.pallas_call(
        functools.partial(partial_kernel, counts),
        out_shape=(
            jax.ShapeDtypeStruct((rows, kv_cols), jnp.float32),
            jax.ShapeDtypeStruct((rows, q_cols), jnp.float32),
        ),
        in_specs=[SMEM] + [VMEM] * (3 + len(arrays)),
        out_specs=(VMEM, VMEM),
        scratch_shapes=[pltpu.VMEM((rows, width), jnp.bfloat16)],
        cost_estimate=pl.CostEstimate(
            flops=4 * rows * width * (kv_cols + q_cols),
            bytes_accessed=4 * (width + rows) * (kv_cols + q_cols),
            transcendentals=0,
        ),
        compiler_params=pltpu.CompilerParams(vmem_limit_bytes=40 * 1024 * 1024),
        name="partial",
    )(place, jnp.concatenate(mods)[:, None], w_kv, w_q, *arrays)
    shape = (len(blocks), length, -1)
    return kv.reshape(shape), q.reshape(shape)


def reduce_scatter(parts, split):
    n = len(parts)
    if n != 4:
        sums = dict(enumerate(parts))
        for bit in [1 << i for i in range(n.bit_length() - 1)]:
            for d in [d for d in range(n) if d in sums and d & bit]:
                sums[d ^ bit] = sums[d ^ bit] + cross(sums.pop(d).astype(jnp.bfloat16), "seq", bit)
        return sums[0].astype(jnp.bfloat16)

    def send(pieces, bit, among):
        if split:
            got = []
            for piece in pieces:
                got.append(cross(piece.astype(jnp.bfloat16), "seq", bit, among))
            return [g.astype(jnp.float32) for g in got]
        got = cross(jnp.stack(pieces).astype(jnp.bfloat16), "seq", bit, among)
        return [got[i].astype(jnp.float32) for i in range(len(pieces))]

    far, two = send([parts[3], parts[2]], 1, (1, 2))
    across, own = send([parts[2] + far, parts[3] + two], 3, (1, 2))
    last = cross((parts[1] + across).astype(jnp.bfloat16), "seq", 1)
    return (parts[0] + last.astype(jnp.float32) + own).astype(jnp.bfloat16)


def gather_weights(mine):
    n = lax.axis_size("seq")
    if n == 4:
        z = lax.axis_index("seq")
        inner = (z == 1) | (z == 2)
        one = cross(mine, "seq", 1)
        middle = cross(mine, "seq", 3, (1, 2))
        middle_two = cross(one, "seq", 3, (1, 2))
        outer_two = cross(middle, "seq", 1, (0, 3))
        outer_three = cross(middle_two, "seq", 1, (0, 3))
        near = [mine, one, jnp.where(inner, middle_two, outer_two), jnp.where(inner, middle, outer_three)]
    else:
        near = [mine]
        for bit in reversed([1 << i for i in range(n.bit_length() - 1)]):
            got = cross(jnp.stack(near), "seq", bit)
            near = near + [got[i] for i in range(len(near))]
        order = [0]
        for bit in reversed([1 << i for i in range(n.bit_length() - 1)]):
            order = order + [d ^ bit for d in order]
        near = [near[order.index(d)] for d in range(n)]
    far = []
    for d in range(1, n):
        far.append(swap(near[d], "grp"))
    return near[1:], far


def spans(modality, doc_ids, own_mod, own_doc, own_pos):
    changed = (modality[1:] != modality[:-1]) | (doc_ids[1:] != doc_ids[:-1])
    begins = jnp.concatenate([jnp.ones((1,), jnp.int32), changed.astype(jnp.int32)])
    blocks = jnp.cumsum(begins)
    own_block = lax.dynamic_slice_in_dim(blocks, own_pos[0], own_pos.shape[0])
    low = jnp.sum((doc_ids[None, :] < own_doc[:, None]).astype(jnp.int32), axis=1)
    end = jnp.sum((blocks[None, :] <= own_block[:, None]).astype(jnp.int32), axis=1) - 1
    return low, jnp.where(own_mod == 1, end, own_pos)


def attention_kernel(starts, limits, q_ref, kv_ref, low_ref, high_ref, o_ref, top, total, acc):
    count, size, _ = kv_ref.shape
    rows = q_ref.shape[0]
    heads = q_ref.shape[1] // HEAD_DIM
    kv_local = kv_ref.shape[2] // (2 * HEAD_DIM)
    repeat = heads // kv_local
    scale = 1.0 / math.sqrt(HEAD_DIM)
    top[...] = jnp.full_like(top, LOW)
    total[...] = jnp.zeros_like(total)
    acc[...] = jnp.zeros_like(acc)

    def visit(number, _):
        start = starts[number]

        @pl.when((start <= limits[1]) & (start + size > limits[0]))
        def _():
            key_pos = start + lax.broadcasted_iota(jnp.int32, (rows, size), 1)
            seen = (key_pos >= low_ref[...]) & (key_pos <= high_ref[...])
            for head in range(heads):
                g = head // repeat
                keys = kv_ref[number, :, g * HEAD_DIM : (g + 1) * HEAD_DIM]
                values = kv_ref[number, :, (kv_local + g) * HEAD_DIM : (kv_local + g + 1) * HEAD_DIM]
                query = q_ref[:, head * HEAD_DIM : (head + 1) * HEAD_DIM]
                scores = lax.dot_general(
                    query, keys, (((1,), (1,)), ((), ())), preferred_element_type=jnp.float32
                )
                scores = jnp.where(seen, scores * scale, LOW)
                old = top[head][:, :1]
                new = jnp.maximum(old, jnp.max(scores, axis=1, keepdims=True))
                weights = jnp.where(seen, jnp.exp(scores - new), 0.0)
                shrink = jnp.exp(old - new)
                total[head] = jnp.broadcast_to(
                    total[head][:, :1] * shrink + jnp.sum(weights, axis=1, keepdims=True),
                    (rows, HEAD_DIM),
                )
                top[head] = jnp.broadcast_to(new, (rows, HEAD_DIM))
                acc[head] = acc[head] * shrink + jnp.dot(
                    weights.astype(jnp.bfloat16), values, preferred_element_type=jnp.float32
                )

        return 0

    lax.fori_loop(0, count, visit, 0)
    for head in range(heads):
        o_ref[:, head * HEAD_DIM : (head + 1) * HEAD_DIM] = (acc[head] / total[head]).astype(
            jnp.bfloat16
        )


def attend(query, kv, starts, low, high):
    rows, width = query.shape
    heads = width // HEAD_DIM
    count, size, _ = kv.shape
    vmem = pl.BlockSpec(memory_space=pltpu.VMEM)
    smem = pl.BlockSpec(memory_space=pltpu.SMEM)
    limits = jnp.stack([low[0], high[-1]])
    return pl.pallas_call(
        attention_kernel,
        out_shape=jax.ShapeDtypeStruct((rows, width), jnp.bfloat16),
        in_specs=[smem, smem, vmem, vmem, vmem, vmem],
        out_specs=vmem,
        scratch_shapes=[
            pltpu.VMEM((heads, rows, HEAD_DIM), jnp.float32),
            pltpu.VMEM((heads, rows, HEAD_DIM), jnp.float32),
            pltpu.VMEM((heads, rows, HEAD_DIM), jnp.float32),
        ],
        cost_estimate=pl.CostEstimate(
            flops=4 * rows * count * size * width,
            bytes_accessed=2 * (2 * rows * width + kv.size),
            transcendentals=rows * count * size * heads,
        ),
        compiler_params=pltpu.CompilerParams(vmem_limit_bytes=32 * 1024 * 1024),
        name="attend",
    )(starts, limits, query, kv, low[:, None], high[:, None])


def project_kernel(turns, place, ours_ref, beside_ref, ours_near, beside_near, own_ref, *rest):
    n = (len(rest) - 4) // 2 + 1
    near, far = rest[: n - 1], rest[n - 1 : 2 * n - 2]
    o_ours, o_beside, held, arrived = rest[2 * n - 2 :]
    count = turns.shape[0]
    first = place[2]

    def fetch(source, kind, d):
        slot = jnp.int32(-1)
        for i in range(count):
            slot = jnp.where(turns[i] == d, i, slot)

        @pl.when(slot >= 0)
        def _():
            at = jnp.maximum(slot, 0)
            pltpu.make_async_copy(source, held.at[kind, at], arrived.at[kind, at]).start()

    for d in range(n):
        fetch(near[d - 1] if d else own_ref.at[first], 0, d)
        fetch(far[d - 1] if d else own_ref.at[1 - first], 1, d)

    contract = (((1,), (1,)), ((), ()))
    halves = []
    for a_ref, near_ref, o_ref in ((ours_ref, ours_near, o_ours), (beside_ref, beside_near, o_beside)):
        a = a_ref[...]
        mine = near_ref[...] != 0
        zero = jnp.zeros_like(a)
        halves.append((jnp.where(mine, a, zero), jnp.where(mine, zero, a), o_ref))
    for i in range(count):
        for kind in range(2):
            pltpu.make_async_copy(own_ref.at[0], held.at[kind, i], arrived.at[kind, i]).wait()
        for a_near, a_far, o_ref in halves:
            o_ref[i] = (
                lax.dot_general(a_near, held[0, i], contract, preferred_element_type=jnp.float32)
                + lax.dot_general(a_far, held[1, i], contract, preferred_element_type=jnp.float32)
            ).astype(jnp.bfloat16)


def project(ours, beside, ours_near, beside_near, weights, turns, place):
    rows, depth = ours.shape
    count = turns.shape[0]
    width = weights[0].shape[1]
    shape = jax.ShapeDtypeStruct((count, rows, width), jnp.bfloat16)
    return pl.pallas_call(
        project_kernel,
        out_shape=(shape, shape),
        in_specs=[SMEM, SMEM] + [VMEM] * 4 + [ANY] * len(weights),
        out_specs=(VMEM, VMEM),
        scratch_shapes=[
            pltpu.VMEM((2, count, width, depth), jnp.bfloat16),
            pltpu.SemaphoreType.DMA((2, count)),
        ],
        cost_estimate=pl.CostEstimate(
            flops=8 * count * rows * depth * width,
            bytes_accessed=4 * count * depth * width + 4 * count * rows * width,
            transcendentals=0,
        ),
        compiler_params=pltpu.CompilerParams(vmem_limit_bytes=32 * 1024 * 1024),
        name="project",
    )(turns, place, ours, beside, ours_near[:, None], beside_near[:, None], *weights)


def body(tokens, norm_gain, w_query, w_key, w_value, w_out, modality, doc_ids):
    length, depth = tokens.shape
    n = lax.axis_size("seq")
    subs = lax.axis_size("sub")
    heads_over = lax.axis_size("head")
    z, s = lax.axis_index("seq"), lax.axis_index("sub")
    x, y = lax.axis_index("head"), lax.axis_index("grp")
    width = depth // n
    place = jnp.stack([z, x, y]).astype(jnp.int32)

    kv_local = max(KV_HEADS // heads_over, 1)
    kv_first = x * KV_HEADS // heads_over
    w_out = jnp.swapaxes(w_out, 1, 2)

    def part_of(array, place, core):
        return lax.dynamic_slice_in_dim(array, (place * subs + core) * length, length)

    mine = lax.dynamic_index_in_dim(w_out, y, 0, keepdims=False)
    near, far = gather_weights(mine)
    weights = [w_out] + near + far

    own_mod = part_of(modality, z, s)
    share_rows = heads_over == 2
    rows = length // 2 if share_rows else length
    sends = norm_columns(tokens, norm_gain, own_mod, place, n, rows)
    blocks = {0: (sends[0],)}
    for d in range(n - 1, 0, -1):
        blocks[d] = (cross(sends[d], "seq", d),)

    def share(weight):
        other = swap(weight, "sub")
        both = jnp.where(
            s == 0,
            jnp.concatenate([weight, other], axis=1),
            jnp.concatenate([other, weight], axis=1),
        )
        return both.reshape(2 * width, weight.shape[2])

    key_cols = lax.dynamic_slice_in_dim(w_key, kv_first * HEAD_DIM, kv_local * HEAD_DIM, 2)
    value_cols = lax.dynamic_slice_in_dim(w_value, kv_first * HEAD_DIM, kv_local * HEAD_DIM, 2)
    w_kv_all = share(jnp.concatenate([key_cols, value_cols], axis=2))
    w_q_all = share(w_query)
    modality, doc_ids = after((modality, doc_ids), sends[0])
    own_doc = part_of(doc_ids, z, s)
    own_pos = (z * subs + s) * length + jnp.arange(length, dtype=jnp.int32)
    low, high = spans(modality, doc_ids, part_of(modality, z, s), own_doc, own_pos)
    for d in range(1, n):
        blocks[d] = after(blocks[d], w_kv_all, w_q_all, low, high)

    early = list(range(n - 1, 1, -1))
    if share_rows:
        for group in (early, [1]):
            held = jnp.stack([blocks[d][0] for d in group])
            other = swap(held, "head")
            for i, d in enumerate(group):
                blocks[d] = (blocks[d][0], other[i])
    parts = {}
    for group in (early, [1, 0]):
        kv, q = partial(
            [blocks[d] for d in group],
            [part_of(modality, z ^ d, s) for d in group],
            w_kv_all,
            w_q_all,
            place,
        )
        for i, d in enumerate(group):
            parts[d] = kv[i], q[i]
    kv = reduce_scatter([parts[d][0] for d in range(n)], False)
    query = reduce_scatter([parts[d][1] for d in range(n)], True)

    same = [kv]
    for d in range(1, n):
        same.append(cross(kv, "seq", d))
    beside_0 = swap(kv, "sub")
    others = swap(jnp.stack(same[1:]), "sub")
    kv_all = jnp.concatenate([jnp.stack(same), beside_0[None], others])
    starts = jnp.stack(
        [((z ^ d) * subs + s) * length for d in range(n)]
        + [((z ^ d) * subs + (1 - s)) * length for d in range(n)]
    ).astype(jnp.int32)
    attended = attend(query, kv_all, starts, low, high)

    beside = swap(attended, "sub")
    ours_near = (own_mod == y).astype(jnp.bfloat16)
    beside_near = (part_of(modality, z, 1 - s) == y).astype(jnp.bfloat16)

    def out(columns):
        turns = (columns ^ z).astype(jnp.int32)
        return project(attended, beside, ours_near, beside_near, weights, turns, place)

    def placed(ours, theirs):
        sibling = swap(theirs, "sub")
        pair = jnp.where(s == 0, jnp.stack([ours, sibling], 1), jnp.stack([sibling, ours], 1))
        return jnp.transpose(pair, (2, 0, 1, 3)).reshape(length, -1)

    if heads_over != 2:
        wide = placed(*out(jnp.arange(n)))
        return lax.psum_scatter(wide, "head", scatter_dimension=1, tiled=True)

    half = jnp.arange(n // 2)
    send_ours, send_beside = out((1 - x) * (n // 2) + half)
    got_beside = swap(send_beside, "head")
    got_ours = swap(send_ours, "head")
    keep_ours, keep_beside = out(x * (n // 2) + half)
    return placed(add(keep_ours, got_ours), add(keep_beside, got_beside))


def solution(mesh):
    placed = (
        P(("grp", "seq", "sub"), None),
        P(),
        P(None, ("seq", "sub"), "head"),
        P(None, ("seq", "sub"), None),
        P(None, ("seq", "sub"), None),
        P(None, "head", ("seq", "sub")),
        P("grp"),
        P("grp"),
    )
    return jax.shard_map(
        body,
        mesh=mesh,
        in_specs=placed,
        out_specs=P(("grp", "seq", "sub"), "head"),
        check_vma=False,
    )
```

time: 268 us -> 227 us (0.85)
  the two profiles are of different devices: /device:TPU:0 before, /device:TPU:22 now
where the time goes in v1:
time: 227 us
  waiting for transfers between devices  103 us (45%)
  starting transfers between devices  53.6 us (24%)
  Pallas kernels  32.7 us (14%)
  other arithmetic  19.5 us (9%)
  local copies, waits for them, and re-layouts  14.9 us (7%)
  between operations  2.64 us (1%)
    ppermute x19, waiting for transfers between devices, cross(): return lax.ppermute(x, axis, [(i ^ bit, i) for i in among or range(size)])  81.6 us
    ppermute x19, starting transfers between devices, cross(): return lax.ppermute(x, axis, [(i ^ bit, i) for i in among or range(size)])  33 us
    ppermute x13, waiting for transfers between devices, swap(): return lax.ppermute(x, axis, [(0, 1), (1, 0)])  21.7 us
    ppermute x13, starting transfers between devices, swap(): return lax.ppermute(x, axis, [(0, 1), (1, 0)])  20.6 us
    pallas_call x1, Pallas kernels, attend(): pl.pallas_call(attention_kernel, out_shape=jax.ShapeDtypeStruct((rows, wi...  13.1 us
    pallas_call x2, Pallas kernels, project(): pl.pallas_call(project_kernel, out_shape=(shape, shape), in_specs=[SMEM,...  9.45 us
    select_n x2, other arithmetic, share(): jnp.where(s == 0, jnp.concatenate([weight, other], axis=1), jnp.concatena...  8.93 us
    pallas_call x2, Pallas kernels, partial(): pl.pallas_call(functools.partial(partial_kernel, counts), out_shape=(jax....  8.54 us
  transfers between devices with their start and end apart: 32, of which 16 were waited for; matrix products, arithmetic and copies ran while one was open for 12% of the time, Pallas kernels for 12%

profile of v1, /device:TPU:22, one launch (start us, length us, event | category | flops | bytes accessed | tf_op | source)
XLA Modules:
  0.0 226.6 jit_solution(7891929386573386216)
XLA Ops:
  0.0 2.3 %dynamic-slice_bitcast_fusion = bf16[448,1024]{1,0:T(8,128)(2,1)} fusion(bf16[2,1024,448]{1,2,0:T(8,128)(2,1)} %param.13, s32[]{:T(128)S(6)} %select_n.98), kind=kLoop, calls=%fused_computation.15 | loop fusion | bytes 1835012 | tf_op jit(solution)/shard_map/jit(dynamic_index_in_dim)/squeeze | solution.py:353
  8.0 2.2 pad_maximum_fusion
  20.9 2.4 %maximum_select_fusion.1 = bf16[2,896,512]{2,1,0:T(8,128)(2,1)S(1)} fusion(bf16[2,448,512]{2,1,0:T(8,128)(2,1)} %collective-permute-done, bf16[2,448,256]{2,1,0:T(8,128)(2,1)} %get-tuple-element.64, bf16[2,448,256]{2,1,0:T(8,128)(2,1)} %get-tuple-element.65, pred[]{:T(512)S(6)} %eq.24), kind=kLoop, calls=%fused_computation.3 | loop fusion | flops 11927552 | bytes 3670017 | tf_op jit(solution)/shard_map/jit(_where)/select_n | solution.py:367
  23.4 6.5 %maximum_select_fusion = bf16[2,896,1024]{2,1,0:T(8,128)(2,1)} fusion(bf16[2,448,1024]{2,1,0:T(8,128)(2,1)} %collective-permute-done.1, bf16[2,448,1024]{2,1,0:T(8,128)(2,1)} %param.10, pred[]{:T(512)S(6)} %eq.24), kind=kLoop, calls=%fused_computation | loop fusion | flops 16515072 | bytes 7340033 | tf_op jit(solution)/shard_map/jit(_where)/select_n | solution.py:367
  29.9 14.1 %collective-permute-done.4.rest_0_ = bf16[128,896]{1,0:T(8,128)(2,1)S(1)} collective-permute-done((bf16[128,896]{1,0:T(8,128)(2,1)S(1)}, bf16[128,896]{1,0:T(8,128)(2,1)S(1)}, u32[]{:S(2)}, u32[]{:S(2)}) %collective-permute-start.4) | collective-permute-done | bytes 229408 | tf_op jit(solution)/shard_map/ppermute | solution.py:24
  46.7 3.7 %collective-permute-start.2 = (bf16[128,896]{1,0:T(8,128)(2,1)S(1)}, bf16[128,896]{1,0:T(8,128)(2,1)}, u32[]{:S(2)}, u32[]{:S(2)}) collective-permute-start(bf16[128,896]{1,0:T(8,128)(2,1)S(1)} %get-tuple-element.25), channel_id=1, source_target_pairs={{4,0},{0,4},{12,8},{8,12},{5,1},{1,5},{13,9},{9,13},{6,2},{2,6},{1... | collective-permute-start | bytes 688136 | tf_op jit(solution)/shard_map/ppermute | solution.py:24
  54.0 2.2 collective-permute-start.22
  61.3 4.1 %partial.3 = (f32[512,512]{1,0:T(8,128)S(1)}, f32[512,1024]{1,0:T(8,128)S(1)}) custom-call(s32[3]{0:T(128)S(1)} %pad_add_fusion.2.place, s32[512,1]{1,0:T(8,128)S(1)} %copy.22.mod_ref, bf16[1792,512]{1,0:T(8,128)(2,1)S(1)} %bitcast.77, bf16[1792,1024]{1,0:T(8,128)(2,1)S(1)} %bitcast.75, bf16[128,896]{1,0:T(8,128)(2,1)S(1)} %collective-permute-done.4.rest_0_, ...), custom_call_target="tpu_custom_call" | custom-call | flops 2818572288 | bytes 8650752 | tf_op jit(solution)/shard_map/partial/pallas_call | solution.py:117
  68.3 8.3 %collective-permute-done.22 = bf16[448,1024]{1,0:T(8,128)(2,1)S(1)} collective-permute-done((bf16[448,1024]{1,0:T(8,128)(2,1)}, bf16[448,1024]{1,0:T(8,128)(2,1)S(1)}, u32[]{:S(2)}, u32[]{:S(2)}) %collective-permute-start.22) | collective-permute-done | bytes 917536 | tf_op jit(solution)/shard_map/ppermute | solution.py:24
  79.4 3.2 %collective-permute-done.7 = bf16[256,1024]{1,0:T(8,128)(2,1)S(1)} collective-permute-done((bf16[256,1024]{1,0:T(8,128)(2,1)S(1)}, bf16[256,1024]{1,0:T(8,128)(2,1)S(1)}, u32[]{:S(2)}, u32[]{:S(2)}) %collective-permute-start.7) | collective-permute-done | bytes 524320 | tf_op jit(solution)/shard_map/ppermute | solution.py:24
  83.8 10.1 %collective-permute-done.10 = bf16[256,1024]{1,0:T(8,128)(2,1)S(1)} collective-permute-done((bf16[256,1024]{1,0:T(8,128)(2,1)S(1)}, bf16[256,1024]{1,0:T(8,128)(2,1)S(1)}, u32[]{:S(2)}, u32[]{:S(2)}) %collective-permute-start.10) | collective-permute-done | bytes 524320 | tf_op jit(solution)/shard_map/ppermute | solution.py:24
  95.8 6.5 %collective-permute-done.12 = bf16[2,256,512]{2,1,0:T(8,128)(2,1)S(1)} collective-permute-done((bf16[2,256,512]{2,1,0:T(8,128)(2,1)S(1)}, bf16[2,256,512]{2,1,0:T(8,128)(2,1)S(1)}, u32[]{:S(2)}, u32[]{:S(2)}) %collective-permute-start.12) | collective-permute-done | bytes 524320 | tf_op jit(solution)/shard_map/ppermute | solution.py:24
  102.2 2.7 %collective-permute-start.8 = (bf16[256,1024]{1,0:T(8,128)(2,1)S(1)}, bf16[256,1024]{1,0:T(8,128)(2,1)S(1)}, u32[]{:S(2)}, u32[]{:S(2)}) collective-permute-start(bf16[256,1024]{1,0:T(8,128)(2,1)S(1)} %get-tuple-element.45), channel_id=1, source_target_pairs={{8,4},{4,8},{9,5},{5,9},{10,6},{6,10},{11,7},{7,11},{24,20},{20,24... | collective-permute-start | bytes 1572872 | tf_op jit(solution)/shard_map/ppermute | solution.py:24
  105.2 3.1 %collective-permute-start.13 = (bf16[2,256,512]{2,1,0:T(8,128)(2,1)S(1)}, bf16[2,256,512]{2,1,0:T(8,128)(2,1)S(1)}, u32[]{:S(2)}, u32[]{:S(2)}) collective-permute-start(bf16[2,256,512]{2,1,0:T(8,128)(2,1)S(1)} %pad_maximum_fusion.3), channel_id=1, source_target_pairs={{8,4},{4,8},{9,5},{5,9},{10,6},{6,10},{11,7},{7,11},{24,20},{20,24... | collective-permute-start | bytes 1572872 | tf_op jit(solution)/shard_map/ppermute | solution.py:24
  108.4 4.5 %partial.2 = (f32[512,512]{1,0:T(8,128)S(1)}, f32[512,1024]{1,0:T(8,128)S(1)}) custom-call(s32[3]{0:T(128)S(1)} %pad_add_fusion.2.place, s32[512,1]{1,0:T(8,128)S(1)} %copy.21.mod_ref, bf16[1792,512]{1,0:T(8,128)(2,1)S(1)} %bitcast.78, bf16[1792,1024]{1,0:T(8,128)(2,1)S(1)} %bitcast.76, bf16[128,896]{1,0:T(8,128)(2,1)} %collective-permute-done.2.rest_0_, ...), custom_call_target="tpu_custom_call" | custom-call | flops 2818572288 | bytes 8650752 | tf_op jit(solution)/shard_map/partial/pallas_call | solution.py:117
  112.8 6.1 %collective-permute-done.8 = bf16[256,1024]{1,0:T(8,128)(2,1)S(1)} collective-permute-done((bf16[256,1024]{1,0:T(8,128)(2,1)S(1)}, bf16[256,1024]{1,0:T(8,128)(2,1)S(1)}, u32[]{:S(2)}, u32[]{:S(2)}) %collective-permute-start.8) | collective-permute-done | bytes 524320 | tf_op jit(solution)/shard_map/ppermute | solution.py:24
  118.9 2.9 %collective-permute-start.11 = (bf16[256,1024]{1,0:T(8,128)(2,1)S(1)}, bf16[256,1024]{1,0:T(8,128)(2,1)S(1)}, u32[]{:S(2)}, u32[]{:S(2)}) collective-permute-start(bf16[256,1024]{1,0:T(8,128)(2,1)S(1)} %get-tuple-element.46), channel_id=1, source_target_pairs={{8,4},{4,8},{9,5},{5,9},{10,6},{6,10},{11,7},{7,11},{24,20},{20,24... | collective-permute-start | bytes 1572872 | tf_op jit(solution)/shard_map/ppermute | solution.py:24
  122.0 8.1 %collective-permute-done.13 = bf16[2,256,512]{2,1,0:T(8,128)(2,1)S(1)} collective-permute-done((bf16[2,256,512]{2,1,0:T(8,128)(2,1)S(1)}, bf16[2,256,512]{2,1,0:T(8,128)(2,1)S(1)}, u32[]{:S(2)}, u32[]{:S(2)}) %collective-permute-start.13) | collective-permute-done | bytes 524320 | tf_op jit(solution)/shard_map/ppermute | solution.py:24
  130.2 2.1 collective-permute-start.14
  132.3 2.2 broadcast_select_fusion.rest_2_
  134.5 13.1 %collective-permute-done.14 = bf16[256,512]{1,0:T(8,128)(2,1)S(1)} collective-permute-done((bf16[256,512]{1,0:T(8,128)(2,1)S(1)}, bf16[256,512]{1,0:T(8,128)(2,1)S(1)}, u32[]{:S(2)}, u32[]{:S(2)}) %collective-permute-start.14) | collective-permute-done | bytes 262176 | tf_op jit(solution)/shard_map/ppermute | solution.py:24
  148.6 2.2 collective-permute-start.16
  151.6 3.3 %collective-permute-done.15 = bf16[256,512]{1,0:T(8,128)(2,1)S(1)} collective-permute-done((bf16[256,512]{1,0:T(8,128)(2,1)S(1)}, bf16[256,512]{1,0:T(8,128)(2,1)S(1)}, u32[]{:S(2)}, u32[]{:S(2)}) %collective-permute-start.15) | collective-permute-done | bytes 262176 | tf_op jit(solution)/shard_map/ppermute | solution.py:24
  156.8 3.6 %collective-permute-done.16 = bf16[256,512]{1,0:T(8,128)(2,1)S(1)} collective-permute-done((bf16[256,512]{1,0:T(8,128)(2,1)S(1)}, bf16[256,512]{1,0:T(8,128)(2,1)S(1)}, u32[]{:S(2)}, u32[]{:S(2)}) %collective-permute-start.16) | collective-permute-done | bytes 262176 | tf_op jit(solution)/shard_map/ppermute | solution.py:24
  160.4 3.8 %collective-permute-done.17 = bf16[256,512]{1,0:T(8,128)(2,1)S(1)} collective-permute-done((bf16[256,512]{1,0:T(8,128)(2,1)S(1)}, bf16[256,512]{1,0:T(8,128)(2,1)S(1)}, u32[]{:S(2)}, u32[]{:S(2)}) %collective-permute-start.17) | collective-permute-done | bytes 262176 | tf_op jit(solution)/shard_map/ppermute | solution.py:24
  164.5 2.2 collective-permute-done.19
  166.7 13.1 %attend.1.ours_ref = bf16[256,1024]{1,0:T(8,128)(2,1)S(1)} custom-call(s32[8]{0:T(128)S(1)} %stack.108.starts, s32[2]{0:T(128)S(1)} %pad_add_fusion.3.limits, bf16[256,1024]{1,0:T(8,128)(2,1)S(1)} %add_convert_fusion.2.q_ref, bf16[8,256,512]{2,1,0:T(8,128)(2,1)S(1)} %constant_dynamic-update-slice_fusion.kv_ref, s32[256,1]{1,0:T(8,128)S(1)} %copy.23.low_ref, ...), custom_call_target="tpu_custom_call" | custom-call | flops 2147483648 | bytes 3145728 | tf_op jit(solution)/shard_map/attend/pallas_call | solution.py:254
  179.8 12.3 %collective-permute-start.20 = (bf16[256,1024]{1,0:T(8,128)(2,1)S(1)}, bf16[256,1024]{1,0:T(8,128)(2,1)}, u32[]{:S(2)}, u32[]{:S(2)}) collective-permute-start(bf16[256,1024]{1,0:T(8,128)(2,1)S(1)} %attend.1.ours_ref), channel_id=1, source_target_pairs={{0,1},{1,0},{2,3},{3,2},{4,5},{5,4},{6,7},{7,6},{8,9},{9,8},{10,11... | collective-permute-start | bytes 1572872 | tf_op jit(solution)/shard_map/ppermute | solution.py:19
  193.7 5.1 %project.3 = (bf16[2,256,448]{2,1,0:T(8,128)(2,1)S(1)}, bf16[2,256,448]{2,1,0:T(8,128)(2,1)S(1)}) custom-call(s32[2]{0:T(128)S(1)} %get-tuple-element.60.turns, s32[3]{0:T(128)S(1)} %pad_add_fusion.2.place, bf16[256,1024]{1,0:T(8,128)(2,1)S(1)} %attend.1.ours_ref, bf16[256,1024]{1,0:T(8,128)(2,1)} %collective-permute-done.20.beside_ref, ...), custom_call_target="tpu_custom_call" | custom-call | flops 1879048192 | bytes 4587520 | tf_op jit(solution)/shard_map/project/pallas_call | solution.py:317
  200.9 4.3 %project.2 = (bf16[2,256,448]{2,1,0:T(8,128)(2,1)S(1)}, bf16[2,256,448]{2,1,0:T(8,128)(2,1)S(1)}) custom-call(s32[2]{0:T(128)S(1)} %get-tuple-element.61.turns, s32[3]{0:T(128)S(1)} %pad_add_fusion.2.place, bf16[256,1024]{1,0:T(8,128)(2,1)S(1)} %attend.1.ours_ref, bf16[256,1024]{1,0:T(8,128)(2,1)} %collective-permute-done.20.beside_ref, ...), custom_call_target="tpu_custom_call" | custom-call | flops 1879048192 | bytes 4587520 | tf_op jit(solution)/shard_map/project/pallas_call | solution.py:317
  205.3 8.4 %collective-permute-done.30 = bf16[2,256,448]{2,1,0:T(8,128)(2,1)S(1)} collective-permute-done((bf16[2,256,448]{2,1,0:T(8,128)(2,1)S(1)}, bf16[2,256,448]{2,1,0:T(8,128)(2,1)S(1)}, u32[]{:S(2)}, u32[]{:S(2)}) %collective-permute-start.30) | collective-permute-done | bytes 458784 | tf_op jit(solution)/shard_map/ppermute | solution.py:19
  213.9 10.4 %collective-permute-done.29 = bf16[2,256,448]{2,1,0:T(8,128)(2,1)S(1)} collective-permute-done((bf16[2,256,448]{2,1,0:T(8,128)(2,1)S(1)}, bf16[2,256,448]{2,1,0:T(8,128)(2,1)S(1)}, u32[]{:S(2)}, u32[]{:S(2)}) %collective-permute-start.29) | collective-permute-done | bytes 458784 | tf_op jit(solution)/shard_map/ppermute | solution.py:19
  (120 shorter events, 44.9 us)
Async XLA Ops:
  2.3 51.7 %collective-permute-start.21 = (bf16[448,1024]{1,0:T(8,128)(2,1)}, bf16[448,1024]{1,0:T(8,128)(2,1)}, u32[]{:S(2)}, u32[]{:S(2)}) collective-permute-start(bf16[448,1024]{1,0:T(8,128)(2,1)} %dynamic-slice_bitcast_fusion), channel_id=1, source_target_pairs={{4,0},{0,4},{12,8},{8,12},{5,1},{1,5},{13,9},{9,13},{6,2},{2,6},{1... | collective-permute-start | bytes 2752520 | tf_op jit(solution)/shard_map/ppermute | solution.py:24
  3.9 52.9 %collective-permute-start.23 = (bf16[448,1024]{1,0:T(8,128)(2,1)}, bf16[448,1024]{1,0:T(8,128)(2,1)}, u32[]{:S(2)}, u32[]{:S(2)}) collective-permute-start(bf16[448,1024]{1,0:T(8,128)(2,1)} %dynamic-slice_bitcast_fusion), channel_id=1, source_target_pairs={{8,4},{4,8},{9,5},{5,9},{10,6},{6,10},{11,7},{7,11},{24,20},{20,24... | collective-permute-start | bytes 2752520 | tf_op jit(solution)/shard_map/ppermute | solution.py:24
  5.8 17.5 %collective-permute-start.1 = (bf16[2,448,1024]{2,1,0:T(8,128)(2,1)}, bf16[2,448,1024]{2,1,0:T(8,128)(2,1)}, u32[]{:S(2)}, u32[]{:S(2)}) collective-permute-start(bf16[2,448,1024]{2,1,0:T(8,128)(2,1)} %param.10), channel_id=1, source_target_pairs={{0,1},{1,0},{2,3},{3,2},{4,5},{5,4},{6,7},{7,6},{8,9},{9,8},{10,11... | collective-permute-start | bytes 5505032 | tf_op jit(solution)/shard_map/ppermute | solution.py:19
  10.1 10.2 %collective-permute-start = (bf16[2,448,512]{2,1,0:T(8,128)(2,1)}, bf16[2,448,512]{2,1,0:T(8,128)(2,1)}, u32[]{:S(2)}, u32[]{:S(2)}) collective-permute-start(bf16[2,448,512]{2,1,0:T(8,128)(2,1)} %pad_maximum_fusion), channel_id=1, source_target_pairs={{0,1},{1,0},{2,3},{3,2},{4,5},{5,4},{6,7},{7,6},{8,9},{9,8},{10,11... | collective-permute-start | bytes 2752520 | tf_op jit(solution)/shard_map/ppermute | solution.py:19
  13.9 30.1 %collective-permute-start.4 = (bf16[128,896]{1,0:T(8,128)(2,1)S(1)}, bf16[128,896]{1,0:T(8,128)(2,1)S(1)}, u32[]{:S(2)}, u32[]{:S(2)}) collective-permute-start(bf16[128,896]{1,0:T(8,128)(2,1)S(1)} %get-tuple-element.28), channel_id=1, source_target_pairs={{12,0},{8,4},{4,8},{0,12},{13,1},{9,5},{5,9},{1,13},{14,2},{10,6},... | collective-permute-start | bytes 688136 | tf_op jit(solution)/shard_map/ppermute | solution.py:24
  20.3 25.0 %collective-permute-start.5 = (bf16[128,896]{1,0:T(8,128)(2,1)S(1)}, bf16[128,896]{1,0:T(8,128)(2,1)S(1)}, u32[]{:S(2)}, u32[]{:S(2)}) collective-permute-start(bf16[128,896]{1,0:T(8,128)(2,1)S(1)} %get-tuple-element.30), channel_id=1, source_target_pairs={{8,0},{12,4},{0,8},{4,12},{9,1},{13,5},{1,9},{5,13},{10,2},{14,6},... | collective-permute-start | bytes 688136 | tf_op jit(solution)/shard_map/ppermute | solution.py:24
  46.1 12.1 %collective-permute-start.6 = (bf16[2,128,896]{2,1,0:T(8,128)(2,1)}, bf16[2,128,896]{2,1,0:T(8,128)(2,1)}, u32[]{:S(2)}, u32[]{:S(2)}) collective-permute-start(bf16[2,128,896]{2,1,0:T(8,128)(2,1)} %pad_maximum_fusion.4), channel_id=1, source_target_pairs={{0,2},{2,0},{1,3},{3,1},{4,6},{6,4},{5,7},{7,5},{8,10},{10,8},{9,1... | collective-permute-start | bytes 1376264 | tf_op jit(solution)/shard_map/ppermute | solution.py:19
  46.7 11.5 %collective-permute-start.2 = (bf16[128,896]{1,0:T(8,128)(2,1)S(1)}, bf16[128,896]{1,0:T(8,128)(2,1)}, u32[]{:S(2)}, u32[]{:S(2)}) collective-permute-start(bf16[128,896]{1,0:T(8,128)(2,1)S(1)} %get-tuple-element.25), channel_id=1, source_target_pairs={{4,0},{0,4},{12,8},{8,12},{5,1},{1,5},{13,9},{9,13},{6,2},{2,6},{1... | collective-permute-start | bytes 688136 | tf_op jit(solution)/shard_map/ppermute | solution.py:24
  54.0 22.5 %collective-permute-start.22 = (bf16[448,1024]{1,0:T(8,128)(2,1)}, bf16[448,1024]{1,0:T(8,128)(2,1)S(1)}, u32[]{:S(2)}, u32[]{:S(2)}) collective-permute-start(bf16[448,1024]{1,0:T(8,128)(2,1)} %collective-permute-done.21.rest_0_), channel_id=1, source_target_pairs={{8,4},{4,8},{9,5},{5,9},{10,6},{6,10},{11,7},{7,11},{24,20},{20,24... | collective-permute-start | bytes 2752520 | tf_op jit(solution)/shard_map/ppermute | solution.py:24
  56.2 136.7 %collective-permute-start.26 = (bf16[448,1024]{1,0:T(8,128)(2,1)}, bf16[448,1024]{1,0:T(8,128)(2,1)}, u32[]{:S(2)}, u32[]{:S(2)}) collective-permute-start(bf16[448,1024]{1,0:T(8,128)(2,1)} %collective-permute-done.21.rest_0_), channel_id=1, source_target_pairs={{0,16},{16,0},{1,17},{17,1},{2,18},{18,2},{3,19},{19,3},{4,20},{20... | collective-permute-start | bytes 2752520 | tf_op jit(solution)/shard_map/ppermute | solution.py:19
  56.8 21.2 %collective-permute-start.24 = (bf16[448,1024]{1,0:T(8,128)(2,1)}, bf16[448,1024]{1,0:T(8,128)(2,1)S(1)}, u32[]{:S(2)}, u32[]{:S(2)}) collective-permute-start(bf16[448,1024]{1,0:T(8,128)(2,1)} %collective-permute-done.23), channel_id=1, source_target_pairs={{4,0},{8,12},{5,1},{9,13},{6,2},{10,14},{7,3},{11,15},{20,16},{24,... | collective-permute-start | bytes 2752520 | tf_op jit(solution)/shard_map/ppermute | solution.py:24
  65.5 17.1 %collective-permute-start.7 = (bf16[256,1024]{1,0:T(8,128)(2,1)S(1)}, bf16[256,1024]{1,0:T(8,128)(2,1)S(1)}, u32[]{:S(2)}, u32[]{:S(2)}) collective-permute-start(bf16[256,1024]{1,0:T(8,128)(2,1)S(1)} %get-tuple-element.47), channel_id=1, source_target_pairs={{0,4},{12,8},{1,5},{13,9},{2,6},{14,10},{3,7},{15,11},{16,20},{28,... | collective-permute-start | bytes 1572872 | tf_op jit(solution)/shard_map/ppermute | solution.py:24
  66.8 27.0 %collective-permute-start.10 = (bf16[256,1024]{1,0:T(8,128)(2,1)S(1)}, bf16[256,1024]{1,0:T(8,128)(2,1)S(1)}, u32[]{:S(2)}, u32[]{:S(2)}) collective-permute-start(bf16[256,1024]{1,0:T(8,128)(2,1)S(1)} %get-tuple-element.48), channel_id=1, source_target_pairs={{0,4},{12,8},{1,5},{13,9},{2,6},{14,10},{3,7},{15,11},{16,20},{28,... | collective-permute-start | bytes 1572872 | tf_op jit(solution)/shard_map/ppermute | solution.py:24
  76.5 28.7 %collective-permute-start.3 = (bf16[1,128,896]{2,1,0:T(8,128)(2,1)}, bf16[1,128,896]{2,1,0:T(8,128)(2,1)S(1)}, u32[]{:S(2)}, u32[]{:S(2)}) collective-permute-start(bf16[1,128,896]{2,1,0:T(8,128)(2,1)} %bitcast.18), channel_id=1, source_target_pairs={{0,2},{2,0},{1,3},{3,1},{4,6},{6,4},{5,7},{7,5},{8,10},{10,8},{9,1... | collective-permute-start | bytes 688136 | tf_op jit(solution)/shard_map/ppermute | solution.py:19
  78.0 24.2 %collective-permute-start.12 = (bf16[2,256,512]{2,1,0:T(8,128)(2,1)S(1)}, bf16[2,256,512]{2,1,0:T(8,128)(2,1)S(1)}, u32[]{:S(2)}, u32[]{:S(2)}) collective-permute-start(bf16[2,256,512]{2,1,0:T(8,128)(2,1)S(1)} %pad_maximum_fusion.2), channel_id=1, source_target_pairs={{0,4},{12,8},{1,5},{13,9},{2,6},{14,10},{3,7},{15,11},{16,20},{28,... | collective-permute-start | bytes 1572872 | tf_op jit(solution)/shard_map/ppermute | solution.py:24
  82.6 110.4 %collective-permute-start.27 = (bf16[448,1024]{1,0:T(8,128)(2,1)S(1)}, bf16[448,1024]{1,0:T(8,128)(2,1)}, u32[]{:S(2)}, u32[]{:S(2)}) collective-permute-start(bf16[448,1024]{1,0:T(8,128)(2,1)S(1)} %broadcast_select_fusion.1.rest_1_), channel_id=1, source_target_pairs={{0,16},{16,0},{1,17},{17,1},{2,18},{18,2},{3,19},{19,3},{4,20},{20... | collective-permute-start | bytes 2752520 | tf_op jit(solution)/shard_map/ppermute | solution.py:19
  93.9 36.4 %collective-permute-start.25 = (bf16[448,1024]{1,0:T(8,128)(2,1)S(1)}, bf16[448,1024]{1,0:T(8,128)(2,1)S(1)}, u32[]{:S(2)}, u32[]{:S(2)}) collective-permute-start(bf16[448,1024]{1,0:T(8,128)(2,1)S(1)} %collective-permute-done.22), channel_id=1, source_target_pairs={{4,0},{8,12},{5,1},{9,13},{6,2},{10,14},{7,3},{11,15},{20,16},{24,... | collective-permute-start | bytes 2752520 | tf_op jit(solution)/shard_map/ppermute | solution.py:24
  102.2 16.7 %collective-permute-start.8 = (bf16[256,1024]{1,0:T(8,128)(2,1)S(1)}, bf16[256,1024]{1,0:T(8,128)(2,1)S(1)}, u32[]{:S(2)}, u32[]{:S(2)}) collective-permute-start(bf16[256,1024]{1,0:T(8,128)(2,1)S(1)} %get-tuple-element.45), channel_id=1, source_target_pairs={{8,4},{4,8},{9,5},{5,9},{10,6},{6,10},{11,7},{7,11},{24,20},{20,24... | collective-permute-start | bytes 1572872 | tf_op jit(solution)/shard_map/ppermute | solution.py:24
  105.2 24.9 %collective-permute-start.13 = (bf16[2,256,512]{2,1,0:T(8,128)(2,1)S(1)}, bf16[2,256,512]{2,1,0:T(8,128)(2,1)S(1)}, u32[]{:S(2)}, u32[]{:S(2)}) collective-permute-start(bf16[2,256,512]{2,1,0:T(8,128)(2,1)S(1)} %pad_maximum_fusion.3), channel_id=1, source_target_pairs={{8,4},{4,8},{9,5},{5,9},{10,6},{6,10},{11,7},{7,11},{24,20},{20,24... | collective-permute-start | bytes 1572872 | tf_op jit(solution)/shard_map/ppermute | solution.py:24
  118.9 29.7 %collective-permute-start.11 = (bf16[256,1024]{1,0:T(8,128)(2,1)S(1)}, bf16[256,1024]{1,0:T(8,128)(2,1)S(1)}, u32[]{:S(2)}, u32[]{:S(2)}) collective-permute-start(bf16[256,1024]{1,0:T(8,128)(2,1)S(1)} %get-tuple-element.46), channel_id=1, source_target_pairs={{8,4},{4,8},{9,5},{5,9},{10,6},{6,10},{11,7},{7,11},{24,20},{20,24... | collective-permute-start | bytes 1572872 | tf_op jit(solution)/shard_map/ppermute | solution.py:24
  130.2 20.7 %collective-permute-start.9 = (bf16[256,1024]{1,0:T(8,128)(2,1)S(1)}, bf16[256,1024]{1,0:T(8,128)(2,1)S(1)}, u32[]{:S(2)}, u32[]{:S(2)}) collective-permute-start(bf16[256,1024]{1,0:T(8,128)(2,1)S(1)} %add_convert_fusion.4), channel_id=1, source_target_pairs={{4,0},{0,4},{12,8},{8,12},{5,1},{1,5},{13,9},{9,13},{6,2},{2,6},{1... | collective-permute-start | bytes 1572872 | tf_op jit(solution)/shard_map/ppermute | solution.py:24
  130.2 17.4 %collective-permute-start.14 = (bf16[256,512]{1,0:T(8,128)(2,1)S(1)}, bf16[256,512]{1,0:T(8,128)(2,1)S(1)}, u32[]{:S(2)}, u32[]{:S(2)}) collective-permute-start(bf16[256,512]{1,0:T(8,128)(2,1)S(1)} %fusion.3), channel_id=1, source_target_pairs={{4,0},{0,4},{12,8},{8,12},{5,1},{1,5},{13,9},{9,13},{6,2},{2,6},{1... | collective-permute-start | bytes 786440 | tf_op jit(solution)/shard_map/ppermute | solution.py:24
  147.8 7.2 %collective-permute-start.15 = (bf16[256,512]{1,0:T(8,128)(2,1)S(1)}, bf16[256,512]{1,0:T(8,128)(2,1)S(1)}, u32[]{:S(2)}, u32[]{:S(2)}) collective-permute-start(bf16[256,512]{1,0:T(8,128)(2,1)S(1)} %get-tuple-element.42), channel_id=1, source_target_pairs={{4,0},{0,4},{12,8},{8,12},{5,1},{1,5},{13,9},{9,13},{6,2},{2,6},{1... | collective-permute-start | bytes 786440 | tf_op jit(solution)/shard_map/ppermute | solution.py:24
  148.6 11.8 %collective-permute-start.16 = (bf16[256,512]{1,0:T(8,128)(2,1)S(1)}, bf16[256,512]{1,0:T(8,128)(2,1)S(1)}, u32[]{:S(2)}, u32[]{:S(2)}) collective-permute-start(bf16[256,512]{1,0:T(8,128)(2,1)S(1)} %get-tuple-element.42), channel_id=1, source_target_pairs={{8,0},{12,4},{0,8},{4,12},{9,1},{13,5},{1,9},{5,13},{10,2},{14,6},... | collective-permute-start | bytes 786440 | tf_op jit(solution)/shard_map/ppermute | solution.py:24
  150.8 13.4 %collective-permute-start.17 = (bf16[256,512]{1,0:T(8,128)(2,1)S(1)}, bf16[256,512]{1,0:T(8,128)(2,1)S(1)}, u32[]{:S(2)}, u32[]{:S(2)}) collective-permute-start(bf16[256,512]{1,0:T(8,128)(2,1)S(1)} %get-tuple-element.42), channel_id=1, source_target_pairs={{12,0},{8,4},{4,8},{0,12},{13,1},{9,5},{5,9},{1,13},{14,2},{10,6},... | collective-permute-start | bytes 786440 | tf_op jit(solution)/shard_map/ppermute | solution.py:24
  155.0 38.0 %collective-permute-start.28 = (bf16[448,1024]{1,0:T(8,128)(2,1)}, bf16[448,1024]{1,0:T(8,128)(2,1)}, u32[]{:S(2)}, u32[]{:S(2)}) collective-permute-start(bf16[448,1024]{1,0:T(8,128)(2,1)} %broadcast_select_fusion.rest_2_), channel_id=1, source_target_pairs={{0,16},{16,0},{1,17},{17,1},{2,18},{18,2},{3,19},{19,3},{4,20},{20... | collective-permute-start | bytes 2752520 | tf_op jit(solution)/shard_map/ppermute | solution.py:19
  160.4 4.1 %collective-permute-start.18 = (bf16[256,512]{1,0:T(8,128)(2,1)S(1)}, bf16[256,512]{1,0:T(8,128)(2,1)S(1)}, u32[]{:S(2)}, u32[]{:S(2)}) collective-permute-start(bf16[256,512]{1,0:T(8,128)(2,1)S(1)} %get-tuple-element.42), channel_id=1, source_target_pairs={{0,1},{1,0},{2,3},{3,2},{4,5},{5,4},{6,7},{7,6},{8,9},{9,8},{10,11... | collective-permute-start | bytes 786440 | tf_op jit(solution)/shard_map/ppermute | solution.py:19
  164.3 2.4 %collective-permute-start.19 = (bf16[3,256,512]{2,1,0:T(8,128)(2,1)S(1)}, bf16[3,256,512]{2,1,0:T(8,128)(2,1)S(1)}, u32[]{:S(2)}, u32[]{:S(2)}) collective-permute-start(bf16[3,256,512]{2,1,0:T(8,128)(2,1)S(1)} %pad_maximum_fusion.1), channel_id=1, source_target_pairs={{0,1},{1,0},{2,3},{3,2},{4,5},{5,4},{6,7},{7,6},{8,9},{9,8},{10,11... | collective-permute-start | bytes 2359304 | tf_op jit(solution)/shard_map/ppermute | solution.py:19
  179.8 13.9 %collective-permute-start.20 = (bf16[256,1024]{1,0:T(8,128)(2,1)S(1)}, bf16[256,1024]{1,0:T(8,128)(2,1)}, u32[]{:S(2)}, u32[]{:S(2)}) collective-permute-start(bf16[256,1024]{1,0:T(8,128)(2,1)S(1)} %attend.1.ours_ref), channel_id=1, source_target_pairs={{0,1},{1,0},{2,3},{3,2},{4,5},{5,4},{6,7},{7,6},{8,9},{9,8},{10,11... | collective-permute-start | bytes 1572872 | tf_op jit(solution)/shard_map/ppermute | solution.py:19
  198.8 14.9 %collective-permute-start.30 = (bf16[2,256,448]{2,1,0:T(8,128)(2,1)S(1)}, bf16[2,256,448]{2,1,0:T(8,128)(2,1)S(1)}, u32[]{:S(2)}, u32[]{:S(2)}) collective-permute-start(bf16[2,256,448]{2,1,0:T(8,128)(2,1)S(1)} %get-tuple-element.38), channel_id=1, source_target_pairs={{0,2},{2,0},{1,3},{3,1},{4,6},{6,4},{5,7},{7,5},{8,10},{10,8},{9,1... | collective-permute-start | bytes 1376264 | tf_op jit(solution)/shard_map/ppermute | solution.py:19
  199.1 25.2 %collective-permute-start.29 = (bf16[2,256,448]{2,1,0:T(8,128)(2,1)S(1)}, bf16[2,256,448]{2,1,0:T(8,128)(2,1)S(1)}, u32[]{:S(2)}, u32[]{:S(2)}) collective-permute-start(bf16[2,256,448]{2,1,0:T(8,128)(2,1)S(1)} %get-tuple-element.36), channel_id=1, source_target_pairs={{0,2},{2,0},{1,3},{3,1},{4,6},{6,4},{5,7},{7,5},{8,10},{10,8},{9,1... | collective-permute-start | bytes 1376264 | tf_op jit(solution)/shard_map/ppermute | solution.py:19
  213.8 10.6 %collective-permute-start.31 = (bf16[2,256,448]{2,1,0:T(8,128)(2,1)S(1)}, bf16[2,256,448]{2,1,0:T(8,128)(2,1)S(1)}, u32[]{:S(2)}, u32[]{:S(2)}) collective-permute-start(bf16[2,256,448]{2,1,0:T(8,128)(2,1)S(1)} %add_convert_fusion), channel_id=1, source_target_pairs={{0,1},{1,0},{2,3},{3,2},{4,5},{5,4},{6,7},{7,6},{8,9},{9,8},{10,11... | collective-permute-start | bytes 1376264 | tf_op jit(solution)/shard_map/ppermute | solution.py:19
  (11 other events, 127.7 us)

commit v2 on v1

--- a/solution.py
+++ b/solution.py
@@ -84,9 +84,13 @@
     )(place, tokens, norm_gain, mod[:, None])
 
 
-def partial_kernel(counts, place, mod_ref, w_kv, w_q, *rest):
+def partial_kernel(counts, narrow, place, mod_ref, w_kv, w_q, *rest):
     total = sum(counts)
-    refs, kv_ref, q_ref, both = rest[:total], rest[total], rest[total + 1], rest[total + 2]
+    refs, outs, (both, held_kv, held_q, arrived) = rest[:total], rest[total:-4], rest[-4:]
+    copies = []
+    for i, (weight, held) in enumerate(((w_kv, held_kv), (w_q, held_q))):
+        copies.append(pltpu.make_async_copy(weight, held, arrived.at[i]))
+        copies[-1].start()
     length, width = both.shape[0] // len(counts), both.shape[1]
     at = 0
     for number, count in enumerate(counts):
@@ -102,27 +106,38 @@
     generate = mod_ref[...] == 1
     zero = jnp.zeros_like(block)
     first, second = jnp.where(generate, zero, block), jnp.where(generate, block, zero)
-    for weight, out in ((w_kv, kv_ref), (w_q, q_ref)):
-        out[...] = jnp.dot(first, weight[:width], preferred_element_type=jnp.float32) + jnp.dot(
-            second, weight[width:], preferred_element_type=jnp.float32
+    for i, held in enumerate((held_kv, held_q)):
+        copies[i].wait()
+        value = jnp.dot(first, held[:width], preferred_element_type=jnp.float32) + jnp.dot(
+            second, held[width:], preferred_element_type=jnp.float32
         )
-
-
-def partial(blocks, mods, w_kv, w_q, place):
+        outs[i][...] = value
+        if narrow:
+            outs[2 + i][...] = value.astype(jnp.bfloat16)
+
+
+def partial(blocks, mods, w_kv, w_q, place, narrow):
     counts = tuple(len(block) for block in blocks)
     arrays = [array for block in blocks for array in block]
     length = mods[0].shape[0]
     rows, width = length * len(blocks), arrays[0].shape[1]
     kv_cols, q_cols = w_kv.shape[1], w_q.shape[1]
-    kv, q = pl.pallas_call(
-        functools.partial(partial_kernel, counts),
-        out_shape=(
-            jax.ShapeDtypeStruct((rows, kv_cols), jnp.float32),
-            jax.ShapeDtypeStruct((rows, q_cols), jnp.float32),
-        ),
-        in_specs=[SMEM] + [VMEM] * (3 + len(arrays)),
-        out_specs=(VMEM, VMEM),
-        scratch_shapes=[pltpu.VMEM((rows, width), jnp.bfloat16)],
+    shapes = [
+        jax.ShapeDtypeStruct((rows, cols), dtype)
+        for dtype in (jnp.float32, jnp.bfloat16)[: 1 + narrow]
+        for cols in (kv_cols, q_cols)
+    ]
+    values = pl.pallas_call(
+        functools.partial(partial_kernel, counts, narrow),
+        out_shape=shapes,
+        in_specs=[SMEM, VMEM, ANY, ANY] + [VMEM] * len(arrays),
+        out_specs=[VMEM] * len(shapes),
+        scratch_shapes=[
+            pltpu.VMEM((rows, width), jnp.bfloat16),
+            pltpu.VMEM(w_kv.shape, jnp.bfloat16),
+            pltpu.VMEM(w_q.shape, jnp.bfloat16),
+            pltpu.SemaphoreType.DMA((2,)),
+        ],
         cost_estimate=pl.CostEstimate(
             flops=4 * rows * width * (kv_cols + q_cols),
             bytes_accessed=4 * (width + rows) * (kv_cols + q_cols),
@@ -131,32 +146,37 @@
         compiler_params=pltpu.CompilerParams(vmem_limit_bytes=40 * 1024 * 1024),
         name="partial",
     )(place, jnp.concatenate(mods)[:, None], w_kv, w_q, *arrays)
-    shape = (len(blocks), length, -1)
-    return kv.reshape(shape), q.reshape(shape)
-
-
-def reduce_scatter(parts, split):
+    return [value.reshape(len(blocks), length, -1) for value in values]
+
+
+def halving(parts):
     n = len(parts)
-    if n != 4:
-        sums = dict(enumerate(parts))
-        for bit in [1 << i for i in range(n.bit_length() - 1)]:
-            for d in [d for d in range(n) if d in sums and d & bit]:
-                sums[d ^ bit] = sums[d ^ bit] + cross(sums.pop(d).astype(jnp.bfloat16), "seq", bit)
-        return sums[0].astype(jnp.bfloat16)
-
-    def send(pieces, bit, among):
-        if split:
-            got = []
-            for piece in pieces:
-                got.append(cross(piece.astype(jnp.bfloat16), "seq", bit, among))
-            return [g.astype(jnp.float32) for g in got]
-        got = cross(jnp.stack(pieces).astype(jnp.bfloat16), "seq", bit, among)
-        return [got[i].astype(jnp.float32) for i in range(len(pieces))]
-
-    far, two = send([parts[3], parts[2]], 1, (1, 2))
-    across, own = send([parts[2] + far, parts[3] + two], 3, (1, 2))
-    last = cross((parts[1] + across).astype(jnp.bfloat16), "seq", 1)
-    return (parts[0] + last.astype(jnp.float32) + own).astype(jnp.bfloat16)
+    sums = dict(enumerate(parts))
+    for bit in [1 << i for i in range(n.bit_length() - 1)]:
+        for d in [d for d in range(n) if d in sums and d & bit]:
+            sums[d ^ bit] = sums[d ^ bit] + cross(sums.pop(d).astype(jnp.bfloat16), "seq", bit)
+    return sums[0].astype(jnp.bfloat16)
+
+
+def along_four(parts, three, two):
+    wide = [p.astype(jnp.float32) for p in parts]
+
+    def hop(value, bit, among):
+        return cross(value, "seq", bit, among).astype(jnp.float32)
+
+    if two is None:
+        got = hop(three, 1, (1, 2))
+        send = (jnp.stack([wide[2], wide[3]]) + got).astype(jnp.bfloat16)
+        got = hop(send, 3, (1, 2))
+        across, own = got[0], got[1]
+    else:
+        far = hop(three, 1, (1, 2))
+        close = hop(two, 1, (1, 2))
+        send = (wide[2] + far).astype(jnp.bfloat16)
+        across = hop(send, 3, (1, 2))
+        own = hop((wide[3] + after(close, send)).astype(jnp.bfloat16), 3, (1, 2))
+    last = hop((wide[1] + across).astype(jnp.bfloat16), 1, None)
+    return (wide[0] + last + own).astype(jnp.bfloat16)
 
 
 def gather_weights(mine):
@@ -272,9 +292,9 @@
 
 
 def project_kernel(turns, place, ours_ref, beside_ref, ours_near, beside_near, own_ref, *rest):
-    n = (len(rest) - 4) // 2 + 1
+    n = (len(rest) - 5) // 2 + 1
     near, far = rest[: n - 1], rest[n - 1 : 2 * n - 2]
-    o_ours, o_beside, held, arrived = rest[2 * n - 2 :]
+    o_ours, o_beside, held, lhs, arrived = rest[2 * n - 2 :]
     count = turns.shape[0]
     first = place[2]
 
@@ -292,21 +312,25 @@
         fetch(near[d - 1] if d else own_ref.at[first], 0, d)
         fetch(far[d - 1] if d else own_ref.at[1 - first], 1, d)
 
-    contract = (((1,), (1,)), ((), ()))
-    halves = []
-    for a_ref, near_ref, o_ref in ((ours_ref, ours_near, o_ours), (beside_ref, beside_near, o_beside)):
+    rows = ours_ref.shape[0]
+    for base, a_ref, near_ref in ((0, ours_ref, ours_near), (rows, beside_ref, beside_near)):
         a = a_ref[...]
         mine = near_ref[...] != 0
         zero = jnp.zeros_like(a)
-        halves.append((jnp.where(mine, a, zero), jnp.where(mine, zero, a), o_ref))
+        lhs[0, base : base + rows] = jnp.where(mine, a, zero)
+        lhs[1, base : base + rows] = jnp.where(mine, zero, a)
+    contract = (((1,), (1,)), ((), ()))
     for i in range(count):
+        value = None
         for kind in range(2):
             pltpu.make_async_copy(own_ref.at[0], held.at[kind, i], arrived.at[kind, i]).wait()
-        for a_near, a_far, o_ref in halves:
-            o_ref[i] = (
-                lax.dot_general(a_near, held[0, i], contract, preferred_element_type=jnp.float32)
-                + lax.dot_general(a_far, held[1, i], contract, preferred_element_type=jnp.float32)
-            ).astype(jnp.bfloat16)
+            term = lax.dot_general(
+                lhs[kind], held[kind, i], contract, preferred_element_type=jnp.float32
+            )
+            value = term if value is None else value + term
+        value = value.astype(jnp.bfloat16)
+        o_ours[i] = value[:rows]
+        o_beside[i] = value[rows:]
 
 
 def project(ours, beside, ours_near, beside_near, weights, turns, place):
@@ -321,6 +345,7 @@
         out_specs=(VMEM, VMEM),
         scratch_shapes=[
             pltpu.VMEM((2, count, width, depth), jnp.bfloat16),
+            pltpu.VMEM((2, 2 * rows, depth), jnp.bfloat16),
             pltpu.SemaphoreType.DMA((2, count)),
         ],
         cost_estimate=pl.CostEstimate(
@@ -362,6 +387,8 @@
     for d in range(n - 1, 0, -1):
         blocks[d] = (cross(sends[d], "seq", d),)
 
+    w_query, w_key, w_value = after((w_query, w_key, w_value), sends[0])
+
     def share(weight):
         other = swap(weight, "sub")
         both = jnp.where(
@@ -382,26 +409,28 @@
     for d in range(1, n):
         blocks[d] = after(blocks[d], w_kv_all, w_q_all, low, high)
 
-    early = list(range(n - 1, 1, -1))
     if share_rows:
-        for group in (early, [1]):
-            held = jnp.stack([blocks[d][0] for d in group])
-            other = swap(held, "head")
-            for i, d in enumerate(group):
-                blocks[d] = (blocks[d][0], other[i])
-    parts = {}
-    for group in (early, [1, 0]):
-        kv, q = partial(
-            [blocks[d] for d in group],
-            [part_of(modality, z ^ d, s) for d in group],
-            w_kv_all,
-            w_q_all,
-            place,
-        )
-        for i, d in enumerate(group):
-            parts[d] = kv[i], q[i]
-    kv = reduce_scatter([parts[d][0] for d in range(n)], False)
-    query = reduce_scatter([parts[d][1] for d in range(n)], True)
+        for d in range(n - 1, 0, -1):
+            blocks[d] = (*blocks[d], swap(blocks[d][0], "head"))
+
+    def parts_of(group, narrow):
+        mods = [part_of(modality, z ^ d, s) for d in group]
+        return partial([blocks[d] for d in group], mods, w_kv_all, w_q_all, place, narrow)
+
+    if n == 4:
+        kv_early, q_early, kv_rounded, q_rounded = parts_of([3, 2], True)
+        kv_ends, q_three, q_two = kv_rounded, q_rounded[0], q_rounded[1]
+        kv_late, q_late = parts_of([1, 0], False)
+        kv_early, q_early = after((kv_early, q_early), kv_late, q_late)
+        kv = along_four([kv_late[1], kv_late[0], kv_early[1], kv_early[0]], kv_ends, None)
+        query = along_four([q_late[1], q_late[0], q_early[1], q_early[0]], q_three, q_two)
+    else:
+        kv_parts, q_parts = [], []
+        for d in range(n):
+            kv_part, q_part = parts_of([d], False)
+            kv_parts.append(kv_part[0])
+            q_parts.append(q_part[0])
+        kv, query = halving(kv_parts), halving(q_parts)
 
     same = [kv]
     for d in range(1, n):

time: 227 us -> 240 us (1.057)
  waiting for transfers between devices: 103 us -> 121 us
  local copies, waits for them, and re-layouts: 14.9 us -> 10.2 us
  other arithmetic: 19.5 us -> 16.6 us
    ppermute x19, waiting for transfers between devices: 81.6 us -> 95.8 us  [cross(): return lax.ppermute(x, axis, [(i ^ bit, i) for i in among or range(size)])]
    ppermute x13 -> x14, waiting for transfers between devices: 21.7 us -> 25.7 us  [swap(): return lax.ppermute(x, axis, [(0, 1), (1, 0)])]
    select_n x2, other arithmetic: 8.93 us -> 5.79 us  [share(): jnp.where(s == 0, jnp.concatenate([weight, other], axis=1), jnp.concatena...]
    ppermute x13 -> x14, starting transfers between devices: 20.6 us -> 19.2 us  [swap(): return lax.ppermute(x, axis, [(0, 1), (1, 0)])]
  transfers between devices with their start and end apart: 32 -> 33, of which waited for: 16 -> 17; matrix products, arithmetic and copies ran while one was open for 12% -> 9% of each run, Pallas kernels for 12% -> 12%
where the time goes in v2:
time: 240 us; the launch traced here: 239 us
  waiting for transfers between devices  121 us (50%)
  starting transfers between devices  54 us (22%)
  Pallas kernels  34 us (14%)
  other arithmetic  16.6 us (7%)
  local copies, waits for them, and re-layouts  10.2 us (4%)
  between operations  2.68 us (1%)
    ppermute x19, waiting for transfers between devices, cross(): return lax.ppermute(x, axis, [(i ^ bit, i) for i in among or range(size)])  95.8 us
    ppermute x19, starting transfers between devices, cross(): return lax.ppermute(x, axis, [(i ^ bit, i) for i in among or range(size)])  34.8 us
    ppermute x14, waiting for transfers between devices, swap(): return lax.ppermute(x, axis, [(0, 1), (1, 0)])  25.7 us
    ppermute x14, starting transfers between devices, swap(): return lax.ppermute(x, axis, [(0, 1), (1, 0)])  19.2 us
    pallas_call x1, Pallas kernels, attend(): pl.pallas_call(attention_kernel, out_shape=jax.ShapeDtypeStruct((rows, wi...  13.1 us
    pallas_call x2, Pallas kernels, project(): pl.pallas_call(project_kernel, out_shape=(shape, shape), in_specs=[SMEM,...  9.69 us
    pallas_call x2, Pallas kernels, partial(): pl.pallas_call(functools.partial(partial_kernel, counts, narrow), out_sha...  9.52 us
    select_n x2, other arithmetic, share(): jnp.where(s == 0, jnp.concatenate([weight, other], axis=1), jnp.concatena...  5.79 us
  transfers between devices with their start and end apart: 33, of which 17 were waited for; matrix products, arithmetic and copies ran while one was open for 9% of the time, Pallas kernels for 12%

profile of v2, /device:TPU:22, one launch (start us, length us, event | category | flops | bytes accessed | tf_op | source)
XLA Modules:
  0.0 238.9 jit_solution(14979271545849219970)
XLA Ops:
  0.0 2.3 dynamic-slice_bitcast_fusion
  18.6 7.3 %collective-permute-done.22.rest_0_ = bf16[448,1024]{1,0:T(8,128)(2,1)} collective-permute-done((bf16[448,1024]{1,0:T(8,128)(2,1)}, bf16[448,1024]{1,0:T(8,128)(2,1)}, u32[]{:S(2)}, u32[]{:S(2)}) %collective-permute-start.22) | collective-permute-done | bytes 917536 | tf_op jit(solution)/shard_map/ppermute | solution.py:24
  25.8 2.3 collective-permute-start.23
  28.2 6.0 %collective-permute-done.24 = bf16[448,1024]{1,0:T(8,128)(2,1)} collective-permute-done((bf16[448,1024]{1,0:T(8,128)(2,1)}, bf16[448,1024]{1,0:T(8,128)(2,1)}, u32[]{:S(2)}, u32[]{:S(2)}) %collective-permute-start.24) | collective-permute-done | bytes 917536 | tf_op jit(solution)/shard_map/ppermute | solution.py:24
  34.2 2.2 collective-permute-start.25
  43.6 4.0 %maximum_select_fusion = bf16[2,896,1024]{2,1,0:T(8,128)(2,1)S(1)} fusion(bf16[2,448,1024]{2,1,0:T(8,128)(2,1)} %collective-permute-done.1, bf16[2,448,1024]{2,1,0:T(8,128)(2,1)S(1)} %copy-done.5, pred[]{:T(512)S(6)} %eq.24), kind=kLoop, calls=%fused_computation | loop fusion | flops 16515072 | bytes 7340033 | tf_op jit(solution)/shard_map/jit(_where)/select_n | solution.py:394
  48.2 16.7 %collective-permute-done.6.rest_2_ = bf16[128,896]{1,0:T(8,128)(2,1)S(1)} collective-permute-done((bf16[128,896]{1,0:T(8,128)(2,1)S(1)}, bf16[128,896]{1,0:T(8,128)(2,1)S(1)}, u32[]{:S(2)}, u32[]{:S(2)}) %collective-permute-start.6) | collective-permute-done | bytes 229408 | tf_op jit(solution)/shard_map/ppermute | solution.py:24
  69.3 4.0 %collective-permute-done.5.rest_1_ = bf16[128,896]{1,0:T(8,128)(2,1)S(1)} collective-permute-done((bf16[128,896]{1,0:T(8,128)(2,1)S(1)}, bf16[128,896]{1,0:T(8,128)(2,1)S(1)}, u32[]{:S(2)}, u32[]{:S(2)}) %collective-permute-start.5) | collective-permute-done | bytes 229408 | tf_op jit(solution)/shard_map/ppermute | solution.py:19
  73.4 5.6 %collective-permute-start.26 = (bf16[448,1024]{1,0:T(8,128)(2,1)}, bf16[448,1024]{1,0:T(8,128)(2,1)S(1)}, u32[]{:S(2)}, u32[]{:S(2)}) collective-permute-start(bf16[448,1024]{1,0:T(8,128)(2,1)} %collective-permute-done.23), channel_id=1, source_target_pairs={{4,0},{8,12},{5,1},{9,13},{6,2},{10,14},{7,3},{11,15},{20,16},{24,... | collective-permute-start | bytes 2752520 | tf_op jit(solution)/shard_map/ppermute | solution.py:24
  79.0 4.8 %partial.3 = (f32[512,512]{1,0:T(8,128)S(1)}, f32[512,1024]{1,0:T(8,128)S(1)}, bf16[512,512]{1,0:T(8,128)(2,1)S(1)}, bf16[512,1024]{1,0:T(8,128)(2,1)S(1)}) custom-call(s32[3]{0:T(128)S(1)} %pad_add_fusion.2.place, s32[512,1]{1,0:T(8,128)S(1)} %copy.22.mod_ref, bf16[1792,512]{1,0:T(8,128)(2,1)S(1)} %bitcast.74, bf16[1792,1024]{1,0:T(8,128)(2,1)S(1)} %bitcast.70, ...), custom_call_target="tpu_custom_call" | custom-call | flops 2818572288 | bytes 8650752 | tf_op jit(solution)/shard_map/partial/pallas_call | solution.py:130
  86.6 4.8 %partial.2 = (f32[512,512]{1,0:T(8,128)S(1)}, f32[512,1024]{1,0:T(8,128)S(1)}) custom-call(s32[3]{0:T(128)S(1)} %pad_add_fusion.2.place, s32[512,1]{1,0:T(8,128)S(1)} %copy.21.mod_ref, bf16[1792,512]{1,0:T(8,128)(2,1)S(1)} %bitcast.75, bf16[1792,1024]{1,0:T(8,128)(2,1)S(1)} %bitcast.71, bf16[128,896]{1,0:T(8,128)(2,1)S(1)} %collective-permute-done.2.rest_0_, ...), custom_call_target="tpu_custom_call" | custom-call | flops 2818572288 | bytes 8650752 | tf_op jit(solution)/shard_map/partial/pallas_call | solution.py:130
  91.5 9.5 %collective-permute-done.8 = bf16[256,1024]{1,0:T(8,128)(2,1)S(1)} collective-permute-done((bf16[256,1024]{1,0:T(8,128)(2,1)S(1)}, bf16[256,1024]{1,0:T(8,128)(2,1)S(1)}, u32[]{:S(2)}, u32[]{:S(2)}) %collective-permute-start.8) | collective-permute-done | bytes 524320 | tf_op jit(solution)/shard_map/ppermute | solution.py:24
  102.4 9.8 %collective-permute-done.13 = bf16[2,256,512]{2,1,0:T(8,128)(2,1)S(1)} collective-permute-done((bf16[2,256,512]{2,1,0:T(8,128)(2,1)S(1)}, bf16[2,256,512]{2,1,0:T(8,128)(2,1)S(1)}, u32[]{:S(2)}, u32[]{:S(2)}) %collective-permute-start.13) | collective-permute-done | bytes 524320 | tf_op jit(solution)/shard_map/ppermute | solution.py:24
  112.2 2.6 %collective-permute-start.9 = (bf16[256,1024]{1,0:T(8,128)(2,1)S(1)}, bf16[256,1024]{1,0:T(8,128)(2,1)S(1)}, u32[]{:S(2)}, u32[]{:S(2)}) collective-permute-start(bf16[256,1024]{1,0:T(8,128)(2,1)S(1)} %fusion.3), channel_id=1, source_target_pairs={{8,4},{4,8},{9,5},{5,9},{10,6},{6,10},{11,7},{7,11},{24,20},{20,24... | collective-permute-start | bytes 1572872 | tf_op jit(solution)/shard_map/ppermute | solution.py:24
  115.1 3.4 %collective-permute-done.11 = bf16[256,1024]{1,0:T(8,128)(2,1)S(1)} collective-permute-done((bf16[256,1024]{1,0:T(8,128)(2,1)S(1)}, bf16[256,1024]{1,0:T(8,128)(2,1)S(1)}, u32[]{:S(2)}, u32[]{:S(2)}) %collective-permute-start.11) | collective-permute-done | bytes 524320 | tf_op jit(solution)/shard_map/ppermute | solution.py:24
  118.6 2.8 %collective-permute-start.14 = (bf16[2,256,512]{2,1,0:T(8,128)(2,1)S(1)}, bf16[2,256,512]{2,1,0:T(8,128)(2,1)S(1)}, u32[]{:S(2)}, u32[]{:S(2)}) collective-permute-start(bf16[2,256,512]{2,1,0:T(8,128)(2,1)S(1)} %fusion), channel_id=1, source_target_pairs={{8,4},{4,8},{9,5},{5,9},{10,6},{6,10},{11,7},{7,11},{24,20},{20,24... | collective-permute-start | bytes 1572872 | tf_op jit(solution)/shard_map/ppermute | solution.py:24
  121.5 6.9 %collective-permute-done.9 = bf16[256,1024]{1,0:T(8,128)(2,1)S(1)} collective-permute-done((bf16[256,1024]{1,0:T(8,128)(2,1)S(1)}, bf16[256,1024]{1,0:T(8,128)(2,1)S(1)}, u32[]{:S(2)}, u32[]{:S(2)}) %collective-permute-start.9) | collective-permute-done | bytes 524320 | tf_op jit(solution)/shard_map/ppermute | solution.py:24
  128.4 2.5 %collective-permute-start.12 = (bf16[256,1024]{1,0:T(8,128)(2,1)S(1)}, bf16[256,1024]{1,0:T(8,128)(2,1)S(1)}, u32[]{:S(2)}, u32[]{:S(2)}) collective-permute-start(bf16[256,1024]{1,0:T(8,128)(2,1)S(1)} %fusion.2), channel_id=1, source_target_pairs={{8,4},{4,8},{9,5},{5,9},{10,6},{6,10},{11,7},{7,11},{24,20},{20,24... | collective-permute-start | bytes 1572872 | tf_op jit(solution)/shard_map/ppermute | solution.py:24
  131.1 8.5 %collective-permute-done.14 = bf16[2,256,512]{2,1,0:T(8,128)(2,1)S(1)} collective-permute-done((bf16[2,256,512]{2,1,0:T(8,128)(2,1)S(1)}, bf16[2,256,512]{2,1,0:T(8,128)(2,1)S(1)}, u32[]{:S(2)}, u32[]{:S(2)}) %collective-permute-start.14) | collective-permute-done | bytes 524320 | tf_op jit(solution)/shard_map/ppermute | solution.py:24
  139.9 2.1 collective-permute-start.15
  142.0 2.2 broadcast_select_fusion.rest_2_
  144.2 15.6 %collective-permute-done.15 = bf16[256,512]{1,0:T(8,128)(2,1)S(1)} collective-permute-done((bf16[256,512]{1,0:T(8,128)(2,1)S(1)}, bf16[256,512]{1,0:T(8,128)(2,1)S(1)}, u32[]{:S(2)}, u32[]{:S(2)}) %collective-permute-start.15) | collective-permute-done | bytes 262176 | tf_op jit(solution)/shard_map/ppermute | solution.py:24
  161.5 2.1 collective-permute-start.18
  163.8 2.6 %collective-permute-done.16 = bf16[256,512]{1,0:T(8,128)(2,1)S(1)} collective-permute-done((bf16[256,512]{1,0:T(8,128)(2,1)S(1)}, bf16[256,512]{1,0:T(8,128)(2,1)S(1)}, u32[]{:S(2)}, u32[]{:S(2)}) %collective-permute-start.16) | collective-permute-done | bytes 262176 | tf_op jit(solution)/shard_map/ppermute | solution.py:24
  168.7 7.6 %collective-permute-done.18 = bf16[256,512]{1,0:T(8,128)(2,1)S(1)} collective-permute-done((bf16[256,512]{1,0:T(8,128)(2,1)S(1)}, bf16[256,512]{1,0:T(8,128)(2,1)S(1)}, u32[]{:S(2)}, u32[]{:S(2)}) %collective-permute-start.18) | collective-permute-done | bytes 262176 | tf_op jit(solution)/shard_map/ppermute | solution.py:24
  176.6 2.2 collective-permute-done.20
  178.8 13.1 %attend.1.ours_ref = bf16[256,1024]{1,0:T(8,128)(2,1)S(1)} custom-call(s32[8]{0:T(128)S(1)} %stack.89.starts, s32[2]{0:T(128)S(1)} %pad_add_fusion.3.limits, bf16[256,1024]{1,0:T(8,128)(2,1)S(1)} %add_convert_fusion.2.q_ref, bf16[8,256,512]{2,1,0:T(8,128)(2,1)S(1)} %constant_dynamic-update-slice_fusion.kv_ref, s32[256,1]{1,0:T(8,128)S(1)} %copy.23.low_ref, ...), custom_call_target="tpu_custom_call" | custom-call | flops 2147483648 | bytes 3145728 | tf_op jit(solution)/shard_map/attend/pallas_call | solution.py:274
  191.9 12.3 %collective-permute-start.21 = (bf16[256,1024]{1,0:T(8,128)(2,1)S(1)}, bf16[256,1024]{1,0:T(8,128)(2,1)}, u32[]{:S(2)}, u32[]{:S(2)}) collective-permute-start(bf16[256,1024]{1,0:T(8,128)(2,1)S(1)} %attend.1.ours_ref), channel_id=1, source_target_pairs={{0,1},{1,0},{2,3},{3,2},{4,5},{5,4},{6,7},{7,6},{8,9},{9,8},{10,11... | collective-permute-start | bytes 1572872 | tf_op jit(solution)/shard_map/ppermute | solution.py:19
  205.8 5.2 %project.3 = (bf16[2,256,448]{2,1,0:T(8,128)(2,1)S(1)}, bf16[2,256,448]{2,1,0:T(8,128)(2,1)S(1)}) custom-call(s32[2]{0:T(128)S(1)} %get-tuple-element.70.turns, s32[3]{0:T(128)S(1)} %pad_add_fusion.2.place, bf16[256,1024]{1,0:T(8,128)(2,1)S(1)} %attend.1.ours_ref, bf16[256,1024]{1,0:T(8,128)(2,1)} %collective-permute-done.21.beside_ref, ...), custom_call_target="tpu_custom_call" | custom-call | flops 1879048192 | bytes 4587520 | tf_op jit(solution)/shard_map/project/pallas_call | solution.py:341
  213.1 4.5 %project.2 = (bf16[2,256,448]{2,1,0:T(8,128)(2,1)S(1)}, bf16[2,256,448]{2,1,0:T(8,128)(2,1)S(1)}) custom-call(s32[2]{0:T(128)S(1)} %get-tuple-element.71.turns, s32[3]{0:T(128)S(1)} %pad_add_fusion.2.place, bf16[256,1024]{1,0:T(8,128)(2,1)S(1)} %attend.1.ours_ref, bf16[256,1024]{1,0:T(8,128)(2,1)} %collective-permute-done.21.beside_ref, ...), custom_call_target="tpu_custom_call" | custom-call | flops 1879048192 | bytes 4587520 | tf_op jit(solution)/shard_map/project/pallas_call | solution.py:341
  217.6 8.3 %collective-permute-done.31 = bf16[2,256,448]{2,1,0:T(8,128)(2,1)S(1)} collective-permute-done((bf16[2,256,448]{2,1,0:T(8,128)(2,1)S(1)}, bf16[2,256,448]{2,1,0:T(8,128)(2,1)S(1)}, u32[]{:S(2)}, u32[]{:S(2)}) %collective-permute-start.31) | collective-permute-done | bytes 458784 | tf_op jit(solution)/shard_map/ppermute | solution.py:19
  226.1 10.4 %collective-permute-done.30 = bf16[2,256,448]{2,1,0:T(8,128)(2,1)S(1)} collective-permute-done((bf16[2,256,448]{2,1,0:T(8,128)(2,1)S(1)}, bf16[2,256,448]{2,1,0:T(8,128)(2,1)S(1)}, u32[]{:S(2)}, u32[]{:S(2)}) %collective-permute-start.30) | collective-permute-done | bytes 458784 | tf_op jit(solution)/shard_map/ppermute | solution.py:19
  (115 shorter events, 42.0 us)
Async XLA Ops:
  2.3 23.5 %collective-permute-start.22 = (bf16[448,1024]{1,0:T(8,128)(2,1)}, bf16[448,1024]{1,0:T(8,128)(2,1)}, u32[]{:S(2)}, u32[]{:S(2)}) collective-permute-start(bf16[448,1024]{1,0:T(8,128)(2,1)} %dynamic-slice_bitcast_fusion), channel_id=1, source_target_pairs={{4,0},{0,4},{12,8},{8,12},{5,1},{1,5},{13,9},{9,13},{6,2},{2,6},{1... | collective-permute-start | bytes 2752520 | tf_op jit(solution)/shard_map/ppermute | solution.py:24
  3.9 30.3 %collective-permute-start.24 = (bf16[448,1024]{1,0:T(8,128)(2,1)}, bf16[448,1024]{1,0:T(8,128)(2,1)}, u32[]{:S(2)}, u32[]{:S(2)}) collective-permute-start(bf16[448,1024]{1,0:T(8,128)(2,1)} %dynamic-slice_bitcast_fusion), channel_id=1, source_target_pairs={{8,4},{4,8},{9,5},{5,9},{10,6},{6,10},{11,7},{7,11},{24,20},{20,24... | collective-permute-start | bytes 2752520 | tf_op jit(solution)/shard_map/ppermute | solution.py:24
  9.8 32.3 %collective-permute-start.1 = (bf16[2,448,1024]{2,1,0:T(8,128)(2,1)}, bf16[2,448,1024]{2,1,0:T(8,128)(2,1)}, u32[]{:S(2)}, u32[]{:S(2)}) collective-permute-start(bf16[2,448,1024]{2,1,0:T(8,128)(2,1)} %param.10), channel_id=1, source_target_pairs={{0,1},{1,0},{2,3},{3,2},{4,5},{5,4},{6,7},{7,6},{8,9},{9,8},{10,11... | collective-permute-start | bytes 5505032 | tf_op jit(solution)/shard_map/ppermute | solution.py:19
  12.1 28.1 %collective-permute-start = (bf16[2,448,512]{2,1,0:T(8,128)(2,1)}, bf16[2,448,512]{2,1,0:T(8,128)(2,1)}, u32[]{:S(2)}, u32[]{:S(2)}) collective-permute-start(bf16[2,448,512]{2,1,0:T(8,128)(2,1)} %pad_maximum_fusion), channel_id=1, source_target_pairs={{0,1},{1,0},{2,3},{3,2},{4,5},{5,4},{6,7},{7,6},{8,9},{9,8},{10,11... | collective-permute-start | bytes 2752520 | tf_op jit(solution)/shard_map/ppermute | solution.py:19
  12.5 35.1 %collective-permute-start.4 = (bf16[128,896]{1,0:T(8,128)(2,1)S(1)}, bf16[128,896]{1,0:T(8,128)(2,1)S(1)}, u32[]{:S(2)}, u32[]{:S(2)}) collective-permute-start(bf16[128,896]{1,0:T(8,128)(2,1)S(1)} %get-tuple-element.39), channel_id=1, source_target_pairs={{12,0},{8,4},{4,8},{0,12},{13,1},{9,5},{5,9},{1,13},{14,2},{10,6},... | collective-permute-start | bytes 688136 | tf_op jit(solution)/shard_map/ppermute | solution.py:24
  25.8 41.1 %collective-permute-start.23 = (bf16[448,1024]{1,0:T(8,128)(2,1)}, bf16[448,1024]{1,0:T(8,128)(2,1)}, u32[]{:S(2)}, u32[]{:S(2)}) collective-permute-start(bf16[448,1024]{1,0:T(8,128)(2,1)} %collective-permute-done.22.rest_0_), channel_id=1, source_target_pairs={{8,4},{4,8},{9,5},{5,9},{10,6},{6,10},{11,7},{7,11},{24,20},{20,24... | collective-permute-start | bytes 2752520 | tf_op jit(solution)/shard_map/ppermute | solution.py:24
  34.2 33.3 %collective-permute-start.25 = (bf16[448,1024]{1,0:T(8,128)(2,1)}, bf16[448,1024]{1,0:T(8,128)(2,1)}, u32[]{:S(2)}, u32[]{:S(2)}) collective-permute-start(bf16[448,1024]{1,0:T(8,128)(2,1)} %collective-permute-done.24), channel_id=1, source_target_pairs={{4,0},{8,12},{5,1},{9,13},{6,2},{10,14},{7,3},{11,15},{20,16},{24,... | collective-permute-start | bytes 2752520 | tf_op jit(solution)/shard_map/ppermute | solution.py:24
  40.2 24.7 %collective-permute-start.6 = (bf16[128,896]{1,0:T(8,128)(2,1)S(1)}, bf16[128,896]{1,0:T(8,128)(2,1)S(1)}, u32[]{:S(2)}, u32[]{:S(2)}) collective-permute-start(bf16[128,896]{1,0:T(8,128)(2,1)S(1)} %get-tuple-element.41), channel_id=1, source_target_pairs={{8,0},{12,4},{0,8},{4,12},{9,1},{13,5},{1,9},{5,13},{10,2},{14,6},... | collective-permute-start | bytes 688136 | tf_op jit(solution)/shard_map/ppermute | solution.py:24
  42.1 23.4 %collective-permute-start.2 = (bf16[128,896]{1,0:T(8,128)(2,1)S(1)}, bf16[128,896]{1,0:T(8,128)(2,1)S(1)}, u32[]{:S(2)}, u32[]{:S(2)}) collective-permute-start(bf16[128,896]{1,0:T(8,128)(2,1)S(1)} %get-tuple-element.36), channel_id=1, source_target_pairs={{4,0},{0,4},{12,8},{8,12},{5,1},{1,5},{13,9},{9,13},{6,2},{2,6},{1... | collective-permute-start | bytes 688136 | tf_op jit(solution)/shard_map/ppermute | solution.py:24
  47.6 157.4 %collective-permute-start.27 = (bf16[448,1024]{1,0:T(8,128)(2,1)}, bf16[448,1024]{1,0:T(8,128)(2,1)}, u32[]{:S(2)}, u32[]{:S(2)}) collective-permute-start(bf16[448,1024]{1,0:T(8,128)(2,1)} %collective-permute-done.22.rest_0_), channel_id=1, source_target_pairs={{0,16},{16,0},{1,17},{17,1},{2,18},{18,2},{3,19},{19,3},{4,20},{20... | collective-permute-start | bytes 2752520 | tf_op jit(solution)/shard_map/ppermute | solution.py:19
  64.9 8.5 %collective-permute-start.5 = (bf16[128,896]{1,0:T(8,128)(2,1)S(1)}, bf16[128,896]{1,0:T(8,128)(2,1)S(1)}, u32[]{:S(2)}, u32[]{:S(2)}) collective-permute-start(bf16[128,896]{1,0:T(8,128)(2,1)S(1)} %collective-permute-done.4.rest_0_), channel_id=1, source_target_pairs={{0,2},{2,0},{1,3},{3,1},{4,6},{6,4},{5,7},{7,5},{8,10},{10,8},{9,1... | collective-permute-start | bytes 688136 | tf_op jit(solution)/shard_map/ppermute | solution.py:19
  65.5 13.5 %collective-permute-start.7 = (bf16[128,896]{1,0:T(8,128)(2,1)S(1)}, bf16[128,896]{1,0:T(8,128)(2,1)S(1)}, u32[]{:S(2)}, u32[]{:S(2)}) collective-permute-start(bf16[128,896]{1,0:T(8,128)(2,1)S(1)} %collective-permute-done.6.rest_2_), channel_id=1, source_target_pairs={{0,2},{2,0},{1,3},{3,1},{4,6},{6,4},{5,7},{7,5},{8,10},{10,8},{9,1... | collective-permute-start | bytes 688136 | tf_op jit(solution)/shard_map/ppermute | solution.py:19
  67.0 18.3 %collective-permute-start.3 = (bf16[128,896]{1,0:T(8,128)(2,1)S(1)}, bf16[128,896]{1,0:T(8,128)(2,1)S(1)}, u32[]{:S(2)}, u32[]{:S(2)}) collective-permute-start(bf16[128,896]{1,0:T(8,128)(2,1)S(1)} %collective-permute-done.2.rest_0_), channel_id=1, source_target_pairs={{0,2},{2,0},{1,3},{3,1},{4,6},{6,4},{5,7},{7,5},{8,10},{10,8},{9,1... | collective-permute-start | bytes 688136 | tf_op jit(solution)/shard_map/ppermute | solution.py:19
  68.8 136.3 %collective-permute-start.28 = (bf16[448,1024]{1,0:T(8,128)(2,1)S(1)}, bf16[448,1024]{1,0:T(8,128)(2,1)}, u32[]{:S(2)}, u32[]{:S(2)}) collective-permute-start(bf16[448,1024]{1,0:T(8,128)(2,1)S(1)} %broadcast_select_fusion.1.rest_1_), channel_id=1, source_target_pairs={{0,16},{16,0},{1,17},{17,1},{2,18},{18,2},{3,19},{19,3},{4,20},{20... | collective-permute-start | bytes 2752520 | tf_op jit(solution)/shard_map/ppermute | solution.py:19
  73.4 66.5 %collective-permute-start.26 = (bf16[448,1024]{1,0:T(8,128)(2,1)}, bf16[448,1024]{1,0:T(8,128)(2,1)S(1)}, u32[]{:S(2)}, u32[]{:S(2)}) collective-permute-start(bf16[448,1024]{1,0:T(8,128)(2,1)} %collective-permute-done.23), channel_id=1, source_target_pairs={{4,0},{8,12},{5,1},{9,13},{6,2},{10,14},{7,3},{11,15},{20,16},{24,... | collective-permute-start | bytes 2752520 | tf_op jit(solution)/shard_map/ppermute | solution.py:24
  83.9 17.1 %collective-permute-start.8 = (bf16[256,1024]{1,0:T(8,128)(2,1)S(1)}, bf16[256,1024]{1,0:T(8,128)(2,1)S(1)}, u32[]{:S(2)}, u32[]{:S(2)}) collective-permute-start(bf16[256,1024]{1,0:T(8,128)(2,1)S(1)} %get-tuple-element.63), channel_id=1, source_target_pairs={{0,4},{12,8},{1,5},{13,9},{2,6},{14,10},{3,7},{15,11},{16,20},{28,... | collective-permute-start | bytes 1572872 | tf_op jit(solution)/shard_map/ppermute | solution.py:24
  85.3 26.9 %collective-permute-start.13 = (bf16[2,256,512]{2,1,0:T(8,128)(2,1)S(1)}, bf16[2,256,512]{2,1,0:T(8,128)(2,1)S(1)}, u32[]{:S(2)}, u32[]{:S(2)}) collective-permute-start(bf16[2,256,512]{2,1,0:T(8,128)(2,1)S(1)} %bitcast.77), channel_id=1, source_target_pairs={{0,4},{12,8},{1,5},{13,9},{2,6},{14,10},{3,7},{15,11},{16,20},{28,... | collective-permute-start | bytes 1572872 | tf_op jit(solution)/shard_map/ppermute | solution.py:24
  101.0 17.5 %collective-permute-start.11 = (bf16[256,1024]{1,0:T(8,128)(2,1)S(1)}, bf16[256,1024]{1,0:T(8,128)(2,1)S(1)}, u32[]{:S(2)}, u32[]{:S(2)}) collective-permute-start(bf16[256,1024]{1,0:T(8,128)(2,1)S(1)} %get-tuple-element.64), channel_id=1, source_target_pairs={{0,4},{12,8},{1,5},{13,9},{2,6},{14,10},{3,7},{15,11},{16,20},{28,... | collective-permute-start | bytes 1572872 | tf_op jit(solution)/shard_map/ppermute | solution.py:24
  112.2 16.2 %collective-permute-start.9 = (bf16[256,1024]{1,0:T(8,128)(2,1)S(1)}, bf16[256,1024]{1,0:T(8,128)(2,1)S(1)}, u32[]{:S(2)}, u32[]{:S(2)}) collective-permute-start(bf16[256,1024]{1,0:T(8,128)(2,1)S(1)} %fusion.3), channel_id=1, source_target_pairs={{8,4},{4,8},{9,5},{5,9},{10,6},{6,10},{11,7},{7,11},{24,20},{20,24... | collective-permute-start | bytes 1572872 | tf_op jit(solution)/shard_map/ppermute | solution.py:24
  118.6 21.1 %collective-permute-start.14 = (bf16[2,256,512]{2,1,0:T(8,128)(2,1)S(1)}, bf16[2,256,512]{2,1,0:T(8,128)(2,1)S(1)}, u32[]{:S(2)}, u32[]{:S(2)}) collective-permute-start(bf16[2,256,512]{2,1,0:T(8,128)(2,1)S(1)} %fusion), channel_id=1, source_target_pairs={{8,4},{4,8},{9,5},{5,9},{10,6},{6,10},{11,7},{7,11},{24,20},{20,24... | collective-permute-start | bytes 1572872 | tf_op jit(solution)/shard_map/ppermute | solution.py:24
  128.4 31.6 %collective-permute-start.12 = (bf16[256,1024]{1,0:T(8,128)(2,1)S(1)}, bf16[256,1024]{1,0:T(8,128)(2,1)S(1)}, u32[]{:S(2)}, u32[]{:S(2)}) collective-permute-start(bf16[256,1024]{1,0:T(8,128)(2,1)S(1)} %fusion.2), channel_id=1, source_target_pairs={{8,4},{4,8},{9,5},{5,9},{10,6},{6,10},{11,7},{7,11},{24,20},{20,24... | collective-permute-start | bytes 1572872 | tf_op jit(solution)/shard_map/ppermute | solution.py:24
  139.6 21.8 %collective-permute-start.10 = (bf16[256,1024]{1,0:T(8,128)(2,1)S(1)}, bf16[256,1024]{1,0:T(8,128)(2,1)S(1)}, u32[]{:S(2)}, u32[]{:S(2)}) collective-permute-start(bf16[256,1024]{1,0:T(8,128)(2,1)S(1)} %add_convert_fusion.3), channel_id=1, source_target_pairs={{4,0},{0,4},{12,8},{8,12},{5,1},{1,5},{13,9},{9,13},{6,2},{2,6},{1... | collective-permute-start | bytes 1572872 | tf_op jit(solution)/shard_map/ppermute | solution.py:24
  139.9 19.9 %collective-permute-start.15 = (bf16[256,512]{1,0:T(8,128)(2,1)S(1)}, bf16[256,512]{1,0:T(8,128)(2,1)S(1)}, u32[]{:S(2)}, u32[]{:S(2)}) collective-permute-start(bf16[256,512]{1,0:T(8,128)(2,1)S(1)} %fusion.8), channel_id=1, source_target_pairs={{4,0},{0,4},{12,8},{8,12},{5,1},{1,5},{13,9},{9,13},{6,2},{2,6},{1... | collective-permute-start | bytes 786440 | tf_op jit(solution)/shard_map/ppermute | solution.py:24
  160.0 6.4 %collective-permute-start.16 = (bf16[256,512]{1,0:T(8,128)(2,1)S(1)}, bf16[256,512]{1,0:T(8,128)(2,1)S(1)}, u32[]{:S(2)}, u32[]{:S(2)}) collective-permute-start(bf16[256,512]{1,0:T(8,128)(2,1)S(1)} %get-tuple-element.58), channel_id=1, source_target_pairs={{4,0},{0,4},{12,8},{8,12},{5,1},{1,5},{13,9},{9,13},{6,2},{2,6},{1... | collective-permute-start | bytes 786440 | tf_op jit(solution)/shard_map/ppermute | solution.py:24
  160.1 8.7 %collective-permute-start.17 = (bf16[256,512]{1,0:T(8,128)(2,1)S(1)}, bf16[256,512]{1,0:T(8,128)(2,1)S(1)}, u32[]{:S(2)}, u32[]{:S(2)}) collective-permute-start(bf16[256,512]{1,0:T(8,128)(2,1)S(1)} %get-tuple-element.58), channel_id=1, source_target_pairs={{8,0},{12,4},{0,8},{4,12},{9,1},{13,5},{1,9},{5,13},{10,2},{14,6},... | collective-permute-start | bytes 786440 | tf_op jit(solution)/shard_map/ppermute | solution.py:24
  161.5 14.8 %collective-permute-start.18 = (bf16[256,512]{1,0:T(8,128)(2,1)S(1)}, bf16[256,512]{1,0:T(8,128)(2,1)S(1)}, u32[]{:S(2)}, u32[]{:S(2)}) collective-permute-start(bf16[256,512]{1,0:T(8,128)(2,1)S(1)} %get-tuple-element.58), channel_id=1, source_target_pairs={{12,0},{8,4},{4,8},{0,12},{13,1},{9,5},{5,9},{1,13},{14,2},{10,6},... | collective-permute-start | bytes 786440 | tf_op jit(solution)/shard_map/ppermute | solution.py:24
  166.4 38.7 %collective-permute-start.29 = (bf16[448,1024]{1,0:T(8,128)(2,1)}, bf16[448,1024]{1,0:T(8,128)(2,1)}, u32[]{:S(2)}, u32[]{:S(2)}) collective-permute-start(bf16[448,1024]{1,0:T(8,128)(2,1)} %broadcast_select_fusion.rest_2_), channel_id=1, source_target_pairs={{0,16},{16,0},{1,17},{17,1},{2,18},{18,2},{3,19},{19,3},{4,20},{20... | collective-permute-start | bytes 2752520 | tf_op jit(solution)/shard_map/ppermute | solution.py:19
  168.7 7.8 %collective-permute-start.19 = (bf16[256,512]{1,0:T(8,128)(2,1)S(1)}, bf16[256,512]{1,0:T(8,128)(2,1)S(1)}, u32[]{:S(2)}, u32[]{:S(2)}) collective-permute-start(bf16[256,512]{1,0:T(8,128)(2,1)S(1)} %get-tuple-element.58), channel_id=1, source_target_pairs={{0,1},{1,0},{2,3},{3,2},{4,5},{5,4},{6,7},{7,6},{8,9},{9,8},{10,11... | collective-permute-start | bytes 786440 | tf_op jit(solution)/shard_map/ppermute | solution.py:19
  191.9 13.9 %collective-permute-start.21 = (bf16[256,1024]{1,0:T(8,128)(2,1)S(1)}, bf16[256,1024]{1,0:T(8,128)(2,1)}, u32[]{:S(2)}, u32[]{:S(2)}) collective-permute-start(bf16[256,1024]{1,0:T(8,128)(2,1)S(1)} %attend.1.ours_ref), channel_id=1, source_target_pairs={{0,1},{1,0},{2,3},{3,2},{4,5},{5,4},{6,7},{7,6},{8,9},{9,8},{10,11... | collective-permute-start | bytes 1572872 | tf_op jit(solution)/shard_map/ppermute | solution.py:19
  211.1 14.9 %collective-permute-start.31 = (bf16[2,256,448]{2,1,0:T(8,128)(2,1)S(1)}, bf16[2,256,448]{2,1,0:T(8,128)(2,1)S(1)}, u32[]{:S(2)}, u32[]{:S(2)}) collective-permute-start(bf16[2,256,448]{2,1,0:T(8,128)(2,1)S(1)} %get-tuple-element.54), channel_id=1, source_target_pairs={{0,2},{2,0},{1,3},{3,1},{4,6},{6,4},{5,7},{7,5},{8,10},{10,8},{9,1... | collective-permute-start | bytes 1376264 | tf_op jit(solution)/shard_map/ppermute | solution.py:19
  211.1 25.4 %collective-permute-start.30 = (bf16[2,256,448]{2,1,0:T(8,128)(2,1)S(1)}, bf16[2,256,448]{2,1,0:T(8,128)(2,1)S(1)}, u32[]{:S(2)}, u32[]{:S(2)}) collective-permute-start(bf16[2,256,448]{2,1,0:T(8,128)(2,1)S(1)} %get-tuple-element.52), channel_id=1, source_target_pairs={{0,2},{2,0},{1,3},{3,1},{4,6},{6,4},{5,7},{7,5},{8,10},{10,8},{9,1... | collective-permute-start | bytes 1376264 | tf_op jit(solution)/shard_map/ppermute | solution.py:19
  226.1 10.6 %collective-permute-start.32 = (bf16[2,256,448]{2,1,0:T(8,128)(2,1)S(1)}, bf16[2,256,448]{2,1,0:T(8,128)(2,1)S(1)}, u32[]{:S(2)}, u32[]{:S(2)}) collective-permute-start(bf16[2,256,448]{2,1,0:T(8,128)(2,1)S(1)} %add_convert_fusion), channel_id=1, source_target_pairs={{0,1},{1,0},{2,3},{3,2},{4,5},{5,4},{6,7},{7,6},{8,9},{9,8},{10,11... | collective-permute-start | bytes 1376264 | tf_op jit(solution)/shard_map/ppermute | solution.py:19
  (9 other events, 83.3 us)

commit v3 on v2

--- a/solution.py
+++ b/solution.py
@@ -34,7 +34,7 @@
 
 VMEM = pl.BlockSpec(memory_space=pltpu.VMEM)
 SMEM = pl.BlockSpec(memory_space=pltpu.SMEM)
-ANY = pl.BlockSpec(memory_space=pl.ANY)
+HBM = pl.BlockSpec(memory_space=pltpu.HBM)
 
 
 def norm_kernel(place, tokens_ref, gain_ref, mod_ref, own_ref, *rest):
@@ -84,14 +84,24 @@
     )(place, tokens, norm_gain, mod[:, None])
 
 
-def partial_kernel(counts, narrow, place, mod_ref, w_kv, w_q, *rest):
+def partial_kernel(counts, narrow, place, mod_ref, *rest):
     total = sum(counts)
-    refs, outs, (both, held_kv, held_q, arrived) = rest[:total], rest[total:-4], rest[-4:]
+    sources, refs, outs = rest[:6], rest[6 : 6 + total], rest[6 + total : -4]
+    both, held_kv, held_q, arrived = rest[-4:]
+    kv_half = held_kv.shape[2] // 2
+    depth = held_kv.shape[1] // 2
     copies = []
-    for i, (weight, held) in enumerate(((w_kv, held_kv), (w_q, held_q))):
-        copies.append(pltpu.make_async_copy(weight, held, arrived.at[i]))
+    for i, source in enumerate(sources):
+        core = place[3] if i % 2 == 0 else 1 - place[3]
+        at = pl.ds(pl.multiple_of(core * depth, depth), depth)
+        target = (
+            held_kv.at[:, at, 0:kv_half],
+            held_kv.at[:, at, kv_half : 2 * kv_half],
+            held_q.at[:, at],
+        )[i // 2]
+        copies.append(pltpu.make_async_copy(source, target, arrived.at[i]))
         copies[-1].start()
-    length, width = both.shape[0] // len(counts), both.shape[1]
+    length = both.shape[0] // len(counts)
     at = 0
     for number, count in enumerate(counts):
         base = number * length
@@ -107,21 +117,22 @@
     zero = jnp.zeros_like(block)
     first, second = jnp.where(generate, zero, block), jnp.where(generate, block, zero)
     for i, held in enumerate((held_kv, held_q)):
-        copies[i].wait()
-        value = jnp.dot(first, held[:width], preferred_element_type=jnp.float32) + jnp.dot(
-            second, held[width:], preferred_element_type=jnp.float32
+        for copy in (copies[:4], copies[4:])[i]:
+            copy.wait()
+        value = jnp.dot(first, held[0], preferred_element_type=jnp.float32) + jnp.dot(
+            second, held[1], preferred_element_type=jnp.float32
         )
         outs[i][...] = value
         if narrow:
             outs[2 + i][...] = value.astype(jnp.bfloat16)
 
 
-def partial(blocks, mods, w_kv, w_q, place, narrow):
+def partial(blocks, mods, weights, place, narrow):
     counts = tuple(len(block) for block in blocks)
     arrays = [array for block in blocks for array in block]
     length = mods[0].shape[0]
     rows, width = length * len(blocks), arrays[0].shape[1]
-    kv_cols, q_cols = w_kv.shape[1], w_q.shape[1]
+    kv_cols, q_cols = 2 * weights[0].shape[2], weights[4].shape[2]
     shapes = [
         jax.ShapeDtypeStruct((rows, cols), dtype)
         for dtype in (jnp.float32, jnp.bfloat16)[: 1 + narrow]
@@ -130,13 +141,13 @@
     values = pl.pallas_call(
         functools.partial(partial_kernel, counts, narrow),
         out_shape=shapes,
-        in_specs=[SMEM, VMEM, ANY, ANY] + [VMEM] * len(arrays),
+        in_specs=[SMEM, VMEM] + [HBM] * len(weights) + [VMEM] * len(arrays),
         out_specs=[VMEM] * len(shapes),
         scratch_shapes=[
             pltpu.VMEM((rows, width), jnp.bfloat16),
-            pltpu.VMEM(w_kv.shape, jnp.bfloat16),
-            pltpu.VMEM(w_q.shape, jnp.bfloat16),
-            pltpu.SemaphoreType.DMA((2,)),
+            pltpu.VMEM((2, width, kv_cols), jnp.bfloat16),
+            pltpu.VMEM((2, width, q_cols), jnp.bfloat16),
+            pltpu.SemaphoreType.DMA((len(weights),)),
         ],
         cost_estimate=pl.CostEstimate(
             flops=4 * rows * width * (kv_cols + q_cols),
@@ -145,7 +156,7 @@
         ),
         compiler_params=pltpu.CompilerParams(vmem_limit_bytes=40 * 1024 * 1024),
         name="partial",
-    )(place, jnp.concatenate(mods)[:, None], w_kv, w_q, *arrays)
+    )(place, jnp.concatenate(mods)[:, None], *weights, *arrays)
     return [value.reshape(len(blocks), length, -1) for value in values]
 
 
@@ -221,46 +232,59 @@
     heads = q_ref.shape[1] // HEAD_DIM
     kv_local = kv_ref.shape[2] // (2 * HEAD_DIM)
     repeat = heads // kv_local
-    scale = 1.0 / math.sqrt(HEAD_DIM)
-    top[...] = jnp.full_like(top, LOW)
+    scale = math.log2(math.e) / math.sqrt(HEAD_DIM)
+    top[...] = jnp.full_like(top, LOW / 10)
     total[...] = jnp.zeros_like(total)
     acc[...] = jnp.zeros_like(acc)
+    transposed = (((1,), (1,)), ((), ()))
 
     def visit(number, _):
         start = starts[number]
-
-        @pl.when((start <= limits[1]) & (start + size > limits[0]))
-        def _():
-            key_pos = start + lax.broadcasted_iota(jnp.int32, (rows, size), 1)
-            seen = (key_pos >= low_ref[...]) & (key_pos <= high_ref[...])
-            for head in range(heads):
-                g = head // repeat
+        last = start + size - 1
+
+        def block(masked):
+            if masked:
+                key_pos = start + lax.broadcasted_iota(jnp.int32, (size, rows), 0)
+                seen = (key_pos >= low_ref[...]) & (key_pos <= high_ref[...])
+            for g in range(kv_local):
                 keys = kv_ref[number, :, g * HEAD_DIM : (g + 1) * HEAD_DIM]
                 values = kv_ref[number, :, (kv_local + g) * HEAD_DIM : (kv_local + g + 1) * HEAD_DIM]
-                query = q_ref[:, head * HEAD_DIM : (head + 1) * HEAD_DIM]
-                scores = lax.dot_general(
-                    query, keys, (((1,), (1,)), ((), ())), preferred_element_type=jnp.float32
-                )
-                scores = jnp.where(seen, scores * scale, LOW)
-                old = top[head][:, :1]
-                new = jnp.maximum(old, jnp.max(scores, axis=1, keepdims=True))
-                weights = jnp.where(seen, jnp.exp(scores - new), 0.0)
-                shrink = jnp.exp(old - new)
-                total[head] = jnp.broadcast_to(
-                    total[head][:, :1] * shrink + jnp.sum(weights, axis=1, keepdims=True),
-                    (rows, HEAD_DIM),
-                )
-                top[head] = jnp.broadcast_to(new, (rows, HEAD_DIM))
-                acc[head] = acc[head] * shrink + jnp.dot(
-                    weights.astype(jnp.bfloat16), values, preferred_element_type=jnp.float32
-                )
+                values = values.T
+                for head in range(g * repeat, (g + 1) * repeat):
+                    query = q_ref[:, head * HEAD_DIM : (head + 1) * HEAD_DIM]
+                    scores = lax.dot_general(
+                        keys, query, transposed, preferred_element_type=jnp.float32
+                    )
+                    if masked:
+                        scores = jnp.where(seen, scores, LOW)
+                    old = top[head : head + 1]
+                    new = jnp.maximum(old, jnp.max(scores, axis=0, keepdims=True))
+                    weights = jnp.exp2((scores - new) * scale)
+                    shrink = jnp.exp2((old - new) * scale)
+                    total[head : head + 1] = total[head : head + 1] * shrink + jnp.sum(
+                        weights, axis=0, keepdims=True
+                    )
+                    top[head : head + 1] = new
+                    acc[head] = acc[head] * shrink + jnp.dot(
+                        values, weights.astype(jnp.bfloat16), preferred_element_type=jnp.float32
+                    )
+
+        inside = (start >= limits[2]) & (last <= limits[3])
+
+        @pl.when(inside)
+        def _():
+            block(False)
+
+        @pl.when(jnp.logical_not(inside) & (start <= limits[1]) & (last >= limits[0]))
+        def _():
+            block(True)
 
         return 0
 
     lax.fori_loop(0, count, visit, 0)
     for head in range(heads):
-        o_ref[:, head * HEAD_DIM : (head + 1) * HEAD_DIM] = (acc[head] / total[head]).astype(
-            jnp.bfloat16
+        o_ref[:, head * HEAD_DIM : (head + 1) * HEAD_DIM] = (
+            (acc[head] / total[head : head + 1]).T.astype(jnp.bfloat16)
         )
 
 
@@ -268,18 +292,16 @@
     rows, width = query.shape
     heads = width // HEAD_DIM
     count, size, _ = kv.shape
-    vmem = pl.BlockSpec(memory_space=pltpu.VMEM)
-    smem = pl.BlockSpec(memory_space=pltpu.SMEM)
-    limits = jnp.stack([low[0], high[-1]])
+    limits = jnp.stack([low[0], high[-1], low[-1], high[0]])
     return pl.pallas_call(
         attention_kernel,
         out_shape=jax.ShapeDtypeStruct((rows, width), jnp.bfloat16),
-        in_specs=[smem, smem, vmem, vmem, vmem, vmem],
-        out_specs=vmem,
+        in_specs=[SMEM, SMEM, VMEM, VMEM, VMEM, VMEM],
+        out_specs=VMEM,
         scratch_shapes=[
-            pltpu.VMEM((heads, rows, HEAD_DIM), jnp.float32),
-            pltpu.VMEM((heads, rows, HEAD_DIM), jnp.float32),
-            pltpu.VMEM((heads, rows, HEAD_DIM), jnp.float32),
+            pltpu.VMEM((heads, rows), jnp.float32),
+            pltpu.VMEM((heads, rows), jnp.float32),
+            pltpu.VMEM((heads, HEAD_DIM, rows), jnp.float32),
         ],
         cost_estimate=pl.CostEstimate(
             flops=4 * rows * count * size * width,
@@ -288,7 +310,7 @@
         ),
         compiler_params=pltpu.CompilerParams(vmem_limit_bytes=32 * 1024 * 1024),
         name="attend",
-    )(starts, limits, query, kv, low[:, None], high[:, None])
+    )(starts, limits, query, kv, low[None, :], high[None, :])
 
 
 def project_kernel(turns, place, ours_ref, beside_ref, ours_near, beside_near, own_ref, *rest):
@@ -341,7 +363,7 @@
     return pl.pallas_call(
         project_kernel,
         out_shape=(shape, shape),
-        in_specs=[SMEM, SMEM] + [VMEM] * 4 + [ANY] * len(weights),
+        in_specs=[SMEM, SMEM] + [VMEM] * 4 + [HBM] * len(weights),
         out_specs=(VMEM, VMEM),
         scratch_shapes=[
             pltpu.VMEM((2, count, width, depth), jnp.bfloat16),
@@ -359,14 +381,13 @@
 
 
 def body(tokens, norm_gain, w_query, w_key, w_value, w_out, modality, doc_ids):
-    length, depth = tokens.shape
+    length, _ = tokens.shape
     n = lax.axis_size("seq")
     subs = lax.axis_size("sub")
     heads_over = lax.axis_size("head")
     z, s = lax.axis_index("seq"), lax.axis_index("sub")
     x, y = lax.axis_index("head"), lax.axis_index("grp")
-    width = depth // n
-    place = jnp.stack([z, x, y]).astype(jnp.int32)
+    place = jnp.stack([z, x, y, s]).astype(jnp.int32)
 
     kv_local = max(KV_HEADS // heads_over, 1)
     kv_first = x * KV_HEADS // heads_over
@@ -389,25 +410,16 @@
 
     w_query, w_key, w_value = after((w_query, w_key, w_value), sends[0])
 
-    def share(weight):
-        other = swap(weight, "sub")
-        both = jnp.where(
-            s == 0,
-            jnp.concatenate([weight, other], axis=1),
-            jnp.concatenate([other, weight], axis=1),
-        )
-        return both.reshape(2 * width, weight.shape[2])
-
     key_cols = lax.dynamic_slice_in_dim(w_key, kv_first * HEAD_DIM, kv_local * HEAD_DIM, 2)
     value_cols = lax.dynamic_slice_in_dim(w_value, kv_first * HEAD_DIM, kv_local * HEAD_DIM, 2)
-    w_kv_all = share(jnp.concatenate([key_cols, value_cols], axis=2))
-    w_q_all = share(w_query)
+    row_weights = []
+    for weight in (key_cols, value_cols, w_query):
+        row_weights += [weight, swap(weight, "sub")]
     modality, doc_ids = after((modality, doc_ids), sends[0])
     own_doc = part_of(doc_ids, z, s)
     own_pos = (z * subs + s) * length + jnp.arange(length, dtype=jnp.int32)
     low, high = spans(modality, doc_ids, part_of(modality, z, s), own_doc, own_pos)
-    for d in range(1, n):
-        blocks[d] = after(blocks[d], w_kv_all, w_q_all, low, high)
+    blocks[1] = after(blocks[1], low, high)
 
     if share_rows:
         for d in range(n - 1, 0, -1):
@@ -415,7 +427,7 @@
 
     def parts_of(group, narrow):
         mods = [part_of(modality, z ^ d, s) for d in group]
-        return partial([blocks[d] for d in group], mods, w_kv_all, w_q_all, place, narrow)
+        return partial([blocks[d] for d in group], mods, row_weights, place, narrow)
 
     if n == 4:
         kv_early, q_early, kv_rounded, q_rounded = parts_of([3, 2], True)

time: 240 us -> 241 us (level)
  the two profiles are of different devices: /device:TPU:22 before, /device:TPU:0 now
where the time goes in v3:
time: 241 us; the launch traced here: 240 us
  waiting for transfers between devices  105 us (44%)
  starting transfers between devices  81.1 us (34%)
  Pallas kernels  27.1 us (11%)
  local copies, waits for them, and re-layouts  13.5 us (6%)
  other arithmetic  11.4 us (5%)
  between operations  2.57 us (1%)
    ppermute x19, starting transfers between devices, cross(): return lax.ppermute(x, axis, [(i ^ bit, i) for i in among or range(size)])  68.6 us
    ppermute x19, waiting for transfers between devices, cross(): return lax.ppermute(x, axis, [(i ^ bit, i) for i in among or range(size)])  61.1 us
    ppermute x15, waiting for transfers between devices, swap(): return lax.ppermute(x, axis, [(0, 1), (1, 0)])  43.5 us
    ppermute x15, starting transfers between devices, swap(): return lax.ppermute(x, axis, [(0, 1), (1, 0)])  12.5 us
    pallas_call x2, Pallas kernels, partial(): pl.pallas_call(functools.partial(partial_kernel, counts, narrow), out_sha...  10.8 us
    pallas_call x2, Pallas kernels, project(): pl.pallas_call(project_kernel, out_shape=(shape, shape), in_specs=[SMEM,...  10.4 us
    unnamed x30, local copies, waits for them, and re-layouts  5.66 us
  transfers between devices with their start and end apart: 34, of which 15 were waited for; matrix products, arithmetic and copies ran while one was open for 6% of the time, Pallas kernels for 9%

profile of v3, /device:TPU:0, one launch (start us, length us, event | category | flops | bytes accessed | tf_op | source)
XLA Modules:
  0.0 240.3 jit_solution(4695980798986825053)
XLA Ops:
  0.0 2.3 dynamic-slice_bitcast_fusion
  2.3 3.1 %collective-permute-start.23 = (bf16[448,1024]{1,0:T(8,128)(2,1)}, bf16[448,1024]{1,0:T(8,128)(2,1)}, u32[]{:S(2)}, u32[]{:S(2)}) collective-permute-start(bf16[448,1024]{1,0:T(8,128)(2,1)} %dynamic-slice_bitcast_fusion), channel_id=1, source_target_pairs={{4,0},{0,4},{12,8},{8,12},{5,1},{1,5},{13,9},{9,13},{6,2},{2,6},{1... | collective-permute-start | bytes 2752520 | tf_op jit(solution)/shard_map/ppermute | solution.py:24
  5.4 1.6 collective-permute-start.25
  8.7 2.5 %norm.1 = (bf16[256,896]{1,0:T(8,128)(2,1)S(1)}, bf16[128,896]{1,0:T(8,128)(2,1)S(1)}, bf16[128,896]{1,0:T(8,128)(2,1)}, bf16[128,896]{1,0:T(8,128)(2,1)}) custom-call(s32[4]{0:T(128)S(1)} %pad_add_fusion.2.place, bf16[256,3584]{1,0:T(8,128)(2,1)S(1)} %copy-done.2, f32[2,3584]{1,0:T(2,128)S(1)} %copy-done.4, s32[256,1]{1,0:T(8,128)S(1)} %copy.18.mod_ref), custom_call_target="tpu_custom_call" | custom-call | flops 5505024 | bytes 3670016 | tf_op jit(solution)/shard_map/norm/pallas_call | solution.py:73
  11.9 2.5 %collective-permute-start.5 = (bf16[128,896]{1,0:T(8,128)(2,1)}, bf16[128,896]{1,0:T(8,128)(2,1)}, u32[]{:S(2)}, u32[]{:S(2)}) collective-permute-start(bf16[128,896]{1,0:T(8,128)(2,1)} %get-tuple-element.37), channel_id=1, source_target_pairs={{12,0},{8,4},{4,8},{0,12},{13,1},{9,5},{5,9},{1,13},{14,2},{10,6},... | collective-permute-start | bytes 688136 | tf_op jit(solution)/shard_map/ppermute | solution.py:24
  14.4 2.5 %collective-permute-start.7 = (bf16[128,896]{1,0:T(8,128)(2,1)}, bf16[128,896]{1,0:T(8,128)(2,1)}, u32[]{:S(2)}, u32[]{:S(2)}) collective-permute-start(bf16[128,896]{1,0:T(8,128)(2,1)} %get-tuple-element.38), channel_id=1, source_target_pairs={{8,0},{12,4},{0,8},{4,12},{9,1},{13,5},{1,9},{5,13},{10,2},{14,6},... | collective-permute-start | bytes 688136 | tf_op jit(solution)/shard_map/ppermute | solution.py:24
  20.4 14.0 %collective-permute-done.5.rest_6_ = bf16[128,896]{1,0:T(8,128)(2,1)} collective-permute-done((bf16[128,896]{1,0:T(8,128)(2,1)}, bf16[128,896]{1,0:T(8,128)(2,1)}, u32[]{:S(2)}, u32[]{:S(2)}) %collective-permute-start.5) | collective-permute-done | bytes 229408 | tf_op jit(solution)/shard_map/ppermute | solution.py:24
  34.4 12.3 %collective-permute-start.3 = (bf16[128,896]{1,0:T(8,128)(2,1)}, bf16[128,896]{1,0:T(8,128)(2,1)}, u32[]{:S(2)}, u32[]{:S(2)}) collective-permute-start(bf16[128,896]{1,0:T(8,128)(2,1)} %copy-done.10), channel_id=1, source_target_pairs={{4,0},{0,4},{12,8},{8,12},{5,1},{1,5},{13,9},{9,13},{6,2},{2,6},{1... | collective-permute-start | bytes 688136 | tf_op jit(solution)/shard_map/ppermute | solution.py:24
  47.8 2.2 collective-permute-done.7.rest_8_
  50.0 4.6 %collective-permute-done.3.rest_6_ = bf16[128,896]{1,0:T(8,128)(2,1)} collective-permute-done((bf16[128,896]{1,0:T(8,128)(2,1)}, bf16[128,896]{1,0:T(8,128)(2,1)}, u32[]{:S(2)}, u32[]{:S(2)}) %collective-permute-start.3) | collective-permute-done | bytes 229408 | tf_op jit(solution)/shard_map/ppermute | solution.py:24
  62.3 2.7 %pad_add_fusion.3.limits = s32[4]{0:T(128)S(1)} fusion(s32[1]{0:T(128)} %get-tuple-element.74, s32[1]{0:T(128)} %get-tuple-element.67, s32[1]{0:T(128)} %get-tuple-element.75, s32[1]{0:T(128)} %get-tuple-element.66), kind=kLoop, calls=%fused_computation.46 | loop fusion | flops 12 | bytes 32 | tf_op jit(solution)/shard_map/stack | solution.py:295
  65.0 2.2 collective-permute-done.6.rest_7_
  68.7 3.4 %collective-permute-done.8.rest_9_ = bf16[128,896]{1,0:T(8,128)(2,1)} collective-permute-done((bf16[128,896]{1,0:T(8,128)(2,1)}, bf16[128,896]{1,0:T(8,128)(2,1)}, u32[]{:S(2)}, u32[]{:S(2)}) %collective-permute-start.8) | collective-permute-done | bytes 229408 | tf_op jit(solution)/shard_map/ppermute | solution.py:19
  74.6 5.5 %partial.3 = (f32[512,512]{1,0:T(8,128)S(1)}, f32[512,1024]{1,0:T(8,128)S(1)}, bf16[512,512]{1,0:T(8,128)(2,1)S(1)}, bf16[512,1024]{1,0:T(8,128)(2,1)S(1)}) custom-call(s32[4]{0:T(128)S(1)} %pad_add_fusion.2.place, s32[512,1]{1,0:T(8,128)S(1)} %copy.20.mod_ref, bf16[2,448,256]{2,1,0:T(8,128)(2,1)S(1)} %constant_dynamic-slice_fusion.1.rest_0_, ...), custom_call_target="tpu_custom_call" | custom-call | flops 2818572288 | bytes 8650752 | tf_op jit(solution)/shard_map/partial/pallas_call | solution.py:141
  80.2 5.5 %collective-permute-start.12 = (bf16[256,1024]{1,0:T(8,128)(2,1)S(1)}, bf16[256,1024]{1,0:T(8,128)(2,1)S(1)}, u32[]{:S(2)}, u32[]{:S(2)}) collective-permute-start(bf16[256,1024]{1,0:T(8,128)(2,1)S(1)} %get-tuple-element.60), channel_id=1, source_target_pairs={{0,4},{12,8},{1,5},{13,9},{2,6},{14,10},{3,7},{15,11},{16,20},{28,... | collective-permute-start | bytes 1572872 | tf_op jit(solution)/shard_map/ppermute | solution.py:24
  89.9 2.2 broadcast_select_fusion.1.rest_1_
  92.3 5.3 %partial.2 = (f32[512,512]{1,0:T(8,128)S(1)}, f32[512,1024]{1,0:T(8,128)S(1)}) custom-call(s32[4]{0:T(128)S(1)} %pad_add_fusion.2.place, s32[512,1]{1,0:T(8,128)S(1)} %copy.19.mod_ref, bf16[2,448,256]{2,1,0:T(8,128)(2,1)S(1)} %constant_dynamic-slice_fusion.1.rest_0_, bf16[2,448,256]{2,1,0:T(8,128)(2,1)S(1)} %collective-permute-done.rest_1_, ...), custom_call_target="tpu_custom_call" | custom-call | flops 2818572288 | bytes 8650752 | tf_op jit(solution)/shard_map/partial/pallas_call | solution.py:141
  97.6 20.6 %collective-permute-done.14 = bf16[2,256,512]{2,1,0:T(8,128)(2,1)S(1)} collective-permute-done((bf16[2,256,512]{2,1,0:T(8,128)(2,1)S(1)}, bf16[2,256,512]{2,1,0:T(8,128)(2,1)S(1)}, u32[]{:S(2)}, u32[]{:S(2)}) %collective-permute-start.14) | collective-permute-done | bytes 524320 | tf_op jit(solution)/shard_map/ppermute | solution.py:24
  121.4 16.5 %collective-permute-start.16 = (bf16[256,512]{1,0:T(8,128)(2,1)S(1)}, bf16[256,512]{1,0:T(8,128)(2,1)S(1)}, u32[]{:S(2)}, u32[]{:S(2)}) collective-permute-start(bf16[256,512]{1,0:T(8,128)(2,1)S(1)} %fusion.8), channel_id=1, source_target_pairs={{4,0},{0,4},{12,8},{8,12},{5,1},{1,5},{13,9},{9,13},{6,2},{2,6},{1... | collective-permute-start | bytes 786440 | tf_op jit(solution)/shard_map/ppermute | solution.py:24
  138.0 11.0 %collective-permute-start.11 = (bf16[256,1024]{1,0:T(8,128)(2,1)S(1)}, bf16[256,1024]{1,0:T(8,128)(2,1)S(1)}, u32[]{:S(2)}, u32[]{:S(2)}) collective-permute-start(bf16[256,1024]{1,0:T(8,128)(2,1)S(1)} %add_convert_fusion.3), channel_id=1, source_target_pairs={{4,0},{0,4},{12,8},{8,12},{5,1},{1,5},{13,9},{9,13},{6,2},{2,6},{1... | collective-permute-start | bytes 1572872 | tf_op jit(solution)/shard_map/ppermute | solution.py:24
  149.2 2.9 %collective-permute-start.18 = (bf16[256,512]{1,0:T(8,128)(2,1)S(1)}, bf16[256,512]{1,0:T(8,128)(2,1)S(1)}, u32[]{:S(2)}, u32[]{:S(2)}) collective-permute-start(bf16[256,512]{1,0:T(8,128)(2,1)S(1)} %get-tuple-element.54), channel_id=1, source_target_pairs={{8,0},{12,4},{0,8},{4,12},{9,1},{13,5},{1,9},{5,13},{10,2},{14,6},... | collective-permute-start | bytes 786440 | tf_op jit(solution)/shard_map/ppermute | solution.py:24
  154.7 12.3 %collective-permute-done.17 = bf16[256,512]{1,0:T(8,128)(2,1)S(1)} collective-permute-done((bf16[256,512]{1,0:T(8,128)(2,1)S(1)}, bf16[256,512]{1,0:T(8,128)(2,1)S(1)}, u32[]{:S(2)}, u32[]{:S(2)}) %collective-permute-start.17) | collective-permute-done | bytes 262176 | tf_op jit(solution)/shard_map/ppermute | solution.py:24
  168.6 7.3 %collective-permute-done.18 = bf16[256,512]{1,0:T(8,128)(2,1)S(1)} collective-permute-done((bf16[256,512]{1,0:T(8,128)(2,1)S(1)}, bf16[256,512]{1,0:T(8,128)(2,1)S(1)}, u32[]{:S(2)}, u32[]{:S(2)}) %collective-permute-start.18) | collective-permute-done | bytes 262176 | tf_op jit(solution)/shard_map/ppermute | solution.py:24
  180.8 3.4 %attend.1.ours_ref = bf16[256,1024]{1,0:T(8,128)(2,1)S(1)} custom-call(s32[8]{0:T(128)S(1)} %stack.93.starts, s32[4]{0:T(128)S(1)} %pad_add_fusion.3.limits, bf16[256,1024]{1,0:T(8,128)(2,1)S(1)} %add_convert_fusion.2.q_ref, bf16[8,256,512]{2,1,0:T(8,128)(2,1)S(1)} %constant_dynamic-update-slice_fusion.kv_ref, s32[1,256]{1,0:T(1,128)S(1)} %bitcast.73, ...), custom_call_target="tpu_custom_call" | custom-call | flops 2147483648 | bytes 3145728 | tf_op jit(solution)/shard_map/attend/pallas_call | solution.py:296
  184.3 2.6 %collective-permute-start.22 = (bf16[256,1024]{1,0:T(8,128)(2,1)S(1)}, bf16[256,1024]{1,0:T(8,128)(2,1)}, u32[]{:S(2)}, u32[]{:S(2)}) collective-permute-start(bf16[256,1024]{1,0:T(8,128)(2,1)S(1)} %attend.1.ours_ref), channel_id=1, source_target_pairs={{0,1},{1,0},{2,3},{3,2},{4,5},{5,4},{6,7},{7,6},{8,9},{9,8},{10,11... | collective-permute-start | bytes 1572872 | tf_op jit(solution)/shard_map/ppermute | solution.py:19
  187.2 3.3 %collective-permute-done.28.rest_3_ = bf16[448,1024]{1,0:T(8,128)(2,1)} collective-permute-done((bf16[448,1024]{1,0:T(8,128)(2,1)}, bf16[448,1024]{1,0:T(8,128)(2,1)}, u32[]{:S(2)}, u32[]{:S(2)}) %collective-permute-start.28) | collective-permute-done | bytes 917536 | tf_op jit(solution)/shard_map/ppermute | solution.py:19
  190.6 15.5 %collective-permute-done.29.rest_4_ = bf16[448,1024]{1,0:T(8,128)(2,1)} collective-permute-done((bf16[448,1024]{1,0:T(8,128)(2,1)}, bf16[448,1024]{1,0:T(8,128)(2,1)}, u32[]{:S(2)}, u32[]{:S(2)}) %collective-permute-start.29) | collective-permute-done | bytes 917536 | tf_op jit(solution)/shard_map/ppermute | solution.py:19
  206.1 9.8 %collective-permute-done.30.rest_5_ = bf16[448,1024]{1,0:T(8,128)(2,1)} collective-permute-done((bf16[448,1024]{1,0:T(8,128)(2,1)}, bf16[448,1024]{1,0:T(8,128)(2,1)}, u32[]{:S(2)}, u32[]{:S(2)}) %collective-permute-start.30) | collective-permute-done | bytes 917536 | tf_op jit(solution)/shard_map/ppermute | solution.py:19
  215.9 5.9 %project.3 = (bf16[2,256,448]{2,1,0:T(8,128)(2,1)}, bf16[2,256,448]{2,1,0:T(8,128)(2,1)S(1)}) custom-call(s32[2]{0:T(128)S(1)} %get-tuple-element.70.turns, s32[4]{0:T(128)S(1)} %pad_add_fusion.2.place, bf16[256,1024]{1,0:T(8,128)(2,1)S(1)} %attend.1.ours_ref, bf16[256,1024]{1,0:T(8,128)(2,1)} %collective-permute-done.22.beside_ref, ...), custom_call_target="tpu_custom_call" | custom-call | flops 1879048192 | bytes 4587520 | tf_op jit(solution)/shard_map/project/pallas_call | solution.py:363
  223.9 4.5 %project.2 = (bf16[2,256,448]{2,1,0:T(8,128)(2,1)S(1)}, bf16[2,256,448]{2,1,0:T(8,128)(2,1)S(1)}) custom-call(s32[2]{0:T(128)S(1)} %get-tuple-element.71.turns, s32[4]{0:T(128)S(1)} %pad_add_fusion.2.place, bf16[256,1024]{1,0:T(8,128)(2,1)S(1)} %attend.1.ours_ref, bf16[256,1024]{1,0:T(8,128)(2,1)} %collective-permute-done.22.beside_ref, ...), custom_call_target="tpu_custom_call" | custom-call | flops 1879048192 | bytes 4587520 | tf_op jit(solution)/shard_map/project/pallas_call | solution.py:363
  229.2 1.9 collective-permute-done.32
  231.3 5.5 %collective-permute-done.31 = bf16[2,256,448]{2,1,0:T(8,128)(2,1)} collective-permute-done((bf16[2,256,448]{2,1,0:T(8,128)(2,1)}, bf16[2,256,448]{2,1,0:T(8,128)(2,1)}, u32[]{:S(2)}, u32[]{:S(2)}) %collective-permute-start.31) | collective-permute-done | bytes 458784 | tf_op jit(solution)/shard_map/ppermute | solution.py:19
  (122 shorter events, 40.2 us)
Async XLA Ops:
  2.3 52.7 %collective-permute-start.23 = (bf16[448,1024]{1,0:T(8,128)(2,1)}, bf16[448,1024]{1,0:T(8,128)(2,1)}, u32[]{:S(2)}, u32[]{:S(2)}) collective-permute-start(bf16[448,1024]{1,0:T(8,128)(2,1)} %dynamic-slice_bitcast_fusion), channel_id=1, source_target_pairs={{4,0},{0,4},{12,8},{8,12},{5,1},{1,5},{13,9},{9,13},{6,2},{2,6},{1... | collective-permute-start | bytes 2752520 | tf_op jit(solution)/shard_map/ppermute | solution.py:24
  5.4 51.3 %collective-permute-start.25 = (bf16[448,1024]{1,0:T(8,128)(2,1)}, bf16[448,1024]{1,0:T(8,128)(2,1)}, u32[]{:S(2)}, u32[]{:S(2)}) collective-permute-start(bf16[448,1024]{1,0:T(8,128)(2,1)} %dynamic-slice_bitcast_fusion), channel_id=1, source_target_pairs={{8,4},{4,8},{9,5},{5,9},{10,6},{6,10},{11,7},{7,11},{24,20},{20,24... | collective-permute-start | bytes 2752520 | tf_op jit(solution)/shard_map/ppermute | solution.py:24
  11.9 60.2 %collective-permute-start.2 = (bf16[2,448,1024]{2,1,0:T(8,128)(2,1)}, bf16[2,448,1024]{2,1,0:T(8,128)(2,1)}, u32[]{:S(2)}, u32[]{:S(2)}) collective-permute-start(bf16[2,448,1024]{2,1,0:T(8,128)(2,1)} %rest_4_.1), channel_id=1, source_target_pairs={{0,1},{1,0},{2,3},{3,2},{4,5},{5,4},{6,7},{7,6},{8,9},{9,8},{10,11... | collective-permute-start | bytes 5505032 | tf_op jit(solution)/shard_map/ppermute | solution.py:19
  11.9 22.5 %collective-permute-start.5 = (bf16[128,896]{1,0:T(8,128)(2,1)}, bf16[128,896]{1,0:T(8,128)(2,1)}, u32[]{:S(2)}, u32[]{:S(2)}) collective-permute-start(bf16[128,896]{1,0:T(8,128)(2,1)} %get-tuple-element.37), channel_id=1, source_target_pairs={{12,0},{8,4},{4,8},{0,12},{13,1},{9,5},{5,9},{1,13},{14,2},{10,6},... | collective-permute-start | bytes 688136 | tf_op jit(solution)/shard_map/ppermute | solution.py:24
  14.4 35.7 %collective-permute-start.7 = (bf16[128,896]{1,0:T(8,128)(2,1)}, bf16[128,896]{1,0:T(8,128)(2,1)}, u32[]{:S(2)}, u32[]{:S(2)}) collective-permute-start(bf16[128,896]{1,0:T(8,128)(2,1)} %get-tuple-element.38), channel_id=1, source_target_pairs={{8,0},{12,4},{0,8},{4,12},{9,1},{13,5},{1,9},{5,13},{10,2},{14,6},... | collective-permute-start | bytes 688136 | tf_op jit(solution)/shard_map/ppermute | solution.py:24
  34.4 20.2 %collective-permute-start.3 = (bf16[128,896]{1,0:T(8,128)(2,1)}, bf16[128,896]{1,0:T(8,128)(2,1)}, u32[]{:S(2)}, u32[]{:S(2)}) collective-permute-start(bf16[128,896]{1,0:T(8,128)(2,1)} %copy-done.10), channel_id=1, source_target_pairs={{4,0},{0,4},{12,8},{8,12},{5,1},{1,5},{13,9},{9,13},{6,2},{2,6},{1... | collective-permute-start | bytes 688136 | tf_op jit(solution)/shard_map/ppermute | solution.py:24
  50.0 8.3 %collective-permute-start = (bf16[2,448,256]{2,1,0:T(8,128)(2,1)S(1)}, bf16[2,448,256]{2,1,0:T(8,128)(2,1)S(1)}, u32[]{:S(2)}, u32[]{:S(2)}) collective-permute-start(bf16[2,448,256]{2,1,0:T(8,128)(2,1)S(1)} %constant_dynamic-slice_fusion.1.rest_0_), channel_id=1, source_target_pairs={{0,1},{1,0},{2,3},{3,2},{4,5},{5,4},{6,7},{7,6},{8,9},{9,8},{10,11... | collective-permute-start | bytes 1376264 | tf_op jit(solution)/shard_map/ppermute | solution.py:19
  54.6 5.3 %collective-permute-start.1 = (bf16[2,448,256]{2,1,0:T(8,128)(2,1)S(1)}, bf16[2,448,256]{2,1,0:T(8,128)(2,1)S(1)}, u32[]{:S(2)}, u32[]{:S(2)}) collective-permute-start(bf16[2,448,256]{2,1,0:T(8,128)(2,1)S(1)} %constant_dynamic-slice_fusion.rest_2_), channel_id=1, source_target_pairs={{0,1},{1,0},{2,3},{3,2},{4,5},{5,4},{6,7},{7,6},{8,9},{9,8},{10,11... | collective-permute-start | bytes 1376264 | tf_op jit(solution)/shard_map/ppermute | solution.py:19
  55.1 32.1 %collective-permute-start.24 = (bf16[448,1024]{1,0:T(8,128)(2,1)}, bf16[448,1024]{1,0:T(8,128)(2,1)}, u32[]{:S(2)}, u32[]{:S(2)}) collective-permute-start(bf16[448,1024]{1,0:T(8,128)(2,1)} %collective-permute-done.23.rest_0_), channel_id=1, source_target_pairs={{8,4},{4,8},{9,5},{5,9},{10,6},{6,10},{11,7},{7,11},{24,20},{20,24... | collective-permute-start | bytes 2752520 | tf_op jit(solution)/shard_map/ppermute | solution.py:24
  56.7 32.0 %collective-permute-start.26 = (bf16[448,1024]{1,0:T(8,128)(2,1)}, bf16[448,1024]{1,0:T(8,128)(2,1)}, u32[]{:S(2)}, u32[]{:S(2)}) collective-permute-start(bf16[448,1024]{1,0:T(8,128)(2,1)} %collective-permute-done.25), channel_id=1, source_target_pairs={{4,0},{8,12},{5,1},{9,13},{6,2},{10,14},{7,3},{11,15},{20,16},{24,... | collective-permute-start | bytes 2752520 | tf_op jit(solution)/shard_map/ppermute | solution.py:24
  58.3 8.9 %collective-permute-start.6 = (bf16[128,896]{1,0:T(8,128)(2,1)}, bf16[128,896]{1,0:T(8,128)(2,1)}, u32[]{:S(2)}, u32[]{:S(2)}) collective-permute-start(bf16[128,896]{1,0:T(8,128)(2,1)} %collective-permute-done.5.rest_6_), channel_id=1, source_target_pairs={{0,2},{2,0},{1,3},{3,1},{4,6},{6,4},{5,7},{7,5},{8,10},{10,8},{9,1... | collective-permute-start | bytes 688136 | tf_op jit(solution)/shard_map/ppermute | solution.py:19
  60.7 11.4 %collective-permute-start.8 = (bf16[128,896]{1,0:T(8,128)(2,1)}, bf16[128,896]{1,0:T(8,128)(2,1)}, u32[]{:S(2)}, u32[]{:S(2)}) collective-permute-start(bf16[128,896]{1,0:T(8,128)(2,1)} %collective-permute-done.7.rest_8_), channel_id=1, source_target_pairs={{0,2},{2,0},{1,3},{3,1},{4,6},{6,4},{5,7},{7,5},{8,10},{10,8},{9,1... | collective-permute-start | bytes 688136 | tf_op jit(solution)/shard_map/ppermute | solution.py:19
  67.2 25.0 %collective-permute-start.4 = (bf16[128,896]{1,0:T(8,128)(2,1)}, bf16[128,896]{1,0:T(8,128)(2,1)S(1)}, u32[]{:S(2)}, u32[]{:S(2)}) collective-permute-start(bf16[128,896]{1,0:T(8,128)(2,1)} %collective-permute-done.3.rest_6_), channel_id=1, source_target_pairs={{0,2},{2,0},{1,3},{3,1},{4,6},{6,4},{5,7},{7,5},{8,10},{10,8},{9,1... | collective-permute-start | bytes 688136 | tf_op jit(solution)/shard_map/ppermute | solution.py:19
  80.2 39.7 %collective-permute-start.12 = (bf16[256,1024]{1,0:T(8,128)(2,1)S(1)}, bf16[256,1024]{1,0:T(8,128)(2,1)S(1)}, u32[]{:S(2)}, u32[]{:S(2)}) collective-permute-start(bf16[256,1024]{1,0:T(8,128)(2,1)S(1)} %get-tuple-element.60), channel_id=1, source_target_pairs={{0,4},{12,8},{1,5},{13,9},{2,6},{14,10},{3,7},{15,11},{16,20},{28,... | collective-permute-start | bytes 1572872 | tf_op jit(solution)/shard_map/ppermute | solution.py:24
  85.8 33.3 %collective-permute-start.9 = (bf16[256,1024]{1,0:T(8,128)(2,1)S(1)}, bf16[256,1024]{1,0:T(8,128)(2,1)S(1)}, u32[]{:S(2)}, u32[]{:S(2)}) collective-permute-start(bf16[256,1024]{1,0:T(8,128)(2,1)S(1)} %get-tuple-element.59), channel_id=1, source_target_pairs={{0,4},{12,8},{1,5},{13,9},{2,6},{14,10},{3,7},{15,11},{16,20},{28,... | collective-permute-start | bytes 1572872 | tf_op jit(solution)/shard_map/ppermute | solution.py:24
  87.2 31.0 %collective-permute-start.14 = (bf16[2,256,512]{2,1,0:T(8,128)(2,1)S(1)}, bf16[2,256,512]{2,1,0:T(8,128)(2,1)S(1)}, u32[]{:S(2)}, u32[]{:S(2)}) collective-permute-start(bf16[2,256,512]{2,1,0:T(8,128)(2,1)S(1)} %bitcast.74), channel_id=1, source_target_pairs={{0,4},{12,8},{1,5},{13,9},{2,6},{14,10},{3,7},{15,11},{16,20},{28,... | collective-permute-start | bytes 1572872 | tf_op jit(solution)/shard_map/ppermute | solution.py:24
  88.6 63.5 %collective-permute-start.27 = (bf16[448,1024]{1,0:T(8,128)(2,1)}, bf16[448,1024]{1,0:T(8,128)(2,1)S(1)}, u32[]{:S(2)}, u32[]{:S(2)}) collective-permute-start(bf16[448,1024]{1,0:T(8,128)(2,1)} %collective-permute-done.24), channel_id=1, source_target_pairs={{4,0},{8,12},{5,1},{9,13},{6,2},{10,14},{7,3},{11,15},{20,16},{24,... | collective-permute-start | bytes 2752520 | tf_op jit(solution)/shard_map/ppermute | solution.py:24
  118.4 2.8 %collective-permute-start.15 = (bf16[2,256,512]{2,1,0:T(8,128)(2,1)S(1)}, bf16[2,256,512]{2,1,0:T(8,128)(2,1)S(1)}, u32[]{:S(2)}, u32[]{:S(2)}) collective-permute-start(bf16[2,256,512]{2,1,0:T(8,128)(2,1)S(1)} %fusion), channel_id=1, source_target_pairs={{8,4},{4,8},{9,5},{5,9},{10,6},{6,10},{11,7},{7,11},{24,20},{20,24... | collective-permute-start | bytes 1572872 | tf_op jit(solution)/shard_map/ppermute | solution.py:24
  119.2 18.6 %collective-permute-start.10 = (bf16[256,1024]{1,0:T(8,128)(2,1)S(1)}, bf16[256,1024]{1,0:T(8,128)(2,1)S(1)}, u32[]{:S(2)}, u32[]{:S(2)}) collective-permute-start(bf16[256,1024]{1,0:T(8,128)(2,1)S(1)} %fusion.3), channel_id=1, source_target_pairs={{8,4},{4,8},{9,5},{5,9},{10,6},{6,10},{11,7},{7,11},{24,20},{20,24... | collective-permute-start | bytes 1572872 | tf_op jit(solution)/shard_map/ppermute | solution.py:24
  120.2 57.8 %collective-permute-start.13 = (bf16[256,1024]{1,0:T(8,128)(2,1)S(1)}, bf16[256,1024]{1,0:T(8,128)(2,1)S(1)}, u32[]{:S(2)}, u32[]{:S(2)}) collective-permute-start(bf16[256,1024]{1,0:T(8,128)(2,1)S(1)} %fusion.2), channel_id=1, source_target_pairs={{8,4},{4,8},{9,5},{5,9},{10,6},{6,10},{11,7},{7,11},{24,20},{20,24... | collective-permute-start | bytes 1572872 | tf_op jit(solution)/shard_map/ppermute | solution.py:24
  121.4 27.6 %collective-permute-start.16 = (bf16[256,512]{1,0:T(8,128)(2,1)S(1)}, bf16[256,512]{1,0:T(8,128)(2,1)S(1)}, u32[]{:S(2)}, u32[]{:S(2)}) collective-permute-start(bf16[256,512]{1,0:T(8,128)(2,1)S(1)} %fusion.8), channel_id=1, source_target_pairs={{4,0},{0,4},{12,8},{8,12},{5,1},{1,5},{13,9},{9,13},{6,2},{2,6},{1... | collective-permute-start | bytes 786440 | tf_op jit(solution)/shard_map/ppermute | solution.py:24
  138.0 40.1 %collective-permute-start.11 = (bf16[256,1024]{1,0:T(8,128)(2,1)S(1)}, bf16[256,1024]{1,0:T(8,128)(2,1)S(1)}, u32[]{:S(2)}, u32[]{:S(2)}) collective-permute-start(bf16[256,1024]{1,0:T(8,128)(2,1)S(1)} %add_convert_fusion.3), channel_id=1, source_target_pairs={{4,0},{0,4},{12,8},{8,12},{5,1},{1,5},{13,9},{9,13},{6,2},{2,6},{1... | collective-permute-start | bytes 1572872 | tf_op jit(solution)/shard_map/ppermute | solution.py:24
  149.2 17.9 %collective-permute-start.17 = (bf16[256,512]{1,0:T(8,128)(2,1)S(1)}, bf16[256,512]{1,0:T(8,128)(2,1)S(1)}, u32[]{:S(2)}, u32[]{:S(2)}) collective-permute-start(bf16[256,512]{1,0:T(8,128)(2,1)S(1)} %get-tuple-element.54), channel_id=1, source_target_pairs={{4,0},{0,4},{12,8},{8,12},{5,1},{1,5},{13,9},{9,13},{6,2},{2,6},{1... | collective-permute-start | bytes 786440 | tf_op jit(solution)/shard_map/ppermute | solution.py:24
  149.2 26.7 %collective-permute-start.18 = (bf16[256,512]{1,0:T(8,128)(2,1)S(1)}, bf16[256,512]{1,0:T(8,128)(2,1)S(1)}, u32[]{:S(2)}, u32[]{:S(2)}) collective-permute-start(bf16[256,512]{1,0:T(8,128)(2,1)S(1)} %get-tuple-element.54), channel_id=1, source_target_pairs={{8,0},{12,4},{0,8},{4,12},{9,1},{13,5},{1,9},{5,13},{10,2},{14,6},... | collective-permute-start | bytes 786440 | tf_op jit(solution)/shard_map/ppermute | solution.py:24
  152.1 25.3 %collective-permute-start.19 = (bf16[256,512]{1,0:T(8,128)(2,1)S(1)}, bf16[256,512]{1,0:T(8,128)(2,1)S(1)}, u32[]{:S(2)}, u32[]{:S(2)}) collective-permute-start(bf16[256,512]{1,0:T(8,128)(2,1)S(1)} %get-tuple-element.54), channel_id=1, source_target_pairs={{12,0},{8,4},{4,8},{0,12},{13,1},{9,5},{5,9},{1,13},{14,2},{10,6},... | collective-permute-start | bytes 786440 | tf_op jit(solution)/shard_map/ppermute | solution.py:24
  167.0 23.5 %collective-permute-start.28 = (bf16[448,1024]{1,0:T(8,128)(2,1)}, bf16[448,1024]{1,0:T(8,128)(2,1)}, u32[]{:S(2)}, u32[]{:S(2)}) collective-permute-start(bf16[448,1024]{1,0:T(8,128)(2,1)} %collective-permute-done.23.rest_0_), channel_id=1, source_target_pairs={{0,16},{16,0},{1,17},{17,1},{2,18},{18,2},{3,19},{19,3},{4,20},{20... | collective-permute-start | bytes 2752520 | tf_op jit(solution)/shard_map/ppermute | solution.py:19
  175.9 30.1 %collective-permute-start.29 = (bf16[448,1024]{1,0:T(8,128)(2,1)}, bf16[448,1024]{1,0:T(8,128)(2,1)}, u32[]{:S(2)}, u32[]{:S(2)}) collective-permute-start(bf16[448,1024]{1,0:T(8,128)(2,1)} %broadcast_select_fusion.1.rest_1_), channel_id=1, source_target_pairs={{0,16},{16,0},{1,17},{17,1},{2,18},{18,2},{3,19},{19,3},{4,20},{20... | collective-permute-start | bytes 2752520 | tf_op jit(solution)/shard_map/ppermute | solution.py:19
  177.4 38.5 %collective-permute-start.30 = (bf16[448,1024]{1,0:T(8,128)(2,1)}, bf16[448,1024]{1,0:T(8,128)(2,1)}, u32[]{:S(2)}, u32[]{:S(2)}) collective-permute-start(bf16[448,1024]{1,0:T(8,128)(2,1)} %broadcast_select_fusion.rest_2_), channel_id=1, source_target_pairs={{0,16},{16,0},{1,17},{17,1},{2,18},{18,2},{3,19},{19,3},{4,20},{20... | collective-permute-start | bytes 2752520 | tf_op jit(solution)/shard_map/ppermute | solution.py:19
  184.3 31.6 %collective-permute-start.22 = (bf16[256,1024]{1,0:T(8,128)(2,1)S(1)}, bf16[256,1024]{1,0:T(8,128)(2,1)}, u32[]{:S(2)}, u32[]{:S(2)}) collective-permute-start(bf16[256,1024]{1,0:T(8,128)(2,1)S(1)} %attend.1.ours_ref), channel_id=1, source_target_pairs={{0,1},{1,0},{2,3},{3,2},{4,5},{5,4},{6,7},{7,6},{8,9},{9,8},{10,11... | collective-permute-start | bytes 1572872 | tf_op jit(solution)/shard_map/ppermute | solution.py:19
  221.8 9.2 %collective-permute-start.32 = (bf16[2,256,448]{2,1,0:T(8,128)(2,1)S(1)}, bf16[2,256,448]{2,1,0:T(8,128)(2,1)S(1)}, u32[]{:S(2)}, u32[]{:S(2)}) collective-permute-start(bf16[2,256,448]{2,1,0:T(8,128)(2,1)S(1)} %get-tuple-element.50), channel_id=1, source_target_pairs={{0,2},{2,0},{1,3},{3,1},{4,6},{6,4},{5,7},{7,5},{8,10},{10,8},{9,1... | collective-permute-start | bytes 1376264 | tf_op jit(solution)/shard_map/ppermute | solution.py:19
  222.6 14.2 %collective-permute-start.31 = (bf16[2,256,448]{2,1,0:T(8,128)(2,1)}, bf16[2,256,448]{2,1,0:T(8,128)(2,1)}, u32[]{:S(2)}, u32[]{:S(2)}) collective-permute-start(bf16[2,256,448]{2,1,0:T(8,128)(2,1)} %get-tuple-element.48), channel_id=1, source_target_pairs={{0,2},{2,0},{1,3},{3,1},{4,6},{6,4},{5,7},{7,5},{8,10},{10,8},{9,1... | collective-permute-start | bytes 1376264 | tf_op jit(solution)/shard_map/ppermute | solution.py:19
  231.2 6.9 %collective-permute-start.33 = (bf16[2,256,448]{2,1,0:T(8,128)(2,1)S(1)}, bf16[2,256,448]{2,1,0:T(8,128)(2,1)S(1)}, u32[]{:S(2)}, u32[]{:S(2)}) collective-permute-start(bf16[2,256,448]{2,1,0:T(8,128)(2,1)S(1)} %add_convert_fusion), channel_id=1, source_target_pairs={{0,1},{1,0},{2,3},{3,2},{4,5},{5,4},{6,7},{7,6},{8,9},{9,8},{10,11... | collective-permute-start | bytes 1376264 | tf_op jit(solution)/shard_map/ppermute | solution.py:19
  (15 other events, 143.4 us)

commit v4 on v3

--- a/solution.py
+++ b/solution.py
@@ -35,6 +35,10 @@
 VMEM = pl.BlockSpec(memory_space=pltpu.VMEM)
 SMEM = pl.BlockSpec(memory_space=pltpu.SMEM)
 HBM = pl.BlockSpec(memory_space=pltpu.HBM)
+
+
+def in_hbm(x):
+    return pltpu.with_memory_space_constraint(x, pltpu.HBM)
 
 
 def norm_kernel(place, tokens_ref, gain_ref, mod_ref, own_ref, *rest):
@@ -156,7 +160,7 @@
         ),
         compiler_params=pltpu.CompilerParams(vmem_limit_bytes=40 * 1024 * 1024),
         name="partial",
-    )(place, jnp.concatenate(mods)[:, None], *weights, *arrays)
+    )(place, jnp.concatenate(mods)[:, None], *[in_hbm(w) for w in weights], *arrays)
     return [value.reshape(len(blocks), length, -1) for value in values]
 
 
@@ -173,21 +177,23 @@
     wide = [p.astype(jnp.float32) for p in parts]
 
     def hop(value, bit, among):
-        return cross(value, "seq", bit, among).astype(jnp.float32)
+        return cross(value, "seq", bit, among)
+
+    def plus(a, b):
+        return (a + b.astype(jnp.float32)).astype(jnp.bfloat16)
 
     if two is None:
         got = hop(three, 1, (1, 2))
-        send = (jnp.stack([wide[2], wide[3]]) + got).astype(jnp.bfloat16)
-        got = hop(send, 3, (1, 2))
+        got = hop(plus(jnp.stack([wide[2], wide[3]]), got), 3, (1, 2))
         across, own = got[0], got[1]
     else:
         far = hop(three, 1, (1, 2))
         close = hop(two, 1, (1, 2))
-        send = (wide[2] + far).astype(jnp.bfloat16)
+        send = plus(wide[2], far)
         across = hop(send, 3, (1, 2))
-        own = hop((wide[3] + after(close, send)).astype(jnp.bfloat16), 3, (1, 2))
-    last = hop((wide[1] + across).astype(jnp.bfloat16), 1, None)
-    return (wide[0] + last + own).astype(jnp.bfloat16)
+        own = hop(plus(wide[3], after(close, send)), 3, (1, 2))
+    last = hop(plus(wide[1], across), 1, None)
+    return (wide[0] + last.astype(jnp.float32) + own.astype(jnp.float32)).astype(jnp.bfloat16)
 
 
 def gather_weights(mine):
@@ -226,16 +232,18 @@
     return low, jnp.where(own_mod == 1, end, own_pos)
 
 
-def attention_kernel(starts, limits, q_ref, kv_ref, low_ref, high_ref, o_ref, top, total, acc):
+def attention_kernel(starts, limits, q_ref, kv_ref, low_ref, high_ref, o_ref, queries, top, total, acc):
     count, size, _ = kv_ref.shape
     rows = q_ref.shape[0]
-    heads = q_ref.shape[1] // HEAD_DIM
-    kv_local = kv_ref.shape[2] // (2 * HEAD_DIM)
-    repeat = heads // kv_local
+    kv_local, many = queries.shape[0], queries.shape[1]
+    repeat = many // rows
     scale = math.log2(math.e) / math.sqrt(HEAD_DIM)
     top[...] = jnp.full_like(top, LOW / 10)
     total[...] = jnp.zeros_like(total)
     acc[...] = jnp.zeros_like(acc)
+    for head in range(kv_local * repeat):
+        g, r = head // repeat, head % repeat
+        queries[g, r * rows : (r + 1) * rows] = q_ref[:, head * HEAD_DIM : (head + 1) * HEAD_DIM]
     transposed = (((1,), (1,)), ((), ()))
 
     def visit(number, _):
@@ -243,31 +251,25 @@
         last = start + size - 1
 
         def block(masked):
-            if masked:
-                key_pos = start + lax.broadcasted_iota(jnp.int32, (size, rows), 0)
-                seen = (key_pos >= low_ref[...]) & (key_pos <= high_ref[...])
             for g in range(kv_local):
                 keys = kv_ref[number, :, g * HEAD_DIM : (g + 1) * HEAD_DIM]
                 values = kv_ref[number, :, (kv_local + g) * HEAD_DIM : (kv_local + g + 1) * HEAD_DIM]
-                values = values.T
-                for head in range(g * repeat, (g + 1) * repeat):
-                    query = q_ref[:, head * HEAD_DIM : (head + 1) * HEAD_DIM]
-                    scores = lax.dot_general(
-                        keys, query, transposed, preferred_element_type=jnp.float32
-                    )
-                    if masked:
-                        scores = jnp.where(seen, scores, LOW)
-                    old = top[head : head + 1]
-                    new = jnp.maximum(old, jnp.max(scores, axis=0, keepdims=True))
-                    weights = jnp.exp2((scores - new) * scale)
-                    shrink = jnp.exp2((old - new) * scale)
-                    total[head : head + 1] = total[head : head + 1] * shrink + jnp.sum(
-                        weights, axis=0, keepdims=True
-                    )
-                    top[head : head + 1] = new
-                    acc[head] = acc[head] * shrink + jnp.dot(
-                        values, weights.astype(jnp.bfloat16), preferred_element_type=jnp.float32
-                    )
+                scores = lax.dot_general(
+                    queries[g], keys, transposed, preferred_element_type=jnp.float32
+                )
+                if masked:
+                    key_pos = start + lax.broadcasted_iota(jnp.int32, (many, size), 1)
+                    seen = (key_pos >= low_ref[...]) & (key_pos <= high_ref[...])
+                    scores = jnp.where(seen, scores, LOW)
+                old = top[g]
+                new = jnp.maximum(old, jnp.max(scores, axis=1, keepdims=True))
+                weights = jnp.exp2((scores - jnp.tile(new, (1, size // 128))) * scale)
+                shrink = jnp.exp2((old - new) * scale)
+                total[g] = total[g] * shrink + jnp.sum(weights, axis=1, keepdims=True)
+                top[g] = new
+                acc[g] = acc[g] * shrink + jnp.dot(
+                    weights.astype(jnp.bfloat16), values, preferred_element_type=jnp.float32
+                )
 
         inside = (start >= limits[2]) & (last <= limits[3])
 
@@ -282,9 +284,10 @@
         return 0
 
     lax.fori_loop(0, count, visit, 0)
-    for head in range(heads):
-        o_ref[:, head * HEAD_DIM : (head + 1) * HEAD_DIM] = (
-            (acc[head] / total[head : head + 1]).T.astype(jnp.bfloat16)
+    for head in range(kv_local * repeat):
+        g, at = head // repeat, pl.ds((head % repeat) * rows, rows)
+        o_ref[:, head * HEAD_DIM : (head + 1) * HEAD_DIM] = (acc[g, at] / total[g, at]).astype(
+            jnp.bfloat16
         )
 
 
@@ -292,6 +295,8 @@
     rows, width = query.shape
     heads = width // HEAD_DIM
     count, size, _ = kv.shape
+    kv_local = kv.shape[2] // (2 * HEAD_DIM)
+    many = rows * heads // kv_local
     limits = jnp.stack([low[0], high[-1], low[-1], high[0]])
     return pl.pallas_call(
         attention_kernel,
@@ -299,9 +304,10 @@
         in_specs=[SMEM, SMEM, VMEM, VMEM, VMEM, VMEM],
         out_specs=VMEM,
         scratch_shapes=[
-            pltpu.VMEM((heads, rows), jnp.float32),
-            pltpu.VMEM((heads, rows), jnp.float32),
-            pltpu.VMEM((heads, HEAD_DIM, rows), jnp.float32),
+            pltpu.VMEM((kv_local, many, HEAD_DIM), jnp.bfloat16),
+            pltpu.VMEM((kv_local, many, HEAD_DIM), jnp.float32),
+            pltpu.VMEM((kv_local, many, HEAD_DIM), jnp.float32),
+            pltpu.VMEM((kv_local, many, HEAD_DIM), jnp.float32),
         ],
         cost_estimate=pl.CostEstimate(
             flops=4 * rows * count * size * width,
@@ -310,7 +316,7 @@
         ),
         compiler_params=pltpu.CompilerParams(vmem_limit_bytes=32 * 1024 * 1024),
         name="attend",
-    )(starts, limits, query, kv, low[None, :], high[None, :])
+    )(starts, limits, query, kv, jnp.tile(low, many // rows)[:, None], jnp.tile(high, many // rows)[:, None])
 
 
 def project_kernel(turns, place, ours_ref, beside_ref, ours_near, beside_near, own_ref, *rest):
@@ -320,19 +326,16 @@
     count = turns.shape[0]
     first = place[2]
 
-    def fetch(source, kind, d):
-        slot = jnp.int32(-1)
-        for i in range(count):
-            slot = jnp.where(turns[i] == d, i, slot)
-
-        @pl.when(slot >= 0)
+    def fetch(i, d):
+        @pl.when(turns[i] == d)
         def _():
-            at = jnp.maximum(slot, 0)
-            pltpu.make_async_copy(source, held.at[kind, at], arrived.at[kind, at]).start()
-
-    for d in range(n):
-        fetch(near[d - 1] if d else own_ref.at[first], 0, d)
-        fetch(far[d - 1] if d else own_ref.at[1 - first], 1, d)
+            sources = (near[d - 1], far[d - 1]) if d else (own_ref.at[first], own_ref.at[1 - first])
+            for kind, source in enumerate(sources):
+                pltpu.make_async_copy(source, held.at[kind, i], arrived.at[kind, i]).start()
+
+    for i in range(count):
+        for d in range(n):
+            fetch(i, d)
 
     rows = ours_ref.shape[0]
     for base, a_ref, near_ref in ((0, ours_ref, ours_near), (rows, beside_ref, beside_near)):

time: 241 us -> 238 us (0.988)
    unnamed x30 -> x38, local copies, waits for them, and re-layouts: 5.66 us -> 4.46 us
  transfers between devices with their start and end apart: 34 -> 34, of which waited for: 15 -> 15; matrix products, arithmetic and copies ran while one was open for 6% -> 7% of each run, Pallas kernels for 9% -> 9%
where the time goes in v4:
time: 238 us
  waiting for transfers between devices  104 us (44%)
  starting transfers between devices  80.7 us (34%)
  Pallas kernels  27.1 us (11%)
  local copies, waits for them, and re-layouts  12.4 us (5%)
  other arithmetic  11 us (5%)
  between operations  2.49 us (1%)
    ppermute x19, starting transfers between devices, cross(): return lax.ppermute(x, axis, [(i ^ bit, i) for i in among or range(size)])  68.8 us
    ppermute x19, waiting for transfers between devices, cross(): return lax.ppermute(x, axis, [(i ^ bit, i) for i in among or range(size)])  60.7 us
    ppermute x15, waiting for transfers between devices, swap(): return lax.ppermute(x, axis, [(0, 1), (1, 0)])  43.4 us
    ppermute x15, starting transfers between devices, swap(): return lax.ppermute(x, axis, [(0, 1), (1, 0)])  11.9 us
    pallas_call x2, Pallas kernels, partial(): pl.pallas_call(functools.partial(partial_kernel, counts, narrow), out_sha...  11.2 us
    pallas_call x2, Pallas kernels, project(): pl.pallas_call(project_kernel, out_shape=(shape, shape), in_specs=[SMEM,...  10.4 us
  transfers between devices with their start and end apart: 34, of which 15 were waited for; matrix products, arithmetic and copies ran while one was open for 7% of the time, Pallas kernels for 9%

profile of v4, /device:TPU:0, one launch (start us, length us, event | category | flops | bytes accessed | tf_op | source)
XLA Modules:
  0.0 237.7 jit_solution(7926868864036288460)
XLA Ops:
  0.0 2.3 dynamic-slice_bitcast_fusion
  2.3 3.1 %collective-permute-start.23 = (bf16[448,1024]{1,0:T(8,128)(2,1)}, bf16[448,1024]{1,0:T(8,128)(2,1)}, u32[]{:S(2)}, u32[]{:S(2)}) collective-permute-start(bf16[448,1024]{1,0:T(8,128)(2,1)} %dynamic-slice_bitcast_fusion), channel_id=1, source_target_pairs={{4,0},{0,4},{12,8},{8,12},{5,1},{1,5},{13,9},{9,13},{6,2},{2,6},{1... | collective-permute-start | bytes 2752520 | tf_op jit(solution)/shard_map/ppermute | solution.py:24
  5.4 1.6 collective-permute-start.25
  8.7 2.5 %norm.1 = (bf16[256,896]{1,0:T(8,128)(2,1)S(1)}, bf16[128,896]{1,0:T(8,128)(2,1)S(1)}, bf16[128,896]{1,0:T(8,128)(2,1)}, bf16[128,896]{1,0:T(8,128)(2,1)}) custom-call(s32[4]{0:T(128)S(1)} %pad_add_fusion.2.place, bf16[256,3584]{1,0:T(8,128)(2,1)S(1)} %copy-done.2, f32[2,3584]{1,0:T(2,128)S(1)} %copy-done.6, s32[256,1]{1,0:T(8,128)S(1)} %copy.20.mod_ref), custom_call_target="tpu_custom_call" | custom-call | flops 5505024 | bytes 3670016 | tf_op jit(solution)/shard_map/norm/pallas_call | solution.py:77
  11.9 2.5 %collective-permute-start.5 = (bf16[128,896]{1,0:T(8,128)(2,1)}, bf16[128,896]{1,0:T(8,128)(2,1)S(1)}, u32[]{:S(2)}, u32[]{:S(2)}) collective-permute-start(bf16[128,896]{1,0:T(8,128)(2,1)} %get-tuple-element.37), channel_id=1, source_target_pairs={{12,0},{8,4},{4,8},{0,12},{13,1},{9,5},{5,9},{1,13},{14,2},{10,6},... | collective-permute-start | bytes 688136 | tf_op jit(solution)/shard_map/ppermute | solution.py:24
  14.4 2.5 %collective-permute-start.7 = (bf16[128,896]{1,0:T(8,128)(2,1)}, bf16[128,896]{1,0:T(8,128)(2,1)S(1)}, u32[]{:S(2)}, u32[]{:S(2)}) collective-permute-start(bf16[128,896]{1,0:T(8,128)(2,1)} %get-tuple-element.38), channel_id=1, source_target_pairs={{8,0},{12,4},{0,8},{4,12},{9,1},{13,5},{1,9},{5,13},{10,2},{14,6},... | collective-permute-start | bytes 688136 | tf_op jit(solution)/shard_map/ppermute | solution.py:24
  19.3 15.0 %collective-permute-done.5.rest_6_ = bf16[128,896]{1,0:T(8,128)(2,1)S(1)} collective-permute-done((bf16[128,896]{1,0:T(8,128)(2,1)}, bf16[128,896]{1,0:T(8,128)(2,1)S(1)}, u32[]{:S(2)}, u32[]{:S(2)}) %collective-permute-start.5) | collective-permute-done | bytes 229408 | tf_op jit(solution)/shard_map/ppermute | solution.py:24
  34.3 12.3 %collective-permute-start.3 = (bf16[128,896]{1,0:T(8,128)(2,1)}, bf16[128,896]{1,0:T(8,128)(2,1)S(1)}, u32[]{:S(2)}, u32[]{:S(2)}) collective-permute-start(bf16[128,896]{1,0:T(8,128)(2,1)} %copy-done.9), channel_id=1, source_target_pairs={{4,0},{0,4},{12,8},{8,12},{5,1},{1,5},{13,9},{9,13},{6,2},{2,6},{1... | collective-permute-start | bytes 688136 | tf_op jit(solution)/shard_map/ppermute | solution.py:24
  49.9 4.5 %collective-permute-done.3.rest_6_ = bf16[128,896]{1,0:T(8,128)(2,1)S(1)} collective-permute-done((bf16[128,896]{1,0:T(8,128)(2,1)}, bf16[128,896]{1,0:T(8,128)(2,1)S(1)}, u32[]{:S(2)}, u32[]{:S(2)}) %collective-permute-start.3) | collective-permute-done | bytes 229408 | tf_op jit(solution)/shard_map/ppermute | solution.py:24
  55.0 1.6 collective-permute-start.24
  57.9 1.6 collective-permute-start.6
  63.1 2.6 %pad_add_fusion.3.limits = s32[4]{0:T(128)S(1)} fusion(s32[1]{0:T(128)} %get-tuple-element.74, s32[1]{0:T(128)} %get-tuple-element.67, s32[1]{0:T(128)} %get-tuple-element.75, s32[1]{0:T(128)} %get-tuple-element.66), kind=kLoop, calls=%fused_computation.48 | loop fusion | flops 12 | bytes 32 | tf_op jit(solution)/shard_map/stack | solution.py:300
  67.9 3.4 %collective-permute-done.8.rest_9_ = bf16[128,896]{1,0:T(8,128)(2,1)S(1)} collective-permute-done((bf16[128,896]{1,0:T(8,128)(2,1)S(1)}, bf16[128,896]{1,0:T(8,128)(2,1)S(1)}, u32[]{:S(2)}, u32[]{:S(2)}) %collective-permute-start.8) | collective-permute-done | bytes 229408 | tf_op jit(solution)/shard_map/ppermute | solution.py:19
  71.3 5.6 %partial.3 = (f32[512,512]{1,0:T(8,128)S(1)}, f32[512,1024]{1,0:T(8,128)S(1)}, bf16[512,512]{1,0:T(8,128)(2,1)S(1)}, bf16[512,1024]{1,0:T(8,128)(2,1)S(1)}) custom-call(s32[4]{0:T(128)S(1)} %pad_add_fusion.2.place, s32[512,1]{1,0:T(8,128)S(1)} %copy.22.mod_ref, bf16[2,448,256]{2,1,0:T(8,128)(2,1)} %copy-done.10, ...), custom_call_target="tpu_custom_call" | custom-call | flops 2818572288 | bytes 8650752 | tf_op jit(solution)/shard_map/partial/pallas_call | solution.py:145
  77.0 5.5 %collective-permute-start.12 = (bf16[256,1024]{1,0:T(8,128)(2,1)S(1)}, bf16[256,1024]{1,0:T(8,128)(2,1)S(1)}, u32[]{:S(2)}, u32[]{:S(2)}) collective-permute-start(bf16[256,1024]{1,0:T(8,128)(2,1)S(1)} %get-tuple-element.60), channel_id=1, source_target_pairs={{0,4},{12,8},{1,5},{13,9},{2,6},{14,10},{3,7},{15,11},{16,20},{28,... | collective-permute-start | bytes 1572872 | tf_op jit(solution)/shard_map/ppermute | solution.py:24
  86.6 2.2 broadcast_select_fusion.1.rest_1_
  88.9 5.6 %partial.2 = (f32[512,512]{1,0:T(8,128)S(1)}, f32[512,1024]{1,0:T(8,128)S(1)}) custom-call(s32[4]{0:T(128)S(1)} %pad_add_fusion.2.place, s32[512,1]{1,0:T(8,128)S(1)} %copy.21.mod_ref, bf16[2,448,256]{2,1,0:T(8,128)(2,1)} %copy-done.10, bf16[2,448,256]{2,1,0:T(8,128)(2,1)} %collective-permute-done.rest_1_, bf16[2,448,256]{2,1,0:T(8,128)(2,1)} %copy-done.11, ...), custom_call_target="tpu_custom_call" | custom-call | flops 2818572288 | bytes 8650752 | tf_op jit(solution)/shard_map/partial/pallas_call | solution.py:145
  94.5 20.4 %collective-permute-done.14 = bf16[2,256,512]{2,1,0:T(8,128)(2,1)S(1)} collective-permute-done((bf16[2,256,512]{2,1,0:T(8,128)(2,1)S(1)}, bf16[2,256,512]{2,1,0:T(8,128)(2,1)S(1)}, u32[]{:S(2)}, u32[]{:S(2)}) %collective-permute-start.14) | collective-permute-done | bytes 524320 | tf_op jit(solution)/shard_map/ppermute | solution.py:24
  117.9 16.6 %collective-permute-start.16 = (bf16[256,512]{1,0:T(8,128)(2,1)S(1)}, bf16[256,512]{1,0:T(8,128)(2,1)S(1)}, u32[]{:S(2)}, u32[]{:S(2)}) collective-permute-start(bf16[256,512]{1,0:T(8,128)(2,1)S(1)} %fusion.6), channel_id=1, source_target_pairs={{4,0},{0,4},{12,8},{8,12},{5,1},{1,5},{13,9},{9,13},{6,2},{2,6},{1... | collective-permute-start | bytes 786440 | tf_op jit(solution)/shard_map/ppermute | solution.py:24
  134.6 11.2 %collective-permute-start.11 = (bf16[256,1024]{1,0:T(8,128)(2,1)S(1)}, bf16[256,1024]{1,0:T(8,128)(2,1)S(1)}, u32[]{:S(2)}, u32[]{:S(2)}) collective-permute-start(bf16[256,1024]{1,0:T(8,128)(2,1)S(1)} %add_convert_fusion.3), channel_id=1, source_target_pairs={{4,0},{0,4},{12,8},{8,12},{5,1},{1,5},{13,9},{9,13},{6,2},{2,6},{1... | collective-permute-start | bytes 1572872 | tf_op jit(solution)/shard_map/ppermute | solution.py:24
  146.0 2.9 %collective-permute-start.18 = (bf16[256,512]{1,0:T(8,128)(2,1)S(1)}, bf16[256,512]{1,0:T(8,128)(2,1)S(1)}, u32[]{:S(2)}, u32[]{:S(2)}) collective-permute-start(bf16[256,512]{1,0:T(8,128)(2,1)S(1)} %get-tuple-element.54), channel_id=1, source_target_pairs={{8,0},{12,4},{0,8},{4,12},{9,1},{13,5},{1,9},{5,13},{10,2},{14,6},... | collective-permute-start | bytes 786440 | tf_op jit(solution)/shard_map/ppermute | solution.py:24
  151.4 12.8 %collective-permute-done.17 = bf16[256,512]{1,0:T(8,128)(2,1)S(1)} collective-permute-done((bf16[256,512]{1,0:T(8,128)(2,1)S(1)}, bf16[256,512]{1,0:T(8,128)(2,1)S(1)}, u32[]{:S(2)}, u32[]{:S(2)}) %collective-permute-start.17) | collective-permute-done | bytes 262176 | tf_op jit(solution)/shard_map/ppermute | solution.py:24
  165.8 7.1 %collective-permute-done.18 = bf16[256,512]{1,0:T(8,128)(2,1)S(1)} collective-permute-done((bf16[256,512]{1,0:T(8,128)(2,1)S(1)}, bf16[256,512]{1,0:T(8,128)(2,1)S(1)}, u32[]{:S(2)}, u32[]{:S(2)}) %collective-permute-start.18) | collective-permute-done | bytes 262176 | tf_op jit(solution)/shard_map/ppermute | solution.py:24
  177.8 3.0 %attend.1.ours_ref = bf16[256,1024]{1,0:T(8,128)(2,1)S(1)} custom-call(s32[8]{0:T(128)S(1)} %stack.93.starts, s32[4]{0:T(128)S(1)} %pad_add_fusion.3.limits, bf16[256,1024]{1,0:T(8,128)(2,1)S(1)} %add_convert_fusion.2.q_ref, bf16[8,256,512]{2,1,0:T(8,128)(2,1)S(1)} %constant_dynamic-update-slice_fusion.kv_ref, s32[1024,1]{1,0:T(8,128)S(1)} %bitcast.78, ...), custom_call_target="tpu_custom_call" | custom-call | flops 2147483648 | bytes 3145728 | tf_op jit(solution)/shard_map/attend/pallas_call | solution.py:301
  180.8 2.1 collective-permute-start.22
  183.2 4.6 %collective-permute-done.28.rest_3_ = bf16[448,1024]{1,0:T(8,128)(2,1)} collective-permute-done((bf16[448,1024]{1,0:T(8,128)(2,1)}, bf16[448,1024]{1,0:T(8,128)(2,1)}, u32[]{:S(2)}, u32[]{:S(2)}) %collective-permute-start.28) | collective-permute-done | bytes 917536 | tf_op jit(solution)/shard_map/ppermute | solution.py:19
  187.8 15.7 %collective-permute-done.29.rest_4_ = bf16[448,1024]{1,0:T(8,128)(2,1)} collective-permute-done((bf16[448,1024]{1,0:T(8,128)(2,1)}, bf16[448,1024]{1,0:T(8,128)(2,1)}, u32[]{:S(2)}, u32[]{:S(2)}) %collective-permute-start.29) | collective-permute-done | bytes 917536 | tf_op jit(solution)/shard_map/ppermute | solution.py:19
  203.5 9.8 %collective-permute-done.30.rest_5_ = bf16[448,1024]{1,0:T(8,128)(2,1)} collective-permute-done((bf16[448,1024]{1,0:T(8,128)(2,1)}, bf16[448,1024]{1,0:T(8,128)(2,1)}, u32[]{:S(2)}, u32[]{:S(2)}) %collective-permute-start.30) | collective-permute-done | bytes 917536 | tf_op jit(solution)/shard_map/ppermute | solution.py:19
  213.3 5.9 %project.3 = (bf16[2,256,448]{2,1,0:T(8,128)(2,1)}, bf16[2,256,448]{2,1,0:T(8,128)(2,1)S(1)}) custom-call(s32[2]{0:T(128)S(1)} %get-tuple-element.70.turns, s32[4]{0:T(128)S(1)} %pad_add_fusion.2.place, bf16[256,1024]{1,0:T(8,128)(2,1)S(1)} %attend.1.ours_ref, bf16[256,1024]{1,0:T(8,128)(2,1)} %collective-permute-done.22.beside_ref, ...), custom_call_target="tpu_custom_call" | custom-call | flops 1879048192 | bytes 4587520 | tf_op jit(solution)/shard_map/project/pallas_call | solution.py:366
  221.3 4.5 %project.2 = (bf16[2,256,448]{2,1,0:T(8,128)(2,1)S(1)}, bf16[2,256,448]{2,1,0:T(8,128)(2,1)S(1)}) custom-call(s32[2]{0:T(128)S(1)} %get-tuple-element.71.turns, s32[4]{0:T(128)S(1)} %pad_add_fusion.2.place, bf16[256,1024]{1,0:T(8,128)(2,1)S(1)} %attend.1.ours_ref, bf16[256,1024]{1,0:T(8,128)(2,1)} %collective-permute-done.22.beside_ref, ...), custom_call_target="tpu_custom_call" | custom-call | flops 1879048192 | bytes 4587520 | tf_op jit(solution)/shard_map/project/pallas_call | solution.py:366
  226.6 1.9 collective-permute-done.32
  228.7 5.5 %collective-permute-done.31 = bf16[2,256,448]{2,1,0:T(8,128)(2,1)} collective-permute-done((bf16[2,256,448]{2,1,0:T(8,128)(2,1)}, bf16[2,256,448]{2,1,0:T(8,128)(2,1)}, u32[]{:S(2)}, u32[]{:S(2)}) %collective-permute-start.31) | collective-permute-done | bytes 458784 | tf_op jit(solution)/shard_map/ppermute | solution.py:19
  (128 shorter events, 37.0 us)
Async XLA Ops:
  2.3 52.6 %collective-permute-start.23 = (bf16[448,1024]{1,0:T(8,128)(2,1)}, bf16[448,1024]{1,0:T(8,128)(2,1)}, u32[]{:S(2)}, u32[]{:S(2)}) collective-permute-start(bf16[448,1024]{1,0:T(8,128)(2,1)} %dynamic-slice_bitcast_fusion), channel_id=1, source_target_pairs={{4,0},{0,4},{12,8},{8,12},{5,1},{1,5},{13,9},{9,13},{6,2},{2,6},{1... | collective-permute-start | bytes 2752520 | tf_op jit(solution)/shard_map/ppermute | solution.py:24
  5.4 51.1 %collective-permute-start.25 = (bf16[448,1024]{1,0:T(8,128)(2,1)}, bf16[448,1024]{1,0:T(8,128)(2,1)}, u32[]{:S(2)}, u32[]{:S(2)}) collective-permute-start(bf16[448,1024]{1,0:T(8,128)(2,1)} %dynamic-slice_bitcast_fusion), channel_id=1, source_target_pairs={{8,4},{4,8},{9,5},{5,9},{10,6},{6,10},{11,7},{7,11},{24,20},{20,24... | collective-permute-start | bytes 2752520 | tf_op jit(solution)/shard_map/ppermute | solution.py:24
  11.9 59.4 %collective-permute-start.2 = (bf16[2,448,1024]{2,1,0:T(8,128)(2,1)}, bf16[2,448,1024]{2,1,0:T(8,128)(2,1)}, u32[]{:S(2)}, u32[]{:S(2)}) collective-permute-start(bf16[2,448,1024]{2,1,0:T(8,128)(2,1)} %rest_4_.1), channel_id=1, source_target_pairs={{0,1},{1,0},{2,3},{3,2},{4,5},{5,4},{6,7},{7,6},{8,9},{9,8},{10,11... | collective-permute-start | bytes 5505032 | tf_op jit(solution)/shard_map/ppermute | solution.py:19
  11.9 22.4 %collective-permute-start.5 = (bf16[128,896]{1,0:T(8,128)(2,1)}, bf16[128,896]{1,0:T(8,128)(2,1)S(1)}, u32[]{:S(2)}, u32[]{:S(2)}) collective-permute-start(bf16[128,896]{1,0:T(8,128)(2,1)} %get-tuple-element.37), channel_id=1, source_target_pairs={{12,0},{8,4},{4,8},{0,12},{13,1},{9,5},{5,9},{1,13},{14,2},{10,6},... | collective-permute-start | bytes 688136 | tf_op jit(solution)/shard_map/ppermute | solution.py:24
  14.4 35.6 %collective-permute-start.7 = (bf16[128,896]{1,0:T(8,128)(2,1)}, bf16[128,896]{1,0:T(8,128)(2,1)S(1)}, u32[]{:S(2)}, u32[]{:S(2)}) collective-permute-start(bf16[128,896]{1,0:T(8,128)(2,1)} %get-tuple-element.38), channel_id=1, source_target_pairs={{8,0},{12,4},{0,8},{4,12},{9,1},{13,5},{1,9},{5,13},{10,2},{14,6},... | collective-permute-start | bytes 688136 | tf_op jit(solution)/shard_map/ppermute | solution.py:24
  34.3 20.2 %collective-permute-start.3 = (bf16[128,896]{1,0:T(8,128)(2,1)}, bf16[128,896]{1,0:T(8,128)(2,1)S(1)}, u32[]{:S(2)}, u32[]{:S(2)}) collective-permute-start(bf16[128,896]{1,0:T(8,128)(2,1)} %copy-done.9), channel_id=1, source_target_pairs={{4,0},{0,4},{12,8},{8,12},{5,1},{1,5},{13,9},{9,13},{6,2},{2,6},{1... | collective-permute-start | bytes 688136 | tf_op jit(solution)/shard_map/ppermute | solution.py:24
  49.9 7.9 %collective-permute-start = (bf16[2,448,256]{2,1,0:T(8,128)(2,1)S(1)}, bf16[2,448,256]{2,1,0:T(8,128)(2,1)}, u32[]{:S(2)}, u32[]{:S(2)}) collective-permute-start(bf16[2,448,256]{2,1,0:T(8,128)(2,1)S(1)} %constant_dynamic-slice_fusion.1.rest_0_), channel_id=1, source_target_pairs={{0,1},{1,0},{2,3},{3,2},{4,5},{5,4},{6,7},{7,6},{8,9},{9,8},{10,11... | collective-permute-start | bytes 1376264 | tf_op jit(solution)/shard_map/ppermute | solution.py:19
  54.5 4.9 %collective-permute-start.1 = (bf16[2,448,256]{2,1,0:T(8,128)(2,1)S(1)}, bf16[2,448,256]{2,1,0:T(8,128)(2,1)}, u32[]{:S(2)}, u32[]{:S(2)}) collective-permute-start(bf16[2,448,256]{2,1,0:T(8,128)(2,1)S(1)} %constant_dynamic-slice_fusion.rest_2_), channel_id=1, source_target_pairs={{0,1},{1,0},{2,3},{3,2},{4,5},{5,4},{6,7},{7,6},{8,9},{9,8},{10,11... | collective-permute-start | bytes 1376264 | tf_op jit(solution)/shard_map/ppermute | solution.py:19
  55.0 28.9 %collective-permute-start.24 = (bf16[448,1024]{1,0:T(8,128)(2,1)}, bf16[448,1024]{1,0:T(8,128)(2,1)}, u32[]{:S(2)}, u32[]{:S(2)}) collective-permute-start(bf16[448,1024]{1,0:T(8,128)(2,1)} %collective-permute-done.23.rest_0_), channel_id=1, source_target_pairs={{8,4},{4,8},{9,5},{5,9},{10,6},{6,10},{11,7},{7,11},{24,20},{20,24... | collective-permute-start | bytes 2752520 | tf_op jit(solution)/shard_map/ppermute | solution.py:24
  56.5 28.8 %collective-permute-start.26 = (bf16[448,1024]{1,0:T(8,128)(2,1)}, bf16[448,1024]{1,0:T(8,128)(2,1)}, u32[]{:S(2)}, u32[]{:S(2)}) collective-permute-start(bf16[448,1024]{1,0:T(8,128)(2,1)} %collective-permute-done.25), channel_id=1, source_target_pairs={{4,0},{8,12},{5,1},{9,13},{6,2},{10,14},{7,3},{11,15},{20,16},{24,... | collective-permute-start | bytes 2752520 | tf_op jit(solution)/shard_map/ppermute | solution.py:24
  57.9 8.5 %collective-permute-start.6 = (bf16[128,896]{1,0:T(8,128)(2,1)S(1)}, bf16[128,896]{1,0:T(8,128)(2,1)S(1)}, u32[]{:S(2)}, u32[]{:S(2)}) collective-permute-start(bf16[128,896]{1,0:T(8,128)(2,1)S(1)} %collective-permute-done.5.rest_6_), channel_id=1, source_target_pairs={{0,2},{2,0},{1,3},{3,1},{4,6},{6,4},{5,7},{7,5},{8,10},{10,8},{9,1... | collective-permute-start | bytes 688136 | tf_op jit(solution)/shard_map/ppermute | solution.py:19
  59.4 11.9 %collective-permute-start.8 = (bf16[128,896]{1,0:T(8,128)(2,1)S(1)}, bf16[128,896]{1,0:T(8,128)(2,1)S(1)}, u32[]{:S(2)}, u32[]{:S(2)}) collective-permute-start(bf16[128,896]{1,0:T(8,128)(2,1)S(1)} %collective-permute-done.7.rest_8_), channel_id=1, source_target_pairs={{0,2},{2,0},{1,3},{3,1},{4,6},{6,4},{5,7},{7,5},{8,10},{10,8},{9,1... | collective-permute-start | bytes 688136 | tf_op jit(solution)/shard_map/ppermute | solution.py:19
  66.4 22.5 %collective-permute-start.4 = (bf16[128,896]{1,0:T(8,128)(2,1)S(1)}, bf16[128,896]{1,0:T(8,128)(2,1)S(1)}, u32[]{:S(2)}, u32[]{:S(2)}) collective-permute-start(bf16[128,896]{1,0:T(8,128)(2,1)S(1)} %collective-permute-done.3.rest_6_), channel_id=1, source_target_pairs={{0,2},{2,0},{1,3},{3,1},{4,6},{6,4},{5,7},{7,5},{8,10},{10,8},{9,1... | collective-permute-start | bytes 688136 | tf_op jit(solution)/shard_map/ppermute | solution.py:19
  77.0 39.7 %collective-permute-start.12 = (bf16[256,1024]{1,0:T(8,128)(2,1)S(1)}, bf16[256,1024]{1,0:T(8,128)(2,1)S(1)}, u32[]{:S(2)}, u32[]{:S(2)}) collective-permute-start(bf16[256,1024]{1,0:T(8,128)(2,1)S(1)} %get-tuple-element.60), channel_id=1, source_target_pairs={{0,4},{12,8},{1,5},{13,9},{2,6},{14,10},{3,7},{15,11},{16,20},{28,... | collective-permute-start | bytes 1572872 | tf_op jit(solution)/shard_map/ppermute | solution.py:24
  82.5 33.4 %collective-permute-start.9 = (bf16[256,1024]{1,0:T(8,128)(2,1)S(1)}, bf16[256,1024]{1,0:T(8,128)(2,1)S(1)}, u32[]{:S(2)}, u32[]{:S(2)}) collective-permute-start(bf16[256,1024]{1,0:T(8,128)(2,1)S(1)} %get-tuple-element.59), channel_id=1, source_target_pairs={{0,4},{12,8},{1,5},{13,9},{2,6},{14,10},{3,7},{15,11},{16,20},{28,... | collective-permute-start | bytes 1572872 | tf_op jit(solution)/shard_map/ppermute | solution.py:24
  83.8 31.1 %collective-permute-start.14 = (bf16[2,256,512]{2,1,0:T(8,128)(2,1)S(1)}, bf16[2,256,512]{2,1,0:T(8,128)(2,1)S(1)}, u32[]{:S(2)}, u32[]{:S(2)}) collective-permute-start(bf16[2,256,512]{2,1,0:T(8,128)(2,1)S(1)} %bitcast.80), channel_id=1, source_target_pairs={{0,4},{12,8},{1,5},{13,9},{2,6},{14,10},{3,7},{15,11},{16,20},{28,... | collective-permute-start | bytes 1572872 | tf_op jit(solution)/shard_map/ppermute | solution.py:24
  85.3 63.6 %collective-permute-start.27 = (bf16[448,1024]{1,0:T(8,128)(2,1)}, bf16[448,1024]{1,0:T(8,128)(2,1)S(1)}, u32[]{:S(2)}, u32[]{:S(2)}) collective-permute-start(bf16[448,1024]{1,0:T(8,128)(2,1)} %collective-permute-done.24), channel_id=1, source_target_pairs={{4,0},{8,12},{5,1},{9,13},{6,2},{10,14},{7,3},{11,15},{20,16},{24,... | collective-permute-start | bytes 2752520 | tf_op jit(solution)/shard_map/ppermute | solution.py:24
  116.0 18.4 %collective-permute-start.10 = (bf16[256,1024]{1,0:T(8,128)(2,1)S(1)}, bf16[256,1024]{1,0:T(8,128)(2,1)S(1)}, u32[]{:S(2)}, u32[]{:S(2)}) collective-permute-start(bf16[256,1024]{1,0:T(8,128)(2,1)S(1)} %fusion.3), channel_id=1, source_target_pairs={{8,4},{4,8},{9,5},{5,9},{10,6},{6,10},{11,7},{7,11},{24,20},{20,24... | collective-permute-start | bytes 1572872 | tf_op jit(solution)/shard_map/ppermute | solution.py:24
  116.9 58.0 %collective-permute-start.13 = (bf16[256,1024]{1,0:T(8,128)(2,1)S(1)}, bf16[256,1024]{1,0:T(8,128)(2,1)S(1)}, u32[]{:S(2)}, u32[]{:S(2)}) collective-permute-start(bf16[256,1024]{1,0:T(8,128)(2,1)S(1)} %fusion.2), channel_id=1, source_target_pairs={{8,4},{4,8},{9,5},{5,9},{10,6},{6,10},{11,7},{7,11},{24,20},{20,24... | collective-permute-start | bytes 1572872 | tf_op jit(solution)/shard_map/ppermute | solution.py:24
  117.9 27.9 %collective-permute-start.16 = (bf16[256,512]{1,0:T(8,128)(2,1)S(1)}, bf16[256,512]{1,0:T(8,128)(2,1)S(1)}, u32[]{:S(2)}, u32[]{:S(2)}) collective-permute-start(bf16[256,512]{1,0:T(8,128)(2,1)S(1)} %fusion.6), channel_id=1, source_target_pairs={{4,0},{0,4},{12,8},{8,12},{5,1},{1,5},{13,9},{9,13},{6,2},{2,6},{1... | collective-permute-start | bytes 786440 | tf_op jit(solution)/shard_map/ppermute | solution.py:24
  134.6 40.4 %collective-permute-start.11 = (bf16[256,1024]{1,0:T(8,128)(2,1)S(1)}, bf16[256,1024]{1,0:T(8,128)(2,1)S(1)}, u32[]{:S(2)}, u32[]{:S(2)}) collective-permute-start(bf16[256,1024]{1,0:T(8,128)(2,1)S(1)} %add_convert_fusion.3), channel_id=1, source_target_pairs={{4,0},{0,4},{12,8},{8,12},{5,1},{1,5},{13,9},{9,13},{6,2},{2,6},{1... | collective-permute-start | bytes 1572872 | tf_op jit(solution)/shard_map/ppermute | solution.py:24
  145.9 18.3 %collective-permute-start.17 = (bf16[256,512]{1,0:T(8,128)(2,1)S(1)}, bf16[256,512]{1,0:T(8,128)(2,1)S(1)}, u32[]{:S(2)}, u32[]{:S(2)}) collective-permute-start(bf16[256,512]{1,0:T(8,128)(2,1)S(1)} %get-tuple-element.54), channel_id=1, source_target_pairs={{4,0},{0,4},{12,8},{8,12},{5,1},{1,5},{13,9},{9,13},{6,2},{2,6},{1... | collective-permute-start | bytes 786440 | tf_op jit(solution)/shard_map/ppermute | solution.py:24
  146.0 26.8 %collective-permute-start.18 = (bf16[256,512]{1,0:T(8,128)(2,1)S(1)}, bf16[256,512]{1,0:T(8,128)(2,1)S(1)}, u32[]{:S(2)}, u32[]{:S(2)}) collective-permute-start(bf16[256,512]{1,0:T(8,128)(2,1)S(1)} %get-tuple-element.54), channel_id=1, source_target_pairs={{8,0},{12,4},{0,8},{4,12},{9,1},{13,5},{1,9},{5,13},{10,2},{14,6},... | collective-permute-start | bytes 786440 | tf_op jit(solution)/shard_map/ppermute | solution.py:24
  148.9 25.4 %collective-permute-start.19 = (bf16[256,512]{1,0:T(8,128)(2,1)S(1)}, bf16[256,512]{1,0:T(8,128)(2,1)S(1)}, u32[]{:S(2)}, u32[]{:S(2)}) collective-permute-start(bf16[256,512]{1,0:T(8,128)(2,1)S(1)} %get-tuple-element.54), channel_id=1, source_target_pairs={{12,0},{8,4},{4,8},{0,12},{13,1},{9,5},{5,9},{1,13},{14,2},{10,6},... | collective-permute-start | bytes 786440 | tf_op jit(solution)/shard_map/ppermute | solution.py:24
  164.2 23.5 %collective-permute-start.28 = (bf16[448,1024]{1,0:T(8,128)(2,1)}, bf16[448,1024]{1,0:T(8,128)(2,1)}, u32[]{:S(2)}, u32[]{:S(2)}) collective-permute-start(bf16[448,1024]{1,0:T(8,128)(2,1)} %collective-permute-done.23.rest_0_), channel_id=1, source_target_pairs={{0,16},{16,0},{1,17},{17,1},{2,18},{18,2},{3,19},{19,3},{4,20},{20... | collective-permute-start | bytes 2752520 | tf_op jit(solution)/shard_map/ppermute | solution.py:19
  172.8 30.6 %collective-permute-start.29 = (bf16[448,1024]{1,0:T(8,128)(2,1)}, bf16[448,1024]{1,0:T(8,128)(2,1)}, u32[]{:S(2)}, u32[]{:S(2)}) collective-permute-start(bf16[448,1024]{1,0:T(8,128)(2,1)} %broadcast_select_fusion.1.rest_1_), channel_id=1, source_target_pairs={{0,16},{16,0},{1,17},{17,1},{2,18},{18,2},{3,19},{19,3},{4,20},{20... | collective-permute-start | bytes 2752520 | tf_op jit(solution)/shard_map/ppermute | solution.py:19
  174.4 38.9 %collective-permute-start.30 = (bf16[448,1024]{1,0:T(8,128)(2,1)}, bf16[448,1024]{1,0:T(8,128)(2,1)}, u32[]{:S(2)}, u32[]{:S(2)}) collective-permute-start(bf16[448,1024]{1,0:T(8,128)(2,1)} %broadcast_select_fusion.rest_2_), channel_id=1, source_target_pairs={{0,16},{16,0},{1,17},{17,1},{2,18},{18,2},{3,19},{19,3},{4,20},{20... | collective-permute-start | bytes 2752520 | tf_op jit(solution)/shard_map/ppermute | solution.py:19
  175.1 2.6 %collective-permute-start.21 = (bf16[3,256,512]{2,1,0:T(8,128)(2,1)S(1)}, bf16[3,256,512]{2,1,0:T(8,128)(2,1)S(1)}, u32[]{:S(2)}, u32[]{:S(2)}) collective-permute-start(bf16[3,256,512]{2,1,0:T(8,128)(2,1)S(1)} %pad_maximum_fusion), channel_id=1, source_target_pairs={{0,1},{1,0},{2,3},{3,2},{4,5},{5,4},{6,7},{7,6},{8,9},{9,8},{10,11... | collective-permute-start | bytes 2359304 | tf_op jit(solution)/shard_map/ppermute | solution.py:19
  180.8 32.5 %collective-permute-start.22 = (bf16[256,1024]{1,0:T(8,128)(2,1)S(1)}, bf16[256,1024]{1,0:T(8,128)(2,1)}, u32[]{:S(2)}, u32[]{:S(2)}) collective-permute-start(bf16[256,1024]{1,0:T(8,128)(2,1)S(1)} %attend.1.ours_ref), channel_id=1, source_target_pairs={{0,1},{1,0},{2,3},{3,2},{4,5},{5,4},{6,7},{7,6},{8,9},{9,8},{10,11... | collective-permute-start | bytes 1572872 | tf_op jit(solution)/shard_map/ppermute | solution.py:19
  219.2 9.2 %collective-permute-start.32 = (bf16[2,256,448]{2,1,0:T(8,128)(2,1)S(1)}, bf16[2,256,448]{2,1,0:T(8,128)(2,1)S(1)}, u32[]{:S(2)}, u32[]{:S(2)}) collective-permute-start(bf16[2,256,448]{2,1,0:T(8,128)(2,1)S(1)} %get-tuple-element.50), channel_id=1, source_target_pairs={{0,2},{2,0},{1,3},{3,1},{4,6},{6,4},{5,7},{7,5},{8,10},{10,8},{9,1... | collective-permute-start | bytes 1376264 | tf_op jit(solution)/shard_map/ppermute | solution.py:19
  220.1 14.1 %collective-permute-start.31 = (bf16[2,256,448]{2,1,0:T(8,128)(2,1)}, bf16[2,256,448]{2,1,0:T(8,128)(2,1)}, u32[]{:S(2)}, u32[]{:S(2)}) collective-permute-start(bf16[2,256,448]{2,1,0:T(8,128)(2,1)} %get-tuple-element.48), channel_id=1, source_target_pairs={{0,2},{2,0},{1,3},{3,1},{4,6},{6,4},{5,7},{7,5},{8,10},{10,8},{9,1... | collective-permute-start | bytes 1376264 | tf_op jit(solution)/shard_map/ppermute | solution.py:19
  228.6 6.9 %collective-permute-start.33 = (bf16[2,256,448]{2,1,0:T(8,128)(2,1)S(1)}, bf16[2,256,448]{2,1,0:T(8,128)(2,1)S(1)}, u32[]{:S(2)}, u32[]{:S(2)}) collective-permute-start(bf16[2,256,448]{2,1,0:T(8,128)(2,1)S(1)} %add_convert_fusion), channel_id=1, source_target_pairs={{0,1},{1,0},{2,3},{3,2},{4,5},{5,4},{6,7},{7,6},{8,9},{9,8},{10,11... | collective-permute-start | bytes 1376264 | tf_op jit(solution)/shard_map/ppermute | solution.py:19
  (16 other events, 243.7 us)

commit v5 on v4

--- a/solution.py
+++ b/solution.py
@@ -451,7 +451,8 @@
     for d in range(1, n):
         same.append(cross(kv, "seq", d))
     beside_0 = swap(kv, "sub")
-    others = swap(jnp.stack(same[1:]), "sub")
+    held = jnp.stack(same[1:])
+    others = swap(held, "sub")
     kv_all = jnp.concatenate([jnp.stack(same), beside_0[None], others])
     starts = jnp.stack(
         [((z ^ d) * subs + s) * length for d in range(n)]
@@ -476,12 +477,16 @@
         wide = placed(*out(jnp.arange(n)))
         return lax.psum_scatter(wide, "head", scatter_dimension=1, tiled=True)
 
-    half = jnp.arange(n // 2)
-    send_ours, send_beside = out((1 - x) * (n // 2) + half)
-    got_beside = swap(send_beside, "head")
-    got_ours = swap(send_ours, "head")
-    keep_ours, keep_beside = out(x * (n // 2) + half)
-    return placed(add(keep_ours, got_ours), add(keep_beside, got_beside))
+    half = n // 2
+    ours, theirs = [], []
+    sent = [out((1 - x) * half + jnp.arange(i, i + 1)) for i in range(half)]
+    for send_ours, send_beside in sent:
+        theirs.append(swap(send_beside, "head"))
+        ours.append(swap(send_ours, "head"))
+    keep_ours, keep_beside = out(x * half + jnp.arange(half))
+    return placed(
+        add(keep_ours, jnp.concatenate(ours)), add(keep_beside, jnp.concatenate(theirs))
+    )
 
 
 def solution(mesh):

time: 238 us -> 240 us (level)
  Pallas kernels: 27.1 us -> 30.1 us
  waiting for transfers between devices: 104 us -> 101 us
    pallas_call x2 -> x3, Pallas kernels: 10.4 us -> 13.4 us  [project(): pl.pallas_call(project_kernel, out_shape=(shape, shape), in_specs=[SMEM,...]
    ppermute x15 -> x17, waiting for transfers between devices: 43.4 us -> 40.5 us  [swap(): return lax.ppermute(x, axis, [(0, 1), (1, 0)])]
    ppermute x15 -> x17, starting transfers between devices: 11.9 us -> 13.5 us  [swap(): return lax.ppermute(x, axis, [(0, 1), (1, 0)])]
  transfers between devices with their start and end apart: 34 -> 36, of which waited for: 15 -> 15; matrix products, arithmetic and copies ran while one was open for 7% -> 7% of each run, Pallas kernels for 9% -> 11%
where the time goes in v5:
time: 240 us; the launch traced here: 239 us
  waiting for transfers between devices  101 us (42%)
  starting transfers between devices  82.3 us (34%)
  Pallas kernels  30.1 us (13%)
  local copies, waits for them, and re-layouts  12.4 us (5%)
  other arithmetic  11 us (5%)
  between operations  2.47 us (1%)
    ppermute x19, starting transfers between devices, cross(): return lax.ppermute(x, axis, [(i ^ bit, i) for i in among or range(size)])  68.8 us
    ppermute x19, waiting for transfers between devices, cross(): return lax.ppermute(x, axis, [(i ^ bit, i) for i in among or range(size)])  60.7 us
    ppermute x17, waiting for transfers between devices, swap(): return lax.ppermute(x, axis, [(0, 1), (1, 0)])  40.5 us
    ppermute x17, starting transfers between devices, swap(): return lax.ppermute(x, axis, [(0, 1), (1, 0)])  13.5 us
    pallas_call x3, Pallas kernels, project(): pl.pallas_call(project_kernel, out_shape=(shape, shape), in_specs=[SMEM,...  13.4 us
    pallas_call x2, Pallas kernels, partial(): pl.pallas_call(functools.partial(partial_kernel, counts, narrow), out_sha...  11.2 us
  transfers between devices with their start and end apart: 36, of which 15 were waited for; matrix products, arithmetic and copies ran while one was open for 7% of the time, Pallas kernels for 11%

profile of v5, /device:TPU:0, one launch (start us, length us, event | category | flops | bytes accessed | tf_op | source)
XLA Modules:
  0.0 239.4 jit_solution(15738316177412966784)
XLA Ops:
  0.0 2.3 dynamic-slice_bitcast_fusion
  2.3 3.1 %collective-permute-start.23 = (bf16[448,1024]{1,0:T(8,128)(2,1)}, bf16[448,1024]{1,0:T(8,128)(2,1)}, u32[]{:S(2)}, u32[]{:S(2)}) collective-permute-start(bf16[448,1024]{1,0:T(8,128)(2,1)} %dynamic-slice_bitcast_fusion), channel_id=1, source_target_pairs={{4,0},{0,4},{12,8},{8,12},{5,1},{1,5},{13,9},{9,13},{6,2},{2,6},{1... | collective-permute-start | bytes 2752520 | tf_op jit(solution)/shard_map/ppermute | solution.py:24
  5.4 1.6 collective-permute-start.25
  8.7 2.4 %norm.1 = (bf16[256,896]{1,0:T(8,128)(2,1)S(1)}, bf16[128,896]{1,0:T(8,128)(2,1)S(1)}, bf16[128,896]{1,0:T(8,128)(2,1)}, bf16[128,896]{1,0:T(8,128)(2,1)}) custom-call(s32[4]{0:T(128)S(1)} %pad_add_fusion.2.place, bf16[256,3584]{1,0:T(8,128)(2,1)S(1)} %copy-done.2, f32[2,3584]{1,0:T(2,128)S(1)} %copy-done.6, s32[256,1]{1,0:T(8,128)S(1)} %copy.22.mod_ref), custom_call_target="tpu_custom_call" | custom-call | flops 5505024 | bytes 3670016 | tf_op jit(solution)/shard_map/norm/pallas_call | solution.py:77
  11.9 2.5 %collective-permute-start.5 = (bf16[128,896]{1,0:T(8,128)(2,1)}, bf16[128,896]{1,0:T(8,128)(2,1)S(1)}, u32[]{:S(2)}, u32[]{:S(2)}) collective-permute-start(bf16[128,896]{1,0:T(8,128)(2,1)} %get-tuple-element.39), channel_id=1, source_target_pairs={{12,0},{8,4},{4,8},{0,12},{13,1},{9,5},{5,9},{1,13},{14,2},{10,6},... | collective-permute-start | bytes 688136 | tf_op jit(solution)/shard_map/ppermute | solution.py:24
  14.4 2.4 %collective-permute-start.7 = (bf16[128,896]{1,0:T(8,128)(2,1)}, bf16[128,896]{1,0:T(8,128)(2,1)S(1)}, u32[]{:S(2)}, u32[]{:S(2)}) collective-permute-start(bf16[128,896]{1,0:T(8,128)(2,1)} %get-tuple-element.40), channel_id=1, source_target_pairs={{8,0},{12,4},{0,8},{4,12},{9,1},{13,5},{1,9},{5,13},{10,2},{14,6},... | collective-permute-start | bytes 688136 | tf_op jit(solution)/shard_map/ppermute | solution.py:24
  19.3 15.0 %collective-permute-done.5.rest_6_ = bf16[128,896]{1,0:T(8,128)(2,1)S(1)} collective-permute-done((bf16[128,896]{1,0:T(8,128)(2,1)}, bf16[128,896]{1,0:T(8,128)(2,1)S(1)}, u32[]{:S(2)}, u32[]{:S(2)}) %collective-permute-start.5) | collective-permute-done | bytes 229408 | tf_op jit(solution)/shard_map/ppermute | solution.py:24
  34.3 12.3 %collective-permute-start.3 = (bf16[128,896]{1,0:T(8,128)(2,1)}, bf16[128,896]{1,0:T(8,128)(2,1)S(1)}, u32[]{:S(2)}, u32[]{:S(2)}) collective-permute-start(bf16[128,896]{1,0:T(8,128)(2,1)} %copy-done.9), channel_id=1, source_target_pairs={{4,0},{0,4},{12,8},{8,12},{5,1},{1,5},{13,9},{9,13},{6,2},{2,6},{1... | collective-permute-start | bytes 688136 | tf_op jit(solution)/shard_map/ppermute | solution.py:24
  49.9 4.5 %collective-permute-done.3.rest_6_ = bf16[128,896]{1,0:T(8,128)(2,1)S(1)} collective-permute-done((bf16[128,896]{1,0:T(8,128)(2,1)}, bf16[128,896]{1,0:T(8,128)(2,1)S(1)}, u32[]{:S(2)}, u32[]{:S(2)}) %collective-permute-start.3) | collective-permute-done | bytes 229408 | tf_op jit(solution)/shard_map/ppermute | solution.py:24
  63.1 2.6 %pad_add_fusion.3.limits = s32[4]{0:T(128)S(1)} fusion(s32[1]{0:T(128)} %get-tuple-element.76, s32[1]{0:T(128)} %get-tuple-element.71, s32[1]{0:T(128)} %get-tuple-element.77, s32[1]{0:T(128)} %get-tuple-element.70), kind=kLoop, calls=%fused_computation.48 | loop fusion | flops 12 | bytes 32 | tf_op jit(solution)/shard_map/stack | solution.py:300
  67.9 3.4 %collective-permute-done.8.rest_9_ = bf16[128,896]{1,0:T(8,128)(2,1)S(1)} collective-permute-done((bf16[128,896]{1,0:T(8,128)(2,1)S(1)}, bf16[128,896]{1,0:T(8,128)(2,1)S(1)}, u32[]{:S(2)}, u32[]{:S(2)}) %collective-permute-start.8) | collective-permute-done | bytes 229408 | tf_op jit(solution)/shard_map/ppermute | solution.py:19
  71.3 5.6 %partial.3 = (f32[512,512]{1,0:T(8,128)S(1)}, f32[512,1024]{1,0:T(8,128)S(1)}, bf16[512,512]{1,0:T(8,128)(2,1)S(1)}, bf16[512,1024]{1,0:T(8,128)(2,1)S(1)}) custom-call(s32[4]{0:T(128)S(1)} %pad_add_fusion.2.place, s32[512,1]{1,0:T(8,128)S(1)} %copy.24.mod_ref, bf16[2,448,256]{2,1,0:T(8,128)(2,1)} %copy-done.10, ...), custom_call_target="tpu_custom_call" | custom-call | flops 2818572288 | bytes 8650752 | tf_op jit(solution)/shard_map/partial/pallas_call | solution.py:145
  77.0 5.5 %collective-permute-start.12 = (bf16[256,1024]{1,0:T(8,128)(2,1)S(1)}, bf16[256,1024]{1,0:T(8,128)(2,1)S(1)}, u32[]{:S(2)}, u32[]{:S(2)}) collective-permute-start(bf16[256,1024]{1,0:T(8,128)(2,1)S(1)} %get-tuple-element.64), channel_id=1, source_target_pairs={{0,4},{12,8},{1,5},{13,9},{2,6},{14,10},{3,7},{15,11},{16,20},{28,... | collective-permute-start | bytes 1572872 | tf_op jit(solution)/shard_map/ppermute | solution.py:24
  86.6 2.2 broadcast_select_fusion.1.rest_1_
  88.9 5.6 %partial.2 = (f32[512,512]{1,0:T(8,128)S(1)}, f32[512,1024]{1,0:T(8,128)S(1)}) custom-call(s32[4]{0:T(128)S(1)} %pad_add_fusion.2.place, s32[512,1]{1,0:T(8,128)S(1)} %copy.23.mod_ref, bf16[2,448,256]{2,1,0:T(8,128)(2,1)} %copy-done.10, bf16[2,448,256]{2,1,0:T(8,128)(2,1)} %collective-permute-done.rest_1_, bf16[2,448,256]{2,1,0:T(8,128)(2,1)} %copy-done.11, ...), custom_call_target="tpu_custom_call" | custom-call | flops 2818572288 | bytes 8650752 | tf_op jit(solution)/shard_map/partial/pallas_call | solution.py:145
  94.5 20.4 %collective-permute-done.14 = bf16[2,256,512]{2,1,0:T(8,128)(2,1)S(1)} collective-permute-done((bf16[2,256,512]{2,1,0:T(8,128)(2,1)S(1)}, bf16[2,256,512]{2,1,0:T(8,128)(2,1)S(1)}, u32[]{:S(2)}, u32[]{:S(2)}) %collective-permute-start.14) | collective-permute-done | bytes 524320 | tf_op jit(solution)/shard_map/ppermute | solution.py:24
  117.9 16.6 %collective-permute-start.16 = (bf16[256,512]{1,0:T(8,128)(2,1)S(1)}, bf16[256,512]{1,0:T(8,128)(2,1)S(1)}, u32[]{:S(2)}, u32[]{:S(2)}) collective-permute-start(bf16[256,512]{1,0:T(8,128)(2,1)S(1)} %fusion.6), channel_id=1, source_target_pairs={{4,0},{0,4},{12,8},{8,12},{5,1},{1,5},{13,9},{9,13},{6,2},{2,6},{1... | collective-permute-start | bytes 786440 | tf_op jit(solution)/shard_map/ppermute | solution.py:24
  134.6 11.2 %collective-permute-start.11 = (bf16[256,1024]{1,0:T(8,128)(2,1)S(1)}, bf16[256,1024]{1,0:T(8,128)(2,1)S(1)}, u32[]{:S(2)}, u32[]{:S(2)}) collective-permute-start(bf16[256,1024]{1,0:T(8,128)(2,1)S(1)} %add_convert_fusion.3), channel_id=1, source_target_pairs={{4,0},{0,4},{12,8},{8,12},{5,1},{1,5},{13,9},{9,13},{6,2},{2,6},{1... | collective-permute-start | bytes 1572872 | tf_op jit(solution)/shard_map/ppermute | solution.py:24
  146.0 2.9 %collective-permute-start.18 = (bf16[256,512]{1,0:T(8,128)(2,1)S(1)}, bf16[256,512]{1,0:T(8,128)(2,1)S(1)}, u32[]{:S(2)}, u32[]{:S(2)}) collective-permute-start(bf16[256,512]{1,0:T(8,128)(2,1)S(1)} %get-tuple-element.58), channel_id=1, source_target_pairs={{8,0},{12,4},{0,8},{4,12},{9,1},{13,5},{1,9},{5,13},{10,2},{14,6},... | collective-permute-start | bytes 786440 | tf_op jit(solution)/shard_map/ppermute | solution.py:24
  151.4 12.8 %collective-permute-done.17 = bf16[256,512]{1,0:T(8,128)(2,1)S(1)} collective-permute-done((bf16[256,512]{1,0:T(8,128)(2,1)S(1)}, bf16[256,512]{1,0:T(8,128)(2,1)S(1)}, u32[]{:S(2)}, u32[]{:S(2)}) %collective-permute-start.17) | collective-permute-done | bytes 262176 | tf_op jit(solution)/shard_map/ppermute | solution.py:24
  165.8 7.1 %collective-permute-done.18 = bf16[256,512]{1,0:T(8,128)(2,1)S(1)} collective-permute-done((bf16[256,512]{1,0:T(8,128)(2,1)S(1)}, bf16[256,512]{1,0:T(8,128)(2,1)S(1)}, u32[]{:S(2)}, u32[]{:S(2)}) %collective-permute-start.18) | collective-permute-done | bytes 262176 | tf_op jit(solution)/shard_map/ppermute | solution.py:24
  177.8 3.0 %attend.1.ours_ref = bf16[256,1024]{1,0:T(8,128)(2,1)S(1)} custom-call(s32[8]{0:T(128)S(1)} %stack.93.starts, s32[4]{0:T(128)S(1)} %pad_add_fusion.3.limits, bf16[256,1024]{1,0:T(8,128)(2,1)S(1)} %add_convert_fusion.2.q_ref, bf16[8,256,512]{2,1,0:T(8,128)(2,1)S(1)} %constant_dynamic-update-slice_fusion.kv_ref, s32[1024,1]{1,0:T(8,128)S(1)} %bitcast.80, ...), custom_call_target="tpu_custom_call" | custom-call | flops 2147483648 | bytes 3145728 | tf_op jit(solution)/shard_map/attend/pallas_call | solution.py:301
  180.8 2.1 collective-permute-start.22
  183.2 4.6 %collective-permute-done.28.rest_3_ = bf16[448,1024]{1,0:T(8,128)(2,1)} collective-permute-done((bf16[448,1024]{1,0:T(8,128)(2,1)}, bf16[448,1024]{1,0:T(8,128)(2,1)}, u32[]{:S(2)}, u32[]{:S(2)}) %collective-permute-start.28) | collective-permute-done | bytes 917536 | tf_op jit(solution)/shard_map/ppermute | solution.py:19
  187.8 15.7 %collective-permute-done.29.rest_4_ = bf16[448,1024]{1,0:T(8,128)(2,1)} collective-permute-done((bf16[448,1024]{1,0:T(8,128)(2,1)}, bf16[448,1024]{1,0:T(8,128)(2,1)}, u32[]{:S(2)}, u32[]{:S(2)}) %collective-permute-start.29) | collective-permute-done | bytes 917536 | tf_op jit(solution)/shard_map/ppermute | solution.py:19
  203.5 9.8 %collective-permute-done.30.rest_5_ = bf16[448,1024]{1,0:T(8,128)(2,1)} collective-permute-done((bf16[448,1024]{1,0:T(8,128)(2,1)}, bf16[448,1024]{1,0:T(8,128)(2,1)}, u32[]{:S(2)}, u32[]{:S(2)}) %collective-permute-start.30) | collective-permute-done | bytes 917536 | tf_op jit(solution)/shard_map/ppermute | solution.py:19
  213.3 4.5 %project.5 = (bf16[1,256,448]{2,1,0:T(8,128)(2,1)}, bf16[1,256,448]{2,1,0:T(8,128)(2,1)S(1)}) custom-call(s32[1]{0:T(128)S(6)} %xor.35.turns, s32[4]{0:T(128)S(1)} %pad_add_fusion.2.place, bf16[256,1024]{1,0:T(8,128)(2,1)S(1)} %attend.1.ours_ref, bf16[256,1024]{1,0:T(8,128)(2,1)} %collective-permute-done.22.beside_ref, ...), custom_call_target="tpu_custom_call" | custom-call | flops 939524096 | bytes 2293760 | tf_op jit(solution)/shard_map/project/pallas_call | solution.py:366
  219.3 4.4 %project.4 = (bf16[1,256,448]{2,1,0:T(8,128)(2,1)}, bf16[1,256,448]{2,1,0:T(8,128)(2,1)S(1)}) custom-call(s32[1]{0:T(128)S(6)} %xor.34.turns, s32[4]{0:T(128)S(1)} %pad_add_fusion.2.place, bf16[256,1024]{1,0:T(8,128)(2,1)S(1)} %attend.1.ours_ref, bf16[256,1024]{1,0:T(8,128)(2,1)} %collective-permute-done.22.beside_ref, ...), custom_call_target="tpu_custom_call" | custom-call | flops 939524096 | bytes 2293760 | tf_op jit(solution)/shard_map/project/pallas_call | solution.py:366
  223.9 2.0 collective-permute-start.32
  226.0 4.5 %project.3 = (bf16[2,256,448]{2,1,0:T(8,128)(2,1)S(1)}, bf16[2,256,448]{2,1,0:T(8,128)(2,1)S(1)}) custom-call(s32[2]{0:T(128)S(1)} %add_xor_fusion.turns, s32[4]{0:T(128)S(1)} %pad_add_fusion.2.place, bf16[256,1024]{1,0:T(8,128)(2,1)S(1)} %attend.1.ours_ref, bf16[256,1024]{1,0:T(8,128)(2,1)} %collective-permute-done.22.beside_ref, ...), custom_call_target="tpu_custom_call" | custom-call | flops 1879048192 | bytes 4587520 | tf_op jit(solution)/shard_map/project/pallas_call | solution.py:366
  231.5 1.6 collective-permute-done.32
  233.1 2.8 %collective-permute-done.31 = bf16[1,256,448]{2,1,0:T(8,128)(2,1)} collective-permute-done((bf16[1,256,448]{2,1,0:T(8,128)(2,1)}, bf16[1,256,448]{2,1,0:T(8,128)(2,1)}, u32[]{:S(2)}, u32[]{:S(2)}) %collective-permute-start.31) | collective-permute-done | bytes 229408 | tf_op jit(solution)/shard_map/ppermute | solution.py:19
  (133 shorter events, 39.8 us)
Async XLA Ops:
  2.3 52.6 %collective-permute-start.23 = (bf16[448,1024]{1,0:T(8,128)(2,1)}, bf16[448,1024]{1,0:T(8,128)(2,1)}, u32[]{:S(2)}, u32[]{:S(2)}) collective-permute-start(bf16[448,1024]{1,0:T(8,128)(2,1)} %dynamic-slice_bitcast_fusion), channel_id=1, source_target_pairs={{4,0},{0,4},{12,8},{8,12},{5,1},{1,5},{13,9},{9,13},{6,2},{2,6},{1... | collective-permute-start | bytes 2752520 | tf_op jit(solution)/shard_map/ppermute | solution.py:24
  5.4 51.1 %collective-permute-start.25 = (bf16[448,1024]{1,0:T(8,128)(2,1)}, bf16[448,1024]{1,0:T(8,128)(2,1)}, u32[]{:S(2)}, u32[]{:S(2)}) collective-permute-start(bf16[448,1024]{1,0:T(8,128)(2,1)} %dynamic-slice_bitcast_fusion), channel_id=1, source_target_pairs={{8,4},{4,8},{9,5},{5,9},{10,6},{6,10},{11,7},{7,11},{24,20},{20,24... | collective-permute-start | bytes 2752520 | tf_op jit(solution)/shard_map/ppermute | solution.py:24
  11.9 59.4 %collective-permute-start.2 = (bf16[2,448,1024]{2,1,0:T(8,128)(2,1)}, bf16[2,448,1024]{2,1,0:T(8,128)(2,1)}, u32[]{:S(2)}, u32[]{:S(2)}) collective-permute-start(bf16[2,448,1024]{2,1,0:T(8,128)(2,1)} %rest_4_.1), channel_id=1, source_target_pairs={{0,1},{1,0},{2,3},{3,2},{4,5},{5,4},{6,7},{7,6},{8,9},{9,8},{10,11... | collective-permute-start | bytes 5505032 | tf_op jit(solution)/shard_map/ppermute | solution.py:19
  11.9 22.4 %collective-permute-start.5 = (bf16[128,896]{1,0:T(8,128)(2,1)}, bf16[128,896]{1,0:T(8,128)(2,1)S(1)}, u32[]{:S(2)}, u32[]{:S(2)}) collective-permute-start(bf16[128,896]{1,0:T(8,128)(2,1)} %get-tuple-element.39), channel_id=1, source_target_pairs={{12,0},{8,4},{4,8},{0,12},{13,1},{9,5},{5,9},{1,13},{14,2},{10,6},... | collective-permute-start | bytes 688136 | tf_op jit(solution)/shard_map/ppermute | solution.py:24
  14.4 35.5 %collective-permute-start.7 = (bf16[128,896]{1,0:T(8,128)(2,1)}, bf16[128,896]{1,0:T(8,128)(2,1)S(1)}, u32[]{:S(2)}, u32[]{:S(2)}) collective-permute-start(bf16[128,896]{1,0:T(8,128)(2,1)} %get-tuple-element.40), channel_id=1, source_target_pairs={{8,0},{12,4},{0,8},{4,12},{9,1},{13,5},{1,9},{5,13},{10,2},{14,6},... | collective-permute-start | bytes 688136 | tf_op jit(solution)/shard_map/ppermute | solution.py:24
  34.3 20.2 %collective-permute-start.3 = (bf16[128,896]{1,0:T(8,128)(2,1)}, bf16[128,896]{1,0:T(8,128)(2,1)S(1)}, u32[]{:S(2)}, u32[]{:S(2)}) collective-permute-start(bf16[128,896]{1,0:T(8,128)(2,1)} %copy-done.9), channel_id=1, source_target_pairs={{4,0},{0,4},{12,8},{8,12},{5,1},{1,5},{13,9},{9,13},{6,2},{2,6},{1... | collective-permute-start | bytes 688136 | tf_op jit(solution)/shard_map/ppermute | solution.py:24
  49.9 7.9 %collective-permute-start = (bf16[2,448,256]{2,1,0:T(8,128)(2,1)S(1)}, bf16[2,448,256]{2,1,0:T(8,128)(2,1)}, u32[]{:S(2)}, u32[]{:S(2)}) collective-permute-start(bf16[2,448,256]{2,1,0:T(8,128)(2,1)S(1)} %constant_dynamic-slice_fusion.1.rest_0_), channel_id=1, source_target_pairs={{0,1},{1,0},{2,3},{3,2},{4,5},{5,4},{6,7},{7,6},{8,9},{9,8},{10,11... | collective-permute-start | bytes 1376264 | tf_op jit(solution)/shard_map/ppermute | solution.py:19
  55.0 28.9 %collective-permute-start.24 = (bf16[448,1024]{1,0:T(8,128)(2,1)}, bf16[448,1024]{1,0:T(8,128)(2,1)}, u32[]{:S(2)}, u32[]{:S(2)}) collective-permute-start(bf16[448,1024]{1,0:T(8,128)(2,1)} %collective-permute-done.23.rest_0_), channel_id=1, source_target_pairs={{8,4},{4,8},{9,5},{5,9},{10,6},{6,10},{11,7},{7,11},{24,20},{20,24... | collective-permute-start | bytes 2752520 | tf_op jit(solution)/shard_map/ppermute | solution.py:24
  56.5 28.8 %collective-permute-start.26 = (bf16[448,1024]{1,0:T(8,128)(2,1)}, bf16[448,1024]{1,0:T(8,128)(2,1)}, u32[]{:S(2)}, u32[]{:S(2)}) collective-permute-start(bf16[448,1024]{1,0:T(8,128)(2,1)} %collective-permute-done.25), channel_id=1, source_target_pairs={{4,0},{8,12},{5,1},{9,13},{6,2},{10,14},{7,3},{11,15},{20,16},{24,... | collective-permute-start | bytes 2752520 | tf_op jit(solution)/shard_map/ppermute | solution.py:24
  57.8 8.5 %collective-permute-start.6 = (bf16[128,896]{1,0:T(8,128)(2,1)S(1)}, bf16[128,896]{1,0:T(8,128)(2,1)S(1)}, u32[]{:S(2)}, u32[]{:S(2)}) collective-permute-start(bf16[128,896]{1,0:T(8,128)(2,1)S(1)} %collective-permute-done.5.rest_6_), channel_id=1, source_target_pairs={{0,2},{2,0},{1,3},{3,1},{4,6},{6,4},{5,7},{7,5},{8,10},{10,8},{9,1... | collective-permute-start | bytes 688136 | tf_op jit(solution)/shard_map/ppermute | solution.py:19
  59.4 11.9 %collective-permute-start.8 = (bf16[128,896]{1,0:T(8,128)(2,1)S(1)}, bf16[128,896]{1,0:T(8,128)(2,1)S(1)}, u32[]{:S(2)}, u32[]{:S(2)}) collective-permute-start(bf16[128,896]{1,0:T(8,128)(2,1)S(1)} %collective-permute-done.7.rest_8_), channel_id=1, source_target_pairs={{0,2},{2,0},{1,3},{3,1},{4,6},{6,4},{5,7},{7,5},{8,10},{10,8},{9,1... | collective-permute-start | bytes 688136 | tf_op jit(solution)/shard_map/ppermute | solution.py:19
  66.4 22.5 %collective-permute-start.4 = (bf16[128,896]{1,0:T(8,128)(2,1)S(1)}, bf16[128,896]{1,0:T(8,128)(2,1)S(1)}, u32[]{:S(2)}, u32[]{:S(2)}) collective-permute-start(bf16[128,896]{1,0:T(8,128)(2,1)S(1)} %collective-permute-done.3.rest_6_), channel_id=1, source_target_pairs={{0,2},{2,0},{1,3},{3,1},{4,6},{6,4},{5,7},{7,5},{8,10},{10,8},{9,1... | collective-permute-start | bytes 688136 | tf_op jit(solution)/shard_map/ppermute | solution.py:19
  77.0 39.7 %collective-permute-start.12 = (bf16[256,1024]{1,0:T(8,128)(2,1)S(1)}, bf16[256,1024]{1,0:T(8,128)(2,1)S(1)}, u32[]{:S(2)}, u32[]{:S(2)}) collective-permute-start(bf16[256,1024]{1,0:T(8,128)(2,1)S(1)} %get-tuple-element.64), channel_id=1, source_target_pairs={{0,4},{12,8},{1,5},{13,9},{2,6},{14,10},{3,7},{15,11},{16,20},{28,... | collective-permute-start | bytes 1572872 | tf_op jit(solution)/shard_map/ppermute | solution.py:24
  82.5 33.4 %collective-permute-start.9 = (bf16[256,1024]{1,0:T(8,128)(2,1)S(1)}, bf16[256,1024]{1,0:T(8,128)(2,1)S(1)}, u32[]{:S(2)}, u32[]{:S(2)}) collective-permute-start(bf16[256,1024]{1,0:T(8,128)(2,1)S(1)} %get-tuple-element.63), channel_id=1, source_target_pairs={{0,4},{12,8},{1,5},{13,9},{2,6},{14,10},{3,7},{15,11},{16,20},{28,... | collective-permute-start | bytes 1572872 | tf_op jit(solution)/shard_map/ppermute | solution.py:24
  83.8 31.2 %collective-permute-start.14 = (bf16[2,256,512]{2,1,0:T(8,128)(2,1)S(1)}, bf16[2,256,512]{2,1,0:T(8,128)(2,1)S(1)}, u32[]{:S(2)}, u32[]{:S(2)}) collective-permute-start(bf16[2,256,512]{2,1,0:T(8,128)(2,1)S(1)} %bitcast.82), channel_id=1, source_target_pairs={{0,4},{12,8},{1,5},{13,9},{2,6},{14,10},{3,7},{15,11},{16,20},{28,... | collective-permute-start | bytes 1572872 | tf_op jit(solution)/shard_map/ppermute | solution.py:24
  85.3 63.6 %collective-permute-start.27 = (bf16[448,1024]{1,0:T(8,128)(2,1)}, bf16[448,1024]{1,0:T(8,128)(2,1)S(1)}, u32[]{:S(2)}, u32[]{:S(2)}) collective-permute-start(bf16[448,1024]{1,0:T(8,128)(2,1)} %collective-permute-done.24), channel_id=1, source_target_pairs={{4,0},{8,12},{5,1},{9,13},{6,2},{10,14},{7,3},{11,15},{20,16},{24,... | collective-permute-start | bytes 2752520 | tf_op jit(solution)/shard_map/ppermute | solution.py:24
  116.0 18.4 %collective-permute-start.10 = (bf16[256,1024]{1,0:T(8,128)(2,1)S(1)}, bf16[256,1024]{1,0:T(8,128)(2,1)S(1)}, u32[]{:S(2)}, u32[]{:S(2)}) collective-permute-start(bf16[256,1024]{1,0:T(8,128)(2,1)S(1)} %fusion.3), channel_id=1, source_target_pairs={{8,4},{4,8},{9,5},{5,9},{10,6},{6,10},{11,7},{7,11},{24,20},{20,24... | collective-permute-start | bytes 1572872 | tf_op jit(solution)/shard_map/ppermute | solution.py:24
  116.9 58.0 %collective-permute-start.13 = (bf16[256,1024]{1,0:T(8,128)(2,1)S(1)}, bf16[256,1024]{1,0:T(8,128)(2,1)S(1)}, u32[]{:S(2)}, u32[]{:S(2)}) collective-permute-start(bf16[256,1024]{1,0:T(8,128)(2,1)S(1)} %fusion.2), channel_id=1, source_target_pairs={{8,4},{4,8},{9,5},{5,9},{10,6},{6,10},{11,7},{7,11},{24,20},{20,24... | collective-permute-start | bytes 1572872 | tf_op jit(solution)/shard_map/ppermute | solution.py:24
  117.9 27.9 %collective-permute-start.16 = (bf16[256,512]{1,0:T(8,128)(2,1)S(1)}, bf16[256,512]{1,0:T(8,128)(2,1)S(1)}, u32[]{:S(2)}, u32[]{:S(2)}) collective-permute-start(bf16[256,512]{1,0:T(8,128)(2,1)S(1)} %fusion.6), channel_id=1, source_target_pairs={{4,0},{0,4},{12,8},{8,12},{5,1},{1,5},{13,9},{9,13},{6,2},{2,6},{1... | collective-permute-start | bytes 786440 | tf_op jit(solution)/shard_map/ppermute | solution.py:24
  134.6 40.4 %collective-permute-start.11 = (bf16[256,1024]{1,0:T(8,128)(2,1)S(1)}, bf16[256,1024]{1,0:T(8,128)(2,1)S(1)}, u32[]{:S(2)}, u32[]{:S(2)}) collective-permute-start(bf16[256,1024]{1,0:T(8,128)(2,1)S(1)} %add_convert_fusion.3), channel_id=1, source_target_pairs={{4,0},{0,4},{12,8},{8,12},{5,1},{1,5},{13,9},{9,13},{6,2},{2,6},{1... | collective-permute-start | bytes 1572872 | tf_op jit(solution)/shard_map/ppermute | solution.py:24
  145.9 18.3 %collective-permute-start.17 = (bf16[256,512]{1,0:T(8,128)(2,1)S(1)}, bf16[256,512]{1,0:T(8,128)(2,1)S(1)}, u32[]{:S(2)}, u32[]{:S(2)}) collective-permute-start(bf16[256,512]{1,0:T(8,128)(2,1)S(1)} %get-tuple-element.58), channel_id=1, source_target_pairs={{4,0},{0,4},{12,8},{8,12},{5,1},{1,5},{13,9},{9,13},{6,2},{2,6},{1... | collective-permute-start | bytes 786440 | tf_op jit(solution)/shard_map/ppermute | solution.py:24
  146.0 26.8 %collective-permute-start.18 = (bf16[256,512]{1,0:T(8,128)(2,1)S(1)}, bf16[256,512]{1,0:T(8,128)(2,1)S(1)}, u32[]{:S(2)}, u32[]{:S(2)}) collective-permute-start(bf16[256,512]{1,0:T(8,128)(2,1)S(1)} %get-tuple-element.58), channel_id=1, source_target_pairs={{8,0},{12,4},{0,8},{4,12},{9,1},{13,5},{1,9},{5,13},{10,2},{14,6},... | collective-permute-start | bytes 786440 | tf_op jit(solution)/shard_map/ppermute | solution.py:24
  148.9 25.4 %collective-permute-start.19 = (bf16[256,512]{1,0:T(8,128)(2,1)S(1)}, bf16[256,512]{1,0:T(8,128)(2,1)S(1)}, u32[]{:S(2)}, u32[]{:S(2)}) collective-permute-start(bf16[256,512]{1,0:T(8,128)(2,1)S(1)} %get-tuple-element.58), channel_id=1, source_target_pairs={{12,0},{8,4},{4,8},{0,12},{13,1},{9,5},{5,9},{1,13},{14,2},{10,6},... | collective-permute-start | bytes 786440 | tf_op jit(solution)/shard_map/ppermute | solution.py:24
  164.2 23.5 %collective-permute-start.28 = (bf16[448,1024]{1,0:T(8,128)(2,1)}, bf16[448,1024]{1,0:T(8,128)(2,1)}, u32[]{:S(2)}, u32[]{:S(2)}) collective-permute-start(bf16[448,1024]{1,0:T(8,128)(2,1)} %collective-permute-done.23.rest_0_), channel_id=1, source_target_pairs={{0,16},{16,0},{1,17},{17,1},{2,18},{18,2},{3,19},{19,3},{4,20},{20... | collective-permute-start | bytes 2752520 | tf_op jit(solution)/shard_map/ppermute | solution.py:19
  172.8 30.6 %collective-permute-start.29 = (bf16[448,1024]{1,0:T(8,128)(2,1)}, bf16[448,1024]{1,0:T(8,128)(2,1)}, u32[]{:S(2)}, u32[]{:S(2)}) collective-permute-start(bf16[448,1024]{1,0:T(8,128)(2,1)} %broadcast_select_fusion.1.rest_1_), channel_id=1, source_target_pairs={{0,16},{16,0},{1,17},{17,1},{2,18},{18,2},{3,19},{19,3},{4,20},{20... | collective-permute-start | bytes 2752520 | tf_op jit(solution)/shard_map/ppermute | solution.py:19
  174.4 38.9 %collective-permute-start.30 = (bf16[448,1024]{1,0:T(8,128)(2,1)}, bf16[448,1024]{1,0:T(8,128)(2,1)}, u32[]{:S(2)}, u32[]{:S(2)}) collective-permute-start(bf16[448,1024]{1,0:T(8,128)(2,1)} %broadcast_select_fusion.rest_2_), channel_id=1, source_target_pairs={{0,16},{16,0},{1,17},{17,1},{2,18},{18,2},{3,19},{19,3},{4,20},{20... | collective-permute-start | bytes 2752520 | tf_op jit(solution)/shard_map/ppermute | solution.py:19
  180.8 32.5 %collective-permute-start.22 = (bf16[256,1024]{1,0:T(8,128)(2,1)S(1)}, bf16[256,1024]{1,0:T(8,128)(2,1)}, u32[]{:S(2)}, u32[]{:S(2)}) collective-permute-start(bf16[256,1024]{1,0:T(8,128)(2,1)S(1)} %attend.1.ours_ref), channel_id=1, source_target_pairs={{0,1},{1,0},{2,3},{3,2},{4,5},{5,4},{6,7},{7,6},{8,9},{9,8},{10,11... | collective-permute-start | bytes 1572872 | tf_op jit(solution)/shard_map/ppermute | solution.py:19
  217.8 13.5 %collective-permute-start.34 = (bf16[1,256,448]{2,1,0:T(8,128)(2,1)S(1)}, bf16[1,256,448]{2,1,0:T(8,128)(2,1)S(1)}, u32[]{:S(2)}, u32[]{:S(2)}) collective-permute-start(bf16[1,256,448]{2,1,0:T(8,128)(2,1)S(1)} %get-tuple-element.54), channel_id=1, source_target_pairs={{0,2},{2,0},{1,3},{3,1},{4,6},{6,4},{5,7},{7,5},{8,10},{10,8},{9,1... | collective-permute-start | bytes 688136 | tf_op jit(solution)/shard_map/ppermute | solution.py:19
  223.8 7.5 %collective-permute-start.33 = (bf16[1,256,448]{2,1,0:T(8,128)(2,1)S(1)}, bf16[1,256,448]{2,1,0:T(8,128)(2,1)S(1)}, u32[]{:S(2)}, u32[]{:S(2)}) collective-permute-start(bf16[1,256,448]{2,1,0:T(8,128)(2,1)S(1)} %get-tuple-element.53), channel_id=1, source_target_pairs={{0,2},{2,0},{1,3},{3,1},{4,6},{6,4},{5,7},{7,5},{8,10},{10,8},{9,1... | collective-permute-start | bytes 688136 | tf_op jit(solution)/shard_map/ppermute | solution.py:19
  223.9 9.3 %collective-permute-start.32 = (bf16[1,256,448]{2,1,0:T(8,128)(2,1)}, bf16[1,256,448]{2,1,0:T(8,128)(2,1)}, u32[]{:S(2)}, u32[]{:S(2)}) collective-permute-start(bf16[1,256,448]{2,1,0:T(8,128)(2,1)} %get-tuple-element.51), channel_id=1, source_target_pairs={{0,2},{2,0},{1,3},{3,1},{4,6},{6,4},{5,7},{7,5},{8,10},{10,8},{9,1... | collective-permute-start | bytes 688136 | tf_op jit(solution)/shard_map/ppermute | solution.py:19
  225.9 10.1 %collective-permute-start.31 = (bf16[1,256,448]{2,1,0:T(8,128)(2,1)}, bf16[1,256,448]{2,1,0:T(8,128)(2,1)}, u32[]{:S(2)}, u32[]{:S(2)}) collective-permute-start(bf16[1,256,448]{2,1,0:T(8,128)(2,1)} %get-tuple-element.50), channel_id=1, source_target_pairs={{0,2},{2,0},{1,3},{3,1},{4,6},{6,4},{5,7},{7,5},{8,10},{10,8},{9,1... | collective-permute-start | bytes 688136 | tf_op jit(solution)/shard_map/ppermute | solution.py:19
  231.4 5.9 %collective-permute-start.35 = (bf16[2,256,448]{2,1,0:T(8,128)(2,1)S(1)}, bf16[2,256,448]{2,1,0:T(8,128)(2,1)S(1)}, u32[]{:S(2)}, u32[]{:S(2)}) collective-permute-start(bf16[2,256,448]{2,1,0:T(8,128)(2,1)S(1)} %add_convert_fusion), channel_id=1, source_target_pairs={{0,1},{1,0},{2,3},{3,2},{4,5},{5,4},{6,7},{7,6},{8,9},{9,8},{10,11... | collective-permute-start | bytes 1376264 | tf_op jit(solution)/shard_map/ppermute | solution.py:19
  (18 other events, 251.2 us)

commit v6 on v5

--- a/solution.py
+++ b/solution.py
@@ -11,6 +11,7 @@
 
 HEAD_DIM = 128
 KV_HEADS = 4
+RUN = 64
 EPS = 1e-06
 LOW = -1e30
 
@@ -41,13 +42,14 @@
     return pltpu.with_memory_space_constraint(x, pltpu.HBM)
 
 
-def norm_kernel(place, tokens_ref, gain_ref, mod_ref, own_ref, *rest):
+def norm_kernel(place, modality, tokens_ref, gain_ref, own_ref, *rest):
     send_refs, scratch = rest[:-1], rest[-1]
     width = own_ref.shape[1]
-    values = tokens_ref[...].astype(jnp.float32)
-    factor = lax.rsqrt(jnp.mean(values * values, axis=1, keepdims=True) + EPS)
-    gain = jnp.where(mod_ref[...] == 1, gain_ref[1:2, :], gain_ref[0:1, :])
-    scratch[...] = (values * factor * gain).astype(jnp.bfloat16)
+    for at in range(0, tokens_ref.shape[0], RUN):
+        values = tokens_ref[at : at + RUN].astype(jnp.float32)
+        factor = lax.rsqrt(jnp.mean(values * values, axis=1, keepdims=True) + EPS)
+        gain = jnp.where(modality[place[4] + at] == 1, gain_ref[1:2, :], gain_ref[0:1, :])
+        scratch[at : at + RUN] = (values * factor * gain).astype(jnp.bfloat16)
 
     def columns(d):
         return pl.ds(pl.multiple_of((place[0] ^ d) * width, width), width)
@@ -58,7 +60,7 @@
         ref[...] = scratch[pl.ds(pl.multiple_of(place[1] * rows, rows), rows), columns(d)]
 
 
-def norm_columns(tokens, norm_gain, mod, place, n, rows):
+def norm_columns(tokens, norm_gain, modality, mod, place, n, rows):
     length, depth = tokens.shape
     width = depth // n
     if width % 128:
@@ -77,25 +79,27 @@
     return pl.pallas_call(
         norm_kernel,
         out_shape=shapes,
-        in_specs=[SMEM, VMEM, VMEM, VMEM],
+        in_specs=[SMEM, SMEM, VMEM, VMEM],
         out_specs=[VMEM] * n,
         scratch_shapes=[pltpu.VMEM((length, depth), jnp.bfloat16)],
         cost_estimate=pl.CostEstimate(
             flops=6 * length * depth, bytes_accessed=4 * length * depth, transcendentals=length
         ),
-        compiler_params=pltpu.CompilerParams(vmem_limit_bytes=32 * 1024 * 1024),
+        compiler_params=pltpu.CompilerParams(vmem_limit_bytes=12 * 1024 * 1024),
         name="norm",
-    )(place, tokens, norm_gain, mod[:, None])
-
-
-def partial_kernel(counts, narrow, place, mod_ref, *rest):
+    )(place, modality, tokens, norm_gain)
+
+
+def partial_kernel(counts, narrow, place, modality, begins, *rest):
     total = sum(counts)
-    sources, refs, outs = rest[:6], rest[6 : 6 + total], rest[6 + total : -4]
-    both, held_kv, held_q, arrived = rest[-4:]
+    sources, refs, outs = rest[:6], rest[6 : 6 + total], rest[6 + total : -8]
+    both, other, held_kv, held_q, arrived = rest[-8:-3]
+    wide_kv, wide_q, left = rest[-3:]
     kv_half = held_kv.shape[2] // 2
     depth = held_kv.shape[1] // 2
     copies = []
-    for i, source in enumerate(sources):
+    for i in (4, 5, 0, 1, 2, 3):
+        source = sources[i]
         core = place[3] if i % 2 == 0 else 1 - place[3]
         at = pl.ds(pl.multiple_of(core * depth, depth), depth)
         target = (
@@ -105,6 +109,7 @@
         )[i // 2]
         copies.append(pltpu.make_async_copy(source, target, arrived.at[i]))
         copies[-1].start()
+    stores = []
     length = both.shape[0] // len(counts)
     at = 0
     for number, count in enumerate(counts):
@@ -116,52 +121,67 @@
             both[pl.ds(pl.multiple_of(base + place[1] * half, half), half)] = refs[at][...]
             both[pl.ds(pl.multiple_of(base + (1 - place[1]) * half, half), half)] = refs[at + 1][...]
         at += count
-    block = both[...]
-    generate = mod_ref[...] == 1
-    zero = jnp.zeros_like(block)
-    first, second = jnp.where(generate, zero, block), jnp.where(generate, block, zero)
-    for i, held in enumerate((held_kv, held_q)):
-        for copy in (copies[:4], copies[4:])[i]:
+    for number in range(len(counts)):
+        for step in range(0, length, RUN):
+            at = pl.ds(number * length + step, RUN)
+            generate = modality[begins[number] + step] == 1
+            block = both[at]
+            zero = jnp.zeros_like(block)
+            both[at] = jnp.where(generate, zero, block)
+            other[at] = jnp.where(generate, block, zero)
+    first, second = both[...], other[...]
+    for i, held, wide in ((1, held_q, wide_q), (0, held_kv, wide_kv)):
+        for copy in (copies[2:], copies[:2])[i]:
             copy.wait()
         value = jnp.dot(first, held[0], preferred_element_type=jnp.float32) + jnp.dot(
             second, held[1], preferred_element_type=jnp.float32
         )
-        outs[i][...] = value
-        if narrow:
-            outs[2 + i][...] = value.astype(jnp.bfloat16)
-
-
-def partial(blocks, mods, weights, place, narrow):
+        wide[...] = value
+        stores.append(pltpu.make_async_copy(wide, outs[i], left.at[i]))
+        stores[-1].start()
+        if narrow and i == 0:
+            outs[2][...] = value.astype(jnp.bfloat16)
+        elif narrow:
+            for number in range(len(counts)):
+                part = value[number * length : (number + 1) * length]
+                outs[3 + number][...] = part.astype(jnp.bfloat16)
+    for store in stores:
+        store.wait()
+
+
+def partial(blocks, begins, length, modality, weights, place, narrow):
     counts = tuple(len(block) for block in blocks)
     arrays = [array for block in blocks for array in block]
-    length = mods[0].shape[0]
     rows, width = length * len(blocks), arrays[0].shape[1]
     kv_cols, q_cols = 2 * weights[0].shape[2], weights[4].shape[2]
-    shapes = [
-        jax.ShapeDtypeStruct((rows, cols), dtype)
-        for dtype in (jnp.float32, jnp.bfloat16)[: 1 + narrow]
-        for cols in (kv_cols, q_cols)
-    ]
+    shapes = [pltpu.HBM((rows, cols), jnp.float32) for cols in (kv_cols, q_cols)]
+    if narrow:
+        shapes.append(jax.ShapeDtypeStruct((rows, kv_cols), jnp.bfloat16))
+        shapes += [jax.ShapeDtypeStruct((length, q_cols), jnp.bfloat16)] * len(blocks)
     values = pl.pallas_call(
         functools.partial(partial_kernel, counts, narrow),
         out_shape=shapes,
-        in_specs=[SMEM, VMEM] + [HBM] * len(weights) + [VMEM] * len(arrays),
-        out_specs=[VMEM] * len(shapes),
+        in_specs=[SMEM] * 3 + [HBM] * len(weights) + [VMEM] * len(arrays),
+        out_specs=[HBM] * 2 + [VMEM] * (len(shapes) - 2),
         scratch_shapes=[
+            pltpu.VMEM((rows, width), jnp.bfloat16),
             pltpu.VMEM((rows, width), jnp.bfloat16),
             pltpu.VMEM((2, width, kv_cols), jnp.bfloat16),
             pltpu.VMEM((2, width, q_cols), jnp.bfloat16),
             pltpu.SemaphoreType.DMA((len(weights),)),
+            pltpu.VMEM((rows, kv_cols), jnp.float32),
+            pltpu.VMEM((rows, q_cols), jnp.float32),
+            pltpu.SemaphoreType.DMA((2,)),
         ],
         cost_estimate=pl.CostEstimate(
             flops=4 * rows * width * (kv_cols + q_cols),
             bytes_accessed=4 * (width + rows) * (kv_cols + q_cols),
             transcendentals=0,
         ),
-        compiler_params=pltpu.CompilerParams(vmem_limit_bytes=40 * 1024 * 1024),
+        compiler_params=pltpu.CompilerParams(vmem_limit_bytes=24 * 1024 * 1024),
         name="partial",
-    )(place, jnp.concatenate(mods)[:, None], *[in_hbm(w) for w in weights], *arrays)
-    return [value.reshape(len(blocks), length, -1) for value in values]
+    )(place, modality, begins, *[in_hbm(w) for w in weights], *arrays)
+    return [value.reshape(len(blocks), length, -1) for value in values[:3]] + list(values[3:])
 
 
 def halving(parts):
@@ -291,7 +311,7 @@
         )
 
 
-def attend(query, kv, starts, low, high):
+def attend(query, kv, starts, low, high, low_column, high_column):
     rows, width = query.shape
     heads = width // HEAD_DIM
     count, size, _ = kv.shape
@@ -314,9 +334,9 @@
             bytes_accessed=2 * (2 * rows * width + kv.size),
             transcendentals=rows * count * size * heads,
         ),
-        compiler_params=pltpu.CompilerParams(vmem_limit_bytes=32 * 1024 * 1024),
+        compiler_params=pltpu.CompilerParams(vmem_limit_bytes=20 * 1024 * 1024),
         name="attend",
-    )(starts, limits, query, kv, jnp.tile(low, many // rows)[:, None], jnp.tile(high, many // rows)[:, None])
+    )(starts, limits, query, kv, low_column, high_column)
 
 
 def project_kernel(turns, place, ours_ref, beside_ref, ours_near, beside_near, own_ref, *rest):
@@ -378,7 +398,7 @@
             bytes_accessed=4 * count * depth * width + 4 * count * rows * width,
             transcendentals=0,
         ),
-        compiler_params=pltpu.CompilerParams(vmem_limit_bytes=32 * 1024 * 1024),
+        compiler_params=pltpu.CompilerParams(vmem_limit_bytes=16 * 1024 * 1024),
         name="project",
     )(turns, place, ours, beside, ours_near[:, None], beside_near[:, None], *weights)
 
@@ -390,7 +410,7 @@
     heads_over = lax.axis_size("head")
     z, s = lax.axis_index("seq"), lax.axis_index("sub")
     x, y = lax.axis_index("head"), lax.axis_index("grp")
-    place = jnp.stack([z, x, y, s]).astype(jnp.int32)
+    place = jnp.stack([z, x, y, s, (z * subs + s) * length]).astype(jnp.int32)
 
     kv_local = max(KV_HEADS // heads_over, 1)
     kv_first = x * KV_HEADS // heads_over
@@ -406,7 +426,7 @@
     own_mod = part_of(modality, z, s)
     share_rows = heads_over == 2
     rows = length // 2 if share_rows else length
-    sends = norm_columns(tokens, norm_gain, own_mod, place, n, rows)
+    sends = norm_columns(tokens, norm_gain, modality, own_mod, place, n, rows)
     blocks = {0: (sends[0],)}
     for d in range(n - 1, 0, -1):
         blocks[d] = (cross(sends[d], "seq", d),)
@@ -422,19 +442,21 @@
     own_doc = part_of(doc_ids, z, s)
     own_pos = (z * subs + s) * length + jnp.arange(length, dtype=jnp.int32)
     low, high = spans(modality, doc_ids, part_of(modality, z, s), own_doc, own_pos)
-    blocks[1] = after(blocks[1], low, high)
+    repeat = w_query.shape[2] // HEAD_DIM // kv_local
+    low_column, high_column = jnp.tile(low, repeat)[:, None], jnp.tile(high, repeat)[:, None]
 
     if share_rows:
         for d in range(n - 1, 0, -1):
             blocks[d] = (*blocks[d], swap(blocks[d][0], "head"))
+    blocks[n - 1] = after(blocks[n - 1], low_column, high_column)
 
     def parts_of(group, narrow):
-        mods = [part_of(modality, z ^ d, s) for d in group]
-        return partial([blocks[d] for d in group], mods, row_weights, place, narrow)
+        begins = jnp.stack([((z ^ d) * subs + s) * length for d in group]).astype(jnp.int32)
+        arrays = [blocks[d] for d in group]
+        return partial(arrays, begins, length, modality, row_weights, place, narrow)
 
     if n == 4:
-        kv_early, q_early, kv_rounded, q_rounded = parts_of([3, 2], True)
-        kv_ends, q_three, q_two = kv_rounded, q_rounded[0], q_rounded[1]
+        kv_early, q_early, kv_ends, q_three, q_two = parts_of([3, 2], True)
         kv_late, q_late = parts_of([1, 0], False)
         kv_early, q_early = after((kv_early, q_early), kv_late, q_late)
         kv = along_four([kv_late[1], kv_late[0], kv_early[1], kv_early[0]], kv_ends, None)
@@ -458,7 +480,7 @@
         [((z ^ d) * subs + s) * length for d in range(n)]
         + [((z ^ d) * subs + (1 - s)) * length for d in range(n)]
     ).astype(jnp.int32)
-    attended = attend(query, kv_all, starts, low, high)
+    attended = attend(query, kv_all, starts, low, high, low_column, high_column)
 
     beside = swap(attended, "sub")
     ours_near = (own_mod == y).astype(jnp.bfloat16)
@@ -468,13 +490,11 @@
         turns = (columns ^ z).astype(jnp.int32)
         return project(attended, beside, ours_near, beside_near, weights, turns, place)
 
-    def placed(ours, theirs):
+    if heads_over != 2:
+        ours, theirs = out(jnp.arange(n))
         sibling = swap(theirs, "sub")
         pair = jnp.where(s == 0, jnp.stack([ours, sibling], 1), jnp.stack([sibling, ours], 1))
-        return jnp.transpose(pair, (2, 0, 1, 3)).reshape(length, -1)
-
-    if heads_over != 2:
-        wide = placed(*out(jnp.arange(n)))
+        wide = jnp.transpose(pair, (2, 0, 1, 3)).reshape(length, -1)
         return lax.psum_scatter(wide, "head", scatter_dimension=1, tiled=True)
 
     half = n // 2
@@ -484,9 +504,42 @@
         theirs.append(swap(send_beside, "head"))
         ours.append(swap(send_ours, "head"))
     keep_ours, keep_beside = out(x * half + jnp.arange(half))
-    return placed(
-        add(keep_ours, jnp.concatenate(ours)), add(keep_beside, jnp.concatenate(theirs))
-    )
+    done = add(keep_beside, jnp.concatenate(theirs))
+    sibling = swap(done, "sub")
+    return finish(place, keep_ours, ours, sibling)
+
+
+def finish_kernel(place, keep_ref, *rest):
+    got_refs, sibling_ref, o_ref = rest[:-2], rest[-2], rest[-1]
+    width = keep_ref.shape[2]
+
+    def fill(core):
+        for i, got_ref in enumerate(got_refs):
+            own = keep_ref[i].astype(jnp.float32) + got_ref[0].astype(jnp.float32)
+            for piece, slot in ((own.astype(jnp.bfloat16), core), (sibling_ref[i], 1 - core)):
+                at = (2 * i + slot) * width
+                o_ref[:, at : at + width] = piece
+
+    for core in range(2):
+
+        @pl.when(place[3] == core)
+        def _():
+            fill(core)
+
+
+def finish(place, keep, got, sibling):
+    count, rows, width = keep.shape
+    return pl.pallas_call(
+        finish_kernel,
+        out_shape=jax.ShapeDtypeStruct((rows, 2 * count * width), jnp.bfloat16),
+        in_specs=[SMEM] + [VMEM] * (2 + len(got)),
+        out_specs=VMEM,
+        cost_estimate=pl.CostEstimate(
+            flops=count * rows * width, bytes_accessed=12 * count * rows * width, transcendentals=0
+        ),
+        compiler_params=pltpu.CompilerParams(vmem_limit_bytes=12 * 1024 * 1024),
+        name="finish",
+    )(place, keep, *got, sibling)
 
 
 def solution(mesh):

time: 240 us -> 258 us (1.075)
  waiting for transfers between devices: 101 us -> 127 us
  starting transfers between devices: 82.3 us -> 70 us
  Pallas kernels: 30.1 us -> 34.4 us
    ppermute x19, waiting for transfers between devices: 60.7 us -> 75.5 us  [cross(): return lax.ppermute(x, axis, [(i ^ bit, i) for i in among or range(size)])]
    ppermute x19, starting transfers between devices: 68.8 us -> 56.6 us  [cross(): return lax.ppermute(x, axis, [(i ^ bit, i) for i in among or range(size)])]
    ppermute x17, waiting for transfers between devices: 40.5 us -> 51.7 us  [swap(): return lax.ppermute(x, axis, [(0, 1), (1, 0)])]
    pallas_call x2, Pallas kernels: 11.2 us -> 15 us  [partial(): pl.pallas_call(functools.partial(partial_kernel, counts, narrow), out_sha...]
    unnamed x38 -> x52, local copies, waits for them, and re-layouts: 4.46 us -> 5.81 us
  transfers between devices with their start and end apart: 36 -> 36, of which waited for: 15 -> 15; matrix products, arithmetic and copies ran while one was open for 7% -> 6% of each run, Pallas kernels for 11% -> 11%
where the time goes in v6:
time: 258 us; the launch traced here: 257 us
  waiting for transfers between devices  127 us (49%)
  starting transfers between devices  70 us (27%)
  Pallas kernels  34.4 us (13%)
  local copies, waits for them, and re-layouts  13.9 us (5%)
  other arithmetic  8.82 us (3%)
    ppermute x19, waiting for transfers between devices, cross(): return lax.ppermute(x, axis, [(i ^ bit, i) for i in among or range(size)])  75.5 us
    ppermute x19, starting transfers between devices, cross(): return lax.ppermute(x, axis, [(i ^ bit, i) for i in among or range(size)])  56.6 us
    ppermute x17, waiting for transfers between devices, swap(): return lax.ppermute(x, axis, [(0, 1), (1, 0)])  51.7 us
    pallas_call x2, Pallas kernels, partial(): pl.pallas_call(functools.partial(partial_kernel, counts, narrow), out_sha...  15 us
    ppermute x17, starting transfers between devices, swap(): return lax.ppermute(x, axis, [(0, 1), (1, 0)])  13.4 us
    pallas_call x3, Pallas kernels, project(): pl.pallas_call(project_kernel, out_shape=(shape, shape), in_specs=[SMEM,...  12.1 us
    unnamed x52, local copies, waits for them, and re-layouts  5.81 us
  transfers between devices with their start and end apart: 36, of which 15 were waited for; matrix products, arithmetic and copies ran while one was open for 6% of the time, Pallas kernels for 11%

profile of v6, /device:TPU:0, one launch (start us, length us, event | category | flops | bytes accessed | tf_op | source)
XLA Modules:
  0.0 256.7 jit_solution(8093592567364361117)
XLA Ops:
  0.0 2.3 dynamic-slice_bitcast_fusion
  2.3 3.1 %collective-permute-start.23 = (bf16[448,1024]{1,0:T(8,128)(2,1)}, bf16[448,1024]{1,0:T(8,128)(2,1)}, u32[]{:S(2)}, u32[]{:S(2)}) collective-permute-start(bf16[448,1024]{1,0:T(8,128)(2,1)} %dynamic-slice_bitcast_fusion), channel_id=1, source_target_pairs={{4,0},{0,4},{12,8},{8,12},{5,1},{1,5},{13,9},{9,13},{6,2},{2,6},{1... | collective-permute-start | bytes 2752520 | tf_op jit(solution)/shard_map/ppermute | solution.py:25
  5.4 1.7 collective-permute-start.25
  8.6 2.5 norm.1
  11.8 2.5 collective-permute-start.5
  14.3 2.4 collective-permute-start.7
  20.8 13.5 %collective-permute-done.5.rest_6_ = bf16[128,896]{1,0:T(8,128)(2,1)S(1)} collective-permute-done((bf16[128,896]{1,0:T(8,128)(2,1)}, bf16[128,896]{1,0:T(8,128)(2,1)S(1)}, u32[]{:S(2)}, u32[]{:S(2)}) %collective-permute-start.5) | collective-permute-done | bytes 229408 | tf_op jit(solution)/shard_map/ppermute | solution.py:25
  34.3 15.5 %collective-permute-done.7.rest_8_ = bf16[128,896]{1,0:T(8,128)(2,1)S(1)} collective-permute-done((bf16[128,896]{1,0:T(8,128)(2,1)}, bf16[128,896]{1,0:T(8,128)(2,1)S(1)}, u32[]{:S(2)}, u32[]{:S(2)}) %collective-permute-start.7) | collective-permute-done | bytes 229408 | tf_op jit(solution)/shard_map/ppermute | solution.py:25
  49.9 6.7 %collective-permute-done.3.rest_6_ = bf16[128,896]{1,0:T(8,128)(2,1)} collective-permute-done((bf16[128,896]{1,0:T(8,128)(2,1)}, bf16[128,896]{1,0:T(8,128)(2,1)}, u32[]{:S(2)}, u32[]{:S(2)}) %collective-permute-start.3) | collective-permute-done | bytes 229408 | tf_op jit(solution)/shard_map/ppermute | solution.py:25
  58.1 1.6 collective-permute-start.24
  67.0 2.6 %pad_add_fusion.limits = s32[4]{0:T(128)S(1)} fusion(s32[1]{0:T(128)} %get-tuple-element.66, s32[1]{0:T(128)} %get-tuple-element.64, s32[1]{0:T(128)} %get-tuple-element.65, s32[1]{0:T(128)} %get-tuple-element.63), kind=kLoop, calls=%fused_computation.41 | loop fusion | flops 12 | bytes 32 | tf_op jit(solution)/shard_map/stack | solution.py:320
  74.4 7.4 %partial.3 = (f32[512,512]{1,0:T(8,128)}, f32[512,1024]{1,0:T(8,128)}, bf16[512,512]{1,0:T(8,128)(2,1)S(1)}, bf16[256,1024]{1,0:T(8,128)(2,1)S(1)}, bf16[256,1024]{1,0:T(8,128)(2,1)S(1)}) custom-call(s32[5]{0:T(128)S(1)} %stack.82.place, s32[2048]{0:T(1024)S(1)} %copy-done.6, s32[2]{0:T(128)S(1)} %pad_add_fusion.2.begins, bf16[2,448,256]{2,1,0:T(8,128)(2,1)} %copy-done.19, ...), custom_call_target="tpu_custom_call" | custom-call | flops 2818572288 | bytes 8650752 | tf_op jit(solution)/shard_map/partial/pallas_call | solution.py:161
  81.8 5.6 %collective-permute-start.12 = (bf16[256,1024]{1,0:T(8,128)(2,1)S(1)}, bf16[256,1024]{1,0:T(8,128)(2,1)S(1)}, u32[]{:S(2)}, u32[]{:S(2)}) collective-permute-start(bf16[256,1024]{1,0:T(8,128)(2,1)S(1)} %get-tuple-element.48), channel_id=1, source_target_pairs={{0,4},{12,8},{1,5},{13,9},{2,6},{14,10},{3,7},{15,11},{16,20},{28,... | collective-permute-start | bytes 1572872 | tf_op jit(solution)/shard_map/ppermute | solution.py:25
  91.4 2.2 broadcast_select_fusion.1.rest_1_
  93.7 7.6 %partial.2 = (f32[512,512]{1,0:T(8,128)}, f32[512,1024]{1,0:T(8,128)}) custom-call(s32[5]{0:T(128)S(1)} %stack.82.place, s32[2048]{0:T(1024)S(1)} %copy-done.6, s32[2]{0:T(128)S(1)} %pad_add_fusion.1.begins, bf16[2,448,256]{2,1,0:T(8,128)(2,1)} %copy-done.19, bf16[2,448,256]{2,1,0:T(8,128)(2,1)} %collective-permute-done.rest_1_, ...), custom_call_target="tpu_custom_call" | custom-call | flops 2818572288 | bytes 8650752 | tf_op jit(solution)/shard_map/partial/pallas_call | solution.py:161
  101.4 19.6 %collective-permute-done.14 = bf16[2,256,512]{2,1,0:T(8,128)(2,1)S(1)} collective-permute-done((bf16[2,256,512]{2,1,0:T(8,128)(2,1)S(1)}, bf16[2,256,512]{2,1,0:T(8,128)(2,1)S(1)}, u32[]{:S(2)}, u32[]{:S(2)}) %collective-permute-start.14) | collective-permute-done | bytes 524320 | tf_op jit(solution)/shard_map/ppermute | solution.py:25
  124.1 16.5 %collective-permute-start.16 = (bf16[256,512]{1,0:T(8,128)(2,1)S(1)}, bf16[256,512]{1,0:T(8,128)(2,1)S(1)}, u32[]{:S(2)}, u32[]{:S(2)}) collective-permute-start(bf16[256,512]{1,0:T(8,128)(2,1)S(1)} %fusion.4), channel_id=1, source_target_pairs={{4,0},{0,4},{12,8},{8,12},{5,1},{1,5},{13,9},{9,13},{6,2},{2,6},{1... | collective-permute-start | bytes 786440 | tf_op jit(solution)/shard_map/ppermute | solution.py:25
  140.8 11.1 %collective-permute-start.11 = (bf16[256,1024]{1,0:T(8,128)(2,1)S(1)}, bf16[256,1024]{1,0:T(8,128)(2,1)S(1)}, u32[]{:S(2)}, u32[]{:S(2)}) collective-permute-start(bf16[256,1024]{1,0:T(8,128)(2,1)S(1)} %add_convert_fusion.2), channel_id=1, source_target_pairs={{4,0},{0,4},{12,8},{8,12},{5,1},{1,5},{13,9},{9,13},{6,2},{2,6},{1... | collective-permute-start | bytes 1572872 | tf_op jit(solution)/shard_map/ppermute | solution.py:25
  152.1 2.9 %collective-permute-start.18 = (bf16[256,512]{1,0:T(8,128)(2,1)S(1)}, bf16[256,512]{1,0:T(8,128)(2,1)S(1)}, u32[]{:S(2)}, u32[]{:S(2)}) collective-permute-start(bf16[256,512]{1,0:T(8,128)(2,1)S(1)} %get-tuple-element.60), channel_id=1, source_target_pairs={{8,0},{12,4},{0,8},{4,12},{9,1},{13,5},{1,9},{5,13},{10,2},{14,6},... | collective-permute-start | bytes 786440 | tf_op jit(solution)/shard_map/ppermute | solution.py:25
  157.6 16.2 %collective-permute-done.17 = bf16[256,512]{1,0:T(8,128)(2,1)S(1)} collective-permute-done((bf16[256,512]{1,0:T(8,128)(2,1)S(1)}, bf16[256,512]{1,0:T(8,128)(2,1)S(1)}, u32[]{:S(2)}, u32[]{:S(2)}) %collective-permute-start.17) | collective-permute-done | bytes 262176 | tf_op jit(solution)/shard_map/ppermute | solution.py:25
  175.3 3.9 %collective-permute-done.18 = bf16[256,512]{1,0:T(8,128)(2,1)S(1)} collective-permute-done((bf16[256,512]{1,0:T(8,128)(2,1)S(1)}, bf16[256,512]{1,0:T(8,128)(2,1)S(1)}, u32[]{:S(2)}, u32[]{:S(2)}) %collective-permute-start.18) | collective-permute-done | bytes 262176 | tf_op jit(solution)/shard_map/ppermute | solution.py:25
  184.1 3.0 %attend.1.ours_ref = bf16[256,1024]{1,0:T(8,128)(2,1)S(1)} custom-call(s32[8]{0:T(128)S(1)} %stack.90.starts, s32[4]{0:T(128)S(1)} %pad_add_fusion.limits, bf16[256,1024]{1,0:T(8,128)(2,1)S(1)} %add_convert_fusion.1.q_ref, bf16[8,256,512]{2,1,0:T(8,128)(2,1)S(1)} %constant_dynamic-update-slice_fusion.kv_ref, s32[1024,1]{1,0:T(8,128)S(1)} %copy-done.3, ...), custom_call_target="tpu_custom_call" | custom-call | flops 2147483648 | bytes 3145728 | tf_op jit(solution)/shard_map/attend/pallas_call | solution.py:321
  187.2 2.1 collective-permute-start.22
  189.6 7.7 %collective-permute-done.28.rest_3_ = bf16[448,1024]{1,0:T(8,128)(2,1)} collective-permute-done((bf16[448,1024]{1,0:T(8,128)(2,1)}, bf16[448,1024]{1,0:T(8,128)(2,1)}, u32[]{:S(2)}, u32[]{:S(2)}) %collective-permute-start.28) | collective-permute-done | bytes 917536 | tf_op jit(solution)/shard_map/ppermute | solution.py:20
  197.3 18.5 %collective-permute-done.29.rest_4_ = bf16[448,1024]{1,0:T(8,128)(2,1)} collective-permute-done((bf16[448,1024]{1,0:T(8,128)(2,1)}, bf16[448,1024]{1,0:T(8,128)(2,1)}, u32[]{:S(2)}, u32[]{:S(2)}) %collective-permute-start.29) | collective-permute-done | bytes 917536 | tf_op jit(solution)/shard_map/ppermute | solution.py:20
  215.9 9.8 %collective-permute-done.30.rest_5_ = bf16[448,1024]{1,0:T(8,128)(2,1)} collective-permute-done((bf16[448,1024]{1,0:T(8,128)(2,1)}, bf16[448,1024]{1,0:T(8,128)(2,1)}, u32[]{:S(2)}, u32[]{:S(2)}) %collective-permute-start.30) | collective-permute-done | bytes 917536 | tf_op jit(solution)/shard_map/ppermute | solution.py:20
  225.7 3.8 %project.5 = (bf16[1,256,448]{2,1,0:T(8,128)(2,1)S(1)}, bf16[1,256,448]{2,1,0:T(8,128)(2,1)S(1)}) custom-call(s32[1]{0:T(128)S(6)} %xor.35.turns, s32[5]{0:T(128)S(1)} %stack.82.place, bf16[256,1024]{1,0:T(8,128)(2,1)S(1)} %attend.1.ours_ref, bf16[256,1024]{1,0:T(8,128)(2,1)} %collective-permute-done.22.beside_ref, bf16[256,1]{1,0:T(8,128)(2,1)S(1)} %reshape.65.ours_near, ...), custom_call_target="tpu_custom_call" | custom-call | flops 939524096 | bytes 2293760 | tf_op jit(solution)/shard_map/project/pallas_call | solution.py:386
  230.2 3.8 %project.4 = (bf16[1,256,448]{2,1,0:T(8,128)(2,1)S(1)}, bf16[1,256,448]{2,1,0:T(8,128)(2,1)S(1)}) custom-call(s32[1]{0:T(128)S(6)} %xor.34.turns, s32[5]{0:T(128)S(1)} %stack.82.place, bf16[256,1024]{1,0:T(8,128)(2,1)S(1)} %attend.1.ours_ref, bf16[256,1024]{1,0:T(8,128)(2,1)} %collective-permute-done.22.beside_ref, bf16[256,1]{1,0:T(8,128)(2,1)S(1)} %reshape.65.ours_near, ...), custom_call_target="tpu_custom_call" | custom-call | flops 939524096 | bytes 2293760 | tf_op jit(solution)/shard_map/project/pallas_call | solution.py:386
  234.8 4.5 %project.3 = (bf16[2,256,448]{2,1,0:T(8,128)(2,1)S(1)}, bf16[2,256,448]{2,1,0:T(8,128)(2,1)S(1)}) custom-call(s32[2]{0:T(128)S(1)} %add_xor_fusion.turns, s32[5]{0:T(128)S(1)} %stack.82.place, bf16[256,1024]{1,0:T(8,128)(2,1)S(1)} %attend.1.ours_ref, bf16[256,1024]{1,0:T(8,128)(2,1)} %collective-permute-done.22.beside_ref, ...), custom_call_target="tpu_custom_call" | custom-call | flops 1879048192 | bytes 4587520 | tf_op jit(solution)/shard_map/project/pallas_call | solution.py:386
  242.7 7.2 %collective-permute-done.31.rest_0_ = bf16[1,256,448]{2,1,0:T(8,128)(2,1)S(1)} collective-permute-done((bf16[1,256,448]{2,1,0:T(8,128)(2,1)S(1)}, bf16[1,256,448]{2,1,0:T(8,128)(2,1)S(1)}, u32[]{:S(2)}, u32[]{:S(2)}) %collective-permute-start.31) | collective-permute-done | bytes 229408 | tf_op jit(solution)/shard_map/ppermute | solution.py:20
  249.9 5.1 %collective-permute-done.32.rest_1_ = bf16[1,256,448]{2,1,0:T(8,128)(2,1)S(1)} collective-permute-done((bf16[1,256,448]{2,1,0:T(8,128)(2,1)S(1)}, bf16[1,256,448]{2,1,0:T(8,128)(2,1)S(1)}, u32[]{:S(2)}, u32[]{:S(2)}) %collective-permute-start.32) | collective-permute-done | bytes 229408 | tf_op jit(solution)/shard_map/ppermute | solution.py:20
  255.0 1.7 finish.1
  (144 shorter events, 39.7 us)
Async XLA Ops:
  2.3 55.8 %collective-permute-start.23 = (bf16[448,1024]{1,0:T(8,128)(2,1)}, bf16[448,1024]{1,0:T(8,128)(2,1)}, u32[]{:S(2)}, u32[]{:S(2)}) collective-permute-start(bf16[448,1024]{1,0:T(8,128)(2,1)} %dynamic-slice_bitcast_fusion), channel_id=1, source_target_pairs={{4,0},{0,4},{12,8},{8,12},{5,1},{1,5},{13,9},{9,13},{6,2},{2,6},{1... | collective-permute-start | bytes 2752520 | tf_op jit(solution)/shard_map/ppermute | solution.py:25
  5.4 54.3 %collective-permute-start.25 = (bf16[448,1024]{1,0:T(8,128)(2,1)}, bf16[448,1024]{1,0:T(8,128)(2,1)}, u32[]{:S(2)}, u32[]{:S(2)}) collective-permute-start(bf16[448,1024]{1,0:T(8,128)(2,1)} %dynamic-slice_bitcast_fusion), channel_id=1, source_target_pairs={{8,4},{4,8},{9,5},{5,9},{10,6},{6,10},{11,7},{7,11},{24,20},{20,24... | collective-permute-start | bytes 2752520 | tf_op jit(solution)/shard_map/ppermute | solution.py:25
  11.8 59.8 %collective-permute-start.2 = (bf16[2,448,1024]{2,1,0:T(8,128)(2,1)}, bf16[2,448,1024]{2,1,0:T(8,128)(2,1)}, u32[]{:S(2)}, u32[]{:S(2)}) collective-permute-start(bf16[2,448,1024]{2,1,0:T(8,128)(2,1)} %rest_4_.1), channel_id=1, source_target_pairs={{0,1},{1,0},{2,3},{3,2},{4,5},{5,4},{6,7},{7,6},{8,9},{9,8},{10,11... | collective-permute-start | bytes 5505032 | tf_op jit(solution)/shard_map/ppermute | solution.py:20
  11.8 22.5 %collective-permute-start.5 = (bf16[128,896]{1,0:T(8,128)(2,1)}, bf16[128,896]{1,0:T(8,128)(2,1)S(1)}, u32[]{:S(2)}, u32[]{:S(2)}) collective-permute-start(bf16[128,896]{1,0:T(8,128)(2,1)} %get-tuple-element.40), channel_id=1, source_target_pairs={{12,0},{8,4},{4,8},{0,12},{13,1},{9,5},{5,9},{1,13},{14,2},{10,6},... | collective-permute-start | bytes 688136 | tf_op jit(solution)/shard_map/ppermute | solution.py:25
  14.3 35.5 %collective-permute-start.7 = (bf16[128,896]{1,0:T(8,128)(2,1)}, bf16[128,896]{1,0:T(8,128)(2,1)S(1)}, u32[]{:S(2)}, u32[]{:S(2)}) collective-permute-start(bf16[128,896]{1,0:T(8,128)(2,1)} %get-tuple-element.43), channel_id=1, source_target_pairs={{8,0},{12,4},{0,8},{4,12},{9,1},{13,5},{1,9},{5,13},{10,2},{14,6},... | collective-permute-start | bytes 688136 | tf_op jit(solution)/shard_map/ppermute | solution.py:25
  34.3 27.8 %collective-permute-start = (bf16[2,448,256]{2,1,0:T(8,128)(2,1)S(1)}, bf16[2,448,256]{2,1,0:T(8,128)(2,1)}, u32[]{:S(2)}, u32[]{:S(2)}) collective-permute-start(bf16[2,448,256]{2,1,0:T(8,128)(2,1)S(1)} %constant_dynamic-slice_fusion.1.rest_0_), channel_id=1, source_target_pairs={{0,1},{1,0},{2,3},{3,2},{4,5},{5,4},{6,7},{7,6},{8,9},{9,8},{10,11... | collective-permute-start | bytes 1376264 | tf_op jit(solution)/shard_map/ppermute | solution.py:20
  49.8 6.8 %collective-permute-start.3 = (bf16[128,896]{1,0:T(8,128)(2,1)}, bf16[128,896]{1,0:T(8,128)(2,1)}, u32[]{:S(2)}, u32[]{:S(2)}) collective-permute-start(bf16[128,896]{1,0:T(8,128)(2,1)} %copy-done.12), channel_id=1, source_target_pairs={{4,0},{0,4},{12,8},{8,12},{5,1},{1,5},{13,9},{9,13},{6,2},{2,6},{1... | collective-permute-start | bytes 688136 | tf_op jit(solution)/shard_map/ppermute | solution.py:25
  58.1 30.7 %collective-permute-start.24 = (bf16[448,1024]{1,0:T(8,128)(2,1)}, bf16[448,1024]{1,0:T(8,128)(2,1)}, u32[]{:S(2)}, u32[]{:S(2)}) collective-permute-start(bf16[448,1024]{1,0:T(8,128)(2,1)} %collective-permute-done.23.rest_0_), channel_id=1, source_target_pairs={{8,4},{4,8},{9,5},{5,9},{10,6},{6,10},{11,7},{7,11},{24,20},{20,24... | collective-permute-start | bytes 2752520 | tf_op jit(solution)/shard_map/ppermute | solution.py:25
  59.7 30.4 %collective-permute-start.26 = (bf16[448,1024]{1,0:T(8,128)(2,1)}, bf16[448,1024]{1,0:T(8,128)(2,1)}, u32[]{:S(2)}, u32[]{:S(2)}) collective-permute-start(bf16[448,1024]{1,0:T(8,128)(2,1)} %collective-permute-done.25), channel_id=1, source_target_pairs={{4,0},{8,12},{5,1},{9,13},{6,2},{10,14},{7,3},{11,15},{20,16},{24,... | collective-permute-start | bytes 2752520 | tf_op jit(solution)/shard_map/ppermute | solution.py:25
  62.1 7.5 %collective-permute-start.1 = (bf16[2,448,256]{2,1,0:T(8,128)(2,1)S(1)}, bf16[2,448,256]{2,1,0:T(8,128)(2,1)}, u32[]{:S(2)}, u32[]{:S(2)}) collective-permute-start(bf16[2,448,256]{2,1,0:T(8,128)(2,1)S(1)} %constant_dynamic-slice_fusion.rest_2_), channel_id=1, source_target_pairs={{0,1},{1,0},{2,3},{3,2},{4,5},{5,4},{6,7},{7,6},{8,9},{9,8},{10,11... | collective-permute-start | bytes 1376264 | tf_op jit(solution)/shard_map/ppermute | solution.py:20
  62.8 8.1 %collective-permute-start.8 = (bf16[128,896]{1,0:T(8,128)(2,1)S(1)}, bf16[128,896]{1,0:T(8,128)(2,1)S(1)}, u32[]{:S(2)}, u32[]{:S(2)}) collective-permute-start(bf16[128,896]{1,0:T(8,128)(2,1)S(1)} %collective-permute-done.7.rest_8_), channel_id=1, source_target_pairs={{0,2},{2,0},{1,3},{3,1},{4,6},{6,4},{5,7},{7,5},{8,10},{10,8},{9,1... | collective-permute-start | bytes 688136 | tf_op jit(solution)/shard_map/ppermute | solution.py:20
  69.6 24.1 %collective-permute-start.4 = (bf16[128,896]{1,0:T(8,128)(2,1)}, bf16[128,896]{1,0:T(8,128)(2,1)S(1)}, u32[]{:S(2)}, u32[]{:S(2)}) collective-permute-start(bf16[128,896]{1,0:T(8,128)(2,1)} %collective-permute-done.3.rest_6_), channel_id=1, source_target_pairs={{0,2},{2,0},{1,3},{3,1},{4,6},{6,4},{5,7},{7,5},{8,10},{10,8},{9,1... | collective-permute-start | bytes 688136 | tf_op jit(solution)/shard_map/ppermute | solution.py:20
  81.8 41.2 %collective-permute-start.12 = (bf16[256,1024]{1,0:T(8,128)(2,1)S(1)}, bf16[256,1024]{1,0:T(8,128)(2,1)S(1)}, u32[]{:S(2)}, u32[]{:S(2)}) collective-permute-start(bf16[256,1024]{1,0:T(8,128)(2,1)S(1)} %get-tuple-element.48), channel_id=1, source_target_pairs={{0,4},{12,8},{1,5},{13,9},{2,6},{14,10},{3,7},{15,11},{16,20},{28,... | collective-permute-start | bytes 1572872 | tf_op jit(solution)/shard_map/ppermute | solution.py:25
  87.5 34.5 %collective-permute-start.9 = (bf16[256,1024]{1,0:T(8,128)(2,1)S(1)}, bf16[256,1024]{1,0:T(8,128)(2,1)S(1)}, u32[]{:S(2)}, u32[]{:S(2)}) collective-permute-start(bf16[256,1024]{1,0:T(8,128)(2,1)S(1)} %get-tuple-element.47), channel_id=1, source_target_pairs={{0,4},{12,8},{1,5},{13,9},{2,6},{14,10},{3,7},{15,11},{16,20},{28,... | collective-permute-start | bytes 1572872 | tf_op jit(solution)/shard_map/ppermute | solution.py:25
  88.8 32.2 %collective-permute-start.14 = (bf16[2,256,512]{2,1,0:T(8,128)(2,1)S(1)}, bf16[2,256,512]{2,1,0:T(8,128)(2,1)S(1)}, u32[]{:S(2)}, u32[]{:S(2)}) collective-permute-start(bf16[2,256,512]{2,1,0:T(8,128)(2,1)S(1)} %bitcast.68), channel_id=1, source_target_pairs={{0,4},{12,8},{1,5},{13,9},{2,6},{14,10},{3,7},{15,11},{16,20},{28,... | collective-permute-start | bytes 1572872 | tf_op jit(solution)/shard_map/ppermute | solution.py:25
  90.1 64.9 %collective-permute-start.27 = (bf16[448,1024]{1,0:T(8,128)(2,1)}, bf16[448,1024]{1,0:T(8,128)(2,1)S(1)}, u32[]{:S(2)}, u32[]{:S(2)}) collective-permute-start(bf16[448,1024]{1,0:T(8,128)(2,1)} %collective-permute-done.24), channel_id=1, source_target_pairs={{4,0},{8,12},{5,1},{9,13},{6,2},{10,14},{7,3},{11,15},{20,16},{24,... | collective-permute-start | bytes 2752520 | tf_op jit(solution)/shard_map/ppermute | solution.py:25
  122.2 18.4 %collective-permute-start.10 = (bf16[256,1024]{1,0:T(8,128)(2,1)S(1)}, bf16[256,1024]{1,0:T(8,128)(2,1)S(1)}, u32[]{:S(2)}, u32[]{:S(2)}) collective-permute-start(bf16[256,1024]{1,0:T(8,128)(2,1)S(1)} %fusion.2), channel_id=1, source_target_pairs={{8,4},{4,8},{9,5},{5,9},{10,6},{6,10},{11,7},{7,11},{24,20},{20,24... | collective-permute-start | bytes 1572872 | tf_op jit(solution)/shard_map/ppermute | solution.py:25
  123.2 58.2 %collective-permute-start.13 = (bf16[256,1024]{1,0:T(8,128)(2,1)S(1)}, bf16[256,1024]{1,0:T(8,128)(2,1)S(1)}, u32[]{:S(2)}, u32[]{:S(2)}) collective-permute-start(bf16[256,1024]{1,0:T(8,128)(2,1)S(1)} %fusion.1), channel_id=1, source_target_pairs={{8,4},{4,8},{9,5},{5,9},{10,6},{6,10},{11,7},{7,11},{24,20},{20,24... | collective-permute-start | bytes 1572872 | tf_op jit(solution)/shard_map/ppermute | solution.py:25
  124.1 27.8 %collective-permute-start.16 = (bf16[256,512]{1,0:T(8,128)(2,1)S(1)}, bf16[256,512]{1,0:T(8,128)(2,1)S(1)}, u32[]{:S(2)}, u32[]{:S(2)}) collective-permute-start(bf16[256,512]{1,0:T(8,128)(2,1)S(1)} %fusion.4), channel_id=1, source_target_pairs={{4,0},{0,4},{12,8},{8,12},{5,1},{1,5},{13,9},{9,13},{6,2},{2,6},{1... | collective-permute-start | bytes 786440 | tf_op jit(solution)/shard_map/ppermute | solution.py:25
  140.8 40.6 %collective-permute-start.11 = (bf16[256,1024]{1,0:T(8,128)(2,1)S(1)}, bf16[256,1024]{1,0:T(8,128)(2,1)S(1)}, u32[]{:S(2)}, u32[]{:S(2)}) collective-permute-start(bf16[256,1024]{1,0:T(8,128)(2,1)S(1)} %add_convert_fusion.2), channel_id=1, source_target_pairs={{4,0},{0,4},{12,8},{8,12},{5,1},{1,5},{13,9},{9,13},{6,2},{2,6},{1... | collective-permute-start | bytes 1572872 | tf_op jit(solution)/shard_map/ppermute | solution.py:25
  152.0 21.8 %collective-permute-start.17 = (bf16[256,512]{1,0:T(8,128)(2,1)S(1)}, bf16[256,512]{1,0:T(8,128)(2,1)S(1)}, u32[]{:S(2)}, u32[]{:S(2)}) collective-permute-start(bf16[256,512]{1,0:T(8,128)(2,1)S(1)} %get-tuple-element.60), channel_id=1, source_target_pairs={{4,0},{0,4},{12,8},{8,12},{5,1},{1,5},{13,9},{9,13},{6,2},{2,6},{1... | collective-permute-start | bytes 786440 | tf_op jit(solution)/shard_map/ppermute | solution.py:25
  152.1 27.1 %collective-permute-start.18 = (bf16[256,512]{1,0:T(8,128)(2,1)S(1)}, bf16[256,512]{1,0:T(8,128)(2,1)S(1)}, u32[]{:S(2)}, u32[]{:S(2)}) collective-permute-start(bf16[256,512]{1,0:T(8,128)(2,1)S(1)} %get-tuple-element.60), channel_id=1, source_target_pairs={{8,0},{12,4},{0,8},{4,12},{9,1},{13,5},{1,9},{5,13},{10,2},{14,6},... | collective-permute-start | bytes 786440 | tf_op jit(solution)/shard_map/ppermute | solution.py:25
  155.0 25.7 %collective-permute-start.19 = (bf16[256,512]{1,0:T(8,128)(2,1)S(1)}, bf16[256,512]{1,0:T(8,128)(2,1)S(1)}, u32[]{:S(2)}, u32[]{:S(2)}) collective-permute-start(bf16[256,512]{1,0:T(8,128)(2,1)S(1)} %get-tuple-element.60), channel_id=1, source_target_pairs={{12,0},{8,4},{4,8},{0,12},{13,1},{9,5},{5,9},{1,13},{14,2},{10,6},... | collective-permute-start | bytes 786440 | tf_op jit(solution)/shard_map/ppermute | solution.py:25
  173.8 23.5 %collective-permute-start.28 = (bf16[448,1024]{1,0:T(8,128)(2,1)}, bf16[448,1024]{1,0:T(8,128)(2,1)}, u32[]{:S(2)}, u32[]{:S(2)}) collective-permute-start(bf16[448,1024]{1,0:T(8,128)(2,1)} %collective-permute-done.23.rest_0_), channel_id=1, source_target_pairs={{0,16},{16,0},{1,17},{17,1},{2,18},{18,2},{3,19},{19,3},{4,20},{20... | collective-permute-start | bytes 2752520 | tf_op jit(solution)/shard_map/ppermute | solution.py:20
  179.2 36.7 %collective-permute-start.29 = (bf16[448,1024]{1,0:T(8,128)(2,1)}, bf16[448,1024]{1,0:T(8,128)(2,1)}, u32[]{:S(2)}, u32[]{:S(2)}) collective-permute-start(bf16[448,1024]{1,0:T(8,128)(2,1)} %broadcast_select_fusion.1.rest_1_), channel_id=1, source_target_pairs={{0,16},{16,0},{1,17},{17,1},{2,18},{18,2},{3,19},{19,3},{4,20},{20... | collective-permute-start | bytes 2752520 | tf_op jit(solution)/shard_map/ppermute | solution.py:20
  180.7 45.0 %collective-permute-start.30 = (bf16[448,1024]{1,0:T(8,128)(2,1)}, bf16[448,1024]{1,0:T(8,128)(2,1)}, u32[]{:S(2)}, u32[]{:S(2)}) collective-permute-start(bf16[448,1024]{1,0:T(8,128)(2,1)} %broadcast_select_fusion.rest_2_), channel_id=1, source_target_pairs={{0,16},{16,0},{1,17},{17,1},{2,18},{18,2},{3,19},{19,3},{4,20},{20... | collective-permute-start | bytes 2752520 | tf_op jit(solution)/shard_map/ppermute | solution.py:20
  187.2 38.5 %collective-permute-start.22 = (bf16[256,1024]{1,0:T(8,128)(2,1)S(1)}, bf16[256,1024]{1,0:T(8,128)(2,1)}, u32[]{:S(2)}, u32[]{:S(2)}) collective-permute-start(bf16[256,1024]{1,0:T(8,128)(2,1)S(1)} %attend.1.ours_ref), channel_id=1, source_target_pairs={{0,1},{1,0},{2,3},{3,2},{4,5},{5,4},{6,7},{7,6},{8,9},{9,8},{10,11... | collective-permute-start | bytes 1572872 | tf_op jit(solution)/shard_map/ppermute | solution.py:20
  229.5 9.7 %collective-permute-start.34 = (bf16[1,256,448]{2,1,0:T(8,128)(2,1)S(1)}, bf16[1,256,448]{2,1,0:T(8,128)(2,1)S(1)}, u32[]{:S(2)}, u32[]{:S(2)}) collective-permute-start(bf16[1,256,448]{2,1,0:T(8,128)(2,1)S(1)} %get-tuple-element.58), channel_id=1, source_target_pairs={{0,2},{2,0},{1,3},{3,1},{4,6},{6,4},{5,7},{7,5},{8,10},{10,8},{9,1... | collective-permute-start | bytes 688136 | tf_op jit(solution)/shard_map/ppermute | solution.py:20
  234.0 6.4 %collective-permute-start.33 = (bf16[1,256,448]{2,1,0:T(8,128)(2,1)S(1)}, bf16[1,256,448]{2,1,0:T(8,128)(2,1)S(1)}, u32[]{:S(2)}, u32[]{:S(2)}) collective-permute-start(bf16[1,256,448]{2,1,0:T(8,128)(2,1)S(1)} %get-tuple-element.57), channel_id=1, source_target_pairs={{0,2},{2,0},{1,3},{3,1},{4,6},{6,4},{5,7},{7,5},{8,10},{10,8},{9,1... | collective-permute-start | bytes 688136 | tf_op jit(solution)/shard_map/ppermute | solution.py:20
  240.6 14.4 %collective-permute-start.35 = (bf16[2,256,448]{2,1,0:T(8,128)(2,1)S(1)}, bf16[2,256,448]{2,1,0:T(8,128)(2,1)S(1)}, u32[]{:S(2)}, u32[]{:S(2)}) collective-permute-start(bf16[2,256,448]{2,1,0:T(8,128)(2,1)S(1)} %add_convert_fusion), channel_id=1, source_target_pairs={{0,1},{1,0},{2,3},{3,2},{4,5},{5,4},{6,7},{7,6},{8,9},{9,8},{10,11... | collective-permute-start | bytes 1376264 | tf_op jit(solution)/shard_map/ppermute | solution.py:20
  240.7 9.2 %collective-permute-start.31 = (bf16[1,256,448]{2,1,0:T(8,128)(2,1)S(1)}, bf16[1,256,448]{2,1,0:T(8,128)(2,1)S(1)}, u32[]{:S(2)}, u32[]{:S(2)}) collective-permute-start(bf16[1,256,448]{2,1,0:T(8,128)(2,1)S(1)} %get-tuple-element.54), channel_id=1, source_target_pairs={{0,2},{2,0},{1,3},{3,1},{4,6},{6,4},{5,7},{7,5},{8,10},{10,8},{9,1... | collective-permute-start | bytes 688136 | tf_op jit(solution)/shard_map/ppermute | solution.py:20
  241.6 13.4 %collective-permute-start.32 = (bf16[1,256,448]{2,1,0:T(8,128)(2,1)S(1)}, bf16[1,256,448]{2,1,0:T(8,128)(2,1)S(1)}, u32[]{:S(2)}, u32[]{:S(2)}) collective-permute-start(bf16[1,256,448]{2,1,0:T(8,128)(2,1)S(1)} %get-tuple-element.55), channel_id=1, source_target_pairs={{0,2},{2,0},{1,3},{3,1},{4,6},{6,4},{5,7},{7,5},{8,10},{10,8},{9,1... | collective-permute-start | bytes 688136 | tf_op jit(solution)/shard_map/ppermute | solution.py:20
  (26 other events, 259.6 us)

commit v7 on v6

--- a/solution.py
+++ b/solution.py
@@ -93,66 +93,83 @@
 def partial_kernel(counts, narrow, place, modality, begins, *rest):
     total = sum(counts)
     sources, refs, outs = rest[:6], rest[6 : 6 + total], rest[6 + total : -8]
-    both, other, held_kv, held_q, arrived = rest[-8:-3]
-    wide_kv, wide_q, left = rest[-3:]
+    both, other, held_kv, held_q, wide_kv, wide_q, arrived, left = rest[-8:]
+    length = both.shape[0] // len(counts)
+    half = length // 2
     kv_half = held_kv.shape[2] // 2
     depth = held_kv.shape[1] // 2
     copies = []
-    for i in (4, 5, 0, 1, 2, 3):
-        source = sources[i]
-        core = place[3] if i % 2 == 0 else 1 - place[3]
-        at = pl.ds(pl.multiple_of(core * depth, depth), depth)
-        target = (
-            held_kv.at[:, at, 0:kv_half],
-            held_kv.at[:, at, kv_half : 2 * kv_half],
-            held_q.at[:, at],
-        )[i // 2]
-        copies.append(pltpu.make_async_copy(source, target, arrived.at[i]))
+
+    def fetch(source, target):
+        copies.append(pltpu.make_async_copy(source, target, arrived.at[len(copies)]))
         copies[-1].start()
-    stores = []
-    length = both.shape[0] // len(counts)
+
     at = 0
     for number, count in enumerate(counts):
         base = number * length
         if count == 1:
-            both[base : base + length] = refs[at][...]
+            fetch(refs[at], both.at[base : base + length])
         else:
-            half = length // 2
-            both[pl.ds(pl.multiple_of(base + place[1] * half, half), half)] = refs[at][...]
-            both[pl.ds(pl.multiple_of(base + (1 - place[1]) * half, half), half)] = refs[at + 1][...]
+            for which in range(2):
+                row = base + (place[1] if which == 0 else 1 - place[1]) * half
+                fetch(refs[at + which], both.at[pl.ds(pl.multiple_of(row, half), half)])
         at += count
+    for i, source in enumerate(sources):
+        core = place[3] if i % 2 == 0 else 1 - place[3]
+        rows = pl.ds(pl.multiple_of(core * depth, depth), depth)
+        target = (
+            held_kv.at[:, rows, 0:kv_half],
+            held_kv.at[:, rows, kv_half : 2 * kv_half],
+            held_q.at[:, rows],
+        )[i // 2]
+        fetch(source, target)
+    for copy in copies[:total]:
+        copy.wait()
     for number in range(len(counts)):
         for step in range(0, length, RUN):
-            at = pl.ds(number * length + step, RUN)
+            rows = pl.ds(number * length + step, RUN)
             generate = modality[begins[number] + step] == 1
-            block = both[at]
+            block = both[rows]
             zero = jnp.zeros_like(block)
-            both[at] = jnp.where(generate, zero, block)
-            other[at] = jnp.where(generate, block, zero)
+            both[rows] = jnp.where(generate, zero, block)
+            other[rows] = jnp.where(generate, block, zero)
     first, second = both[...], other[...]
-    for i, held, wide in ((1, held_q, wide_q), (0, held_kv, wide_kv)):
-        for copy in (copies[2:], copies[:2])[i]:
-            copy.wait()
-        value = jnp.dot(first, held[0], preferred_element_type=jnp.float32) + jnp.dot(
-            second, held[1], preferred_element_type=jnp.float32
+    pieces = wide_q.shape[0]
+    width = wide_q.shape[2]
+    stores = []
+
+    def project(held, cols, wide, out):
+        value = jnp.dot(first, held[0, :, cols], preferred_element_type=jnp.float32) + jnp.dot(
+            second, held[1, :, cols], preferred_element_type=jnp.float32
         )
         wide[...] = value
-        stores.append(pltpu.make_async_copy(wide, outs[i], left.at[i]))
+        stores.append(pltpu.make_async_copy(wide, out, left.at[len(stores)]))
         stores[-1].start()
-        if narrow and i == 0:
-            outs[2][...] = value.astype(jnp.bfloat16)
-        elif narrow:
+        return value.astype(jnp.bfloat16)
+
+    for copy in copies[total : total + 4]:
+        copy.wait()
+    value = project(held_kv, slice(None), wide_kv, outs[0])
+    if narrow:
+        outs[2][...] = value
+    for copy in copies[total + 4 :]:
+        copy.wait()
+    for piece in range(pieces):
+        cols = slice(piece * width, (piece + 1) * width)
+        value = project(held_q, cols, wide_q.at[piece], outs[1].at[:, cols])
+        if narrow:
             for number in range(len(counts)):
-                part = value[number * length : (number + 1) * length]
-                outs[3 + number][...] = part.astype(jnp.bfloat16)
+                outs[3 + number][:, cols] = value[number * length : (number + 1) * length]
     for store in stores:
         store.wait()
 
 
 def partial(blocks, begins, length, modality, weights, place, narrow):
     counts = tuple(len(block) for block in blocks)
-    arrays = [array for block in blocks for array in block]
+    places = [pair for block in blocks for pair in enumerate(block)]
+    arrays = [array for _, array in places]
     rows, width = length * len(blocks), arrays[0].shape[1]
+    pieces = 2 if weights[4].shape[2] % 256 == 0 else 1
     kv_cols, q_cols = 2 * weights[0].shape[2], weights[4].shape[2]
     shapes = [pltpu.HBM((rows, cols), jnp.float32) for cols in (kv_cols, q_cols)]
     if narrow:
@@ -161,17 +178,17 @@
     values = pl.pallas_call(
         functools.partial(partial_kernel, counts, narrow),
         out_shape=shapes,
-        in_specs=[SMEM] * 3 + [HBM] * len(weights) + [VMEM] * len(arrays),
+        in_specs=[SMEM] * 3 + [HBM] * len(weights) + [VMEM if i else HBM for i, _ in places],
         out_specs=[HBM] * 2 + [VMEM] * (len(shapes) - 2),
         scratch_shapes=[
             pltpu.VMEM((rows, width), jnp.bfloat16),
             pltpu.VMEM((rows, width), jnp.bfloat16),
             pltpu.VMEM((2, width, kv_cols), jnp.bfloat16),
             pltpu.VMEM((2, width, q_cols), jnp.bfloat16),
-            pltpu.SemaphoreType.DMA((len(weights),)),
             pltpu.VMEM((rows, kv_cols), jnp.float32),
-            pltpu.VMEM((rows, q_cols), jnp.float32),
-            pltpu.SemaphoreType.DMA((2,)),
+            pltpu.VMEM((pieces, rows, q_cols // pieces), jnp.float32),
+            pltpu.SemaphoreType.DMA((len(weights) + len(arrays),)),
+            pltpu.SemaphoreType.DMA((1 + pieces,)),
         ],
         cost_estimate=pl.CostEstimate(
             flops=4 * rows * width * (kv_cols + q_cols),
@@ -180,7 +197,13 @@
         ),
         compiler_params=pltpu.CompilerParams(vmem_limit_bytes=24 * 1024 * 1024),
         name="partial",
-    )(place, modality, begins, *[in_hbm(w) for w in weights], *arrays)
+    )(
+        place,
+        modality,
+        begins,
+        *[in_hbm(w) for w in weights],
+        *[a if i else in_hbm(a) for i, a in places],
+    )
     return [value.reshape(len(blocks), length, -1) for value in values[:3]] + list(values[3:])
 
 
@@ -252,8 +275,11 @@
     return low, jnp.where(own_mod == 1, end, own_pos)
 
 
-def attention_kernel(starts, limits, q_ref, kv_ref, low_ref, high_ref, o_ref, queries, top, total, acc):
+def attention_kernel(starts, limits, q_ref, span_ref, *rest):
+    sources, (o_ref, kv_ref, queries, bounds, top, total, acc, arrived) = rest[:-8], rest[-8:]
     count, size, _ = kv_ref.shape
+    for number, source in enumerate(sources):
+        pltpu.make_async_copy(source, kv_ref.at[number], arrived.at[number]).start()
     rows = q_ref.shape[0]
     kv_local, many = queries.shape[0], queries.shape[1]
     repeat = many // rows
@@ -264,11 +290,15 @@
     for head in range(kv_local * repeat):
         g, r = head // repeat, head % repeat
         queries[g, r * rows : (r + 1) * rows] = q_ref[:, head * HEAD_DIM : (head + 1) * HEAD_DIM]
+    columns = span_ref[...].T
+    for r in range(repeat):
+        bounds[r * rows : (r + 1) * rows] = columns
     transposed = (((1,), (1,)), ((), ()))
 
     def visit(number, _):
         start = starts[number]
         last = start + size - 1
+        pltpu.make_async_copy(sources[0], kv_ref.at[number], arrived.at[number]).wait()
 
         def block(masked):
             for g in range(kv_local):
@@ -279,7 +309,7 @@
                 )
                 if masked:
                     key_pos = start + lax.broadcasted_iota(jnp.int32, (many, size), 1)
-                    seen = (key_pos >= low_ref[...]) & (key_pos <= high_ref[...])
+                    seen = (key_pos >= bounds[:, 0:1]) & (key_pos <= bounds[:, 1:2])
                     scores = jnp.where(seen, scores, LOW)
                 old = top[g]
                 new = jnp.maximum(old, jnp.max(scores, axis=1, keepdims=True))
@@ -311,32 +341,41 @@
         )
 
 
-def attend(query, kv, starts, low, high, low_column, high_column):
+def attend(query, kv, starts, limits, span):
     rows, width = query.shape
     heads = width // HEAD_DIM
-    count, size, _ = kv.shape
-    kv_local = kv.shape[2] // (2 * HEAD_DIM)
+    count, (size, kv_cols) = len(kv), kv[0].shape
+    kv_local = kv_cols // (2 * HEAD_DIM)
     many = rows * heads // kv_local
-    limits = jnp.stack([low[0], high[-1], low[-1], high[0]])
     return pl.pallas_call(
         attention_kernel,
         out_shape=jax.ShapeDtypeStruct((rows, width), jnp.bfloat16),
-        in_specs=[SMEM, SMEM, VMEM, VMEM, VMEM, VMEM],
+        in_specs=[SMEM, SMEM, VMEM, VMEM] + [HBM] * (count // 2) + [VMEM] * (count // 2),
         out_specs=VMEM,
         scratch_shapes=[
+            pltpu.VMEM((count, size, kv_cols), jnp.bfloat16),
             pltpu.VMEM((kv_local, many, HEAD_DIM), jnp.bfloat16),
+            pltpu.VMEM((many, 8), jnp.int32),
             pltpu.VMEM((kv_local, many, HEAD_DIM), jnp.float32),
             pltpu.VMEM((kv_local, many, HEAD_DIM), jnp.float32),
             pltpu.VMEM((kv_local, many, HEAD_DIM), jnp.float32),
+            pltpu.SemaphoreType.DMA((count,)),
         ],
         cost_estimate=pl.CostEstimate(
             flops=4 * rows * count * size * width,
-            bytes_accessed=2 * (2 * rows * width + kv.size),
+            bytes_accessed=2 * (2 * rows * width + count * size * kv_cols),
             transcendentals=rows * count * size * heads,
         ),
         compiler_params=pltpu.CompilerParams(vmem_limit_bytes=20 * 1024 * 1024),
         name="attend",
-    )(starts, limits, query, kv, low_column, high_column)
+    )(
+        starts,
+        limits,
+        query,
+        span,
+        *[in_hbm(block) for block in kv[: count // 2]],
+        *kv[count // 2 :],
+    )
 
 
 def project_kernel(turns, place, ours_ref, beside_ref, ours_near, beside_near, own_ref, *rest):
@@ -442,13 +481,13 @@
     own_doc = part_of(doc_ids, z, s)
     own_pos = (z * subs + s) * length + jnp.arange(length, dtype=jnp.int32)
     low, high = spans(modality, doc_ids, part_of(modality, z, s), own_doc, own_pos)
-    repeat = w_query.shape[2] // HEAD_DIM // kv_local
-    low_column, high_column = jnp.tile(low, repeat)[:, None], jnp.tile(high, repeat)[:, None]
+    span = jnp.concatenate([low[None], high[None], jnp.zeros((6, length), jnp.int32)])
+    limits = jnp.stack([low[0], high[-1], low[-1], high[0]])
 
     if share_rows:
         for d in range(n - 1, 0, -1):
             blocks[d] = (*blocks[d], swap(blocks[d][0], "head"))
-    blocks[n - 1] = after(blocks[n - 1], low_column, high_column)
+    blocks[n - 1] = after(blocks[n - 1], span, limits)
 
     def parts_of(group, narrow):
         begins = jnp.stack([((z ^ d) * subs + s) * length for d in group]).astype(jnp.int32)
@@ -472,15 +511,14 @@
     same = [kv]
     for d in range(1, n):
         same.append(cross(kv, "seq", d))
-    beside_0 = swap(kv, "sub")
-    held = jnp.stack(same[1:])
-    others = swap(held, "sub")
-    kv_all = jnp.concatenate([jnp.stack(same), beside_0[None], others])
+    beside = []
+    for d in range(n):
+        beside.append(swap(same[d], "sub"))
     starts = jnp.stack(
         [((z ^ d) * subs + s) * length for d in range(n)]
         + [((z ^ d) * subs + (1 - s)) * length for d in range(n)]
     ).astype(jnp.int32)
-    attended = attend(query, kv_all, starts, low, high, low_column, high_column)
+    attended = attend(query, same + beside, starts, limits, span)
 
     beside = swap(attended, "sub")
     ours_near = (own_mod == y).astype(jnp.bfloat16)

time: 258 us -> 254 us (0.984)
  local copies, waits for them, and re-layouts: 13.9 us -> 10.5 us
  waiting for transfers between devices: 127 us -> 130 us
    ppermute x17 -> x19, waiting for transfers between devices: 51.7 us -> 70.3 us  [swap(): return lax.ppermute(x, axis, [(0, 1), (1, 0)])]
    ppermute x19, waiting for transfers between devices: 75.5 us -> 59.7 us  [cross(): return lax.ppermute(x, axis, [(i ^ bit, i) for i in among or range(size)])]
    unnamed x52 -> x42, local copies, waits for them, and re-layouts: 5.81 us -> 3.83 us
    ppermute x17 -> x19, starting transfers between devices: 13.4 us -> 13.3 us  [swap(): return lax.ppermute(x, axis, [(0, 1), (1, 0)])]
  transfers between devices with their start and end apart: 36 -> 38, of which waited for: 15 -> 17; matrix products, arithmetic and copies ran while one was open for 6% -> 5% of each run, Pallas kernels for 11% -> 12%
where the time goes in v7:
time: 254 us; the launch traced here: 253 us
  waiting for transfers between devices  130 us (51%)
  starting transfers between devices  67.6 us (27%)
  Pallas kernels  34.8 us (14%)
  local copies, waits for them, and re-layouts  10.5 us (4%)
  other arithmetic  7.58 us (3%)
    ppermute x19, waiting for transfers between devices, swap(): return lax.ppermute(x, axis, [(0, 1), (1, 0)])  70.3 us
    ppermute x19, waiting for transfers between devices, cross(): return lax.ppermute(x, axis, [(i ^ bit, i) for i in among or range(size)])  59.7 us
    ppermute x19, starting transfers between devices, cross(): return lax.ppermute(x, axis, [(i ^ bit, i) for i in among or range(size)])  54.3 us
    pallas_call x2, Pallas kernels, partial(): pl.pallas_call(functools.partial(partial_kernel, counts, narrow), out_sha...  14.8 us
    ppermute x19, starting transfers between devices, swap(): return lax.ppermute(x, axis, [(0, 1), (1, 0)])  13.3 us
    pallas_call x3, Pallas kernels, project(): pl.pallas_call(project_kernel, out_shape=(shape, shape), in_specs=[SMEM,...  12.1 us
  transfers between devices with their start and end apart: 38, of which 17 were waited for; matrix products, arithmetic and copies ran while one was open for 5% of the time, Pallas kernels for 12%

profile of v7, /device:TPU:0, one launch (start us, length us, event | category | flops | bytes accessed | tf_op | source)
XLA Modules:
  0.0 253.0 jit_solution(18079895832905656220)
XLA Ops:
  0.0 2.3 dynamic-slice_bitcast_fusion
  2.3 3.1 %collective-permute-start.25 = (bf16[448,1024]{1,0:T(8,128)(2,1)}, bf16[448,1024]{1,0:T(8,128)(2,1)}, u32[]{:S(2)}, u32[]{:S(2)}) collective-permute-start(bf16[448,1024]{1,0:T(8,128)(2,1)} %dynamic-slice_bitcast_fusion), channel_id=1, source_target_pairs={{4,0},{0,4},{12,8},{8,12},{5,1},{1,5},{13,9},{9,13},{6,2},{2,6},{1... | collective-permute-start | bytes 2752520 | tf_op jit(solution)/shard_map/ppermute | solution.py:25
  8.6 2.5 norm.1
  11.8 2.5 collective-permute-start.5
  14.3 2.4 collective-permute-start.7
  20.9 13.5 %collective-permute-done.5.rest_6_ = bf16[128,896]{1,0:T(8,128)(2,1)} collective-permute-done((bf16[128,896]{1,0:T(8,128)(2,1)}, bf16[128,896]{1,0:T(8,128)(2,1)}, u32[]{:S(2)}, u32[]{:S(2)}) %collective-permute-start.5) | collective-permute-done | bytes 229408 | tf_op jit(solution)/shard_map/ppermute | solution.py:25
  34.4 15.5 %collective-permute-done.7.rest_8_ = bf16[128,896]{1,0:T(8,128)(2,1)} collective-permute-done((bf16[128,896]{1,0:T(8,128)(2,1)}, bf16[128,896]{1,0:T(8,128)(2,1)}, u32[]{:S(2)}, u32[]{:S(2)}) %collective-permute-start.7) | collective-permute-done | bytes 229408 | tf_op jit(solution)/shard_map/ppermute | solution.py:25
  51.1 5.7 %collective-permute-done.3.rest_6_ = bf16[128,896]{1,0:T(8,128)(2,1)} collective-permute-done((bf16[128,896]{1,0:T(8,128)(2,1)}, bf16[128,896]{1,0:T(8,128)(2,1)}, u32[]{:S(2)}, u32[]{:S(2)}) %collective-permute-start.3) | collective-permute-done | bytes 229408 | tf_op jit(solution)/shard_map/ppermute | solution.py:25
  60.7 2.3 collective-permute-done.6.rest_7_
  64.5 2.6 %pad_add_fusion.limits = s32[4]{0:T(128)S(1)} fusion(s32[1]{0:T(128)} %get-tuple-element.65, s32[1]{0:T(128)} %get-tuple-element.62, s32[1]{0:T(128)} %get-tuple-element.66, s32[1]{0:T(128)} %get-tuple-element.61), kind=kLoop, calls=%fused_computation.33 | loop fusion | flops 12 | bytes 32 | tf_op jit(solution)/shard_map/stack | solution.py:485
  69.1 2.2 collective-permute-done.8.rest_9_
  73.0 7.5 %partial.3 = (f32[512,512]{1,0:T(8,128)}, f32[512,1024]{1,0:T(8,128)}, bf16[512,512]{1,0:T(8,128)(2,1)S(1)}, bf16[256,1024]{1,0:T(8,128)(2,1)S(1)}, bf16[256,1024]{1,0:T(8,128)(2,1)S(1)}) custom-call(s32[5]{0:T(128)S(1)} %stack.64.place, s32[2048]{0:T(1024)S(1)} %copy-done.4, s32[2]{0:T(128)S(1)} %pad_add_fusion.2.begins, bf16[2,448,256]{2,1,0:T(8,128)(2,1)} %copy-done.13, ...), custom_call_target="tpu_custom_call" | custom-call | flops 2818572288 | bytes 8650752 | tf_op jit(solution)/shard_map/partial/pallas_call | solution.py:178
  80.5 2.5 %collective-permute-start.9 = (bf16[256,1024]{1,0:T(8,128)(2,1)S(1)}, bf16[256,1024]{1,0:T(8,128)(2,1)S(1)}, u32[]{:S(2)}, u32[]{:S(2)}) collective-permute-start(bf16[256,1024]{1,0:T(8,128)(2,1)S(1)} %get-tuple-element.47), channel_id=1, source_target_pairs={{0,4},{12,8},{1,5},{13,9},{2,6},{14,10},{3,7},{15,11},{16,20},{28,... | collective-permute-start | bytes 1572872 | tf_op jit(solution)/shard_map/ppermute | solution.py:25
  88.3 7.3 %partial.2 = (f32[512,512]{1,0:T(8,128)}, f32[512,1024]{1,0:T(8,128)}) custom-call(s32[5]{0:T(128)S(1)} %stack.64.place, s32[2048]{0:T(1024)S(1)} %copy-done.4, s32[2]{0:T(128)S(1)} %pad_add_fusion.1.begins, bf16[2,448,256]{2,1,0:T(8,128)(2,1)} %copy-done.13, bf16[2,448,256]{2,1,0:T(8,128)(2,1)} %copy-done.17, bf16[2,448,256]{2,1,0:T(8,128)(2,1)} %copy-done.14, ...), custom_call_target="tpu_custom_call" | custom-call | flops 2818572288 | bytes 8650752 | tf_op jit(solution)/shard_map/partial/pallas_call | solution.py:178
  95.6 10.9 %collective-permute-done.14 = bf16[2,256,512]{2,1,0:T(8,128)(2,1)S(1)} collective-permute-done((bf16[2,256,512]{2,1,0:T(8,128)(2,1)S(1)}, bf16[2,256,512]{2,1,0:T(8,128)(2,1)S(1)}, u32[]{:S(2)}, u32[]{:S(2)}) %collective-permute-start.14) | collective-permute-done | bytes 524320 | tf_op jit(solution)/shard_map/ppermute | solution.py:25
  108.5 6.0 %collective-permute-done.12 = bf16[256,1024]{1,0:T(8,128)(2,1)S(1)} collective-permute-done((bf16[256,1024]{1,0:T(8,128)(2,1)S(1)}, bf16[256,1024]{1,0:T(8,128)(2,1)S(1)}, u32[]{:S(2)}, u32[]{:S(2)}) %collective-permute-start.12) | collective-permute-done | bytes 524320 | tf_op jit(solution)/shard_map/ppermute | solution.py:25
  115.6 10.5 %collective-permute-start.16 = (bf16[256,512]{1,0:T(8,128)(2,1)S(1)}, bf16[256,512]{1,0:T(8,128)(2,1)S(1)}, u32[]{:S(2)}, u32[]{:S(2)}) collective-permute-start(bf16[256,512]{1,0:T(8,128)(2,1)S(1)} %fusion.4), channel_id=1, source_target_pairs={{4,0},{0,4},{12,8},{8,12},{5,1},{1,5},{13,9},{9,13},{6,2},{2,6},{1... | collective-permute-start | bytes 786440 | tf_op jit(solution)/shard_map/ppermute | solution.py:25
  126.3 16.8 %collective-permute-start.11 = (bf16[256,1024]{1,0:T(8,128)(2,1)S(1)}, bf16[256,1024]{1,0:T(8,128)(2,1)S(1)}, u32[]{:S(2)}, u32[]{:S(2)}) collective-permute-start(bf16[256,1024]{1,0:T(8,128)(2,1)S(1)} %add_convert_fusion.2), channel_id=1, source_target_pairs={{4,0},{0,4},{12,8},{8,12},{5,1},{1,5},{13,9},{9,13},{6,2},{2,6},{1... | collective-permute-start | bytes 1572872 | tf_op jit(solution)/shard_map/ppermute | solution.py:25
  144.3 4.0 %collective-permute-start.18 = (bf16[256,512]{1,0:T(8,128)(2,1)S(1)}, bf16[256,512]{1,0:T(8,128)(2,1)S(1)}, u32[]{:S(2)}, u32[]{:S(2)}) collective-permute-start(bf16[256,512]{1,0:T(8,128)(2,1)S(1)} %fusion.3.rest_0_), channel_id=1, source_target_pairs={{8,0},{12,4},{0,8},{4,12},{9,1},{13,5},{1,9},{5,13},{10,2},{14,6},... | collective-permute-start | bytes 786440 | tf_op jit(solution)/shard_map/ppermute | solution.py:25
  149.9 6.0 %collective-permute-done.17.rest_1_ = bf16[256,512]{1,0:T(8,128)(2,1)S(1)} collective-permute-done((bf16[256,512]{1,0:T(8,128)(2,1)S(1)}, bf16[256,512]{1,0:T(8,128)(2,1)S(1)}, u32[]{:S(2)}, u32[]{:S(2)}) %collective-permute-start.17) | collective-permute-done | bytes 262176 | tf_op jit(solution)/shard_map/ppermute | solution.py:25
  158.9 2.1 collective-permute-done.19.rest_3_
  164.4 3.7 %attend.1.ours_ref = bf16[256,1024]{1,0:T(8,128)(2,1)S(1)} custom-call(s32[8]{0:T(128)S(1)} %stack.72.starts, s32[4]{0:T(128)S(1)} %pad_add_fusion.limits, bf16[256,1024]{1,0:T(8,128)(2,1)S(1)} %add_convert_fusion.1.q_ref, s32[8,256]{1,0:T(8,128)S(1)} %add_add_fusion.span_ref, bf16[256,512]{1,0:T(8,128)(2,1)} %copy-done.15, bf16[256,512]{1,0:T(8,128)(2,1)} %copy-done.18, ...), custom_call_target="tpu_custom_call" | custom-call | flops 2147483648 | bytes 3145728 | tf_op jit(solution)/shard_map/attend/pallas_call | solution.py:350
  168.1 2.0 collective-permute-start.24
  170.5 9.9 %collective-permute-done.30.rest_3_ = bf16[448,1024]{1,0:T(8,128)(2,1)} collective-permute-done((bf16[448,1024]{1,0:T(8,128)(2,1)}, bf16[448,1024]{1,0:T(8,128)(2,1)}, u32[]{:S(2)}, u32[]{:S(2)}) %collective-permute-start.30) | collective-permute-done | bytes 917536 | tf_op jit(solution)/shard_map/ppermute | solution.py:20
  180.4 19.7 %collective-permute-done.31.rest_4_ = bf16[448,1024]{1,0:T(8,128)(2,1)} collective-permute-done((bf16[448,1024]{1,0:T(8,128)(2,1)}, bf16[448,1024]{1,0:T(8,128)(2,1)}, u32[]{:S(2)}, u32[]{:S(2)}) %collective-permute-start.31) | collective-permute-done | bytes 917536 | tf_op jit(solution)/shard_map/ppermute | solution.py:20
  200.1 19.2 %collective-permute-done.32.rest_5_ = bf16[448,1024]{1,0:T(8,128)(2,1)} collective-permute-done((bf16[448,1024]{1,0:T(8,128)(2,1)}, bf16[448,1024]{1,0:T(8,128)(2,1)}, u32[]{:S(2)}, u32[]{:S(2)}) %collective-permute-start.32) | collective-permute-done | bytes 917536 | tf_op jit(solution)/shard_map/ppermute | solution.py:20
  219.3 3.8 %project.5 = (bf16[1,256,448]{2,1,0:T(8,128)(2,1)S(1)}, bf16[1,256,448]{2,1,0:T(8,128)(2,1)S(1)}) custom-call(s32[1]{0:T(128)S(6)} %xor.35.turns, s32[5]{0:T(128)S(1)} %stack.64.place, bf16[256,1024]{1,0:T(8,128)(2,1)S(1)} %attend.1.ours_ref, bf16[256,1024]{1,0:T(8,128)(2,1)} %collective-permute-done.24.beside_ref, bf16[256,1]{1,0:T(8,128)(2,1)S(1)} %reshape.63.ours_near, ...), custom_call_target="tpu_custom_call" | custom-call | flops 939524096 | bytes 2293760 | tf_op jit(solution)/shard_map/project/pallas_call | solution.py:425
  224.6 3.8 %project.4 = (bf16[1,256,448]{2,1,0:T(8,128)(2,1)S(1)}, bf16[1,256,448]{2,1,0:T(8,128)(2,1)S(1)}) custom-call(s32[1]{0:T(128)S(6)} %xor.34.turns, s32[5]{0:T(128)S(1)} %stack.64.place, bf16[256,1024]{1,0:T(8,128)(2,1)S(1)} %attend.1.ours_ref, bf16[256,1024]{1,0:T(8,128)(2,1)} %collective-permute-done.24.beside_ref, bf16[256,1]{1,0:T(8,128)(2,1)S(1)} %reshape.63.ours_near, ...), custom_call_target="tpu_custom_call" | custom-call | flops 939524096 | bytes 2293760 | tf_op jit(solution)/shard_map/project/pallas_call | solution.py:425
  228.5 4.5 %project.3 = (bf16[2,256,448]{2,1,0:T(8,128)(2,1)S(1)}, bf16[2,256,448]{2,1,0:T(8,128)(2,1)S(1)}) custom-call(s32[2]{0:T(128)S(1)} %add_xor_fusion.turns, s32[5]{0:T(128)S(1)} %stack.64.place, bf16[256,1024]{1,0:T(8,128)(2,1)S(1)} %attend.1.ours_ref, bf16[256,1024]{1,0:T(8,128)(2,1)} %collective-permute-done.24.beside_ref, ...), custom_call_target="tpu_custom_call" | custom-call | flops 1879048192 | bytes 4587520 | tf_op jit(solution)/shard_map/project/pallas_call | solution.py:425
  233.0 3.7 %collective-permute-done.35 = bf16[1,256,448]{2,1,0:T(8,128)(2,1)S(1)} collective-permute-done((bf16[1,256,448]{2,1,0:T(8,128)(2,1)S(1)}, bf16[1,256,448]{2,1,0:T(8,128)(2,1)S(1)}, u32[]{:S(2)}, u32[]{:S(2)}) %collective-permute-start.35) | collective-permute-done | bytes 229408 | tf_op jit(solution)/shard_map/ppermute | solution.py:20
  239.0 7.2 %collective-permute-done.33.rest_0_ = bf16[1,256,448]{2,1,0:T(8,128)(2,1)S(1)} collective-permute-done((bf16[1,256,448]{2,1,0:T(8,128)(2,1)S(1)}, bf16[1,256,448]{2,1,0:T(8,128)(2,1)S(1)}, u32[]{:S(2)}, u32[]{:S(2)}) %collective-permute-start.33) | collective-permute-done | bytes 229408 | tf_op jit(solution)/shard_map/ppermute | solution.py:20
  246.2 5.1 %collective-permute-done.34.rest_1_ = bf16[1,256,448]{2,1,0:T(8,128)(2,1)S(1)} collective-permute-done((bf16[1,256,448]{2,1,0:T(8,128)(2,1)S(1)}, bf16[1,256,448]{2,1,0:T(8,128)(2,1)S(1)}, u32[]{:S(2)}, u32[]{:S(2)}) %collective-permute-start.34) | collective-permute-done | bytes 229408 | tf_op jit(solution)/shard_map/ppermute | solution.py:20
  (136 shorter events, 40.1 us)
Async XLA Ops:
  2.3 56.7 %collective-permute-start.25 = (bf16[448,1024]{1,0:T(8,128)(2,1)}, bf16[448,1024]{1,0:T(8,128)(2,1)}, u32[]{:S(2)}, u32[]{:S(2)}) collective-permute-start(bf16[448,1024]{1,0:T(8,128)(2,1)} %dynamic-slice_bitcast_fusion), channel_id=1, source_target_pairs={{4,0},{0,4},{12,8},{8,12},{5,1},{1,5},{13,9},{9,13},{6,2},{2,6},{1... | collective-permute-start | bytes 2752520 | tf_op jit(solution)/shard_map/ppermute | solution.py:25
  5.4 62.4 %collective-permute-start.27 = (bf16[448,1024]{1,0:T(8,128)(2,1)}, bf16[448,1024]{1,0:T(8,128)(2,1)}, u32[]{:S(2)}, u32[]{:S(2)}) collective-permute-start(bf16[448,1024]{1,0:T(8,128)(2,1)} %dynamic-slice_bitcast_fusion), channel_id=1, source_target_pairs={{8,4},{4,8},{9,5},{5,9},{10,6},{6,10},{11,7},{7,11},{24,20},{20,24... | collective-permute-start | bytes 2752520 | tf_op jit(solution)/shard_map/ppermute | solution.py:25
  11.8 60.2 %collective-permute-start.2 = (bf16[2,448,1024]{2,1,0:T(8,128)(2,1)}, bf16[2,448,1024]{2,1,0:T(8,128)(2,1)}, u32[]{:S(2)}, u32[]{:S(2)}) collective-permute-start(bf16[2,448,1024]{2,1,0:T(8,128)(2,1)} %rest_4_.1), channel_id=1, source_target_pairs={{0,1},{1,0},{2,3},{3,2},{4,5},{5,4},{6,7},{7,6},{8,9},{9,8},{10,11... | collective-permute-start | bytes 5505032 | tf_op jit(solution)/shard_map/ppermute | solution.py:20
  11.8 22.6 %collective-permute-start.5 = (bf16[128,896]{1,0:T(8,128)(2,1)}, bf16[128,896]{1,0:T(8,128)(2,1)}, u32[]{:S(2)}, u32[]{:S(2)}) collective-permute-start(bf16[128,896]{1,0:T(8,128)(2,1)} %get-tuple-element.40), channel_id=1, source_target_pairs={{12,0},{8,4},{4,8},{0,12},{13,1},{9,5},{5,9},{1,13},{14,2},{10,6},... | collective-permute-start | bytes 688136 | tf_op jit(solution)/shard_map/ppermute | solution.py:25
  14.3 35.6 %collective-permute-start.7 = (bf16[128,896]{1,0:T(8,128)(2,1)}, bf16[128,896]{1,0:T(8,128)(2,1)}, u32[]{:S(2)}, u32[]{:S(2)}) collective-permute-start(bf16[128,896]{1,0:T(8,128)(2,1)} %get-tuple-element.43), channel_id=1, source_target_pairs={{8,0},{12,4},{0,8},{4,12},{9,1},{13,5},{1,9},{5,13},{10,2},{14,6},... | collective-permute-start | bytes 688136 | tf_op jit(solution)/shard_map/ppermute | solution.py:25
  34.4 24.5 %collective-permute-start = (bf16[2,448,256]{2,1,0:T(8,128)(2,1)S(1)}, bf16[2,448,256]{2,1,0:T(8,128)(2,1)S(1)}, u32[]{:S(2)}, u32[]{:S(2)}) collective-permute-start(bf16[2,448,256]{2,1,0:T(8,128)(2,1)S(1)} %constant_dynamic-slice_fusion.1.rest_0_), channel_id=1, source_target_pairs={{0,1},{1,0},{2,3},{3,2},{4,5},{5,4},{6,7},{7,6},{8,9},{9,8},{10,11... | collective-permute-start | bytes 1376264 | tf_op jit(solution)/shard_map/ppermute | solution.py:20
  58.9 8.4 %collective-permute-start.1 = (bf16[2,448,256]{2,1,0:T(8,128)(2,1)S(1)}, bf16[2,448,256]{2,1,0:T(8,128)(2,1)}, u32[]{:S(2)}, u32[]{:S(2)}) collective-permute-start(bf16[2,448,256]{2,1,0:T(8,128)(2,1)S(1)} %constant_dynamic-slice_fusion.rest_2_), channel_id=1, source_target_pairs={{0,1},{1,0},{2,3},{3,2},{4,5},{5,4},{6,7},{7,6},{8,9},{9,8},{10,11... | collective-permute-start | bytes 1376264 | tf_op jit(solution)/shard_map/ppermute | solution.py:20
  59.0 27.9 %collective-permute-start.26 = (bf16[448,1024]{1,0:T(8,128)(2,1)}, bf16[448,1024]{1,0:T(8,128)(2,1)}, u32[]{:S(2)}, u32[]{:S(2)}) collective-permute-start(bf16[448,1024]{1,0:T(8,128)(2,1)} %collective-permute-done.25.rest_0_), channel_id=1, source_target_pairs={{8,4},{4,8},{9,5},{5,9},{10,6},{6,10},{11,7},{7,11},{24,20},{20,24... | collective-permute-start | bytes 2752520 | tf_op jit(solution)/shard_map/ppermute | solution.py:25
  63.0 8.4 %collective-permute-start.8 = (bf16[128,896]{1,0:T(8,128)(2,1)}, bf16[128,896]{1,0:T(8,128)(2,1)S(1)}, u32[]{:S(2)}, u32[]{:S(2)}) collective-permute-start(bf16[128,896]{1,0:T(8,128)(2,1)} %collective-permute-done.7.rest_8_), channel_id=1, source_target_pairs={{0,2},{2,0},{1,3},{3,1},{4,6},{6,4},{5,7},{7,5},{8,10},{10,8},{9,1... | collective-permute-start | bytes 688136 | tf_op jit(solution)/shard_map/ppermute | solution.py:20
  67.3 18.4 %collective-permute-start.4 = (bf16[128,896]{1,0:T(8,128)(2,1)}, bf16[128,896]{1,0:T(8,128)(2,1)S(1)}, u32[]{:S(2)}, u32[]{:S(2)}) collective-permute-start(bf16[128,896]{1,0:T(8,128)(2,1)} %collective-permute-done.3.rest_6_), channel_id=1, source_target_pairs={{0,2},{2,0},{1,3},{3,1},{4,6},{6,4},{5,7},{7,5},{8,10},{10,8},{9,1... | collective-permute-start | bytes 688136 | tf_op jit(solution)/shard_map/ppermute | solution.py:20
  67.8 75.5 %collective-permute-start.28 = (bf16[448,1024]{1,0:T(8,128)(2,1)}, bf16[448,1024]{1,0:T(8,128)(2,1)S(1)}, u32[]{:S(2)}, u32[]{:S(2)}) collective-permute-start(bf16[448,1024]{1,0:T(8,128)(2,1)} %collective-permute-done.27), channel_id=1, source_target_pairs={{4,0},{8,12},{5,1},{9,13},{6,2},{10,14},{7,3},{11,15},{20,16},{24,... | collective-permute-start | bytes 2752520 | tf_op jit(solution)/shard_map/ppermute | solution.py:25
  80.5 27.1 %collective-permute-start.9 = (bf16[256,1024]{1,0:T(8,128)(2,1)S(1)}, bf16[256,1024]{1,0:T(8,128)(2,1)S(1)}, u32[]{:S(2)}, u32[]{:S(2)}) collective-permute-start(bf16[256,1024]{1,0:T(8,128)(2,1)S(1)} %get-tuple-element.47), channel_id=1, source_target_pairs={{0,4},{12,8},{1,5},{13,9},{2,6},{14,10},{3,7},{15,11},{16,20},{28,... | collective-permute-start | bytes 1572872 | tf_op jit(solution)/shard_map/ppermute | solution.py:25
  83.0 23.5 %collective-permute-start.14 = (bf16[2,256,512]{2,1,0:T(8,128)(2,1)S(1)}, bf16[2,256,512]{2,1,0:T(8,128)(2,1)S(1)}, u32[]{:S(2)}, u32[]{:S(2)}) collective-permute-start(bf16[2,256,512]{2,1,0:T(8,128)(2,1)S(1)} %bitcast.49), channel_id=1, source_target_pairs={{0,4},{12,8},{1,5},{13,9},{2,6},{14,10},{3,7},{15,11},{16,20},{28,... | collective-permute-start | bytes 1572872 | tf_op jit(solution)/shard_map/ppermute | solution.py:25
  85.6 28.9 %collective-permute-start.12 = (bf16[256,1024]{1,0:T(8,128)(2,1)S(1)}, bf16[256,1024]{1,0:T(8,128)(2,1)S(1)}, u32[]{:S(2)}, u32[]{:S(2)}) collective-permute-start(bf16[256,1024]{1,0:T(8,128)(2,1)S(1)} %get-tuple-element.48), channel_id=1, source_target_pairs={{0,4},{12,8},{1,5},{13,9},{2,6},{14,10},{3,7},{15,11},{16,20},{28,... | collective-permute-start | bytes 1572872 | tf_op jit(solution)/shard_map/ppermute | solution.py:25
  87.0 61.3 %collective-permute-start.29 = (bf16[448,1024]{1,0:T(8,128)(2,1)}, bf16[448,1024]{1,0:T(8,128)(2,1)S(1)}, u32[]{:S(2)}, u32[]{:S(2)}) collective-permute-start(bf16[448,1024]{1,0:T(8,128)(2,1)} %collective-permute-done.26), channel_id=1, source_target_pairs={{4,0},{8,12},{5,1},{9,13},{6,2},{10,14},{7,3},{11,15},{20,16},{24,... | collective-permute-start | bytes 2752520 | tf_op jit(solution)/shard_map/ppermute | solution.py:25
  106.7 8.9 %collective-permute-start.15 = (bf16[2,256,512]{2,1,0:T(8,128)(2,1)S(1)}, bf16[2,256,512]{2,1,0:T(8,128)(2,1)S(1)}, u32[]{:S(2)}, u32[]{:S(2)}) collective-permute-start(bf16[2,256,512]{2,1,0:T(8,128)(2,1)S(1)} %fusion), channel_id=1, source_target_pairs={{8,4},{4,8},{9,5},{5,9},{10,6},{6,10},{11,7},{7,11},{24,20},{20,24... | collective-permute-start | bytes 1572872 | tf_op jit(solution)/shard_map/ppermute | solution.py:25
  107.7 18.4 %collective-permute-start.10 = (bf16[256,1024]{1,0:T(8,128)(2,1)S(1)}, bf16[256,1024]{1,0:T(8,128)(2,1)S(1)}, u32[]{:S(2)}, u32[]{:S(2)}) collective-permute-start(bf16[256,1024]{1,0:T(8,128)(2,1)S(1)} %fusion.2), channel_id=1, source_target_pairs={{8,4},{4,8},{9,5},{5,9},{10,6},{6,10},{11,7},{7,11},{24,20},{20,24... | collective-permute-start | bytes 1572872 | tf_op jit(solution)/shard_map/ppermute | solution.py:25
  114.7 35.2 %collective-permute-start.13 = (bf16[256,1024]{1,0:T(8,128)(2,1)S(1)}, bf16[256,1024]{1,0:T(8,128)(2,1)S(1)}, u32[]{:S(2)}, u32[]{:S(2)}) collective-permute-start(bf16[256,1024]{1,0:T(8,128)(2,1)S(1)} %fusion.1), channel_id=1, source_target_pairs={{8,4},{4,8},{9,5},{5,9},{10,6},{6,10},{11,7},{7,11},{24,20},{20,24... | collective-permute-start | bytes 1572872 | tf_op jit(solution)/shard_map/ppermute | solution.py:25
  115.6 27.4 %collective-permute-start.16 = (bf16[256,512]{1,0:T(8,128)(2,1)S(1)}, bf16[256,512]{1,0:T(8,128)(2,1)S(1)}, u32[]{:S(2)}, u32[]{:S(2)}) collective-permute-start(bf16[256,512]{1,0:T(8,128)(2,1)S(1)} %fusion.4), channel_id=1, source_target_pairs={{4,0},{0,4},{12,8},{8,12},{5,1},{1,5},{13,9},{9,13},{6,2},{2,6},{1... | collective-permute-start | bytes 786440 | tf_op jit(solution)/shard_map/ppermute | solution.py:25
  126.3 30.6 %collective-permute-start.11 = (bf16[256,1024]{1,0:T(8,128)(2,1)S(1)}, bf16[256,1024]{1,0:T(8,128)(2,1)S(1)}, u32[]{:S(2)}, u32[]{:S(2)}) collective-permute-start(bf16[256,1024]{1,0:T(8,128)(2,1)S(1)} %add_convert_fusion.2), channel_id=1, source_target_pairs={{4,0},{0,4},{12,8},{8,12},{5,1},{1,5},{13,9},{9,13},{6,2},{2,6},{1... | collective-permute-start | bytes 1572872 | tf_op jit(solution)/shard_map/ppermute | solution.py:25
  143.2 12.6 %collective-permute-start.17 = (bf16[256,512]{1,0:T(8,128)(2,1)S(1)}, bf16[256,512]{1,0:T(8,128)(2,1)S(1)}, u32[]{:S(2)}, u32[]{:S(2)}) collective-permute-start(bf16[256,512]{1,0:T(8,128)(2,1)S(1)} %fusion.3.rest_0_), channel_id=1, source_target_pairs={{4,0},{0,4},{12,8},{8,12},{5,1},{1,5},{13,9},{9,13},{6,2},{2,6},{1... | collective-permute-start | bytes 786440 | tf_op jit(solution)/shard_map/ppermute | solution.py:25
  144.3 14.1 %collective-permute-start.18 = (bf16[256,512]{1,0:T(8,128)(2,1)S(1)}, bf16[256,512]{1,0:T(8,128)(2,1)S(1)}, u32[]{:S(2)}, u32[]{:S(2)}) collective-permute-start(bf16[256,512]{1,0:T(8,128)(2,1)S(1)} %fusion.3.rest_0_), channel_id=1, source_target_pairs={{8,0},{12,4},{0,8},{4,12},{9,1},{13,5},{1,9},{5,13},{10,2},{14,6},... | collective-permute-start | bytes 786440 | tf_op jit(solution)/shard_map/ppermute | solution.py:25
  148.3 12.7 %collective-permute-start.19 = (bf16[256,512]{1,0:T(8,128)(2,1)S(1)}, bf16[256,512]{1,0:T(8,128)(2,1)S(1)}, u32[]{:S(2)}, u32[]{:S(2)}) collective-permute-start(bf16[256,512]{1,0:T(8,128)(2,1)S(1)} %fusion.3.rest_0_), channel_id=1, source_target_pairs={{12,0},{8,4},{4,8},{0,12},{13,1},{9,5},{5,9},{1,13},{14,2},{10,6},... | collective-permute-start | bytes 786440 | tf_op jit(solution)/shard_map/ppermute | solution.py:25
  149.9 12.7 %collective-permute-start.20 = (bf16[256,512]{1,0:T(8,128)(2,1)S(1)}, bf16[256,512]{1,0:T(8,128)(2,1)S(1)}, u32[]{:S(2)}, u32[]{:S(2)}) collective-permute-start(bf16[256,512]{1,0:T(8,128)(2,1)S(1)} %fusion.3.rest_0_), channel_id=1, source_target_pairs={{0,1},{1,0},{2,3},{3,2},{4,5},{5,4},{6,7},{7,6},{8,9},{9,8},{10,11... | collective-permute-start | bytes 786440 | tf_op jit(solution)/shard_map/ppermute | solution.py:20
  156.9 23.5 %collective-permute-start.30 = (bf16[448,1024]{1,0:T(8,128)(2,1)}, bf16[448,1024]{1,0:T(8,128)(2,1)}, u32[]{:S(2)}, u32[]{:S(2)}) collective-permute-start(bf16[448,1024]{1,0:T(8,128)(2,1)} %collective-permute-done.25.rest_0_), channel_id=1, source_target_pairs={{0,16},{16,0},{1,17},{17,1},{2,18},{18,2},{3,19},{19,3},{4,20},{20... | collective-permute-start | bytes 2752520 | tf_op jit(solution)/shard_map/ppermute | solution.py:20
  158.4 41.7 %collective-permute-start.31 = (bf16[448,1024]{1,0:T(8,128)(2,1)}, bf16[448,1024]{1,0:T(8,128)(2,1)}, u32[]{:S(2)}, u32[]{:S(2)}) collective-permute-start(bf16[448,1024]{1,0:T(8,128)(2,1)} %broadcast_select_fusion.1.rest_1_), channel_id=1, source_target_pairs={{0,16},{16,0},{1,17},{17,1},{2,18},{18,2},{3,19},{19,3},{4,20},{20... | collective-permute-start | bytes 2752520 | tf_op jit(solution)/shard_map/ppermute | solution.py:20
  161.0 58.3 %collective-permute-start.32 = (bf16[448,1024]{1,0:T(8,128)(2,1)}, bf16[448,1024]{1,0:T(8,128)(2,1)}, u32[]{:S(2)}, u32[]{:S(2)}) collective-permute-start(bf16[448,1024]{1,0:T(8,128)(2,1)} %broadcast_select_fusion.rest_2_), channel_id=1, source_target_pairs={{0,16},{16,0},{1,17},{17,1},{2,18},{18,2},{3,19},{19,3},{4,20},{20... | collective-permute-start | bytes 2752520 | tf_op jit(solution)/shard_map/ppermute | solution.py:20
  168.1 51.2 %collective-permute-start.24 = (bf16[256,1024]{1,0:T(8,128)(2,1)S(1)}, bf16[256,1024]{1,0:T(8,128)(2,1)}, u32[]{:S(2)}, u32[]{:S(2)}) collective-permute-start(bf16[256,1024]{1,0:T(8,128)(2,1)S(1)} %attend.1.ours_ref), channel_id=1, source_target_pairs={{0,1},{1,0},{2,3},{3,2},{4,5},{5,4},{6,7},{7,6},{8,9},{9,8},{10,11... | collective-permute-start | bytes 1572872 | tf_op jit(solution)/shard_map/ppermute | solution.py:20
  223.1 9.9 %collective-permute-start.36 = (bf16[1,256,448]{2,1,0:T(8,128)(2,1)S(1)}, bf16[1,256,448]{2,1,0:T(8,128)(2,1)S(1)}, u32[]{:S(2)}, u32[]{:S(2)}) collective-permute-start(bf16[1,256,448]{2,1,0:T(8,128)(2,1)S(1)} %get-tuple-element.58), channel_id=1, source_target_pairs={{0,2},{2,0},{1,3},{3,1},{4,6},{6,4},{5,7},{7,5},{8,10},{10,8},{9,1... | collective-permute-start | bytes 688136 | tf_op jit(solution)/shard_map/ppermute | solution.py:20
  236.8 14.4 %collective-permute-start.37 = (bf16[2,256,448]{2,1,0:T(8,128)(2,1)S(1)}, bf16[2,256,448]{2,1,0:T(8,128)(2,1)S(1)}, u32[]{:S(2)}, u32[]{:S(2)}) collective-permute-start(bf16[2,256,448]{2,1,0:T(8,128)(2,1)S(1)} %add_convert_fusion), channel_id=1, source_target_pairs={{0,1},{1,0},{2,3},{3,2},{4,5},{5,4},{6,7},{7,6},{8,9},{9,8},{10,11... | collective-permute-start | bytes 1376264 | tf_op jit(solution)/shard_map/ppermute | solution.py:20
  236.9 9.2 %collective-permute-start.33 = (bf16[1,256,448]{2,1,0:T(8,128)(2,1)S(1)}, bf16[1,256,448]{2,1,0:T(8,128)(2,1)S(1)}, u32[]{:S(2)}, u32[]{:S(2)}) collective-permute-start(bf16[1,256,448]{2,1,0:T(8,128)(2,1)S(1)} %get-tuple-element.54), channel_id=1, source_target_pairs={{0,2},{2,0},{1,3},{3,1},{4,6},{6,4},{5,7},{7,5},{8,10},{10,8},{9,1... | collective-permute-start | bytes 688136 | tf_op jit(solution)/shard_map/ppermute | solution.py:20
  238.4 12.9 %collective-permute-start.34 = (bf16[1,256,448]{2,1,0:T(8,128)(2,1)S(1)}, bf16[1,256,448]{2,1,0:T(8,128)(2,1)S(1)}, u32[]{:S(2)}, u32[]{:S(2)}) collective-permute-start(bf16[1,256,448]{2,1,0:T(8,128)(2,1)S(1)} %get-tuple-element.55), channel_id=1, source_target_pairs={{0,2},{2,0},{1,3},{3,1},{4,6},{6,4},{5,7},{7,5},{8,10},{10,8},{9,1... | collective-permute-start | bytes 688136 | tf_op jit(solution)/shard_map/ppermute | solution.py:20
  (27 other events, 367.4 us)

commit v8 on v7

--- a/solution.py
+++ b/solution.py
@@ -350,7 +350,7 @@
     return pl.pallas_call(
         attention_kernel,
         out_shape=jax.ShapeDtypeStruct((rows, width), jnp.bfloat16),
-        in_specs=[SMEM, SMEM, VMEM, VMEM] + [HBM] * (count // 2) + [VMEM] * (count // 2),
+        in_specs=[SMEM, SMEM, VMEM, VMEM] + [HBM] * (count // 2 + 1) + [VMEM] * (count // 2 - 1),
         out_specs=VMEM,
         scratch_shapes=[
             pltpu.VMEM((count, size, kv_cols), jnp.bfloat16),
@@ -373,15 +373,19 @@
         limits,
         query,
         span,
-        *[in_hbm(block) for block in kv[: count // 2]],
-        *kv[count // 2 :],
+        *[in_hbm(block) for block in kv[: count // 2 + 1]],
+        *kv[count // 2 + 1 :],
     )
 
 
-def project_kernel(turns, place, ours_ref, beside_ref, ours_near, beside_near, own_ref, *rest):
-    n = (len(rest) - 5) // 2 + 1
-    near, far = rest[: n - 1], rest[n - 1 : 2 * n - 2]
-    o_ours, o_beside, held, lhs, arrived = rest[2 * n - 2 :]
+def project_kernel(n, groups, turns, place, *rest):
+    inputs, own_ref, near, far = (
+        rest[: 2 * groups],
+        rest[2 * groups],
+        rest[2 * groups + 1 : 2 * groups + n],
+        rest[2 * groups + n : 2 * groups + 2 * n - 1],
+    )
+    outs, (held, lhs, arrived) = rest[2 * groups + 2 * n - 1 : -3], rest[-3:]
     count = turns.shape[0]
     first = place[2]
 
@@ -396,13 +400,13 @@
         for d in range(n):
             fetch(i, d)
 
-    rows = ours_ref.shape[0]
-    for base, a_ref, near_ref in ((0, ours_ref, ours_near), (rows, beside_ref, beside_near)):
-        a = a_ref[...]
-        mine = near_ref[...] != 0
+    rows = inputs[0].shape[0]
+    for group in range(groups):
+        a = inputs[2 * group][...]
+        mine = inputs[2 * group + 1][...] != 0
         zero = jnp.zeros_like(a)
-        lhs[0, base : base + rows] = jnp.where(mine, a, zero)
-        lhs[1, base : base + rows] = jnp.where(mine, zero, a)
+        lhs[0, group * rows : (group + 1) * rows] = jnp.where(mine, a, zero)
+        lhs[1, group * rows : (group + 1) * rows] = jnp.where(mine, zero, a)
     contract = (((1,), (1,)), ((), ()))
     for i in range(count):
         value = None
@@ -413,33 +417,32 @@
             )
             value = term if value is None else value + term
         value = value.astype(jnp.bfloat16)
-        o_ours[i] = value[:rows]
-        o_beside[i] = value[rows:]
-
-
-def project(ours, beside, ours_near, beside_near, weights, turns, place):
-    rows, depth = ours.shape
-    count = turns.shape[0]
+        for group in range(groups):
+            outs[group][i] = value[group * rows : (group + 1) * rows]
+
+
+def project(tokens, weights, turns, place):
+    rows, depth = tokens[0][0].shape
+    groups, count = len(tokens), turns.shape[0]
     width = weights[0].shape[1]
-    shape = jax.ShapeDtypeStruct((count, rows, width), jnp.bfloat16)
     return pl.pallas_call(
-        project_kernel,
-        out_shape=(shape, shape),
-        in_specs=[SMEM, SMEM] + [VMEM] * 4 + [HBM] * len(weights),
-        out_specs=(VMEM, VMEM),
+        functools.partial(project_kernel, (len(weights) + 1) // 2, groups),
+        out_shape=[jax.ShapeDtypeStruct((count, rows, width), jnp.bfloat16)] * groups,
+        in_specs=[SMEM, SMEM] + [VMEM] * (2 * groups) + [HBM] * len(weights),
+        out_specs=[VMEM] * groups,
         scratch_shapes=[
             pltpu.VMEM((2, count, width, depth), jnp.bfloat16),
-            pltpu.VMEM((2, 2 * rows, depth), jnp.bfloat16),
+            pltpu.VMEM((2, groups * rows, depth), jnp.bfloat16),
             pltpu.SemaphoreType.DMA((2, count)),
         ],
         cost_estimate=pl.CostEstimate(
-            flops=8 * count * rows * depth * width,
-            bytes_accessed=4 * count * depth * width + 4 * count * rows * width,
+            flops=4 * groups * count * rows * depth * width,
+            bytes_accessed=4 * count * depth * width + 2 * groups * count * rows * width,
             transcendentals=0,
         ),
         compiler_params=pltpu.CompilerParams(vmem_limit_bytes=16 * 1024 * 1024),
         name="project",
-    )(turns, place, ours, beside, ours_near[:, None], beside_near[:, None], *weights)
+    )(turns, place, *[a for pair in tokens for a in (pair[0], pair[1][:, None])], *weights)
 
 
 def body(tokens, norm_gain, w_query, w_key, w_value, w_out, modality, doc_ids):
@@ -524,12 +527,13 @@
     ours_near = (own_mod == y).astype(jnp.bfloat16)
     beside_near = (part_of(modality, z, 1 - s) == y).astype(jnp.bfloat16)
 
-    def out(columns):
-        turns = (columns ^ z).astype(jnp.int32)
-        return project(attended, beside, ours_near, beside_near, weights, turns, place)
+    our_rows, beside_rows = (attended, ours_near), (beside, beside_near)
+
+    def out(tokens, columns):
+        return project(tokens, weights, (columns ^ z).astype(jnp.int32), place)
 
     if heads_over != 2:
-        ours, theirs = out(jnp.arange(n))
+        ours, theirs = out([our_rows, beside_rows], jnp.arange(n))
         sibling = swap(theirs, "sub")
         pair = jnp.where(s == 0, jnp.stack([ours, sibling], 1), jnp.stack([sibling, ours], 1))
         wide = jnp.transpose(pair, (2, 0, 1, 3)).reshape(length, -1)
@@ -537,11 +541,17 @@
 
     half = n // 2
     ours, theirs = [], []
-    sent = [out((1 - x) * half + jnp.arange(i, i + 1)) for i in range(half)]
-    for send_ours, send_beside in sent:
-        theirs.append(swap(send_beside, "head"))
-        ours.append(swap(send_ours, "head"))
-    keep_ours, keep_beside = out(x * half + jnp.arange(half))
+
+    def piece(tokens, i):
+        return out([tokens], (1 - x) * half + jnp.arange(i, i + 1))[0]
+
+    for i in range(half):
+        sent = piece(our_rows, i)
+        ours.append(swap(sent, "head"))
+    for i in range(half):
+        sent = piece(beside_rows, i)
+        theirs.append(swap(sent, "head"))
+    keep_ours, keep_beside = out([our_rows, beside_rows], x * half + jnp.arange(half))
     done = add(keep_beside, jnp.concatenate(theirs))
     sibling = swap(done, "sub")
     return finish(place, keep_ours, ours, sibling)

time: 254 us -> 256 us (level)
  Pallas kernels: 34.8 us -> 39.3 us
    pallas_call x3 -> x5, Pallas kernels: 12.1 us -> 16.6 us  [project(): pl.pallas_call(functools.partial(project_kernel, (len(weights) + 1) // 2,...]
  transfers between devices with their start and end apart: 38 -> 38, of which waited for: 17 -> 17; matrix products, arithmetic and copies ran while one was open for 5% -> 5% of each run, Pallas kernels for 12% -> 13%
where the time goes in v8:
time: 256 us; the launch traced here: 255 us
  waiting for transfers between devices  128 us (50%)
  starting transfers between devices  67.4 us (26%)
  Pallas kernels  39.3 us (15%)
  local copies, waits for them, and re-layouts  10.4 us (4%)
  other arithmetic  7.37 us (3%)
    ppermute x19, waiting for transfers between devices, swap(): return lax.ppermute(x, axis, [(0, 1), (1, 0)])  68.8 us
    ppermute x19, waiting for transfers between devices, cross(): return lax.ppermute(x, axis, [(i ^ bit, i) for i in among or range(size)])  59.6 us
    ppermute x19, starting transfers between devices, cross(): return lax.ppermute(x, axis, [(i ^ bit, i) for i in among or range(size)])  54.2 us
    pallas_call x5, Pallas kernels, project(): pl.pallas_call(functools.partial(project_kernel, (len(weights) + 1) // 2,...  16.6 us
    pallas_call x2, Pallas kernels, partial(): pl.pallas_call(functools.partial(partial_kernel, counts, narrow), out_sha...  14.8 us
    ppermute x19, starting transfers between devices, swap(): return lax.ppermute(x, axis, [(0, 1), (1, 0)])  13.2 us
  transfers between devices with their start and end apart: 38, of which 17 were waited for; matrix products, arithmetic and copies ran while one was open for 5% of the time, Pallas kernels for 13%

profile of v8, /device:TPU:0, one launch (start us, length us, event | category | flops | bytes accessed | tf_op | source)
XLA Modules:
  0.0 255.2 jit_solution(8480579430286999068)
XLA Ops:
  0.0 2.3 dynamic-slice_bitcast_fusion
  2.3 3.1 %collective-permute-start.25 = (bf16[448,1024]{1,0:T(8,128)(2,1)}, bf16[448,1024]{1,0:T(8,128)(2,1)}, u32[]{:S(2)}, u32[]{:S(2)}) collective-permute-start(bf16[448,1024]{1,0:T(8,128)(2,1)} %dynamic-slice_bitcast_fusion), channel_id=1, source_target_pairs={{4,0},{0,4},{12,8},{8,12},{5,1},{1,5},{13,9},{9,13},{6,2},{2,6},{1... | collective-permute-start | bytes 2752520 | tf_op jit(solution)/shard_map/ppermute | solution.py:25
  8.6 2.5 norm.1
  11.8 2.5 collective-permute-start.5
  14.3 2.4 collective-permute-start.7
  20.8 13.6 %collective-permute-done.5.rest_6_ = bf16[128,896]{1,0:T(8,128)(2,1)} collective-permute-done((bf16[128,896]{1,0:T(8,128)(2,1)}, bf16[128,896]{1,0:T(8,128)(2,1)}, u32[]{:S(2)}, u32[]{:S(2)}) %collective-permute-start.5) | collective-permute-done | bytes 229408 | tf_op jit(solution)/shard_map/ppermute | solution.py:25
  34.4 15.5 %collective-permute-done.7.rest_8_ = bf16[128,896]{1,0:T(8,128)(2,1)} collective-permute-done((bf16[128,896]{1,0:T(8,128)(2,1)}, bf16[128,896]{1,0:T(8,128)(2,1)}, u32[]{:S(2)}, u32[]{:S(2)}) %collective-permute-start.7) | collective-permute-done | bytes 229408 | tf_op jit(solution)/shard_map/ppermute | solution.py:25
  51.1 5.7 %collective-permute-done.3.rest_6_ = bf16[128,896]{1,0:T(8,128)(2,1)} collective-permute-done((bf16[128,896]{1,0:T(8,128)(2,1)}, bf16[128,896]{1,0:T(8,128)(2,1)}, u32[]{:S(2)}, u32[]{:S(2)}) %collective-permute-start.3) | collective-permute-done | bytes 229408 | tf_op jit(solution)/shard_map/ppermute | solution.py:25
  60.6 2.3 collective-permute-done.6.rest_7_
  64.5 2.4 pad_add_fusion.limits
  68.9 2.6 %collective-permute-done.8.rest_9_ = bf16[128,896]{1,0:T(8,128)(2,1)S(1)} collective-permute-done((bf16[128,896]{1,0:T(8,128)(2,1)}, bf16[128,896]{1,0:T(8,128)(2,1)S(1)}, u32[]{:S(2)}, u32[]{:S(2)}) %collective-permute-start.8) | collective-permute-done | bytes 229408 | tf_op jit(solution)/shard_map/ppermute | solution.py:20
  73.2 7.5 %partial.3 = (f32[512,512]{1,0:T(8,128)}, f32[512,1024]{1,0:T(8,128)}, bf16[512,512]{1,0:T(8,128)(2,1)S(1)}, bf16[256,1024]{1,0:T(8,128)(2,1)S(1)}, bf16[256,1024]{1,0:T(8,128)(2,1)S(1)}) custom-call(s32[5]{0:T(128)S(1)} %stack.64.place, s32[2048]{0:T(1024)S(1)} %copy-done.4, s32[2]{0:T(128)S(1)} %pad_add_fusion.2.begins, bf16[2,448,256]{2,1,0:T(8,128)(2,1)} %copy-done.13, ...), custom_call_target="tpu_custom_call" | custom-call | flops 2818572288 | bytes 8650752 | tf_op jit(solution)/shard_map/partial/pallas_call | solution.py:178
  80.7 2.3 collective-permute-start.9
  88.2 7.3 %partial.2 = (f32[512,512]{1,0:T(8,128)}, f32[512,1024]{1,0:T(8,128)}) custom-call(s32[5]{0:T(128)S(1)} %stack.64.place, s32[2048]{0:T(1024)S(1)} %copy-done.4, s32[2]{0:T(128)S(1)} %pad_add_fusion.1.begins, bf16[2,448,256]{2,1,0:T(8,128)(2,1)} %copy-done.13, bf16[2,448,256]{2,1,0:T(8,128)(2,1)} %copy-done.17, bf16[2,448,256]{2,1,0:T(8,128)(2,1)} %copy-done.14, ...), custom_call_target="tpu_custom_call" | custom-call | flops 2818572288 | bytes 8650752 | tf_op jit(solution)/shard_map/partial/pallas_call | solution.py:178
  95.6 10.9 %collective-permute-done.14 = bf16[2,256,512]{2,1,0:T(8,128)(2,1)S(1)} collective-permute-done((bf16[2,256,512]{2,1,0:T(8,128)(2,1)S(1)}, bf16[2,256,512]{2,1,0:T(8,128)(2,1)S(1)}, u32[]{:S(2)}, u32[]{:S(2)}) %collective-permute-start.14) | collective-permute-done | bytes 524320 | tf_op jit(solution)/shard_map/ppermute | solution.py:25
  108.5 5.9 %collective-permute-done.12 = bf16[256,1024]{1,0:T(8,128)(2,1)S(1)} collective-permute-done((bf16[256,1024]{1,0:T(8,128)(2,1)S(1)}, bf16[256,1024]{1,0:T(8,128)(2,1)S(1)}, u32[]{:S(2)}, u32[]{:S(2)}) %collective-permute-start.12) | collective-permute-done | bytes 524320 | tf_op jit(solution)/shard_map/ppermute | solution.py:25
  115.5 10.6 %collective-permute-start.16 = (bf16[256,512]{1,0:T(8,128)(2,1)S(1)}, bf16[256,512]{1,0:T(8,128)(2,1)S(1)}, u32[]{:S(2)}, u32[]{:S(2)}) collective-permute-start(bf16[256,512]{1,0:T(8,128)(2,1)S(1)} %fusion.4), channel_id=1, source_target_pairs={{4,0},{0,4},{12,8},{8,12},{5,1},{1,5},{13,9},{9,13},{6,2},{2,6},{1... | collective-permute-start | bytes 786440 | tf_op jit(solution)/shard_map/ppermute | solution.py:25
  126.3 16.8 %collective-permute-start.11 = (bf16[256,1024]{1,0:T(8,128)(2,1)S(1)}, bf16[256,1024]{1,0:T(8,128)(2,1)S(1)}, u32[]{:S(2)}, u32[]{:S(2)}) collective-permute-start(bf16[256,1024]{1,0:T(8,128)(2,1)S(1)} %add_convert_fusion.2), channel_id=1, source_target_pairs={{4,0},{0,4},{12,8},{8,12},{5,1},{1,5},{13,9},{9,13},{6,2},{2,6},{1... | collective-permute-start | bytes 1572872 | tf_op jit(solution)/shard_map/ppermute | solution.py:25
  144.3 3.9 %collective-permute-start.18 = (bf16[256,512]{1,0:T(8,128)(2,1)S(1)}, bf16[256,512]{1,0:T(8,128)(2,1)S(1)}, u32[]{:S(2)}, u32[]{:S(2)}) collective-permute-start(bf16[256,512]{1,0:T(8,128)(2,1)S(1)} %fusion.3.rest_0_), channel_id=1, source_target_pairs={{8,0},{12,4},{0,8},{4,12},{9,1},{13,5},{1,9},{5,13},{10,2},{14,6},... | collective-permute-start | bytes 786440 | tf_op jit(solution)/shard_map/ppermute | solution.py:25
  149.8 6.0 %collective-permute-done.17.rest_1_ = bf16[256,512]{1,0:T(8,128)(2,1)S(1)} collective-permute-done((bf16[256,512]{1,0:T(8,128)(2,1)S(1)}, bf16[256,512]{1,0:T(8,128)(2,1)S(1)}, u32[]{:S(2)}, u32[]{:S(2)}) %collective-permute-start.17) | collective-permute-done | bytes 262176 | tf_op jit(solution)/shard_map/ppermute | solution.py:25
  164.4 3.7 %attend.1.rest_0_ = bf16[256,1024]{1,0:T(8,128)(2,1)S(1)} custom-call(s32[8]{0:T(128)S(1)} %stack.72.starts, s32[4]{0:T(128)S(1)} %pad_add_fusion.limits, bf16[256,1024]{1,0:T(8,128)(2,1)S(1)} %add_convert_fusion.1.q_ref, s32[8,256]{1,0:T(8,128)S(1)} %add_add_fusion.span_ref, bf16[256,512]{1,0:T(8,128)(2,1)} %copy-done.15, bf16[256,512]{1,0:T(8,128)(2,1)} %copy-done.18, ...), custom_call_target="tpu_custom_call" | custom-call | flops 2147483648 | bytes 3145728 | tf_op jit(solution)/shard_map/attend/pallas_call | solution.py:350
  170.3 10.1 %collective-permute-done.30.rest_8_.rest_6_ = bf16[448,1024]{1,0:T(8,128)(2,1)} collective-permute-done((bf16[448,1024]{1,0:T(8,128)(2,1)}, bf16[448,1024]{1,0:T(8,128)(2,1)}, u32[]{:S(2)}, u32[]{:S(2)}) %collective-permute-start.30) | collective-permute-done | bytes 917536 | tf_op jit(solution)/shard_map/ppermute | solution.py:20
  180.4 19.7 %collective-permute-done.31.rest_9_.rest_7_ = bf16[448,1024]{1,0:T(8,128)(2,1)} collective-permute-done((bf16[448,1024]{1,0:T(8,128)(2,1)}, bf16[448,1024]{1,0:T(8,128)(2,1)}, u32[]{:S(2)}, u32[]{:S(2)}) %collective-permute-start.31) | collective-permute-done | bytes 917536 | tf_op jit(solution)/shard_map/ppermute | solution.py:20
  200.1 19.2 %collective-permute-done.32.rest_10_.rest_8_ = bf16[448,1024]{1,0:T(8,128)(2,1)} collective-permute-done((bf16[448,1024]{1,0:T(8,128)(2,1)}, bf16[448,1024]{1,0:T(8,128)(2,1)}, u32[]{:S(2)}, u32[]{:S(2)}) %collective-permute-start.32) | collective-permute-done | bytes 917536 | tf_op jit(solution)/shard_map/ppermute | solution.py:20
  219.3 3.3 %project.9 = bf16[1,256,448]{2,1,0:T(8,128)(2,1)S(1)} custom-call(s32[1]{0:T(128)S(6)} %xor.39.turns, s32[5]{0:T(128)S(1)} %stack.64.place, bf16[256,1024]{1,0:T(8,128)(2,1)} %collective-permute-done.24.rest_2_.rest_0_, bf16[256,1]{1,0:T(8,128)(2,1)S(1)} %reshape.64.rest_3_.rest_1_, bf16[2,448,1024]{2,1,0:T(8,128)(2,1)S(1)} %bitcast.46, ...), custom_call_target="tpu_custom_call" | custom-call | flops 469762048 | bytes 2064384 | tf_op jit(solution)/shard_map/project/pallas_call | solution.py:428
  223.8 3.3 %project.8 = bf16[1,256,448]{2,1,0:T(8,128)(2,1)S(1)} custom-call(s32[1]{0:T(128)S(6)} %xor.38.turns, s32[5]{0:T(128)S(1)} %stack.64.place, bf16[256,1024]{1,0:T(8,128)(2,1)} %collective-permute-done.24.rest_2_.rest_0_, bf16[256,1]{1,0:T(8,128)(2,1)S(1)} %reshape.64.rest_3_.rest_1_, bf16[2,448,1024]{2,1,0:T(8,128)(2,1)S(1)} %bitcast.47, ...), custom_call_target="tpu_custom_call" | custom-call | flops 469762048 | bytes 2064384 | tf_op jit(solution)/shard_map/project/pallas_call | solution.py:428
  227.3 4.5 %project.5 = (bf16[2,256,448]{2,1,0:T(8,128)(2,1)S(1)}, bf16[2,256,448]{2,1,0:T(8,128)(2,1)S(1)}) custom-call(s32[2]{0:T(128)S(1)} %add_xor_fusion.turns, s32[5]{0:T(128)S(1)} %stack.64.place, bf16[256,1024]{1,0:T(8,128)(2,1)S(1)} %attend.1.rest_0_, bf16[256,1]{1,0:T(8,128)(2,1)S(1)} %reshape.63.rest_1_, ...), custom_call_target="tpu_custom_call" | custom-call | flops 1879048192 | bytes 4587520 | tf_op jit(solution)/shard_map/project/pallas_call | solution.py:428
  231.8 4.3 %collective-permute-done.35 = bf16[1,256,448]{2,1,0:T(8,128)(2,1)S(1)} collective-permute-done((bf16[1,256,448]{2,1,0:T(8,128)(2,1)S(1)}, bf16[1,256,448]{2,1,0:T(8,128)(2,1)S(1)}, u32[]{:S(2)}, u32[]{:S(2)}) %collective-permute-start.35) | collective-permute-done | bytes 229408 | tf_op jit(solution)/shard_map/ppermute | solution.py:20
  236.3 2.8 %project.6 = bf16[1,256,448]{2,1,0:T(8,128)(2,1)S(1)} custom-call(s32[1]{0:T(128)S(6)} %xor.38.turns, s32[5]{0:T(128)S(1)} %stack.64.place, bf16[256,1024]{1,0:T(8,128)(2,1)S(1)} %attend.1.rest_0_, bf16[256,1]{1,0:T(8,128)(2,1)S(1)} %reshape.63.rest_1_, bf16[2,448,1024]{2,1,0:T(8,128)(2,1)S(1)} %bitcast.49, ...), custom_call_target="tpu_custom_call" | custom-call | flops 469762048 | bytes 2064384 | tf_op jit(solution)/shard_map/project/pallas_call | solution.py:428
  239.6 2.8 %project.7 = bf16[1,256,448]{2,1,0:T(8,128)(2,1)S(1)} custom-call(s32[1]{0:T(128)S(6)} %xor.39.turns, s32[5]{0:T(128)S(1)} %stack.64.place, bf16[256,1024]{1,0:T(8,128)(2,1)S(1)} %attend.1.rest_0_, bf16[256,1]{1,0:T(8,128)(2,1)S(1)} %reshape.63.rest_1_, bf16[2,448,1024]{2,1,0:T(8,128)(2,1)S(1)} %bitcast.50, ...), custom_call_target="tpu_custom_call" | custom-call | flops 469762048 | bytes 2064384 | tf_op jit(solution)/shard_map/project/pallas_call | solution.py:428
  244.1 4.3 %collective-permute-done.33.rest_0_ = bf16[1,256,448]{2,1,0:T(8,128)(2,1)S(1)} collective-permute-done((bf16[1,256,448]{2,1,0:T(8,128)(2,1)S(1)}, bf16[1,256,448]{2,1,0:T(8,128)(2,1)S(1)}, u32[]{:S(2)}, u32[]{:S(2)}) %collective-permute-start.33) | collective-permute-done | bytes 229408 | tf_op jit(solution)/shard_map/ppermute | solution.py:20
  248.4 5.1 %collective-permute-done.34.rest_1_ = bf16[1,256,448]{2,1,0:T(8,128)(2,1)S(1)} collective-permute-done((bf16[1,256,448]{2,1,0:T(8,128)(2,1)S(1)}, bf16[1,256,448]{2,1,0:T(8,128)(2,1)S(1)}, u32[]{:S(2)}, u32[]{:S(2)}) %collective-permute-start.34) | collective-permute-done | bytes 229408 | tf_op jit(solution)/shard_map/ppermute | solution.py:20
  (140 shorter events, 43.9 us)
Async XLA Ops:
  2.3 56.6 %collective-permute-start.25 = (bf16[448,1024]{1,0:T(8,128)(2,1)}, bf16[448,1024]{1,0:T(8,128)(2,1)}, u32[]{:S(2)}, u32[]{:S(2)}) collective-permute-start(bf16[448,1024]{1,0:T(8,128)(2,1)} %dynamic-slice_bitcast_fusion), channel_id=1, source_target_pairs={{4,0},{0,4},{12,8},{8,12},{5,1},{1,5},{13,9},{9,13},{6,2},{2,6},{1... | collective-permute-start | bytes 2752520 | tf_op jit(solution)/shard_map/ppermute | solution.py:25
  5.4 62.2 %collective-permute-start.27 = (bf16[448,1024]{1,0:T(8,128)(2,1)}, bf16[448,1024]{1,0:T(8,128)(2,1)}, u32[]{:S(2)}, u32[]{:S(2)}) collective-permute-start(bf16[448,1024]{1,0:T(8,128)(2,1)} %dynamic-slice_bitcast_fusion), channel_id=1, source_target_pairs={{8,4},{4,8},{9,5},{5,9},{10,6},{6,10},{11,7},{7,11},{24,20},{20,24... | collective-permute-start | bytes 2752520 | tf_op jit(solution)/shard_map/ppermute | solution.py:25
  11.8 60.5 %collective-permute-start.2 = (bf16[2,448,1024]{2,1,0:T(8,128)(2,1)}, bf16[2,448,1024]{2,1,0:T(8,128)(2,1)}, u32[]{:S(2)}, u32[]{:S(2)}) collective-permute-start(bf16[2,448,1024]{2,1,0:T(8,128)(2,1)} %rest_4_.1), channel_id=1, source_target_pairs={{0,1},{1,0},{2,3},{3,2},{4,5},{5,4},{6,7},{7,6},{8,9},{9,8},{10,11... | collective-permute-start | bytes 5505032 | tf_op jit(solution)/shard_map/ppermute | solution.py:20
  11.8 22.6 %collective-permute-start.5 = (bf16[128,896]{1,0:T(8,128)(2,1)}, bf16[128,896]{1,0:T(8,128)(2,1)}, u32[]{:S(2)}, u32[]{:S(2)}) collective-permute-start(bf16[128,896]{1,0:T(8,128)(2,1)} %get-tuple-element.36), channel_id=1, source_target_pairs={{12,0},{8,4},{4,8},{0,12},{13,1},{9,5},{5,9},{1,13},{14,2},{10,6},... | collective-permute-start | bytes 688136 | tf_op jit(solution)/shard_map/ppermute | solution.py:25
  14.3 35.7 %collective-permute-start.7 = (bf16[128,896]{1,0:T(8,128)(2,1)}, bf16[128,896]{1,0:T(8,128)(2,1)}, u32[]{:S(2)}, u32[]{:S(2)}) collective-permute-start(bf16[128,896]{1,0:T(8,128)(2,1)} %get-tuple-element.39), channel_id=1, source_target_pairs={{8,0},{12,4},{0,8},{4,12},{9,1},{13,5},{1,9},{5,13},{10,2},{14,6},... | collective-permute-start | bytes 688136 | tf_op jit(solution)/shard_map/ppermute | solution.py:25
  34.4 24.4 %collective-permute-start = (bf16[2,448,256]{2,1,0:T(8,128)(2,1)S(1)}, bf16[2,448,256]{2,1,0:T(8,128)(2,1)S(1)}, u32[]{:S(2)}, u32[]{:S(2)}) collective-permute-start(bf16[2,448,256]{2,1,0:T(8,128)(2,1)S(1)} %constant_dynamic-slice_fusion.1.rest_0_), channel_id=1, source_target_pairs={{0,1},{1,0},{2,3},{3,2},{4,5},{5,4},{6,7},{7,6},{8,9},{9,8},{10,11... | collective-permute-start | bytes 1376264 | tf_op jit(solution)/shard_map/ppermute | solution.py:20
  59.0 28.0 %collective-permute-start.26 = (bf16[448,1024]{1,0:T(8,128)(2,1)}, bf16[448,1024]{1,0:T(8,128)(2,1)}, u32[]{:S(2)}, u32[]{:S(2)}) collective-permute-start(bf16[448,1024]{1,0:T(8,128)(2,1)} %collective-permute-done.25.rest_5_.rest_3_), channel_id=1, source_target_pairs={{8,4},{4,8},{9,5},{5,9},{10,6},{6,10},{11,7},{7,11},{24,20},{20,24... | collective-permute-start | bytes 2752520 | tf_op jit(solution)/shard_map/ppermute | solution.py:25
  63.0 8.6 %collective-permute-start.8 = (bf16[128,896]{1,0:T(8,128)(2,1)}, bf16[128,896]{1,0:T(8,128)(2,1)S(1)}, u32[]{:S(2)}, u32[]{:S(2)}) collective-permute-start(bf16[128,896]{1,0:T(8,128)(2,1)} %collective-permute-done.7.rest_8_), channel_id=1, source_target_pairs={{0,2},{2,0},{1,3},{3,1},{4,6},{6,4},{5,7},{7,5},{8,10},{10,8},{9,1... | collective-permute-start | bytes 688136 | tf_op jit(solution)/shard_map/ppermute | solution.py:20
  67.1 18.5 %collective-permute-start.4 = (bf16[128,896]{1,0:T(8,128)(2,1)}, bf16[128,896]{1,0:T(8,128)(2,1)S(1)}, u32[]{:S(2)}, u32[]{:S(2)}) collective-permute-start(bf16[128,896]{1,0:T(8,128)(2,1)} %collective-permute-done.3.rest_6_), channel_id=1, source_target_pairs={{0,2},{2,0},{1,3},{3,1},{4,6},{6,4},{5,7},{7,5},{8,10},{10,8},{9,1... | collective-permute-start | bytes 688136 | tf_op jit(solution)/shard_map/ppermute | solution.py:20
  67.6 75.6 %collective-permute-start.28 = (bf16[448,1024]{1,0:T(8,128)(2,1)}, bf16[448,1024]{1,0:T(8,128)(2,1)S(1)}, u32[]{:S(2)}, u32[]{:S(2)}) collective-permute-start(bf16[448,1024]{1,0:T(8,128)(2,1)} %collective-permute-done.27), channel_id=1, source_target_pairs={{4,0},{8,12},{5,1},{9,13},{6,2},{10,14},{7,3},{11,15},{20,16},{24,... | collective-permute-start | bytes 2752520 | tf_op jit(solution)/shard_map/ppermute | solution.py:25
  80.7 26.8 %collective-permute-start.9 = (bf16[256,1024]{1,0:T(8,128)(2,1)S(1)}, bf16[256,1024]{1,0:T(8,128)(2,1)S(1)}, u32[]{:S(2)}, u32[]{:S(2)}) collective-permute-start(bf16[256,1024]{1,0:T(8,128)(2,1)S(1)} %get-tuple-element.43), channel_id=1, source_target_pairs={{0,4},{12,8},{1,5},{13,9},{2,6},{14,10},{3,7},{15,11},{16,20},{28,... | collective-permute-start | bytes 1572872 | tf_op jit(solution)/shard_map/ppermute | solution.py:25
  83.0 23.5 %collective-permute-start.14 = (bf16[2,256,512]{2,1,0:T(8,128)(2,1)S(1)}, bf16[2,256,512]{2,1,0:T(8,128)(2,1)S(1)}, u32[]{:S(2)}, u32[]{:S(2)}) collective-permute-start(bf16[2,256,512]{2,1,0:T(8,128)(2,1)S(1)} %bitcast.51), channel_id=1, source_target_pairs={{0,4},{12,8},{1,5},{13,9},{2,6},{14,10},{3,7},{15,11},{16,20},{28,... | collective-permute-start | bytes 1572872 | tf_op jit(solution)/shard_map/ppermute | solution.py:25
  85.6 28.8 %collective-permute-start.12 = (bf16[256,1024]{1,0:T(8,128)(2,1)S(1)}, bf16[256,1024]{1,0:T(8,128)(2,1)S(1)}, u32[]{:S(2)}, u32[]{:S(2)}) collective-permute-start(bf16[256,1024]{1,0:T(8,128)(2,1)S(1)} %get-tuple-element.44), channel_id=1, source_target_pairs={{0,4},{12,8},{1,5},{13,9},{2,6},{14,10},{3,7},{15,11},{16,20},{28,... | collective-permute-start | bytes 1572872 | tf_op jit(solution)/shard_map/ppermute | solution.py:25
  86.9 61.2 %collective-permute-start.29 = (bf16[448,1024]{1,0:T(8,128)(2,1)}, bf16[448,1024]{1,0:T(8,128)(2,1)S(1)}, u32[]{:S(2)}, u32[]{:S(2)}) collective-permute-start(bf16[448,1024]{1,0:T(8,128)(2,1)} %collective-permute-done.26), channel_id=1, source_target_pairs={{4,0},{8,12},{5,1},{9,13},{6,2},{10,14},{7,3},{11,15},{20,16},{24,... | collective-permute-start | bytes 2752520 | tf_op jit(solution)/shard_map/ppermute | solution.py:25
  106.7 8.8 %collective-permute-start.15 = (bf16[2,256,512]{2,1,0:T(8,128)(2,1)S(1)}, bf16[2,256,512]{2,1,0:T(8,128)(2,1)S(1)}, u32[]{:S(2)}, u32[]{:S(2)}) collective-permute-start(bf16[2,256,512]{2,1,0:T(8,128)(2,1)S(1)} %fusion), channel_id=1, source_target_pairs={{8,4},{4,8},{9,5},{5,9},{10,6},{6,10},{11,7},{7,11},{24,20},{20,24... | collective-permute-start | bytes 1572872 | tf_op jit(solution)/shard_map/ppermute | solution.py:25
  107.7 18.4 %collective-permute-start.10 = (bf16[256,1024]{1,0:T(8,128)(2,1)S(1)}, bf16[256,1024]{1,0:T(8,128)(2,1)S(1)}, u32[]{:S(2)}, u32[]{:S(2)}) collective-permute-start(bf16[256,1024]{1,0:T(8,128)(2,1)S(1)} %fusion.2), channel_id=1, source_target_pairs={{8,4},{4,8},{9,5},{5,9},{10,6},{6,10},{11,7},{7,11},{24,20},{20,24... | collective-permute-start | bytes 1572872 | tf_op jit(solution)/shard_map/ppermute | solution.py:25
  114.5 35.3 %collective-permute-start.13 = (bf16[256,1024]{1,0:T(8,128)(2,1)S(1)}, bf16[256,1024]{1,0:T(8,128)(2,1)S(1)}, u32[]{:S(2)}, u32[]{:S(2)}) collective-permute-start(bf16[256,1024]{1,0:T(8,128)(2,1)S(1)} %fusion.1), channel_id=1, source_target_pairs={{8,4},{4,8},{9,5},{5,9},{10,6},{6,10},{11,7},{7,11},{24,20},{20,24... | collective-permute-start | bytes 1572872 | tf_op jit(solution)/shard_map/ppermute | solution.py:25
  115.5 27.5 %collective-permute-start.16 = (bf16[256,512]{1,0:T(8,128)(2,1)S(1)}, bf16[256,512]{1,0:T(8,128)(2,1)S(1)}, u32[]{:S(2)}, u32[]{:S(2)}) collective-permute-start(bf16[256,512]{1,0:T(8,128)(2,1)S(1)} %fusion.4), channel_id=1, source_target_pairs={{4,0},{0,4},{12,8},{8,12},{5,1},{1,5},{13,9},{9,13},{6,2},{2,6},{1... | collective-permute-start | bytes 786440 | tf_op jit(solution)/shard_map/ppermute | solution.py:25
  126.3 30.6 %collective-permute-start.11 = (bf16[256,1024]{1,0:T(8,128)(2,1)S(1)}, bf16[256,1024]{1,0:T(8,128)(2,1)S(1)}, u32[]{:S(2)}, u32[]{:S(2)}) collective-permute-start(bf16[256,1024]{1,0:T(8,128)(2,1)S(1)} %add_convert_fusion.2), channel_id=1, source_target_pairs={{4,0},{0,4},{12,8},{8,12},{5,1},{1,5},{13,9},{9,13},{6,2},{2,6},{1... | collective-permute-start | bytes 1572872 | tf_op jit(solution)/shard_map/ppermute | solution.py:25
  143.2 12.7 %collective-permute-start.17 = (bf16[256,512]{1,0:T(8,128)(2,1)S(1)}, bf16[256,512]{1,0:T(8,128)(2,1)S(1)}, u32[]{:S(2)}, u32[]{:S(2)}) collective-permute-start(bf16[256,512]{1,0:T(8,128)(2,1)S(1)} %fusion.3.rest_0_), channel_id=1, source_target_pairs={{4,0},{0,4},{12,8},{8,12},{5,1},{1,5},{13,9},{9,13},{6,2},{2,6},{1... | collective-permute-start | bytes 786440 | tf_op jit(solution)/shard_map/ppermute | solution.py:25
  144.3 14.1 %collective-permute-start.18 = (bf16[256,512]{1,0:T(8,128)(2,1)S(1)}, bf16[256,512]{1,0:T(8,128)(2,1)S(1)}, u32[]{:S(2)}, u32[]{:S(2)}) collective-permute-start(bf16[256,512]{1,0:T(8,128)(2,1)S(1)} %fusion.3.rest_0_), channel_id=1, source_target_pairs={{8,0},{12,4},{0,8},{4,12},{9,1},{13,5},{1,9},{5,13},{10,2},{14,6},... | collective-permute-start | bytes 786440 | tf_op jit(solution)/shard_map/ppermute | solution.py:25
  148.2 12.7 %collective-permute-start.19 = (bf16[256,512]{1,0:T(8,128)(2,1)S(1)}, bf16[256,512]{1,0:T(8,128)(2,1)S(1)}, u32[]{:S(2)}, u32[]{:S(2)}) collective-permute-start(bf16[256,512]{1,0:T(8,128)(2,1)S(1)} %fusion.3.rest_0_), channel_id=1, source_target_pairs={{12,0},{8,4},{4,8},{0,12},{13,1},{9,5},{5,9},{1,13},{14,2},{10,6},... | collective-permute-start | bytes 786440 | tf_op jit(solution)/shard_map/ppermute | solution.py:25
  149.8 12.6 %collective-permute-start.20 = (bf16[256,512]{1,0:T(8,128)(2,1)S(1)}, bf16[256,512]{1,0:T(8,128)(2,1)S(1)}, u32[]{:S(2)}, u32[]{:S(2)}) collective-permute-start(bf16[256,512]{1,0:T(8,128)(2,1)S(1)} %fusion.3.rest_0_), channel_id=1, source_target_pairs={{0,1},{1,0},{2,3},{3,2},{4,5},{5,4},{6,7},{7,6},{8,9},{9,8},{10,11... | collective-permute-start | bytes 786440 | tf_op jit(solution)/shard_map/ppermute | solution.py:20
  156.9 23.5 %collective-permute-start.30 = (bf16[448,1024]{1,0:T(8,128)(2,1)}, bf16[448,1024]{1,0:T(8,128)(2,1)}, u32[]{:S(2)}, u32[]{:S(2)}) collective-permute-start(bf16[448,1024]{1,0:T(8,128)(2,1)} %collective-permute-done.25.rest_5_.rest_3_), channel_id=1, source_target_pairs={{0,16},{16,0},{1,17},{17,1},{2,18},{18,2},{3,19},{19,3},{4,20},{20... | collective-permute-start | bytes 2752520 | tf_op jit(solution)/shard_map/ppermute | solution.py:20
  158.4 41.7 %collective-permute-start.31 = (bf16[448,1024]{1,0:T(8,128)(2,1)}, bf16[448,1024]{1,0:T(8,128)(2,1)}, u32[]{:S(2)}, u32[]{:S(2)}) collective-permute-start(bf16[448,1024]{1,0:T(8,128)(2,1)} %broadcast_select_fusion.1.rest_6_.rest_4_), channel_id=1, source_target_pairs={{0,16},{16,0},{1,17},{17,1},{2,18},{18,2},{3,19},{19,3},{4,20},{20... | collective-permute-start | bytes 2752520 | tf_op jit(solution)/shard_map/ppermute | solution.py:20
  160.9 58.4 %collective-permute-start.32 = (bf16[448,1024]{1,0:T(8,128)(2,1)}, bf16[448,1024]{1,0:T(8,128)(2,1)}, u32[]{:S(2)}, u32[]{:S(2)}) collective-permute-start(bf16[448,1024]{1,0:T(8,128)(2,1)} %broadcast_select_fusion.rest_7_.rest_5_), channel_id=1, source_target_pairs={{0,16},{16,0},{1,17},{17,1},{2,18},{18,2},{3,19},{19,3},{4,20},{20... | collective-permute-start | bytes 2752520 | tf_op jit(solution)/shard_map/ppermute | solution.py:20
  168.1 51.2 %collective-permute-start.24 = (bf16[256,1024]{1,0:T(8,128)(2,1)S(1)}, bf16[256,1024]{1,0:T(8,128)(2,1)}, u32[]{:S(2)}, u32[]{:S(2)}) collective-permute-start(bf16[256,1024]{1,0:T(8,128)(2,1)S(1)} %attend.1.rest_0_), channel_id=1, source_target_pairs={{0,1},{1,0},{2,3},{3,2},{4,5},{5,4},{6,7},{7,6},{8,9},{9,8},{10,11... | collective-permute-start | bytes 1572872 | tf_op jit(solution)/shard_map/ppermute | solution.py:20
  222.6 9.2 %collective-permute-start.36 = (bf16[1,256,448]{2,1,0:T(8,128)(2,1)S(1)}, bf16[1,256,448]{2,1,0:T(8,128)(2,1)S(1)}, u32[]{:S(2)}, u32[]{:S(2)}) collective-permute-start(bf16[1,256,448]{2,1,0:T(8,128)(2,1)S(1)} %project.9), channel_id=1, source_target_pairs={{0,2},{2,0},{1,3},{3,1},{4,6},{6,4},{5,7},{7,5},{8,10},{10,8},{9,1... | collective-permute-start | bytes 688136 | tf_op jit(solution)/shard_map/ppermute | solution.py:20
  227.1 9.0 %collective-permute-start.35 = (bf16[1,256,448]{2,1,0:T(8,128)(2,1)S(1)}, bf16[1,256,448]{2,1,0:T(8,128)(2,1)S(1)}, u32[]{:S(2)}, u32[]{:S(2)}) collective-permute-start(bf16[1,256,448]{2,1,0:T(8,128)(2,1)S(1)} %project.8), channel_id=1, source_target_pairs={{0,2},{2,0},{1,3},{3,1},{4,6},{6,4},{5,7},{7,5},{8,10},{10,8},{9,1... | collective-permute-start | bytes 688136 | tf_op jit(solution)/shard_map/ppermute | solution.py:20
  236.3 17.2 %collective-permute-start.37 = (bf16[2,256,448]{2,1,0:T(8,128)(2,1)S(1)}, bf16[2,256,448]{2,1,0:T(8,128)(2,1)S(1)}, u32[]{:S(2)}, u32[]{:S(2)}) collective-permute-start(bf16[2,256,448]{2,1,0:T(8,128)(2,1)S(1)} %add_convert_fusion), channel_id=1, source_target_pairs={{0,1},{1,0},{2,3},{3,2},{4,5},{5,4},{6,7},{7,6},{8,9},{9,8},{10,11... | collective-permute-start | bytes 1376264 | tf_op jit(solution)/shard_map/ppermute | solution.py:20
  239.1 9.2 %collective-permute-start.33 = (bf16[1,256,448]{2,1,0:T(8,128)(2,1)S(1)}, bf16[1,256,448]{2,1,0:T(8,128)(2,1)S(1)}, u32[]{:S(2)}, u32[]{:S(2)}) collective-permute-start(bf16[1,256,448]{2,1,0:T(8,128)(2,1)S(1)} %project.6), channel_id=1, source_target_pairs={{0,2},{2,0},{1,3},{3,1},{4,6},{6,4},{5,7},{7,5},{8,10},{10,8},{9,1... | collective-permute-start | bytes 688136 | tf_op jit(solution)/shard_map/ppermute | solution.py:20
  242.3 11.2 %collective-permute-start.34 = (bf16[1,256,448]{2,1,0:T(8,128)(2,1)S(1)}, bf16[1,256,448]{2,1,0:T(8,128)(2,1)S(1)}, u32[]{:S(2)}, u32[]{:S(2)}) collective-permute-start(bf16[1,256,448]{2,1,0:T(8,128)(2,1)S(1)} %project.7), channel_id=1, source_target_pairs={{0,2},{2,0},{1,3},{3,1},{4,6},{6,4},{5,7},{7,5},{8,10},{10,8},{9,1... | collective-permute-start | bytes 688136 | tf_op jit(solution)/shard_map/ppermute | solution.py:20
  (28 other events, 369.7 us)

commit v9 on v8

--- a/solution.py
+++ b/solution.py
@@ -43,10 +43,16 @@
 
 
 def norm_kernel(place, modality, tokens_ref, gain_ref, own_ref, *rest):
-    send_refs, scratch = rest[:-1], rest[-1]
+    send_refs, (scratch, arrived) = rest[:-2], rest[-2:]
     width = own_ref.shape[1]
-    for at in range(0, tokens_ref.shape[0], RUN):
-        values = tokens_ref[at : at + RUN].astype(jnp.float32)
+    copies = []
+    for i, at in enumerate(range(0, tokens_ref.shape[0], RUN)):
+        rows = pl.ds(at, RUN)
+        copies.append(pltpu.make_async_copy(tokens_ref.at[rows], scratch.at[rows], arrived.at[i]))
+        copies[-1].start()
+    for i, at in enumerate(range(0, tokens_ref.shape[0], RUN)):
+        copies[i].wait()
+        values = scratch[at : at + RUN].astype(jnp.float32)
         factor = lax.rsqrt(jnp.mean(values * values, axis=1, keepdims=True) + EPS)
         gain = jnp.where(modality[place[4] + at] == 1, gain_ref[1:2, :], gain_ref[0:1, :])
         scratch[at : at + RUN] = (values * factor * gain).astype(jnp.bfloat16)
@@ -79,15 +85,18 @@
     return pl.pallas_call(
         norm_kernel,
         out_shape=shapes,
-        in_specs=[SMEM, SMEM, VMEM, VMEM],
+        in_specs=[SMEM, SMEM, HBM, VMEM],
         out_specs=[VMEM] * n,
-        scratch_shapes=[pltpu.VMEM((length, depth), jnp.bfloat16)],
+        scratch_shapes=[
+            pltpu.VMEM((length, depth), jnp.bfloat16),
+            pltpu.SemaphoreType.DMA((length // RUN,)),
+        ],
         cost_estimate=pl.CostEstimate(
             flops=6 * length * depth, bytes_accessed=4 * length * depth, transcendentals=length
         ),
         compiler_params=pltpu.CompilerParams(vmem_limit_bytes=12 * 1024 * 1024),
         name="norm",
-    )(place, modality, tokens, norm_gain)
+    )(place, modality, in_hbm(tokens), norm_gain)
 
 
 def partial_kernel(counts, narrow, place, modality, begins, *rest):
@@ -216,7 +225,7 @@
     return sums[0].astype(jnp.bfloat16)
 
 
-def along_four(parts, three, two):
+def along_four(parts, three, two, whole):
     wide = [p.astype(jnp.float32) for p in parts]
 
     def hop(value, bit, among):
@@ -236,6 +245,8 @@
         across = hop(send, 3, (1, 2))
         own = hop(plus(wide[3], after(close, send)), 3, (1, 2))
     last = hop(plus(wide[1], across), 1, None)
+    if not whole:
+        return last, own
     return (wide[0] + last.astype(jnp.float32) + own.astype(jnp.float32)).astype(jnp.bfloat16)
 
 
@@ -275,12 +286,13 @@
     return low, jnp.where(own_mod == 1, end, own_pos)
 
 
-def attention_kernel(starts, limits, q_ref, span_ref, *rest):
-    sources, (o_ref, kv_ref, queries, bounds, top, total, acc, arrived) = rest[:-8], rest[-8:]
+def attention_kernel(terms, starts, limits, span_ref, *rest):
+    q_refs, sources = rest[:terms], rest[terms:-8]
+    (o_ref, kv_ref, queries, bounds, top, total, acc, arrived) = rest[-8:]
     count, size, _ = kv_ref.shape
     for number, source in enumerate(sources):
         pltpu.make_async_copy(source, kv_ref.at[number], arrived.at[number]).start()
-    rows = q_ref.shape[0]
+    rows = o_ref.shape[0]
     kv_local, many = queries.shape[0], queries.shape[1]
     repeat = many // rows
     scale = math.log2(math.e) / math.sqrt(HEAD_DIM)
@@ -289,7 +301,11 @@
     acc[...] = jnp.zeros_like(acc)
     for head in range(kv_local * repeat):
         g, r = head // repeat, head % repeat
-        queries[g, r * rows : (r + 1) * rows] = q_ref[:, head * HEAD_DIM : (head + 1) * HEAD_DIM]
+        cols = slice(head * HEAD_DIM, (head + 1) * HEAD_DIM)
+        query = q_refs[0][0, :, cols].astype(jnp.float32)
+        for term in q_refs[1:]:
+            query = query + term[:, cols].astype(jnp.float32)
+        queries[g, r * rows : (r + 1) * rows] = query.astype(jnp.bfloat16)
     columns = span_ref[...].T
     for r in range(repeat):
         bounds[r * rows : (r + 1) * rows] = columns
@@ -342,15 +358,15 @@
 
 
 def attend(query, kv, starts, limits, span):
-    rows, width = query.shape
+    rows, width = query[0].shape[1:]
     heads = width // HEAD_DIM
     count, (size, kv_cols) = len(kv), kv[0].shape
     kv_local = kv_cols // (2 * HEAD_DIM)
     many = rows * heads // kv_local
     return pl.pallas_call(
-        attention_kernel,
+        functools.partial(attention_kernel, len(query)),
         out_shape=jax.ShapeDtypeStruct((rows, width), jnp.bfloat16),
-        in_specs=[SMEM, SMEM, VMEM, VMEM] + [HBM] * (count // 2 + 1) + [VMEM] * (count // 2 - 1),
+        in_specs=[SMEM, SMEM, VMEM] + [VMEM] * len(query) + [HBM] * (count // 2 + 1) + [VMEM] * (count // 2 - 1),
         out_specs=VMEM,
         scratch_shapes=[
             pltpu.VMEM((count, size, kv_cols), jnp.bfloat16),
@@ -371,8 +387,8 @@
     )(
         starts,
         limits,
-        query,
         span,
+        *query,
         *[in_hbm(block) for block in kv[: count // 2 + 1]],
         *kv[count // 2 + 1 :],
     )
@@ -501,15 +517,16 @@
         kv_early, q_early, kv_ends, q_three, q_two = parts_of([3, 2], True)
         kv_late, q_late = parts_of([1, 0], False)
         kv_early, q_early = after((kv_early, q_early), kv_late, q_late)
-        kv = along_four([kv_late[1], kv_late[0], kv_early[1], kv_early[0]], kv_ends, None)
-        query = along_four([q_late[1], q_late[0], q_early[1], q_early[0]], q_three, q_two)
+        kv = along_four([kv_late[1], kv_late[0], kv_early[1], kv_early[0]], kv_ends, None, True)
+        parts = [q_late[1], q_late[0], q_early[1], q_early[0]]
+        query = (q_late[1:], *along_four(parts, q_three, q_two, False))
     else:
         kv_parts, q_parts = [], []
         for d in range(n):
             kv_part, q_part = parts_of([d], False)
             kv_parts.append(kv_part[0])
             q_parts.append(q_part[0])
-        kv, query = halving(kv_parts), halving(q_parts)
+        kv, query = halving(kv_parts), (halving(q_parts)[None],)
 
     same = [kv]
     for d in range(1, n):

time: 256 us -> 244 us (0.953)
  starting transfers between devices: 67.4 us -> 50.2 us
  local copies, waits for them, and re-layouts: 10.4 us -> 18.3 us
  waiting for transfers between devices: 128 us -> 123 us
    ppermute x19, starting transfers between devices: 54.2 us -> 37.4 us  [cross(): return lax.ppermute(x, axis, [(i ^ bit, i) for i in among or range(size)])]
    unnamed x44 -> x50, local copies, waits for them, and re-layouts: 3.82 us -> 11.5 us
    ppermute x19, waiting for transfers between devices: 59.6 us -> 55.2 us  [cross(): return lax.ppermute(x, axis, [(i ^ bit, i) for i in among or range(size)])]
  transfers between devices with their start and end apart: 38 -> 38, of which waited for: 17 -> 15; matrix products, arithmetic and copies ran while one was open for 5% -> 6% of each run, Pallas kernels for 13% -> 13%
where the time goes in v9:
time: 244 us; the launch traced here: 243 us
  waiting for transfers between devices  123 us (50%)
  starting transfers between devices  50.2 us (21%)
  Pallas kernels  40.7 us (17%)
  local copies, waits for them, and re-layouts  18.3 us (8%)
  other arithmetic  8.49 us (3%)
  between operations  2.48 us (1%)
    ppermute x19, waiting for transfers between devices, swap(): return lax.ppermute(x, axis, [(0, 1), (1, 0)])  67.6 us
    ppermute x19, waiting for transfers between devices, cross(): return lax.ppermute(x, axis, [(i ^ bit, i) for i in among or range(size)])  55.2 us
    ppermute x19, starting transfers between devices, cross(): return lax.ppermute(x, axis, [(i ^ bit, i) for i in among or range(size)])  37.4 us
    pallas_call x5, Pallas kernels, project(): pl.pallas_call(functools.partial(project_kernel, (len(weights) + 1) // 2,...  16.6 us
    pallas_call x2, Pallas kernels, partial(): pl.pallas_call(functools.partial(partial_kernel, counts, narrow), out_sha...  14.8 us
    ppermute x19, starting transfers between devices, swap(): return lax.ppermute(x, axis, [(0, 1), (1, 0)])  12.8 us
    unnamed x50, local copies, waits for them, and re-layouts  11.5 us
  transfers between devices with their start and end apart: 38, of which 15 were waited for; matrix products, arithmetic and copies ran while one was open for 6% of the time, Pallas kernels for 13%

profile of v9, /device:TPU:0, one launch (start us, length us, event | category | flops | bytes accessed | tf_op | source)
XLA Modules:
  0.0 243.0 jit_solution(3560926585662315265)
XLA Ops:
  1.7 3.4 %norm.1 = (bf16[256,896]{1,0:T(8,128)(2,1)S(1)}, bf16[128,896]{1,0:T(8,128)(2,1)S(1)}, bf16[128,896]{1,0:T(8,128)(2,1)S(1)}, bf16[128,896]{1,0:T(8,128)(2,1)}) custom-call(s32[5]{0:T(128)S(1)} %stack.64.place, s32[2048]{0:T(1024)S(1)} %copy-done.3, bf16[256,3584]{1,0:T(8,128)(2,1)} %tokens_ref.1, f32[2,3584]{1,0:T(2,128)S(1)} %copy-done.5), custom_call_target="tpu_custom_call" | custom-call | flops 5505024 | bytes 3670016 | tf_op jit(solution)/shard_map/norm/pallas_call | solution.py:85
  5.9 5.1 %collective-permute-start.5 = (bf16[128,896]{1,0:T(8,128)(2,1)}, bf16[128,896]{1,0:T(8,128)(2,1)}, u32[]{:S(2)}, u32[]{:S(2)}) collective-permute-start(bf16[128,896]{1,0:T(8,128)(2,1)} %get-tuple-element.36), channel_id=1, source_target_pairs={{12,0},{8,4},{4,8},{0,12},{13,1},{9,5},{5,9},{1,13},{14,2},{10,6},... | collective-permute-start | bytes 688136 | tf_op jit(solution)/shard_map/ppermute | solution.py:25
  20.8 11.0 %collective-permute-done.7.rest_8_ = bf16[128,896]{1,0:T(8,128)(2,1)} collective-permute-done((bf16[128,896]{1,0:T(8,128)(2,1)S(1)}, bf16[128,896]{1,0:T(8,128)(2,1)}, u32[]{:S(2)}, u32[]{:S(2)}) %collective-permute-start.7) | collective-permute-done | bytes 229408 | tf_op jit(solution)/shard_map/ppermute | solution.py:25
  33.9 1.8 constant_dynamic-slice_fusion.1.rest_0_
  35.8 4.2 %collective-permute-done.6.rest_7_ = bf16[128,896]{1,0:T(8,128)(2,1)S(1)} collective-permute-done((bf16[128,896]{1,0:T(8,128)(2,1)}, bf16[128,896]{1,0:T(8,128)(2,1)S(1)}, u32[]{:S(2)}, u32[]{:S(2)}) %collective-permute-start.6) | collective-permute-done | bytes 229408 | tf_op jit(solution)/shard_map/ppermute | solution.py:20
  40.7 5.7 %collective-permute-done.25.rest_5_.rest_3_ = bf16[448,1024]{1,0:T(8,128)(2,1)} collective-permute-done((bf16[448,1024]{1,0:T(8,128)(2,1)}, bf16[448,1024]{1,0:T(8,128)(2,1)}, u32[]{:S(2)}, u32[]{:S(2)}) %collective-permute-start.25) | collective-permute-done | bytes 917536 | tf_op jit(solution)/shard_map/ppermute | solution.py:25
  49.6 2.6 %pad_add_fusion.limits = s32[4]{0:T(128)S(1)} fusion(s32[1]{0:T(128)} %get-tuple-element.59, s32[1]{0:T(128)} %get-tuple-element.56, s32[1]{0:T(128)} %get-tuple-element.60, s32[1]{0:T(128)} %get-tuple-element.55), kind=kLoop, calls=%fused_computation.33 | loop fusion | flops 12 | bytes 32 | tf_op jit(solution)/shard_map/stack | solution.py:504
  54.2 2.6 %collective-permute-done.8.rest_9_ = bf16[128,896]{1,0:T(8,128)(2,1)S(1)} collective-permute-done((bf16[128,896]{1,0:T(8,128)(2,1)}, bf16[128,896]{1,0:T(8,128)(2,1)S(1)}, u32[]{:S(2)}, u32[]{:S(2)}) %collective-permute-start.8) | collective-permute-done | bytes 229408 | tf_op jit(solution)/shard_map/ppermute | solution.py:20
  59.4 7.5 %partial.3 = (f32[512,512]{1,0:T(8,128)}, f32[512,1024]{1,0:T(8,128)}, bf16[512,512]{1,0:T(8,128)(2,1)S(1)}, bf16[256,1024]{1,0:T(8,128)(2,1)S(1)}, bf16[256,1024]{1,0:T(8,128)(2,1)S(1)}) custom-call(s32[5]{0:T(128)S(1)} %stack.64.place, s32[2048]{0:T(1024)S(1)} %copy-done.4, s32[2]{0:T(128)S(1)} %pad_add_fusion.2.begins, ...), custom_call_target="tpu_custom_call" | custom-call | flops 2818572288 | bytes 8650752 | tf_op jit(solution)/shard_map/partial/pallas_call | solution.py:187
  66.8 4.5 %collective-permute-start.14 = (bf16[2,256,512]{2,1,0:T(8,128)(2,1)S(1)}, bf16[2,256,512]{2,1,0:T(8,128)(2,1)S(1)}, u32[]{:S(2)}, u32[]{:S(2)}) collective-permute-start(bf16[2,256,512]{2,1,0:T(8,128)(2,1)S(1)} %bitcast.53), channel_id=1, source_target_pairs={{0,4},{12,8},{1,5},{13,9},{2,6},{14,10},{3,7},{15,11},{16,20},{28,... | collective-permute-start | bytes 1572872 | tf_op jit(solution)/shard_map/ppermute | solution.py:25
  76.6 7.3 %partial.2 = (f32[512,512]{1,0:T(8,128)}, f32[512,1024]{1,0:T(8,128)}) custom-call(s32[5]{0:T(128)S(1)} %stack.64.place, s32[2048]{0:T(1024)S(1)} %copy-done.4, s32[2]{0:T(128)S(1)} %pad_add_fusion.1.begins, bf16[2,448,256]{2,1,0:T(8,128)(2,1)} %constant_dynamic-slice_fusion.1.rest_0_, bf16[2,448,256]{2,1,0:T(8,128)(2,1)} %collective-permute-done.rest_1_, ...), custom_call_target="tpu_custom_call" | custom-call | flops 2818572288 | bytes 8650752 | tf_op jit(solution)/shard_map/partial/pallas_call | solution.py:187
  84.9 9.9 %collective-permute-done.9 = bf16[256,1024]{1,0:T(8,128)(2,1)S(1)} collective-permute-done((bf16[256,1024]{1,0:T(8,128)(2,1)S(1)}, bf16[256,1024]{1,0:T(8,128)(2,1)S(1)}, u32[]{:S(2)}, u32[]{:S(2)}) %collective-permute-start.9) | collective-permute-done | bytes 524320 | tf_op jit(solution)/shard_map/ppermute | solution.py:25
  95.8 7.1 %collective-permute-done.12 = bf16[256,1024]{1,0:T(8,128)(2,1)S(1)} collective-permute-done((bf16[256,1024]{1,0:T(8,128)(2,1)S(1)}, bf16[256,1024]{1,0:T(8,128)(2,1)S(1)}, u32[]{:S(2)}, u32[]{:S(2)}) %collective-permute-start.12) | collective-permute-done | bytes 524320 | tf_op jit(solution)/shard_map/ppermute | solution.py:25
  104.1 5.3 %collective-permute-start.16 = (bf16[256,512]{1,0:T(8,128)(2,1)S(1)}, bf16[256,512]{1,0:T(8,128)(2,1)S(1)}, u32[]{:S(2)}, u32[]{:S(2)}) collective-permute-start(bf16[256,512]{1,0:T(8,128)(2,1)S(1)} %fusion.4), channel_id=1, source_target_pairs={{4,0},{0,4},{12,8},{8,12},{5,1},{1,5},{13,9},{9,13},{6,2},{2,6},{1... | collective-permute-start | bytes 786440 | tf_op jit(solution)/shard_map/ppermute | solution.py:25
  110.6 5.0 %collective-permute-start.11 = (bf16[256,1024]{1,0:T(8,128)(2,1)S(1)}, bf16[256,1024]{1,0:T(8,128)(2,1)S(1)}, u32[]{:S(2)}, u32[]{:S(2)}) collective-permute-start(bf16[256,1024]{1,0:T(8,128)(2,1)S(1)} %get-tuple-element.51), channel_id=1, source_target_pairs={{4,0},{0,4},{12,8},{8,12},{5,1},{1,5},{13,9},{9,13},{6,2},{2,6},{1... | collective-permute-start | bytes 1572872 | tf_op jit(solution)/shard_map/ppermute | solution.py:25
  116.7 2.1 collective-permute-start.17
  118.8 2.4 %collective-permute-start.19 = (bf16[256,512]{1,0:T(8,128)(2,1)S(1)}, bf16[256,512]{1,0:T(8,128)(2,1)}, u32[]{:S(2)}, u32[]{:S(2)}) collective-permute-start(bf16[256,512]{1,0:T(8,128)(2,1)S(1)} %fusion.3.rest_3_), channel_id=1, source_target_pairs={{12,0},{8,4},{4,8},{0,12},{13,1},{9,5},{5,9},{1,13},{14,2},{10,6},... | collective-permute-start | bytes 786440 | tf_op jit(solution)/shard_map/ppermute | solution.py:25
  122.3 16.0 %collective-permute-done.17.rest_4_ = bf16[256,512]{1,0:T(8,128)(2,1)S(1)} collective-permute-done((bf16[256,512]{1,0:T(8,128)(2,1)S(1)}, bf16[256,512]{1,0:T(8,128)(2,1)S(1)}, u32[]{:S(2)}, u32[]{:S(2)}) %collective-permute-start.17) | collective-permute-done | bytes 262176 | tf_op jit(solution)/shard_map/ppermute | solution.py:25
  138.8 4.6 %collective-permute-done.19.rest_6_ = bf16[256,512]{1,0:T(8,128)(2,1)} collective-permute-done((bf16[256,512]{1,0:T(8,128)(2,1)S(1)}, bf16[256,512]{1,0:T(8,128)(2,1)}, u32[]{:S(2)}, u32[]{:S(2)}) %collective-permute-start.19) | collective-permute-done | bytes 262176 | tf_op jit(solution)/shard_map/ppermute | solution.py:25
  154.1 4.2 %attend.1.rest_0_ = bf16[256,1024]{1,0:T(8,128)(2,1)S(1)} custom-call(s32[8]{0:T(128)S(1)} %stack.72.starts, s32[4]{0:T(128)S(1)} %pad_add_fusion.limits, s32[8,256]{1,0:T(8,128)S(1)} %add_add_fusion.span_ref, f32[1,256,1024]{2,1,0:T(8,128)S(1)} %copy-done.2, bf16[256,1024]{1,0:T(8,128)(2,1)S(1)} %copy-done.9, bf16[256,1024]{1,0:T(8,128)(2,1)S(1)} %copy-done.7, ...), custom_call_target="tpu_custom_call" | custom-call | flops 2147483648 | bytes 3145728 | tf_op jit(solution)/shard_map/attend/pallas_call | solution.py:366
  160.1 8.1 %collective-permute-done.30.rest_8_.rest_6_ = bf16[448,1024]{1,0:T(8,128)(2,1)} collective-permute-done((bf16[448,1024]{1,0:T(8,128)(2,1)}, bf16[448,1024]{1,0:T(8,128)(2,1)}, u32[]{:S(2)}, u32[]{:S(2)}) %collective-permute-start.30) | collective-permute-done | bytes 917536 | tf_op jit(solution)/shard_map/ppermute | solution.py:20
  168.1 19.7 %collective-permute-done.31.rest_9_.rest_7_ = bf16[448,1024]{1,0:T(8,128)(2,1)} collective-permute-done((bf16[448,1024]{1,0:T(8,128)(2,1)}, bf16[448,1024]{1,0:T(8,128)(2,1)}, u32[]{:S(2)}, u32[]{:S(2)}) %collective-permute-start.31) | collective-permute-done | bytes 917536 | tf_op jit(solution)/shard_map/ppermute | solution.py:20
  187.8 19.2 %collective-permute-done.32.rest_10_.rest_8_ = bf16[448,1024]{1,0:T(8,128)(2,1)} collective-permute-done((bf16[448,1024]{1,0:T(8,128)(2,1)}, bf16[448,1024]{1,0:T(8,128)(2,1)}, u32[]{:S(2)}, u32[]{:S(2)}) %collective-permute-start.32) | collective-permute-done | bytes 917536 | tf_op jit(solution)/shard_map/ppermute | solution.py:20
  207.0 3.3 %project.8 = bf16[1,256,448]{2,1,0:T(8,128)(2,1)S(1)} custom-call(s32[1]{0:T(128)S(6)} %xor.38.turns, s32[5]{0:T(128)S(1)} %stack.64.place, bf16[256,1024]{1,0:T(8,128)(2,1)} %collective-permute-done.24.rest_2_.rest_0_, bf16[256,1]{1,0:T(8,128)(2,1)S(1)} %reshape.63.rest_3_.rest_1_, bf16[2,448,1024]{2,1,0:T(8,128)(2,1)S(1)} %bitcast.48, ...), custom_call_target="tpu_custom_call" | custom-call | flops 469762048 | bytes 2064384 | tf_op jit(solution)/shard_map/project/pallas_call | solution.py:444
  210.6 3.3 %project.9 = bf16[1,256,448]{2,1,0:T(8,128)(2,1)S(1)} custom-call(s32[1]{0:T(128)S(6)} %xor.39.turns, s32[5]{0:T(128)S(1)} %stack.64.place, bf16[256,1024]{1,0:T(8,128)(2,1)} %collective-permute-done.24.rest_2_.rest_0_, bf16[256,1]{1,0:T(8,128)(2,1)S(1)} %reshape.63.rest_3_.rest_1_, bf16[2,448,1024]{2,1,0:T(8,128)(2,1)S(1)} %bitcast.49, ...), custom_call_target="tpu_custom_call" | custom-call | flops 469762048 | bytes 2064384 | tf_op jit(solution)/shard_map/project/pallas_call | solution.py:444
  213.9 1.8 collective-permute-start.36
  215.8 4.5 %project.5 = (bf16[2,256,448]{2,1,0:T(8,128)(2,1)S(1)}, bf16[2,256,448]{2,1,0:T(8,128)(2,1)S(1)}) custom-call(s32[2]{0:T(128)S(1)} %add_xor_fusion.turns, s32[5]{0:T(128)S(1)} %stack.64.place, bf16[256,1024]{1,0:T(8,128)(2,1)S(1)} %attend.1.rest_0_, bf16[256,1]{1,0:T(8,128)(2,1)S(1)} %reshape.62.rest_1_, ...), custom_call_target="tpu_custom_call" | custom-call | flops 1879048192 | bytes 4587520 | tf_op jit(solution)/shard_map/project/pallas_call | solution.py:444
  220.3 3.5 %collective-permute-done.36 = bf16[1,256,448]{2,1,0:T(8,128)(2,1)S(1)} collective-permute-done((bf16[1,256,448]{2,1,0:T(8,128)(2,1)S(1)}, bf16[1,256,448]{2,1,0:T(8,128)(2,1)S(1)}, u32[]{:S(2)}, u32[]{:S(2)}) %collective-permute-start.36) | collective-permute-done | bytes 229408 | tf_op jit(solution)/shard_map/ppermute | solution.py:20
  224.1 2.8 %project.7 = bf16[1,256,448]{2,1,0:T(8,128)(2,1)S(1)} custom-call(s32[1]{0:T(128)S(6)} %xor.39.turns, s32[5]{0:T(128)S(1)} %stack.64.place, bf16[256,1024]{1,0:T(8,128)(2,1)S(1)} %attend.1.rest_0_, bf16[256,1]{1,0:T(8,128)(2,1)S(1)} %reshape.62.rest_1_, bf16[2,448,1024]{2,1,0:T(8,128)(2,1)S(1)} %bitcast.51, ...), custom_call_target="tpu_custom_call" | custom-call | flops 469762048 | bytes 2064384 | tf_op jit(solution)/shard_map/project/pallas_call | solution.py:444
  227.2 2.8 %project.6 = bf16[1,256,448]{2,1,0:T(8,128)(2,1)S(1)} custom-call(s32[1]{0:T(128)S(6)} %xor.38.turns, s32[5]{0:T(128)S(1)} %stack.64.place, bf16[256,1024]{1,0:T(8,128)(2,1)S(1)} %attend.1.rest_0_, bf16[256,1]{1,0:T(8,128)(2,1)S(1)} %reshape.62.rest_1_, bf16[2,448,1024]{2,1,0:T(8,128)(2,1)S(1)} %bitcast.52, ...), custom_call_target="tpu_custom_call" | custom-call | flops 469762048 | bytes 2064384 | tf_op jit(solution)/shard_map/project/pallas_call | solution.py:444
  230.9 5.2 %collective-permute-done.34.rest_1_ = bf16[1,256,448]{2,1,0:T(8,128)(2,1)S(1)} collective-permute-done((bf16[1,256,448]{2,1,0:T(8,128)(2,1)S(1)}, bf16[1,256,448]{2,1,0:T(8,128)(2,1)S(1)}, u32[]{:S(2)}, u32[]{:S(2)}) %collective-permute-start.34) | collective-permute-done | bytes 229408 | tf_op jit(solution)/shard_map/ppermute | solution.py:20
  236.1 5.1 %collective-permute-done.33.rest_0_ = bf16[1,256,448]{2,1,0:T(8,128)(2,1)S(1)} collective-permute-done((bf16[1,256,448]{2,1,0:T(8,128)(2,1)S(1)}, bf16[1,256,448]{2,1,0:T(8,128)(2,1)S(1)}, u32[]{:S(2)}, u32[]{:S(2)}) %collective-permute-start.33) | collective-permute-done | bytes 229408 | tf_op jit(solution)/shard_map/ppermute | solution.py:20
  (145 shorter events, 49.1 us)
Async XLA Ops:
  5.9 12.4 %collective-permute-start.5 = (bf16[128,896]{1,0:T(8,128)(2,1)}, bf16[128,896]{1,0:T(8,128)(2,1)}, u32[]{:S(2)}, u32[]{:S(2)}) collective-permute-start(bf16[128,896]{1,0:T(8,128)(2,1)} %get-tuple-element.36), channel_id=1, source_target_pairs={{12,0},{8,4},{4,8},{0,12},{13,1},{9,5},{5,9},{1,13},{14,2},{10,6},... | collective-permute-start | bytes 688136 | tf_op jit(solution)/shard_map/ppermute | solution.py:25
  10.9 46.6 %collective-permute-start.2 = (bf16[2,448,1024]{2,1,0:T(8,128)(2,1)}, bf16[2,448,1024]{2,1,0:T(8,128)(2,1)}, u32[]{:S(2)}, u32[]{:S(2)}) collective-permute-start(bf16[2,448,1024]{2,1,0:T(8,128)(2,1)} %rest_4_.1), channel_id=1, source_target_pairs={{0,1},{1,0},{2,3},{3,2},{4,5},{5,4},{6,7},{7,6},{8,9},{9,8},{10,11... | collective-permute-start | bytes 5505032 | tf_op jit(solution)/shard_map/ppermute | solution.py:20
  10.9 20.8 %collective-permute-start.7 = (bf16[128,896]{1,0:T(8,128)(2,1)S(1)}, bf16[128,896]{1,0:T(8,128)(2,1)}, u32[]{:S(2)}, u32[]{:S(2)}) collective-permute-start(bf16[128,896]{1,0:T(8,128)(2,1)S(1)} %get-tuple-element.39), channel_id=1, source_target_pairs={{8,0},{12,4},{0,8},{4,12},{9,1},{13,5},{1,9},{5,13},{10,2},{14,6},... | collective-permute-start | bytes 688136 | tf_op jit(solution)/shard_map/ppermute | solution.py:25
  10.9 20.8 %collective-permute-start.3 = (bf16[128,896]{1,0:T(8,128)(2,1)S(1)}, bf16[128,896]{1,0:T(8,128)(2,1)S(1)}, u32[]{:S(2)}, u32[]{:S(2)}) collective-permute-start(bf16[128,896]{1,0:T(8,128)(2,1)S(1)} %get-tuple-element.34), channel_id=1, source_target_pairs={{4,0},{0,4},{12,8},{8,12},{5,1},{1,5},{13,9},{9,13},{6,2},{2,6},{1... | collective-permute-start | bytes 688136 | tf_op jit(solution)/shard_map/ppermute | solution.py:25
  12.5 34.0 %collective-permute-start.25 = (bf16[448,1024]{1,0:T(8,128)(2,1)}, bf16[448,1024]{1,0:T(8,128)(2,1)}, u32[]{:S(2)}, u32[]{:S(2)}) collective-permute-start(bf16[448,1024]{1,0:T(8,128)(2,1)} %dynamic-slice_bitcast_fusion), channel_id=1, source_target_pairs={{4,0},{0,4},{12,8},{8,12},{5,1},{1,5},{13,9},{9,13},{6,2},{2,6},{1... | collective-permute-start | bytes 2752520 | tf_op jit(solution)/shard_map/ppermute | solution.py:25
  18.3 34.6 %collective-permute-start.27 = (bf16[448,1024]{1,0:T(8,128)(2,1)}, bf16[448,1024]{1,0:T(8,128)(2,1)}, u32[]{:S(2)}, u32[]{:S(2)}) collective-permute-start(bf16[448,1024]{1,0:T(8,128)(2,1)} %dynamic-slice_bitcast_fusion), channel_id=1, source_target_pairs={{8,4},{4,8},{9,5},{5,9},{10,6},{6,10},{11,7},{7,11},{24,20},{20,24... | collective-permute-start | bytes 2752520 | tf_op jit(solution)/shard_map/ppermute | solution.py:25
  31.7 16.4 %collective-permute-start.1 = (bf16[2,448,256]{2,1,0:T(8,128)(2,1)}, bf16[2,448,256]{2,1,0:T(8,128)(2,1)}, u32[]{:S(2)}, u32[]{:S(2)}) collective-permute-start(bf16[2,448,256]{2,1,0:T(8,128)(2,1)} %constant_dynamic-slice_fusion.rest_2_), channel_id=1, source_target_pairs={{0,1},{1,0},{2,3},{3,2},{4,5},{5,4},{6,7},{7,6},{8,9},{9,8},{10,11... | collective-permute-start | bytes 1376264 | tf_op jit(solution)/shard_map/ppermute | solution.py:20
  40.7 11.6 %collective-permute-start = (bf16[2,448,256]{2,1,0:T(8,128)(2,1)}, bf16[2,448,256]{2,1,0:T(8,128)(2,1)}, u32[]{:S(2)}, u32[]{:S(2)}) collective-permute-start(bf16[2,448,256]{2,1,0:T(8,128)(2,1)} %constant_dynamic-slice_fusion.1.rest_0_), channel_id=1, source_target_pairs={{0,1},{1,0},{2,3},{3,2},{4,5},{5,4},{6,7},{7,6},{8,9},{9,8},{10,11... | collective-permute-start | bytes 1376264 | tf_op jit(solution)/shard_map/ppermute | solution.py:20
  46.4 28.8 %collective-permute-start.26 = (bf16[448,1024]{1,0:T(8,128)(2,1)}, bf16[448,1024]{1,0:T(8,128)(2,1)}, u32[]{:S(2)}, u32[]{:S(2)}) collective-permute-start(bf16[448,1024]{1,0:T(8,128)(2,1)} %collective-permute-done.25.rest_5_.rest_3_), channel_id=1, source_target_pairs={{8,4},{4,8},{9,5},{5,9},{10,6},{6,10},{11,7},{7,11},{24,20},{20,24... | collective-permute-start | bytes 2752520 | tf_op jit(solution)/shard_map/ppermute | solution.py:25
  52.3 21.6 %collective-permute-start.4 = (bf16[128,896]{1,0:T(8,128)(2,1)S(1)}, bf16[128,896]{1,0:T(8,128)(2,1)S(1)}, u32[]{:S(2)}, u32[]{:S(2)}) collective-permute-start(bf16[128,896]{1,0:T(8,128)(2,1)S(1)} %collective-permute-done.3.rest_6_), channel_id=1, source_target_pairs={{0,2},{2,0},{1,3},{3,1},{4,6},{6,4},{5,7},{7,5},{8,10},{10,8},{9,1... | collective-permute-start | bytes 688136 | tf_op jit(solution)/shard_map/ppermute | solution.py:20
  52.9 65.9 %collective-permute-start.28 = (bf16[448,1024]{1,0:T(8,128)(2,1)}, bf16[448,1024]{1,0:T(8,128)(2,1)S(1)}, u32[]{:S(2)}, u32[]{:S(2)}) collective-permute-start(bf16[448,1024]{1,0:T(8,128)(2,1)} %collective-permute-done.27), channel_id=1, source_target_pairs={{4,0},{8,12},{5,1},{9,13},{6,2},{10,14},{7,3},{11,15},{20,16},{24,... | collective-permute-start | bytes 2752520 | tf_op jit(solution)/shard_map/ppermute | solution.py:25
  66.8 17.1 %collective-permute-start.14 = (bf16[2,256,512]{2,1,0:T(8,128)(2,1)S(1)}, bf16[2,256,512]{2,1,0:T(8,128)(2,1)S(1)}, u32[]{:S(2)}, u32[]{:S(2)}) collective-permute-start(bf16[2,256,512]{2,1,0:T(8,128)(2,1)S(1)} %bitcast.53), channel_id=1, source_target_pairs={{0,4},{12,8},{1,5},{13,9},{2,6},{14,10},{3,7},{15,11},{16,20},{28,... | collective-permute-start | bytes 1572872 | tf_op jit(solution)/shard_map/ppermute | solution.py:25
  71.3 23.5 %collective-permute-start.9 = (bf16[256,1024]{1,0:T(8,128)(2,1)S(1)}, bf16[256,1024]{1,0:T(8,128)(2,1)S(1)}, u32[]{:S(2)}, u32[]{:S(2)}) collective-permute-start(bf16[256,1024]{1,0:T(8,128)(2,1)S(1)} %get-tuple-element.43), channel_id=1, source_target_pairs={{0,4},{12,8},{1,5},{13,9},{2,6},{14,10},{3,7},{15,11},{16,20},{28,... | collective-permute-start | bytes 1572872 | tf_op jit(solution)/shard_map/ppermute | solution.py:25
  73.9 29.0 %collective-permute-start.12 = (bf16[256,1024]{1,0:T(8,128)(2,1)S(1)}, bf16[256,1024]{1,0:T(8,128)(2,1)S(1)}, u32[]{:S(2)}, u32[]{:S(2)}) collective-permute-start(bf16[256,1024]{1,0:T(8,128)(2,1)S(1)} %get-tuple-element.44), channel_id=1, source_target_pairs={{0,4},{12,8},{1,5},{13,9},{2,6},{14,10},{3,7},{15,11},{16,20},{28,... | collective-permute-start | bytes 1572872 | tf_op jit(solution)/shard_map/ppermute | solution.py:25
  75.3 43.5 %collective-permute-start.29 = (bf16[448,1024]{1,0:T(8,128)(2,1)}, bf16[448,1024]{1,0:T(8,128)(2,1)S(1)}, u32[]{:S(2)}, u32[]{:S(2)}) collective-permute-start(bf16[448,1024]{1,0:T(8,128)(2,1)} %collective-permute-done.26), channel_id=1, source_target_pairs={{4,0},{8,12},{5,1},{9,13},{6,2},{10,14},{7,3},{11,15},{20,16},{24,... | collective-permute-start | bytes 2752520 | tf_op jit(solution)/shard_map/ppermute | solution.py:25
  84.1 19.9 %collective-permute-start.15 = (bf16[2,256,512]{2,1,0:T(8,128)(2,1)S(1)}, bf16[2,256,512]{2,1,0:T(8,128)(2,1)S(1)}, u32[]{:S(2)}, u32[]{:S(2)}) collective-permute-start(bf16[2,256,512]{2,1,0:T(8,128)(2,1)S(1)} %fusion), channel_id=1, source_target_pairs={{8,4},{4,8},{9,5},{5,9},{10,6},{6,10},{11,7},{7,11},{24,20},{20,24... | collective-permute-start | bytes 1572872 | tf_op jit(solution)/shard_map/ppermute | solution.py:25
  95.0 14.4 %collective-permute-start.10 = (bf16[256,1024]{1,0:T(8,128)(2,1)S(1)}, bf16[256,1024]{1,0:T(8,128)(2,1)S(1)}, u32[]{:S(2)}, u32[]{:S(2)}) collective-permute-start(bf16[256,1024]{1,0:T(8,128)(2,1)S(1)} %fusion.2), channel_id=1, source_target_pairs={{8,4},{4,8},{9,5},{5,9},{10,6},{6,10},{11,7},{7,11},{24,20},{20,24... | collective-permute-start | bytes 1572872 | tf_op jit(solution)/shard_map/ppermute | solution.py:25
  103.1 19.2 %collective-permute-start.13 = (bf16[256,1024]{1,0:T(8,128)(2,1)S(1)}, bf16[256,1024]{1,0:T(8,128)(2,1)S(1)}, u32[]{:S(2)}, u32[]{:S(2)}) collective-permute-start(bf16[256,1024]{1,0:T(8,128)(2,1)S(1)} %fusion.1), channel_id=1, source_target_pairs={{8,4},{4,8},{9,5},{5,9},{10,6},{6,10},{11,7},{7,11},{24,20},{20,24... | collective-permute-start | bytes 1572872 | tf_op jit(solution)/shard_map/ppermute | solution.py:25
  104.1 12.5 %collective-permute-start.16 = (bf16[256,512]{1,0:T(8,128)(2,1)S(1)}, bf16[256,512]{1,0:T(8,128)(2,1)S(1)}, u32[]{:S(2)}, u32[]{:S(2)}) collective-permute-start(bf16[256,512]{1,0:T(8,128)(2,1)S(1)} %fusion.4), channel_id=1, source_target_pairs={{4,0},{0,4},{12,8},{8,12},{5,1},{1,5},{13,9},{9,13},{6,2},{2,6},{1... | collective-permute-start | bytes 786440 | tf_op jit(solution)/shard_map/ppermute | solution.py:25
  110.6 35.5 %collective-permute-start.11 = (bf16[256,1024]{1,0:T(8,128)(2,1)S(1)}, bf16[256,1024]{1,0:T(8,128)(2,1)S(1)}, u32[]{:S(2)}, u32[]{:S(2)}) collective-permute-start(bf16[256,1024]{1,0:T(8,128)(2,1)S(1)} %get-tuple-element.51), channel_id=1, source_target_pairs={{4,0},{0,4},{12,8},{8,12},{5,1},{1,5},{13,9},{9,13},{6,2},{2,6},{1... | collective-permute-start | bytes 1572872 | tf_op jit(solution)/shard_map/ppermute | solution.py:25
  116.7 21.6 %collective-permute-start.17 = (bf16[256,512]{1,0:T(8,128)(2,1)S(1)}, bf16[256,512]{1,0:T(8,128)(2,1)S(1)}, u32[]{:S(2)}, u32[]{:S(2)}) collective-permute-start(bf16[256,512]{1,0:T(8,128)(2,1)S(1)} %fusion.3.rest_3_), channel_id=1, source_target_pairs={{4,0},{0,4},{12,8},{8,12},{5,1},{1,5},{13,9},{9,13},{6,2},{2,6},{1... | collective-permute-start | bytes 786440 | tf_op jit(solution)/shard_map/ppermute | solution.py:25
  118.8 19.6 %collective-permute-start.18 = (bf16[256,512]{1,0:T(8,128)(2,1)S(1)}, bf16[256,512]{1,0:T(8,128)(2,1)}, u32[]{:S(2)}, u32[]{:S(2)}) collective-permute-start(bf16[256,512]{1,0:T(8,128)(2,1)S(1)} %fusion.3.rest_3_), channel_id=1, source_target_pairs={{8,0},{12,4},{0,8},{4,12},{9,1},{13,5},{1,9},{5,13},{10,2},{14,6},... | collective-permute-start | bytes 786440 | tf_op jit(solution)/shard_map/ppermute | solution.py:25
  118.8 24.6 %collective-permute-start.19 = (bf16[256,512]{1,0:T(8,128)(2,1)S(1)}, bf16[256,512]{1,0:T(8,128)(2,1)}, u32[]{:S(2)}, u32[]{:S(2)}) collective-permute-start(bf16[256,512]{1,0:T(8,128)(2,1)S(1)} %fusion.3.rest_3_), channel_id=1, source_target_pairs={{12,0},{8,4},{4,8},{0,12},{13,1},{9,5},{5,9},{1,13},{14,2},{10,6},... | collective-permute-start | bytes 786440 | tf_op jit(solution)/shard_map/ppermute | solution.py:25
  122.3 22.2 %collective-permute-start.20 = (bf16[256,512]{1,0:T(8,128)(2,1)S(1)}, bf16[256,512]{1,0:T(8,128)(2,1)S(1)}, u32[]{:S(2)}, u32[]{:S(2)}) collective-permute-start(bf16[256,512]{1,0:T(8,128)(2,1)S(1)} %fusion.3.rest_3_), channel_id=1, source_target_pairs={{0,1},{1,0},{2,3},{3,2},{4,5},{5,4},{6,7},{7,6},{8,9},{9,8},{10,11... | collective-permute-start | bytes 786440 | tf_op jit(solution)/shard_map/ppermute | solution.py:20
  138.3 11.5 %collective-permute-start.22 = (bf16[256,512]{1,0:T(8,128)(2,1)}, bf16[256,512]{1,0:T(8,128)(2,1)}, u32[]{:S(2)}, u32[]{:S(2)}) collective-permute-start(bf16[256,512]{1,0:T(8,128)(2,1)} %collective-permute-done.18.rest_5_), channel_id=1, source_target_pairs={{0,1},{1,0},{2,3},{3,2},{4,5},{5,4},{6,7},{7,6},{8,9},{9,8},{10,11... | collective-permute-start | bytes 786440 | tf_op jit(solution)/shard_map/ppermute | solution.py:20
  144.5 23.6 %collective-permute-start.30 = (bf16[448,1024]{1,0:T(8,128)(2,1)}, bf16[448,1024]{1,0:T(8,128)(2,1)}, u32[]{:S(2)}, u32[]{:S(2)}) collective-permute-start(bf16[448,1024]{1,0:T(8,128)(2,1)} %collective-permute-done.25.rest_5_.rest_3_), channel_id=1, source_target_pairs={{0,16},{16,0},{1,17},{17,1},{2,18},{18,2},{3,19},{19,3},{4,20},{20... | collective-permute-start | bytes 2752520 | tf_op jit(solution)/shard_map/ppermute | solution.py:20
  146.9 40.9 %collective-permute-start.31 = (bf16[448,1024]{1,0:T(8,128)(2,1)}, bf16[448,1024]{1,0:T(8,128)(2,1)}, u32[]{:S(2)}, u32[]{:S(2)}) collective-permute-start(bf16[448,1024]{1,0:T(8,128)(2,1)} %broadcast_select_fusion.1.rest_6_.rest_4_), channel_id=1, source_target_pairs={{0,16},{16,0},{1,17},{17,1},{2,18},{18,2},{3,19},{19,3},{4,20},{20... | collective-permute-start | bytes 2752520 | tf_op jit(solution)/shard_map/ppermute | solution.py:20
  148.2 58.8 %collective-permute-start.32 = (bf16[448,1024]{1,0:T(8,128)(2,1)}, bf16[448,1024]{1,0:T(8,128)(2,1)}, u32[]{:S(2)}, u32[]{:S(2)}) collective-permute-start(bf16[448,1024]{1,0:T(8,128)(2,1)} %broadcast_select_fusion.rest_7_.rest_5_), channel_id=1, source_target_pairs={{0,16},{16,0},{1,17},{17,1},{2,18},{18,2},{3,19},{19,3},{4,20},{20... | collective-permute-start | bytes 2752520 | tf_op jit(solution)/shard_map/ppermute | solution.py:20
  158.3 48.7 %collective-permute-start.24 = (bf16[256,1024]{1,0:T(8,128)(2,1)S(1)}, bf16[256,1024]{1,0:T(8,128)(2,1)}, u32[]{:S(2)}, u32[]{:S(2)}) collective-permute-start(bf16[256,1024]{1,0:T(8,128)(2,1)S(1)} %attend.1.rest_0_), channel_id=1, source_target_pairs={{0,1},{1,0},{2,3},{3,2},{4,5},{5,4},{6,7},{7,6},{8,9},{9,8},{10,11... | collective-permute-start | bytes 1572872 | tf_op jit(solution)/shard_map/ppermute | solution.py:20
  210.3 10.1 %collective-permute-start.35 = (bf16[1,256,448]{2,1,0:T(8,128)(2,1)S(1)}, bf16[1,256,448]{2,1,0:T(8,128)(2,1)S(1)}, u32[]{:S(2)}, u32[]{:S(2)}) collective-permute-start(bf16[1,256,448]{2,1,0:T(8,128)(2,1)S(1)} %project.8), channel_id=1, source_target_pairs={{0,2},{2,0},{1,3},{3,1},{4,6},{6,4},{5,7},{7,5},{8,10},{10,8},{9,1... | collective-permute-start | bytes 688136 | tf_op jit(solution)/shard_map/ppermute | solution.py:20
  224.0 17.3 %collective-permute-start.37 = (bf16[2,256,448]{2,1,0:T(8,128)(2,1)S(1)}, bf16[2,256,448]{2,1,0:T(8,128)(2,1)S(1)}, u32[]{:S(2)}, u32[]{:S(2)}) collective-permute-start(bf16[2,256,448]{2,1,0:T(8,128)(2,1)S(1)} %add_convert_fusion), channel_id=1, source_target_pairs={{0,1},{1,0},{2,3},{3,2},{4,5},{5,4},{6,7},{7,6},{8,9},{9,8},{10,11... | collective-permute-start | bytes 1376264 | tf_op jit(solution)/shard_map/ppermute | solution.py:20
  230.0 11.3 %collective-permute-start.33 = (bf16[1,256,448]{2,1,0:T(8,128)(2,1)S(1)}, bf16[1,256,448]{2,1,0:T(8,128)(2,1)S(1)}, u32[]{:S(2)}, u32[]{:S(2)}) collective-permute-start(bf16[1,256,448]{2,1,0:T(8,128)(2,1)S(1)} %project.6), channel_id=1, source_target_pairs={{0,2},{2,0},{1,3},{3,1},{4,6},{6,4},{5,7},{7,5},{8,10},{10,8},{9,1... | collective-permute-start | bytes 688136 | tf_op jit(solution)/shard_map/ppermute | solution.py:20
  (31 other events, 270.7 us)

commit v10 on v9

--- a/solution.py
+++ b/solution.py
@@ -287,9 +287,16 @@
 
 
 def attention_kernel(terms, starts, limits, span_ref, *rest):
-    q_refs, sources = rest[:terms], rest[terms:-8]
-    (o_ref, kv_ref, queries, bounds, top, total, acc, arrived) = rest[-8:]
+    inner = len(rest) - 9 - terms
+    q_sources, sources, q_refs = rest[:terms], rest[terms:inner], rest[inner + 1 : inner + 1 + terms]
+    o_ref = rest[inner]
+    kv_ref, queries, bounds, top, total, acc, arrived, landed = rest[-8:]
     count, size, _ = kv_ref.shape
+    landing = []
+    for i, (source, held) in enumerate(zip(q_sources, q_refs)):
+        source = source if i else source.at[source.shape[0] - 1]
+        landing.append(pltpu.make_async_copy(source, held, landed.at[i]))
+        landing[-1].start()
     for number, source in enumerate(sources):
         pltpu.make_async_copy(source, kv_ref.at[number], arrived.at[number]).start()
     rows = o_ref.shape[0]
@@ -299,16 +306,18 @@
     top[...] = jnp.full_like(top, LOW / 10)
     total[...] = jnp.zeros_like(total)
     acc[...] = jnp.zeros_like(acc)
+    columns = span_ref[...].T
+    for r in range(repeat):
+        bounds[r * rows : (r + 1) * rows] = columns
+    for copy in landing:
+        copy.wait()
     for head in range(kv_local * repeat):
         g, r = head // repeat, head % repeat
         cols = slice(head * HEAD_DIM, (head + 1) * HEAD_DIM)
-        query = q_refs[0][0, :, cols].astype(jnp.float32)
+        query = q_refs[0][:, cols].astype(jnp.float32)
         for term in q_refs[1:]:
             query = query + term[:, cols].astype(jnp.float32)
         queries[g, r * rows : (r + 1) * rows] = query.astype(jnp.bfloat16)
-    columns = span_ref[...].T
-    for r in range(repeat):
-        bounds[r * rows : (r + 1) * rows] = columns
     transposed = (((1,), (1,)), ((), ()))
 
     def visit(number, _):
@@ -366,9 +375,12 @@
     return pl.pallas_call(
         functools.partial(attention_kernel, len(query)),
         out_shape=jax.ShapeDtypeStruct((rows, width), jnp.bfloat16),
-        in_specs=[SMEM, SMEM, VMEM] + [VMEM] * len(query) + [HBM] * (count // 2 + 1) + [VMEM] * (count // 2 - 1),
+        in_specs=[SMEM, SMEM, VMEM]
+        + [HBM] * (len(query) + count // 2 + 1)
+        + [VMEM] * (count // 2 - 1),
         out_specs=VMEM,
         scratch_shapes=[
+            *[pltpu.VMEM((rows, width), term.dtype) for term in query],
             pltpu.VMEM((count, size, kv_cols), jnp.bfloat16),
             pltpu.VMEM((kv_local, many, HEAD_DIM), jnp.bfloat16),
             pltpu.VMEM((many, 8), jnp.int32),
@@ -376,6 +388,7 @@
             pltpu.VMEM((kv_local, many, HEAD_DIM), jnp.float32),
             pltpu.VMEM((kv_local, many, HEAD_DIM), jnp.float32),
             pltpu.SemaphoreType.DMA((count,)),
+            pltpu.SemaphoreType.DMA((len(query),)),
         ],
         cost_estimate=pl.CostEstimate(
             flops=4 * rows * count * size * width,
@@ -388,8 +401,7 @@
         starts,
         limits,
         span,
-        *query,
-        *[in_hbm(block) for block in kv[: count // 2 + 1]],
+        *[in_hbm(array) for array in (*query, *kv[: count // 2 + 1])],
         *kv[count // 2 + 1 :],
     )
 
@@ -519,7 +531,7 @@
         kv_early, q_early = after((kv_early, q_early), kv_late, q_late)
         kv = along_four([kv_late[1], kv_late[0], kv_early[1], kv_early[0]], kv_ends, None, True)
         parts = [q_late[1], q_late[0], q_early[1], q_early[0]]
-        query = (q_late[1:], *along_four(parts, q_three, q_two, False))
+        query = (q_late, *along_four(parts, q_three, q_two, False))
     else:
         kv_parts, q_parts = [], []
         for d in range(n):

time: 244 us -> 255 us (1.045)
  starting transfers between devices: 50.2 us -> 70.4 us
  local copies, waits for them, and re-layouts: 18.3 us -> 11.8 us
    ppermute x19, starting transfers between devices: 37.4 us -> 57.6 us  [cross(): return lax.ppermute(x, axis, [(i ^ bit, i) for i in among or range(size)])]
    unnamed x50 -> x52, local copies, waits for them, and re-layouts: 11.5 us -> 7.45 us
    ppermute x19, waiting for transfers between devices: 67.6 us -> 64.9 us  [swap(): return lax.ppermute(x, axis, [(0, 1), (1, 0)])]
  transfers between devices with their start and end apart: 38 -> 38, of which waited for: 15 -> 15; matrix products, arithmetic and copies ran while one was open for 6% -> 4% of each run, Pallas kernels for 13% -> 14%
where the time goes in v10:
time: 255 us; the launch traced here: 254 us
  waiting for transfers between devices  122 us (48%)
  starting transfers between devices  70.4 us (28%)
  Pallas kernels  40.6 us (16%)
  local copies, waits for them, and re-layouts  11.8 us (5%)
  other arithmetic  7.33 us (3%)
    ppermute x19, waiting for transfers between devices, swap(): return lax.ppermute(x, axis, [(0, 1), (1, 0)])  64.9 us
    ppermute x19, starting transfers between devices, cross(): return lax.ppermute(x, axis, [(i ^ bit, i) for i in among or range(size)])  57.6 us
    ppermute x19, waiting for transfers between devices, cross(): return lax.ppermute(x, axis, [(i ^ bit, i) for i in among or range(size)])  56.8 us
    pallas_call x5, Pallas kernels, project(): pl.pallas_call(functools.partial(project_kernel, (len(weights) + 1) // 2,...  16.6 us
    pallas_call x2, Pallas kernels, partial(): pl.pallas_call(functools.partial(partial_kernel, counts, narrow), out_sha...  14.8 us
    ppermute x19, starting transfers between devices, swap(): return lax.ppermute(x, axis, [(0, 1), (1, 0)])  12.9 us
    unnamed x52, local copies, waits for them, and re-layouts  7.45 us
  transfers between devices with their start and end apart: 38, of which 15 were waited for; matrix products, arithmetic and copies ran while one was open for 4% of the time, Pallas kernels for 14%

profile of v10, /device:TPU:0, one launch (start us, length us, event | category | flops | bytes accessed | tf_op | source)
XLA Modules:
  0.0 254.1 jit_solution(13783387905297042728)
XLA Ops:
  0.0 2.3 dynamic-slice_bitcast_fusion
  2.3 3.1 %collective-permute-start.25 = (bf16[448,1024]{1,0:T(8,128)(2,1)}, bf16[448,1024]{1,0:T(8,128)(2,1)}, u32[]{:S(2)}, u32[]{:S(2)}) collective-permute-start(bf16[448,1024]{1,0:T(8,128)(2,1)} %dynamic-slice_bitcast_fusion), channel_id=1, source_target_pairs={{4,0},{0,4},{12,8},{8,12},{5,1},{1,5},{13,9},{9,13},{6,2},{2,6},{1... | collective-permute-start | bytes 2752520 | tf_op jit(solution)/shard_map/ppermute | solution.py:25
  8.5 2.7 %norm.1 = (bf16[256,896]{1,0:T(8,128)(2,1)S(1)}, bf16[128,896]{1,0:T(8,128)(2,1)S(1)}, bf16[128,896]{1,0:T(8,128)(2,1)S(1)}, bf16[128,896]{1,0:T(8,128)(2,1)S(1)}) custom-call(s32[5]{0:T(128)S(1)} %stack.64.place, s32[2048]{0:T(1024)S(1)} %copy-done.2, bf16[256,3584]{1,0:T(8,128)(2,1)} %tokens_ref.1, f32[2,3584]{1,0:T(2,128)S(1)} %copy-done.4), custom_call_target="tpu_custom_call" | custom-call | flops 5505024 | bytes 3670016 | tf_op jit(solution)/shard_map/norm/pallas_call | solution.py:85
  12.0 3.5 %collective-permute-start.3 = (bf16[128,896]{1,0:T(8,128)(2,1)S(1)}, bf16[128,896]{1,0:T(8,128)(2,1)}, u32[]{:S(2)}, u32[]{:S(2)}) collective-permute-start(bf16[128,896]{1,0:T(8,128)(2,1)S(1)} %get-tuple-element.34), channel_id=1, source_target_pairs={{4,0},{0,4},{12,8},{8,12},{5,1},{1,5},{13,9},{9,13},{6,2},{2,6},{1... | collective-permute-start | bytes 688136 | tf_op jit(solution)/shard_map/ppermute | solution.py:25
  20.3 10.9 %collective-permute-done.3.rest_6_ = bf16[128,896]{1,0:T(8,128)(2,1)} collective-permute-done((bf16[128,896]{1,0:T(8,128)(2,1)S(1)}, bf16[128,896]{1,0:T(8,128)(2,1)}, u32[]{:S(2)}, u32[]{:S(2)}) %collective-permute-start.3) | collective-permute-done | bytes 229408 | tf_op jit(solution)/shard_map/ppermute | solution.py:25
  31.2 6.9 %collective-permute-done.5.rest_6_ = bf16[128,896]{1,0:T(8,128)(2,1)} collective-permute-done((bf16[128,896]{1,0:T(8,128)(2,1)S(1)}, bf16[128,896]{1,0:T(8,128)(2,1)}, u32[]{:S(2)}, u32[]{:S(2)}) %collective-permute-start.5) | collective-permute-done | bytes 229408 | tf_op jit(solution)/shard_map/ppermute | solution.py:25
  38.2 3.6 %collective-permute-start.7 = (bf16[128,896]{1,0:T(8,128)(2,1)S(1)}, bf16[128,896]{1,0:T(8,128)(2,1)}, u32[]{:S(2)}, u32[]{:S(2)}) collective-permute-start(bf16[128,896]{1,0:T(8,128)(2,1)S(1)} %get-tuple-element.39), channel_id=1, source_target_pairs={{8,0},{12,4},{0,8},{4,12},{9,1},{13,5},{1,9},{5,13},{10,2},{14,6},... | collective-permute-start | bytes 688136 | tf_op jit(solution)/shard_map/ppermute | solution.py:25
  41.9 9.4 %collective-permute-done.7.rest_8_ = bf16[128,896]{1,0:T(8,128)(2,1)} collective-permute-done((bf16[128,896]{1,0:T(8,128)(2,1)S(1)}, bf16[128,896]{1,0:T(8,128)(2,1)}, u32[]{:S(2)}, u32[]{:S(2)}) %collective-permute-start.7) | collective-permute-done | bytes 229408 | tf_op jit(solution)/shard_map/ppermute | solution.py:25
  55.2 2.6 %collective-permute-done.6.rest_7_ = bf16[128,896]{1,0:T(8,128)(2,1)S(1)} collective-permute-done((bf16[128,896]{1,0:T(8,128)(2,1)}, bf16[128,896]{1,0:T(8,128)(2,1)S(1)}, u32[]{:S(2)}, u32[]{:S(2)}) %collective-permute-start.6) | collective-permute-done | bytes 229408 | tf_op jit(solution)/shard_map/ppermute | solution.py:20
  59.3 2.5 %pad_add_fusion.limits = s32[4]{0:T(128)S(1)} fusion(s32[1]{0:T(128)} %get-tuple-element.57, s32[1]{0:T(128)} %get-tuple-element.54, s32[1]{0:T(128)} %get-tuple-element.58, s32[1]{0:T(128)} %get-tuple-element.53), kind=kLoop, calls=%fused_computation.32 | loop fusion | flops 12 | bytes 32 | tf_op jit(solution)/shard_map/stack | solution.py:516
  65.6 7.5 %partial.3 = (f32[512,512]{1,0:T(8,128)}, f32[512,1024]{1,0:T(8,128)}, bf16[512,512]{1,0:T(8,128)(2,1)S(1)}, bf16[256,1024]{1,0:T(8,128)(2,1)S(1)}, bf16[256,1024]{1,0:T(8,128)(2,1)S(1)}) custom-call(s32[5]{0:T(128)S(1)} %stack.64.place, s32[2048]{0:T(1024)S(1)} %copy-done.3, s32[2]{0:T(128)S(1)} %pad_add_fusion.2.begins, bf16[2,448,256]{2,1,0:T(8,128)(2,1)} %copy-done.16, ...), custom_call_target="tpu_custom_call" | custom-call | flops 2818572288 | bytes 8650752 | tf_op jit(solution)/shard_map/partial/pallas_call | solution.py:187
  73.1 2.9 %collective-permute-start.9 = (bf16[256,1024]{1,0:T(8,128)(2,1)S(1)}, bf16[256,1024]{1,0:T(8,128)(2,1)S(1)}, u32[]{:S(2)}, u32[]{:S(2)}) collective-permute-start(bf16[256,1024]{1,0:T(8,128)(2,1)S(1)} %get-tuple-element.43), channel_id=1, source_target_pairs={{0,4},{12,8},{1,5},{13,9},{2,6},{14,10},{3,7},{15,11},{16,20},{28,... | collective-permute-start | bytes 1572872 | tf_op jit(solution)/shard_map/ppermute | solution.py:25
  77.6 7.3 %partial.2 = (f32[512,512]{1,0:T(8,128)}, f32[512,1024]{1,0:T(8,128)}) custom-call(s32[5]{0:T(128)S(1)} %stack.64.place, s32[2048]{0:T(1024)S(1)} %copy-done.3, s32[2]{0:T(128)S(1)} %pad_add_fusion.1.begins, bf16[2,448,256]{2,1,0:T(8,128)(2,1)} %copy-done.16, bf16[2,448,256]{2,1,0:T(8,128)(2,1)} %copy-done.23, bf16[2,448,256]{2,1,0:T(8,128)(2,1)} %copy-done.17, ...), custom_call_target="tpu_custom_call" | custom-call | flops 2818572288 | bytes 8650752 | tf_op jit(solution)/shard_map/partial/pallas_call | solution.py:187
  87.7 11.9 %collective-permute-done.14 = bf16[2,256,512]{2,1,0:T(8,128)(2,1)S(1)} collective-permute-done((bf16[2,256,512]{2,1,0:T(8,128)(2,1)S(1)}, bf16[2,256,512]{2,1,0:T(8,128)(2,1)S(1)}, u32[]{:S(2)}, u32[]{:S(2)}) %collective-permute-start.14) | collective-permute-done | bytes 524320 | tf_op jit(solution)/shard_map/ppermute | solution.py:25
  101.7 5.3 %collective-permute-done.12 = bf16[256,1024]{1,0:T(8,128)(2,1)S(1)} collective-permute-done((bf16[256,1024]{1,0:T(8,128)(2,1)S(1)}, bf16[256,1024]{1,0:T(8,128)(2,1)S(1)}, u32[]{:S(2)}, u32[]{:S(2)}) %collective-permute-start.12) | collective-permute-done | bytes 524320 | tf_op jit(solution)/shard_map/ppermute | solution.py:25
  108.1 11.1 %collective-permute-start.16 = (bf16[256,512]{1,0:T(8,128)(2,1)S(1)}, bf16[256,512]{1,0:T(8,128)(2,1)S(1)}, u32[]{:S(2)}, u32[]{:S(2)}) collective-permute-start(bf16[256,512]{1,0:T(8,128)(2,1)S(1)} %fusion.4), channel_id=1, source_target_pairs={{4,0},{0,4},{12,8},{8,12},{5,1},{1,5},{13,9},{9,13},{6,2},{2,6},{1... | collective-permute-start | bytes 786440 | tf_op jit(solution)/shard_map/ppermute | solution.py:25
  119.4 16.8 %collective-permute-start.11 = (bf16[256,1024]{1,0:T(8,128)(2,1)S(1)}, bf16[256,1024]{1,0:T(8,128)(2,1)S(1)}, u32[]{:S(2)}, u32[]{:S(2)}) collective-permute-start(bf16[256,1024]{1,0:T(8,128)(2,1)S(1)} %add_convert_fusion.1), channel_id=1, source_target_pairs={{4,0},{0,4},{12,8},{8,12},{5,1},{1,5},{13,9},{9,13},{6,2},{2,6},{1... | collective-permute-start | bytes 1572872 | tf_op jit(solution)/shard_map/ppermute | solution.py:25
  136.4 3.2 %collective-permute-start.18 = (bf16[256,512]{1,0:T(8,128)(2,1)S(1)}, bf16[256,512]{1,0:T(8,128)(2,1)}, u32[]{:S(2)}, u32[]{:S(2)}) collective-permute-start(bf16[256,512]{1,0:T(8,128)(2,1)S(1)} %fusion.3.rest_3_), channel_id=1, source_target_pairs={{8,0},{12,4},{0,8},{4,12},{9,1},{13,5},{1,9},{5,13},{10,2},{14,6},... | collective-permute-start | bytes 786440 | tf_op jit(solution)/shard_map/ppermute | solution.py:25
  141.8 7.1 %collective-permute-done.17.rest_4_ = bf16[256,512]{1,0:T(8,128)(2,1)S(1)} collective-permute-done((bf16[256,512]{1,0:T(8,128)(2,1)S(1)}, bf16[256,512]{1,0:T(8,128)(2,1)S(1)}, u32[]{:S(2)}, u32[]{:S(2)}) %collective-permute-start.17) | collective-permute-done | bytes 262176 | tf_op jit(solution)/shard_map/ppermute | solution.py:25
  149.5 5.2 %collective-permute-done.19.rest_6_ = bf16[256,512]{1,0:T(8,128)(2,1)} collective-permute-done((bf16[256,512]{1,0:T(8,128)(2,1)S(1)}, bf16[256,512]{1,0:T(8,128)(2,1)}, u32[]{:S(2)}, u32[]{:S(2)}) %collective-permute-start.19) | collective-permute-done | bytes 262176 | tf_op jit(solution)/shard_map/ppermute | solution.py:25
  164.4 4.8 %attend.1.rest_0_ = bf16[256,1024]{1,0:T(8,128)(2,1)S(1)} custom-call(s32[8]{0:T(128)S(1)} %stack.72.starts, s32[4]{0:T(128)S(1)} %pad_add_fusion.limits, s32[8,256]{1,0:T(8,128)S(1)} %add_add_fusion.span_ref, f32[2,256,1024]{2,1,0:T(8,128)} %bitcast.56, bf16[256,1024]{1,0:T(8,128)(2,1)} %copy-done.22, bf16[256,1024]{1,0:T(8,128)(2,1)} %copy-done.21, ...), custom_call_target="tpu_custom_call" | custom-call | flops 2147483648 | bytes 3145728 | tf_op jit(solution)/shard_map/attend/pallas_call | solution.py:375
  171.1 8.2 %collective-permute-done.30.rest_8_.rest_6_ = bf16[448,1024]{1,0:T(8,128)(2,1)} collective-permute-done((bf16[448,1024]{1,0:T(8,128)(2,1)}, bf16[448,1024]{1,0:T(8,128)(2,1)}, u32[]{:S(2)}, u32[]{:S(2)}) %collective-permute-start.30) | collective-permute-done | bytes 917536 | tf_op jit(solution)/shard_map/ppermute | solution.py:20
  179.3 19.7 %collective-permute-done.31.rest_9_.rest_7_ = bf16[448,1024]{1,0:T(8,128)(2,1)} collective-permute-done((bf16[448,1024]{1,0:T(8,128)(2,1)}, bf16[448,1024]{1,0:T(8,128)(2,1)}, u32[]{:S(2)}, u32[]{:S(2)}) %collective-permute-start.31) | collective-permute-done | bytes 917536 | tf_op jit(solution)/shard_map/ppermute | solution.py:20
  198.9 19.2 %collective-permute-done.32.rest_10_.rest_8_ = bf16[448,1024]{1,0:T(8,128)(2,1)} collective-permute-done((bf16[448,1024]{1,0:T(8,128)(2,1)}, bf16[448,1024]{1,0:T(8,128)(2,1)}, u32[]{:S(2)}, u32[]{:S(2)}) %collective-permute-start.32) | collective-permute-done | bytes 917536 | tf_op jit(solution)/shard_map/ppermute | solution.py:20
  218.2 3.3 %project.9 = bf16[1,256,448]{2,1,0:T(8,128)(2,1)S(1)} custom-call(s32[1]{0:T(128)S(6)} %xor.39.turns, s32[5]{0:T(128)S(1)} %stack.64.place, bf16[256,1024]{1,0:T(8,128)(2,1)} %collective-permute-done.24.rest_2_.rest_0_, bf16[256,1]{1,0:T(8,128)(2,1)S(1)} %reshape.65.rest_3_.rest_1_, bf16[2,448,1024]{2,1,0:T(8,128)(2,1)S(1)} %bitcast.47, ...), custom_call_target="tpu_custom_call" | custom-call | flops 469762048 | bytes 2064384 | tf_op jit(solution)/shard_map/project/pallas_call | solution.py:456
  223.0 3.3 %project.8 = bf16[1,256,448]{2,1,0:T(8,128)(2,1)S(1)} custom-call(s32[1]{0:T(128)S(6)} %xor.38.turns, s32[5]{0:T(128)S(1)} %stack.64.place, bf16[256,1024]{1,0:T(8,128)(2,1)} %collective-permute-done.24.rest_2_.rest_0_, bf16[256,1]{1,0:T(8,128)(2,1)S(1)} %reshape.65.rest_3_.rest_1_, bf16[2,448,1024]{2,1,0:T(8,128)(2,1)S(1)} %bitcast.48, ...), custom_call_target="tpu_custom_call" | custom-call | flops 469762048 | bytes 2064384 | tf_op jit(solution)/shard_map/project/pallas_call | solution.py:456
  226.5 4.5 %project.5 = (bf16[2,256,448]{2,1,0:T(8,128)(2,1)S(1)}, bf16[2,256,448]{2,1,0:T(8,128)(2,1)S(1)}) custom-call(s32[2]{0:T(128)S(1)} %add_xor_fusion.turns, s32[5]{0:T(128)S(1)} %stack.64.place, bf16[256,1024]{1,0:T(8,128)(2,1)S(1)} %attend.1.rest_0_, bf16[256,1]{1,0:T(8,128)(2,1)S(1)} %reshape.64.rest_1_, ...), custom_call_target="tpu_custom_call" | custom-call | flops 1879048192 | bytes 4587520 | tf_op jit(solution)/shard_map/project/pallas_call | solution.py:456
  231.0 4.0 %collective-permute-done.35 = bf16[1,256,448]{2,1,0:T(8,128)(2,1)S(1)} collective-permute-done((bf16[1,256,448]{2,1,0:T(8,128)(2,1)S(1)}, bf16[1,256,448]{2,1,0:T(8,128)(2,1)S(1)}, u32[]{:S(2)}, u32[]{:S(2)}) %collective-permute-start.35) | collective-permute-done | bytes 229408 | tf_op jit(solution)/shard_map/ppermute | solution.py:20
  235.2 2.8 %project.6 = bf16[1,256,448]{2,1,0:T(8,128)(2,1)S(1)} custom-call(s32[1]{0:T(128)S(6)} %xor.38.turns, s32[5]{0:T(128)S(1)} %stack.64.place, bf16[256,1024]{1,0:T(8,128)(2,1)S(1)} %attend.1.rest_0_, bf16[256,1]{1,0:T(8,128)(2,1)S(1)} %reshape.64.rest_1_, bf16[2,448,1024]{2,1,0:T(8,128)(2,1)S(1)} %bitcast.50, ...), custom_call_target="tpu_custom_call" | custom-call | flops 469762048 | bytes 2064384 | tf_op jit(solution)/shard_map/project/pallas_call | solution.py:456
  238.7 2.8 %project.7 = bf16[1,256,448]{2,1,0:T(8,128)(2,1)S(1)} custom-call(s32[1]{0:T(128)S(6)} %xor.39.turns, s32[5]{0:T(128)S(1)} %stack.64.place, bf16[256,1024]{1,0:T(8,128)(2,1)S(1)} %attend.1.rest_0_, bf16[256,1]{1,0:T(8,128)(2,1)S(1)} %reshape.64.rest_1_, bf16[2,448,1024]{2,1,0:T(8,128)(2,1)S(1)} %bitcast.51, ...), custom_call_target="tpu_custom_call" | custom-call | flops 469762048 | bytes 2064384 | tf_op jit(solution)/shard_map/project/pallas_call | solution.py:456
  242.9 4.3 %collective-permute-done.33.rest_0_ = bf16[1,256,448]{2,1,0:T(8,128)(2,1)S(1)} collective-permute-done((bf16[1,256,448]{2,1,0:T(8,128)(2,1)S(1)}, bf16[1,256,448]{2,1,0:T(8,128)(2,1)S(1)}, u32[]{:S(2)}, u32[]{:S(2)}) %collective-permute-start.33) | collective-permute-done | bytes 229408 | tf_op jit(solution)/shard_map/ppermute | solution.py:20
  247.3 5.1 %collective-permute-done.34.rest_1_ = bf16[1,256,448]{2,1,0:T(8,128)(2,1)S(1)} collective-permute-done((bf16[1,256,448]{2,1,0:T(8,128)(2,1)S(1)}, bf16[1,256,448]{2,1,0:T(8,128)(2,1)S(1)}, u32[]{:S(2)}, u32[]{:S(2)}) %collective-permute-start.34) | collective-permute-done | bytes 229408 | tf_op jit(solution)/shard_map/ppermute | solution.py:20
  (147 shorter events, 44.1 us)
Async XLA Ops:
  2.3 51.2 %collective-permute-start.25 = (bf16[448,1024]{1,0:T(8,128)(2,1)}, bf16[448,1024]{1,0:T(8,128)(2,1)}, u32[]{:S(2)}, u32[]{:S(2)}) collective-permute-start(bf16[448,1024]{1,0:T(8,128)(2,1)} %dynamic-slice_bitcast_fusion), channel_id=1, source_target_pairs={{4,0},{0,4},{12,8},{8,12},{5,1},{1,5},{13,9},{9,13},{6,2},{2,6},{1... | collective-permute-start | bytes 2752520 | tf_op jit(solution)/shard_map/ppermute | solution.py:25
  5.4 57.2 %collective-permute-start.27 = (bf16[448,1024]{1,0:T(8,128)(2,1)}, bf16[448,1024]{1,0:T(8,128)(2,1)}, u32[]{:S(2)}, u32[]{:S(2)}) collective-permute-start(bf16[448,1024]{1,0:T(8,128)(2,1)} %dynamic-slice_bitcast_fusion), channel_id=1, source_target_pairs={{8,4},{4,8},{9,5},{5,9},{10,6},{6,10},{11,7},{7,11},{24,20},{20,24... | collective-permute-start | bytes 2752520 | tf_op jit(solution)/shard_map/ppermute | solution.py:25
  12.0 53.6 %collective-permute-start.2 = (bf16[2,448,1024]{2,1,0:T(8,128)(2,1)}, bf16[2,448,1024]{2,1,0:T(8,128)(2,1)}, u32[]{:S(2)}, u32[]{:S(2)}) collective-permute-start(bf16[2,448,1024]{2,1,0:T(8,128)(2,1)} %rest_4_.1), channel_id=1, source_target_pairs={{0,1},{1,0},{2,3},{3,2},{4,5},{5,4},{6,7},{7,6},{8,9},{9,8},{10,11... | collective-permute-start | bytes 5505032 | tf_op jit(solution)/shard_map/ppermute | solution.py:20
  12.0 19.2 %collective-permute-start.3 = (bf16[128,896]{1,0:T(8,128)(2,1)S(1)}, bf16[128,896]{1,0:T(8,128)(2,1)}, u32[]{:S(2)}, u32[]{:S(2)}) collective-permute-start(bf16[128,896]{1,0:T(8,128)(2,1)S(1)} %get-tuple-element.34), channel_id=1, source_target_pairs={{4,0},{0,4},{12,8},{8,12},{5,1},{1,5},{13,9},{9,13},{6,2},{2,6},{1... | collective-permute-start | bytes 688136 | tf_op jit(solution)/shard_map/ppermute | solution.py:25
  15.5 22.7 %collective-permute-start.5 = (bf16[128,896]{1,0:T(8,128)(2,1)S(1)}, bf16[128,896]{1,0:T(8,128)(2,1)}, u32[]{:S(2)}, u32[]{:S(2)}) collective-permute-start(bf16[128,896]{1,0:T(8,128)(2,1)S(1)} %get-tuple-element.36), channel_id=1, source_target_pairs={{12,0},{8,4},{4,8},{0,12},{13,1},{9,5},{5,9},{1,13},{14,2},{10,6},... | collective-permute-start | bytes 688136 | tf_op jit(solution)/shard_map/ppermute | solution.py:25
  31.2 22.2 %collective-permute-start = (bf16[2,448,256]{2,1,0:T(8,128)(2,1)S(1)}, bf16[2,448,256]{2,1,0:T(8,128)(2,1)S(1)}, u32[]{:S(2)}, u32[]{:S(2)}) collective-permute-start(bf16[2,448,256]{2,1,0:T(8,128)(2,1)S(1)} %constant_dynamic-slice_fusion.1.rest_0_), channel_id=1, source_target_pairs={{0,1},{1,0},{2,3},{3,2},{4,5},{5,4},{6,7},{7,6},{8,9},{9,8},{10,11... | collective-permute-start | bytes 1376264 | tf_op jit(solution)/shard_map/ppermute | solution.py:20
  38.2 13.1 %collective-permute-start.7 = (bf16[128,896]{1,0:T(8,128)(2,1)S(1)}, bf16[128,896]{1,0:T(8,128)(2,1)}, u32[]{:S(2)}, u32[]{:S(2)}) collective-permute-start(bf16[128,896]{1,0:T(8,128)(2,1)S(1)} %get-tuple-element.39), channel_id=1, source_target_pairs={{8,0},{12,4},{0,8},{4,12},{9,1},{13,5},{1,9},{5,13},{10,2},{14,6},... | collective-permute-start | bytes 688136 | tf_op jit(solution)/shard_map/ppermute | solution.py:25
  53.6 32.8 %collective-permute-start.26 = (bf16[448,1024]{1,0:T(8,128)(2,1)}, bf16[448,1024]{1,0:T(8,128)(2,1)}, u32[]{:S(2)}, u32[]{:S(2)}) collective-permute-start(bf16[448,1024]{1,0:T(8,128)(2,1)} %collective-permute-done.25.rest_5_.rest_3_), channel_id=1, source_target_pairs={{8,4},{4,8},{9,5},{5,9},{10,6},{6,10},{11,7},{7,11},{24,20},{20,24... | collective-permute-start | bytes 2752520 | tf_op jit(solution)/shard_map/ppermute | solution.py:25
  62.0 15.5 %collective-permute-start.4 = (bf16[128,896]{1,0:T(8,128)(2,1)}, bf16[128,896]{1,0:T(8,128)(2,1)S(1)}, u32[]{:S(2)}, u32[]{:S(2)}) collective-permute-start(bf16[128,896]{1,0:T(8,128)(2,1)} %collective-permute-done.3.rest_6_), channel_id=1, source_target_pairs={{0,2},{2,0},{1,3},{3,1},{4,6},{6,4},{5,7},{7,5},{8,10},{10,8},{9,1... | collective-permute-start | bytes 688136 | tf_op jit(solution)/shard_map/ppermute | solution.py:20
  62.6 73.8 %collective-permute-start.28 = (bf16[448,1024]{1,0:T(8,128)(2,1)}, bf16[448,1024]{1,0:T(8,128)(2,1)S(1)}, u32[]{:S(2)}, u32[]{:S(2)}) collective-permute-start(bf16[448,1024]{1,0:T(8,128)(2,1)} %collective-permute-done.27), channel_id=1, source_target_pairs={{4,0},{8,12},{5,1},{9,13},{6,2},{10,14},{7,3},{11,15},{20,16},{24,... | collective-permute-start | bytes 2752520 | tf_op jit(solution)/shard_map/ppermute | solution.py:25
  73.1 27.5 %collective-permute-start.9 = (bf16[256,1024]{1,0:T(8,128)(2,1)S(1)}, bf16[256,1024]{1,0:T(8,128)(2,1)S(1)}, u32[]{:S(2)}, u32[]{:S(2)}) collective-permute-start(bf16[256,1024]{1,0:T(8,128)(2,1)S(1)} %get-tuple-element.43), channel_id=1, source_target_pairs={{0,4},{12,8},{1,5},{13,9},{2,6},{14,10},{3,7},{15,11},{16,20},{28,... | collective-permute-start | bytes 1572872 | tf_op jit(solution)/shard_map/ppermute | solution.py:25
  76.1 23.5 %collective-permute-start.14 = (bf16[2,256,512]{2,1,0:T(8,128)(2,1)S(1)}, bf16[2,256,512]{2,1,0:T(8,128)(2,1)S(1)}, u32[]{:S(2)}, u32[]{:S(2)}) collective-permute-start(bf16[2,256,512]{2,1,0:T(8,128)(2,1)S(1)} %bitcast.52), channel_id=1, source_target_pairs={{0,4},{12,8},{1,5},{13,9},{2,6},{14,10},{3,7},{15,11},{16,20},{28,... | collective-permute-start | bytes 1572872 | tf_op jit(solution)/shard_map/ppermute | solution.py:25
  84.8 22.1 %collective-permute-start.12 = (bf16[256,1024]{1,0:T(8,128)(2,1)S(1)}, bf16[256,1024]{1,0:T(8,128)(2,1)S(1)}, u32[]{:S(2)}, u32[]{:S(2)}) collective-permute-start(bf16[256,1024]{1,0:T(8,128)(2,1)S(1)} %get-tuple-element.44), channel_id=1, source_target_pairs={{0,4},{12,8},{1,5},{13,9},{2,6},{14,10},{3,7},{15,11},{16,20},{28,... | collective-permute-start | bytes 1572872 | tf_op jit(solution)/shard_map/ppermute | solution.py:25
  86.3 53.3 %collective-permute-start.29 = (bf16[448,1024]{1,0:T(8,128)(2,1)}, bf16[448,1024]{1,0:T(8,128)(2,1)S(1)}, u32[]{:S(2)}, u32[]{:S(2)}) collective-permute-start(bf16[448,1024]{1,0:T(8,128)(2,1)} %collective-permute-done.26), channel_id=1, source_target_pairs={{4,0},{8,12},{5,1},{9,13},{6,2},{10,14},{7,3},{11,15},{20,16},{24,... | collective-permute-start | bytes 2752520 | tf_op jit(solution)/shard_map/ppermute | solution.py:25
  100.8 18.4 %collective-permute-start.10 = (bf16[256,1024]{1,0:T(8,128)(2,1)S(1)}, bf16[256,1024]{1,0:T(8,128)(2,1)S(1)}, u32[]{:S(2)}, u32[]{:S(2)}) collective-permute-start(bf16[256,1024]{1,0:T(8,128)(2,1)S(1)} %fusion.2), channel_id=1, source_target_pairs={{8,4},{4,8},{9,5},{5,9},{10,6},{6,10},{11,7},{7,11},{24,20},{20,24... | collective-permute-start | bytes 1572872 | tf_op jit(solution)/shard_map/ppermute | solution.py:25
  107.1 34.7 %collective-permute-start.13 = (bf16[256,1024]{1,0:T(8,128)(2,1)S(1)}, bf16[256,1024]{1,0:T(8,128)(2,1)S(1)}, u32[]{:S(2)}, u32[]{:S(2)}) collective-permute-start(bf16[256,1024]{1,0:T(8,128)(2,1)S(1)} %fusion.1), channel_id=1, source_target_pairs={{8,4},{4,8},{9,5},{5,9},{10,6},{6,10},{11,7},{7,11},{24,20},{20,24... | collective-permute-start | bytes 1572872 | tf_op jit(solution)/shard_map/ppermute | solution.py:25
  108.1 28.1 %collective-permute-start.16 = (bf16[256,512]{1,0:T(8,128)(2,1)S(1)}, bf16[256,512]{1,0:T(8,128)(2,1)S(1)}, u32[]{:S(2)}, u32[]{:S(2)}) collective-permute-start(bf16[256,512]{1,0:T(8,128)(2,1)S(1)} %fusion.4), channel_id=1, source_target_pairs={{4,0},{0,4},{12,8},{8,12},{5,1},{1,5},{13,9},{9,13},{6,2},{2,6},{1... | collective-permute-start | bytes 786440 | tf_op jit(solution)/shard_map/ppermute | solution.py:25
  119.4 36.3 %collective-permute-start.11 = (bf16[256,1024]{1,0:T(8,128)(2,1)S(1)}, bf16[256,1024]{1,0:T(8,128)(2,1)S(1)}, u32[]{:S(2)}, u32[]{:S(2)}) collective-permute-start(bf16[256,1024]{1,0:T(8,128)(2,1)S(1)} %add_convert_fusion.1), channel_id=1, source_target_pairs={{4,0},{0,4},{12,8},{8,12},{5,1},{1,5},{13,9},{9,13},{6,2},{2,6},{1... | collective-permute-start | bytes 1572872 | tf_op jit(solution)/shard_map/ppermute | solution.py:25
  136.3 12.7 %collective-permute-start.17 = (bf16[256,512]{1,0:T(8,128)(2,1)S(1)}, bf16[256,512]{1,0:T(8,128)(2,1)S(1)}, u32[]{:S(2)}, u32[]{:S(2)}) collective-permute-start(bf16[256,512]{1,0:T(8,128)(2,1)S(1)} %fusion.3.rest_3_), channel_id=1, source_target_pairs={{4,0},{0,4},{12,8},{8,12},{5,1},{1,5},{13,9},{9,13},{6,2},{2,6},{1... | collective-permute-start | bytes 786440 | tf_op jit(solution)/shard_map/ppermute | solution.py:25
  136.4 12.6 %collective-permute-start.18 = (bf16[256,512]{1,0:T(8,128)(2,1)S(1)}, bf16[256,512]{1,0:T(8,128)(2,1)}, u32[]{:S(2)}, u32[]{:S(2)}) collective-permute-start(bf16[256,512]{1,0:T(8,128)(2,1)S(1)} %fusion.3.rest_3_), channel_id=1, source_target_pairs={{8,0},{12,4},{0,8},{4,12},{9,1},{13,5},{1,9},{5,13},{10,2},{14,6},... | collective-permute-start | bytes 786440 | tf_op jit(solution)/shard_map/ppermute | solution.py:25
  139.6 15.0 %collective-permute-start.19 = (bf16[256,512]{1,0:T(8,128)(2,1)S(1)}, bf16[256,512]{1,0:T(8,128)(2,1)}, u32[]{:S(2)}, u32[]{:S(2)}) collective-permute-start(bf16[256,512]{1,0:T(8,128)(2,1)S(1)} %fusion.3.rest_3_), channel_id=1, source_target_pairs={{12,0},{8,4},{4,8},{0,12},{13,1},{9,5},{5,9},{1,13},{14,2},{10,6},... | collective-permute-start | bytes 786440 | tf_op jit(solution)/shard_map/ppermute | solution.py:25
  141.8 15.5 %collective-permute-start.20 = (bf16[256,512]{1,0:T(8,128)(2,1)S(1)}, bf16[256,512]{1,0:T(8,128)(2,1)S(1)}, u32[]{:S(2)}, u32[]{:S(2)}) collective-permute-start(bf16[256,512]{1,0:T(8,128)(2,1)S(1)} %fusion.3.rest_3_), channel_id=1, source_target_pairs={{0,1},{1,0},{2,3},{3,2},{4,5},{5,4},{6,7},{7,6},{8,9},{9,8},{10,11... | collective-permute-start | bytes 786440 | tf_op jit(solution)/shard_map/ppermute | solution.py:20
  148.9 8.8 %collective-permute-start.21 = (bf16[256,512]{1,0:T(8,128)(2,1)S(1)}, bf16[256,512]{1,0:T(8,128)(2,1)S(1)}, u32[]{:S(2)}, u32[]{:S(2)}) collective-permute-start(bf16[256,512]{1,0:T(8,128)(2,1)S(1)} %collective-permute-done.17.rest_4_), channel_id=1, source_target_pairs={{0,1},{1,0},{2,3},{3,2},{4,5},{5,4},{6,7},{7,6},{8,9},{9,8},{10,11... | collective-permute-start | bytes 786440 | tf_op jit(solution)/shard_map/ppermute | solution.py:20
  148.9 11.2 %collective-permute-start.22 = (bf16[256,512]{1,0:T(8,128)(2,1)}, bf16[256,512]{1,0:T(8,128)(2,1)S(1)}, u32[]{:S(2)}, u32[]{:S(2)}) collective-permute-start(bf16[256,512]{1,0:T(8,128)(2,1)} %collective-permute-done.18.rest_5_), channel_id=1, source_target_pairs={{0,1},{1,0},{2,3},{3,2},{4,5},{5,4},{6,7},{7,6},{8,9},{9,8},{10,11... | collective-permute-start | bytes 786440 | tf_op jit(solution)/shard_map/ppermute | solution.py:20
  155.7 23.6 %collective-permute-start.30 = (bf16[448,1024]{1,0:T(8,128)(2,1)}, bf16[448,1024]{1,0:T(8,128)(2,1)}, u32[]{:S(2)}, u32[]{:S(2)}) collective-permute-start(bf16[448,1024]{1,0:T(8,128)(2,1)} %collective-permute-done.25.rest_5_.rest_3_), channel_id=1, source_target_pairs={{0,16},{16,0},{1,17},{17,1},{2,18},{18,2},{3,19},{19,3},{4,20},{20... | collective-permute-start | bytes 2752520 | tf_op jit(solution)/shard_map/ppermute | solution.py:20
  157.3 41.7 %collective-permute-start.31 = (bf16[448,1024]{1,0:T(8,128)(2,1)}, bf16[448,1024]{1,0:T(8,128)(2,1)}, u32[]{:S(2)}, u32[]{:S(2)}) collective-permute-start(bf16[448,1024]{1,0:T(8,128)(2,1)} %broadcast_select_fusion.1.rest_6_.rest_4_), channel_id=1, source_target_pairs={{0,16},{16,0},{1,17},{17,1},{2,18},{18,2},{3,19},{19,3},{4,20},{20... | collective-permute-start | bytes 2752520 | tf_op jit(solution)/shard_map/ppermute | solution.py:20
  158.7 59.5 %collective-permute-start.32 = (bf16[448,1024]{1,0:T(8,128)(2,1)}, bf16[448,1024]{1,0:T(8,128)(2,1)}, u32[]{:S(2)}, u32[]{:S(2)}) collective-permute-start(bf16[448,1024]{1,0:T(8,128)(2,1)} %broadcast_select_fusion.rest_7_.rest_5_), channel_id=1, source_target_pairs={{0,16},{16,0},{1,17},{17,1},{2,18},{18,2},{3,19},{19,3},{4,20},{20... | collective-permute-start | bytes 2752520 | tf_op jit(solution)/shard_map/ppermute | solution.py:20
  169.3 48.9 %collective-permute-start.24 = (bf16[256,1024]{1,0:T(8,128)(2,1)S(1)}, bf16[256,1024]{1,0:T(8,128)(2,1)}, u32[]{:S(2)}, u32[]{:S(2)}) collective-permute-start(bf16[256,1024]{1,0:T(8,128)(2,1)S(1)} %attend.1.rest_0_), channel_id=1, source_target_pairs={{0,1},{1,0},{2,3},{3,2},{4,5},{5,4},{6,7},{7,6},{8,9},{9,8},{10,11... | collective-permute-start | bytes 1572872 | tf_op jit(solution)/shard_map/ppermute | solution.py:20
  221.4 9.5 %collective-permute-start.36 = (bf16[1,256,448]{2,1,0:T(8,128)(2,1)S(1)}, bf16[1,256,448]{2,1,0:T(8,128)(2,1)S(1)}, u32[]{:S(2)}, u32[]{:S(2)}) collective-permute-start(bf16[1,256,448]{2,1,0:T(8,128)(2,1)S(1)} %project.9), channel_id=1, source_target_pairs={{0,2},{2,0},{1,3},{3,1},{4,6},{6,4},{5,7},{7,5},{8,10},{10,8},{9,1... | collective-permute-start | bytes 688136 | tf_op jit(solution)/shard_map/ppermute | solution.py:20
  235.1 17.2 %collective-permute-start.37 = (bf16[2,256,448]{2,1,0:T(8,128)(2,1)S(1)}, bf16[2,256,448]{2,1,0:T(8,128)(2,1)S(1)}, u32[]{:S(2)}, u32[]{:S(2)}) collective-permute-start(bf16[2,256,448]{2,1,0:T(8,128)(2,1)S(1)} %add_convert_fusion), channel_id=1, source_target_pairs={{0,1},{1,0},{2,3},{3,2},{4,5},{5,4},{6,7},{7,6},{8,9},{9,8},{10,11... | collective-permute-start | bytes 1376264 | tf_op jit(solution)/shard_map/ppermute | solution.py:20
  238.0 9.2 %collective-permute-start.33 = (bf16[1,256,448]{2,1,0:T(8,128)(2,1)S(1)}, bf16[1,256,448]{2,1,0:T(8,128)(2,1)S(1)}, u32[]{:S(2)}, u32[]{:S(2)}) collective-permute-start(bf16[1,256,448]{2,1,0:T(8,128)(2,1)S(1)} %project.6), channel_id=1, source_target_pairs={{0,2},{2,0},{1,3},{3,1},{4,6},{6,4},{5,7},{7,5},{8,10},{10,8},{9,1... | collective-permute-start | bytes 688136 | tf_op jit(solution)/shard_map/ppermute | solution.py:20
  241.5 10.9 %collective-permute-start.34 = (bf16[1,256,448]{2,1,0:T(8,128)(2,1)S(1)}, bf16[1,256,448]{2,1,0:T(8,128)(2,1)S(1)}, u32[]{:S(2)}, u32[]{:S(2)}) collective-permute-start(bf16[1,256,448]{2,1,0:T(8,128)(2,1)S(1)} %project.7), channel_id=1, source_target_pairs={{0,2},{2,0},{1,3},{3,1},{4,6},{6,4},{5,7},{7,5},{8,10},{10,8},{9,1... | collective-permute-start | bytes 688136 | tf_op jit(solution)/shard_map/ppermute | solution.py:20
  (32 other events, 381.5 us)

commit v11 on v10

--- a/solution.py
+++ b/solution.py
@@ -376,8 +376,7 @@
         functools.partial(attention_kernel, len(query)),
         out_shape=jax.ShapeDtypeStruct((rows, width), jnp.bfloat16),
         in_specs=[SMEM, SMEM, VMEM]
-        + [HBM] * (len(query) + count // 2 + 1)
-        + [VMEM] * (count // 2 - 1),
+        + [HBM] * (len(query) + count),
         out_specs=VMEM,
         scratch_shapes=[
             *[pltpu.VMEM((rows, width), term.dtype) for term in query],
@@ -401,8 +400,7 @@
         starts,
         limits,
         span,
-        *[in_hbm(array) for array in (*query, *kv[: count // 2 + 1])],
-        *kv[count // 2 + 1 :],
+        *[in_hbm(array) for array in (*query, *kv)],
     )
 
 

time: 255 us -> 255 us (level)
  local copies, waits for them, and re-layouts: 11.8 us -> 6.75 us
  waiting for transfers between devices: 122 us -> 127 us
    unnamed x52 -> x46, local copies, waits for them, and re-layouts: 7.45 us -> 2.42 us
    ppermute x19, waiting for transfers between devices: 64.9 us -> 69.8 us  [swap(): return lax.ppermute(x, axis, [(0, 1), (1, 0)])]
where the time goes in v11:
time: 255 us; the launch traced here: 254 us
  waiting for transfers between devices  127 us (50%)
  starting transfers between devices  69.7 us (27%)
  Pallas kernels  40.9 us (16%)
  other arithmetic  7.23 us (3%)
  local copies, waits for them, and re-layouts  6.75 us (3%)
    ppermute x19, waiting for transfers between devices, swap(): return lax.ppermute(x, axis, [(0, 1), (1, 0)])  69.8 us
    ppermute x19, waiting for transfers between devices, cross(): return lax.ppermute(x, axis, [(i ^ bit, i) for i in among or range(size)])  57.4 us
    ppermute x19, starting transfers between devices, cross(): return lax.ppermute(x, axis, [(i ^ bit, i) for i in among or range(size)])  56.6 us
    pallas_call x5, Pallas kernels, project(): pl.pallas_call(functools.partial(project_kernel, (len(weights) + 1) // 2,...  16.6 us
    pallas_call x2, Pallas kernels, partial(): pl.pallas_call(functools.partial(partial_kernel, counts, narrow), out_sha...  14.8 us
    ppermute x19, starting transfers between devices, swap(): return lax.ppermute(x, axis, [(0, 1), (1, 0)])  13.1 us
  transfers between devices with their start and end apart: 38, of which 15 were waited for; matrix products, arithmetic and copies ran while one was open for 4% of the time, Pallas kernels for 14%

profile of v11, /device:TPU:0, one launch (start us, length us, event | category | flops | bytes accessed | tf_op | source)
XLA Modules:
  0.0 253.9 jit_solution(5224565223612005862)
XLA Ops:
  0.0 2.3 dynamic-slice_bitcast_fusion
  2.3 3.1 %collective-permute-start.25 = (bf16[448,1024]{1,0:T(8,128)(2,1)}, bf16[448,1024]{1,0:T(8,128)(2,1)}, u32[]{:S(2)}, u32[]{:S(2)}) collective-permute-start(bf16[448,1024]{1,0:T(8,128)(2,1)} %dynamic-slice_bitcast_fusion), channel_id=1, source_target_pairs={{4,0},{0,4},{12,8},{8,12},{5,1},{1,5},{13,9},{9,13},{6,2},{2,6},{1... | collective-permute-start | bytes 2752520 | tf_op jit(solution)/shard_map/ppermute | solution.py:25
  8.5 2.7 %norm.1 = (bf16[256,896]{1,0:T(8,128)(2,1)S(1)}, bf16[128,896]{1,0:T(8,128)(2,1)S(1)}, bf16[128,896]{1,0:T(8,128)(2,1)S(1)}, bf16[128,896]{1,0:T(8,128)(2,1)S(1)}) custom-call(s32[5]{0:T(128)S(1)} %stack.64.place, s32[2048]{0:T(1024)S(1)} %copy-done.2, bf16[256,3584]{1,0:T(8,128)(2,1)} %tokens_ref.1, f32[2,3584]{1,0:T(2,128)S(1)} %copy-done.4), custom_call_target="tpu_custom_call" | custom-call | flops 5505024 | bytes 3670016 | tf_op jit(solution)/shard_map/norm/pallas_call | solution.py:85
  12.0 3.5 %collective-permute-start.3 = (bf16[128,896]{1,0:T(8,128)(2,1)S(1)}, bf16[128,896]{1,0:T(8,128)(2,1)}, u32[]{:S(2)}, u32[]{:S(2)}) collective-permute-start(bf16[128,896]{1,0:T(8,128)(2,1)S(1)} %get-tuple-element.34), channel_id=1, source_target_pairs={{4,0},{0,4},{12,8},{8,12},{5,1},{1,5},{13,9},{9,13},{6,2},{2,6},{1... | collective-permute-start | bytes 688136 | tf_op jit(solution)/shard_map/ppermute | solution.py:25
  20.3 11.0 %collective-permute-done.3.rest_6_ = bf16[128,896]{1,0:T(8,128)(2,1)} collective-permute-done((bf16[128,896]{1,0:T(8,128)(2,1)S(1)}, bf16[128,896]{1,0:T(8,128)(2,1)}, u32[]{:S(2)}, u32[]{:S(2)}) %collective-permute-start.3) | collective-permute-done | bytes 229408 | tf_op jit(solution)/shard_map/ppermute | solution.py:25
  31.2 6.9 %collective-permute-done.5.rest_6_ = bf16[128,896]{1,0:T(8,128)(2,1)} collective-permute-done((bf16[128,896]{1,0:T(8,128)(2,1)S(1)}, bf16[128,896]{1,0:T(8,128)(2,1)}, u32[]{:S(2)}, u32[]{:S(2)}) %collective-permute-start.5) | collective-permute-done | bytes 229408 | tf_op jit(solution)/shard_map/ppermute | solution.py:25
  38.2 3.6 %collective-permute-start.7 = (bf16[128,896]{1,0:T(8,128)(2,1)S(1)}, bf16[128,896]{1,0:T(8,128)(2,1)}, u32[]{:S(2)}, u32[]{:S(2)}) collective-permute-start(bf16[128,896]{1,0:T(8,128)(2,1)S(1)} %get-tuple-element.39), channel_id=1, source_target_pairs={{8,0},{12,4},{0,8},{4,12},{9,1},{13,5},{1,9},{5,13},{10,2},{14,6},... | collective-permute-start | bytes 688136 | tf_op jit(solution)/shard_map/ppermute | solution.py:25
  41.9 9.4 %collective-permute-done.7.rest_8_ = bf16[128,896]{1,0:T(8,128)(2,1)} collective-permute-done((bf16[128,896]{1,0:T(8,128)(2,1)S(1)}, bf16[128,896]{1,0:T(8,128)(2,1)}, u32[]{:S(2)}, u32[]{:S(2)}) %collective-permute-start.7) | collective-permute-done | bytes 229408 | tf_op jit(solution)/shard_map/ppermute | solution.py:25
  55.2 2.6 %collective-permute-done.6.rest_7_ = bf16[128,896]{1,0:T(8,128)(2,1)S(1)} collective-permute-done((bf16[128,896]{1,0:T(8,128)(2,1)}, bf16[128,896]{1,0:T(8,128)(2,1)S(1)}, u32[]{:S(2)}, u32[]{:S(2)}) %collective-permute-start.6) | collective-permute-done | bytes 229408 | tf_op jit(solution)/shard_map/ppermute | solution.py:20
  59.3 2.4 pad_add_fusion.limits
  65.7 7.5 %partial.3 = (f32[512,512]{1,0:T(8,128)}, f32[512,1024]{1,0:T(8,128)}, bf16[512,512]{1,0:T(8,128)(2,1)S(1)}, bf16[256,1024]{1,0:T(8,128)(2,1)S(1)}, bf16[256,1024]{1,0:T(8,128)(2,1)S(1)}) custom-call(s32[5]{0:T(128)S(1)} %stack.64.place, s32[2048]{0:T(1024)S(1)} %copy-done.3, s32[2]{0:T(128)S(1)} %pad_add_fusion.2.begins, bf16[2,448,256]{2,1,0:T(8,128)(2,1)} %copy-done.10, ...), custom_call_target="tpu_custom_call" | custom-call | flops 2818572288 | bytes 8650752 | tf_op jit(solution)/shard_map/partial/pallas_call | solution.py:187
  73.2 2.7 %collective-permute-start.9 = (bf16[256,1024]{1,0:T(8,128)(2,1)S(1)}, bf16[256,1024]{1,0:T(8,128)(2,1)S(1)}, u32[]{:S(2)}, u32[]{:S(2)}) collective-permute-start(bf16[256,1024]{1,0:T(8,128)(2,1)S(1)} %get-tuple-element.43), channel_id=1, source_target_pairs={{0,4},{12,8},{1,5},{13,9},{2,6},{14,10},{3,7},{15,11},{16,20},{28,... | collective-permute-start | bytes 1572872 | tf_op jit(solution)/shard_map/ppermute | solution.py:25
  77.4 7.3 %partial.2 = (f32[512,512]{1,0:T(8,128)}, f32[512,1024]{1,0:T(8,128)}) custom-call(s32[5]{0:T(128)S(1)} %stack.64.place, s32[2048]{0:T(1024)S(1)} %copy-done.3, s32[2]{0:T(128)S(1)} %pad_add_fusion.1.begins, bf16[2,448,256]{2,1,0:T(8,128)(2,1)} %copy-done.10, bf16[2,448,256]{2,1,0:T(8,128)(2,1)} %copy-done.17, bf16[2,448,256]{2,1,0:T(8,128)(2,1)} %copy-done.11, ...), custom_call_target="tpu_custom_call" | custom-call | flops 2818572288 | bytes 8650752 | tf_op jit(solution)/shard_map/partial/pallas_call | solution.py:187
  87.6 11.9 %collective-permute-done.14 = bf16[2,256,512]{2,1,0:T(8,128)(2,1)S(1)} collective-permute-done((bf16[2,256,512]{2,1,0:T(8,128)(2,1)S(1)}, bf16[2,256,512]{2,1,0:T(8,128)(2,1)S(1)}, u32[]{:S(2)}, u32[]{:S(2)}) %collective-permute-start.14) | collective-permute-done | bytes 524320 | tf_op jit(solution)/shard_map/ppermute | solution.py:25
  101.5 5.3 %collective-permute-done.12 = bf16[256,1024]{1,0:T(8,128)(2,1)S(1)} collective-permute-done((bf16[256,1024]{1,0:T(8,128)(2,1)S(1)}, bf16[256,1024]{1,0:T(8,128)(2,1)S(1)}, u32[]{:S(2)}, u32[]{:S(2)}) %collective-permute-start.12) | collective-permute-done | bytes 524320 | tf_op jit(solution)/shard_map/ppermute | solution.py:25
  108.0 11.1 %collective-permute-start.16 = (bf16[256,512]{1,0:T(8,128)(2,1)S(1)}, bf16[256,512]{1,0:T(8,128)(2,1)S(1)}, u32[]{:S(2)}, u32[]{:S(2)}) collective-permute-start(bf16[256,512]{1,0:T(8,128)(2,1)S(1)} %fusion.4), channel_id=1, source_target_pairs={{4,0},{0,4},{12,8},{8,12},{5,1},{1,5},{13,9},{9,13},{6,2},{2,6},{1... | collective-permute-start | bytes 786440 | tf_op jit(solution)/shard_map/ppermute | solution.py:25
  119.3 16.1 %collective-permute-start.11 = (bf16[256,1024]{1,0:T(8,128)(2,1)S(1)}, bf16[256,1024]{1,0:T(8,128)(2,1)S(1)}, u32[]{:S(2)}, u32[]{:S(2)}) collective-permute-start(bf16[256,1024]{1,0:T(8,128)(2,1)S(1)} %add_convert_fusion.1), channel_id=1, source_target_pairs={{4,0},{0,4},{12,8},{8,12},{5,1},{1,5},{13,9},{9,13},{6,2},{2,6},{1... | collective-permute-start | bytes 1572872 | tf_op jit(solution)/shard_map/ppermute | solution.py:25
  135.5 3.9 %collective-permute-start.18 = (bf16[256,512]{1,0:T(8,128)(2,1)S(1)}, bf16[256,512]{1,0:T(8,128)(2,1)S(1)}, u32[]{:S(2)}, u32[]{:S(2)}) collective-permute-start(bf16[256,512]{1,0:T(8,128)(2,1)S(1)} %fusion.3.rest_3_), channel_id=1, source_target_pairs={{8,0},{12,4},{0,8},{4,12},{9,1},{13,5},{1,9},{5,13},{10,2},{14,6},... | collective-permute-start | bytes 786440 | tf_op jit(solution)/shard_map/ppermute | solution.py:25
  141.0 7.1 %collective-permute-done.17.rest_4_ = bf16[256,512]{1,0:T(8,128)(2,1)S(1)} collective-permute-done((bf16[256,512]{1,0:T(8,128)(2,1)S(1)}, bf16[256,512]{1,0:T(8,128)(2,1)S(1)}, u32[]{:S(2)}, u32[]{:S(2)}) %collective-permute-start.17) | collective-permute-done | bytes 262176 | tf_op jit(solution)/shard_map/ppermute | solution.py:25
  148.6 5.8 %collective-permute-done.19.rest_6_ = bf16[256,512]{1,0:T(8,128)(2,1)S(1)} collective-permute-done((bf16[256,512]{1,0:T(8,128)(2,1)S(1)}, bf16[256,512]{1,0:T(8,128)(2,1)S(1)}, u32[]{:S(2)}, u32[]{:S(2)}) %collective-permute-start.19) | collective-permute-done | bytes 262176 | tf_op jit(solution)/shard_map/ppermute | solution.py:25
  159.3 5.1 %attend.1.rest_0_ = bf16[256,1024]{1,0:T(8,128)(2,1)S(1)} custom-call(s32[8]{0:T(128)S(1)} %stack.72.starts, s32[4]{0:T(128)S(1)} %pad_add_fusion.limits, s32[8,256]{1,0:T(8,128)S(1)} %add_add_fusion.span_ref, f32[2,256,1024]{2,1,0:T(8,128)} %bitcast.56, bf16[256,1024]{1,0:T(8,128)(2,1)} %copy-done.16, bf16[256,1024]{1,0:T(8,128)(2,1)} %copy-done.15, ...), custom_call_target="tpu_custom_call" | custom-call | flops 2147483648 | bytes 3145728 | tf_op jit(solution)/shard_map/attend/pallas_call | solution.py:375
  166.2 12.8 %collective-permute-done.30.rest_8_.rest_6_ = bf16[448,1024]{1,0:T(8,128)(2,1)} collective-permute-done((bf16[448,1024]{1,0:T(8,128)(2,1)}, bf16[448,1024]{1,0:T(8,128)(2,1)}, u32[]{:S(2)}, u32[]{:S(2)}) %collective-permute-start.30) | collective-permute-done | bytes 917536 | tf_op jit(solution)/shard_map/ppermute | solution.py:20
  179.1 19.7 %collective-permute-done.31.rest_9_.rest_7_ = bf16[448,1024]{1,0:T(8,128)(2,1)} collective-permute-done((bf16[448,1024]{1,0:T(8,128)(2,1)}, bf16[448,1024]{1,0:T(8,128)(2,1)}, u32[]{:S(2)}, u32[]{:S(2)}) %collective-permute-start.31) | collective-permute-done | bytes 917536 | tf_op jit(solution)/shard_map/ppermute | solution.py:20
  198.7 19.2 %collective-permute-done.32.rest_10_.rest_8_ = bf16[448,1024]{1,0:T(8,128)(2,1)} collective-permute-done((bf16[448,1024]{1,0:T(8,128)(2,1)}, bf16[448,1024]{1,0:T(8,128)(2,1)}, u32[]{:S(2)}, u32[]{:S(2)}) %collective-permute-start.32) | collective-permute-done | bytes 917536 | tf_op jit(solution)/shard_map/ppermute | solution.py:20
  217.9 3.3 %project.9 = bf16[1,256,448]{2,1,0:T(8,128)(2,1)S(1)} custom-call(s32[1]{0:T(128)S(6)} %xor.39.turns, s32[5]{0:T(128)S(1)} %stack.64.place, bf16[256,1024]{1,0:T(8,128)(2,1)} %collective-permute-done.24.rest_2_.rest_0_, bf16[256,1]{1,0:T(8,128)(2,1)S(1)} %reshape.65.rest_3_.rest_1_, bf16[2,448,1024]{2,1,0:T(8,128)(2,1)S(1)} %bitcast.47, ...), custom_call_target="tpu_custom_call" | custom-call | flops 469762048 | bytes 2064384 | tf_op jit(solution)/shard_map/project/pallas_call | solution.py:454
  222.8 3.3 %project.8 = bf16[1,256,448]{2,1,0:T(8,128)(2,1)S(1)} custom-call(s32[1]{0:T(128)S(6)} %xor.38.turns, s32[5]{0:T(128)S(1)} %stack.64.place, bf16[256,1024]{1,0:T(8,128)(2,1)} %collective-permute-done.24.rest_2_.rest_0_, bf16[256,1]{1,0:T(8,128)(2,1)S(1)} %reshape.65.rest_3_.rest_1_, bf16[2,448,1024]{2,1,0:T(8,128)(2,1)S(1)} %bitcast.48, ...), custom_call_target="tpu_custom_call" | custom-call | flops 469762048 | bytes 2064384 | tf_op jit(solution)/shard_map/project/pallas_call | solution.py:454
  226.2 4.5 %project.5 = (bf16[2,256,448]{2,1,0:T(8,128)(2,1)S(1)}, bf16[2,256,448]{2,1,0:T(8,128)(2,1)S(1)}) custom-call(s32[2]{0:T(128)S(1)} %add_xor_fusion.turns, s32[5]{0:T(128)S(1)} %stack.64.place, bf16[256,1024]{1,0:T(8,128)(2,1)S(1)} %attend.1.rest_0_, bf16[256,1]{1,0:T(8,128)(2,1)S(1)} %reshape.64.rest_1_, ...), custom_call_target="tpu_custom_call" | custom-call | flops 1879048192 | bytes 4587520 | tf_op jit(solution)/shard_map/project/pallas_call | solution.py:454
  230.8 4.0 %collective-permute-done.35 = bf16[1,256,448]{2,1,0:T(8,128)(2,1)S(1)} collective-permute-done((bf16[1,256,448]{2,1,0:T(8,128)(2,1)S(1)}, bf16[1,256,448]{2,1,0:T(8,128)(2,1)S(1)}, u32[]{:S(2)}, u32[]{:S(2)}) %collective-permute-start.35) | collective-permute-done | bytes 229408 | tf_op jit(solution)/shard_map/ppermute | solution.py:20
  235.0 2.8 %project.6 = bf16[1,256,448]{2,1,0:T(8,128)(2,1)S(1)} custom-call(s32[1]{0:T(128)S(6)} %xor.38.turns, s32[5]{0:T(128)S(1)} %stack.64.place, bf16[256,1024]{1,0:T(8,128)(2,1)S(1)} %attend.1.rest_0_, bf16[256,1]{1,0:T(8,128)(2,1)S(1)} %reshape.64.rest_1_, bf16[2,448,1024]{2,1,0:T(8,128)(2,1)S(1)} %bitcast.50, ...), custom_call_target="tpu_custom_call" | custom-call | flops 469762048 | bytes 2064384 | tf_op jit(solution)/shard_map/project/pallas_call | solution.py:454
  238.5 2.8 %project.7 = bf16[1,256,448]{2,1,0:T(8,128)(2,1)S(1)} custom-call(s32[1]{0:T(128)S(6)} %xor.39.turns, s32[5]{0:T(128)S(1)} %stack.64.place, bf16[256,1024]{1,0:T(8,128)(2,1)S(1)} %attend.1.rest_0_, bf16[256,1]{1,0:T(8,128)(2,1)S(1)} %reshape.64.rest_1_, bf16[2,448,1024]{2,1,0:T(8,128)(2,1)S(1)} %bitcast.51, ...), custom_call_target="tpu_custom_call" | custom-call | flops 469762048 | bytes 2064384 | tf_op jit(solution)/shard_map/project/pallas_call | solution.py:454
  242.7 4.3 %collective-permute-done.33.rest_0_ = bf16[1,256,448]{2,1,0:T(8,128)(2,1)S(1)} collective-permute-done((bf16[1,256,448]{2,1,0:T(8,128)(2,1)S(1)}, bf16[1,256,448]{2,1,0:T(8,128)(2,1)S(1)}, u32[]{:S(2)}, u32[]{:S(2)}) %collective-permute-start.33) | collective-permute-done | bytes 229408 | tf_op jit(solution)/shard_map/ppermute | solution.py:20
  247.0 5.1 %collective-permute-done.34.rest_1_ = bf16[1,256,448]{2,1,0:T(8,128)(2,1)S(1)} collective-permute-done((bf16[1,256,448]{2,1,0:T(8,128)(2,1)S(1)}, bf16[1,256,448]{2,1,0:T(8,128)(2,1)S(1)}, u32[]{:S(2)}, u32[]{:S(2)}) %collective-permute-start.34) | collective-permute-done | bytes 229408 | tf_op jit(solution)/shard_map/ppermute | solution.py:20
  (141 shorter events, 38.7 us)
Async XLA Ops:
  2.3 51.2 %collective-permute-start.25 = (bf16[448,1024]{1,0:T(8,128)(2,1)}, bf16[448,1024]{1,0:T(8,128)(2,1)}, u32[]{:S(2)}, u32[]{:S(2)}) collective-permute-start(bf16[448,1024]{1,0:T(8,128)(2,1)} %dynamic-slice_bitcast_fusion), channel_id=1, source_target_pairs={{4,0},{0,4},{12,8},{8,12},{5,1},{1,5},{13,9},{9,13},{6,2},{2,6},{1... | collective-permute-start | bytes 2752520 | tf_op jit(solution)/shard_map/ppermute | solution.py:25
  5.4 57.1 %collective-permute-start.27 = (bf16[448,1024]{1,0:T(8,128)(2,1)}, bf16[448,1024]{1,0:T(8,128)(2,1)}, u32[]{:S(2)}, u32[]{:S(2)}) collective-permute-start(bf16[448,1024]{1,0:T(8,128)(2,1)} %dynamic-slice_bitcast_fusion), channel_id=1, source_target_pairs={{8,4},{4,8},{9,5},{5,9},{10,6},{6,10},{11,7},{7,11},{24,20},{20,24... | collective-permute-start | bytes 2752520 | tf_op jit(solution)/shard_map/ppermute | solution.py:25
  12.0 53.7 %collective-permute-start.2 = (bf16[2,448,1024]{2,1,0:T(8,128)(2,1)}, bf16[2,448,1024]{2,1,0:T(8,128)(2,1)}, u32[]{:S(2)}, u32[]{:S(2)}) collective-permute-start(bf16[2,448,1024]{2,1,0:T(8,128)(2,1)} %rest_4_.1), channel_id=1, source_target_pairs={{0,1},{1,0},{2,3},{3,2},{4,5},{5,4},{6,7},{7,6},{8,9},{9,8},{10,11... | collective-permute-start | bytes 5505032 | tf_op jit(solution)/shard_map/ppermute | solution.py:20
  12.0 19.3 %collective-permute-start.3 = (bf16[128,896]{1,0:T(8,128)(2,1)S(1)}, bf16[128,896]{1,0:T(8,128)(2,1)}, u32[]{:S(2)}, u32[]{:S(2)}) collective-permute-start(bf16[128,896]{1,0:T(8,128)(2,1)S(1)} %get-tuple-element.34), channel_id=1, source_target_pairs={{4,0},{0,4},{12,8},{8,12},{5,1},{1,5},{13,9},{9,13},{6,2},{2,6},{1... | collective-permute-start | bytes 688136 | tf_op jit(solution)/shard_map/ppermute | solution.py:25
  15.4 22.7 %collective-permute-start.5 = (bf16[128,896]{1,0:T(8,128)(2,1)S(1)}, bf16[128,896]{1,0:T(8,128)(2,1)}, u32[]{:S(2)}, u32[]{:S(2)}) collective-permute-start(bf16[128,896]{1,0:T(8,128)(2,1)S(1)} %get-tuple-element.36), channel_id=1, source_target_pairs={{12,0},{8,4},{4,8},{0,12},{13,1},{9,5},{5,9},{1,13},{14,2},{10,6},... | collective-permute-start | bytes 688136 | tf_op jit(solution)/shard_map/ppermute | solution.py:25
  31.2 22.1 %collective-permute-start = (bf16[2,448,256]{2,1,0:T(8,128)(2,1)S(1)}, bf16[2,448,256]{2,1,0:T(8,128)(2,1)S(1)}, u32[]{:S(2)}, u32[]{:S(2)}) collective-permute-start(bf16[2,448,256]{2,1,0:T(8,128)(2,1)S(1)} %constant_dynamic-slice_fusion.1.rest_0_), channel_id=1, source_target_pairs={{0,1},{1,0},{2,3},{3,2},{4,5},{5,4},{6,7},{7,6},{8,9},{9,8},{10,11... | collective-permute-start | bytes 1376264 | tf_op jit(solution)/shard_map/ppermute | solution.py:20
  38.2 13.1 %collective-permute-start.7 = (bf16[128,896]{1,0:T(8,128)(2,1)S(1)}, bf16[128,896]{1,0:T(8,128)(2,1)}, u32[]{:S(2)}, u32[]{:S(2)}) collective-permute-start(bf16[128,896]{1,0:T(8,128)(2,1)S(1)} %get-tuple-element.39), channel_id=1, source_target_pairs={{8,0},{12,4},{0,8},{4,12},{9,1},{13,5},{1,9},{5,13},{10,2},{14,6},... | collective-permute-start | bytes 688136 | tf_op jit(solution)/shard_map/ppermute | solution.py:25
  53.5 32.7 %collective-permute-start.26 = (bf16[448,1024]{1,0:T(8,128)(2,1)}, bf16[448,1024]{1,0:T(8,128)(2,1)}, u32[]{:S(2)}, u32[]{:S(2)}) collective-permute-start(bf16[448,1024]{1,0:T(8,128)(2,1)} %collective-permute-done.25.rest_5_.rest_3_), channel_id=1, source_target_pairs={{8,4},{4,8},{9,5},{5,9},{10,6},{6,10},{11,7},{7,11},{24,20},{20,24... | collective-permute-start | bytes 2752520 | tf_op jit(solution)/shard_map/ppermute | solution.py:25
  61.9 15.5 %collective-permute-start.4 = (bf16[128,896]{1,0:T(8,128)(2,1)}, bf16[128,896]{1,0:T(8,128)(2,1)S(1)}, u32[]{:S(2)}, u32[]{:S(2)}) collective-permute-start(bf16[128,896]{1,0:T(8,128)(2,1)} %collective-permute-done.3.rest_6_), channel_id=1, source_target_pairs={{0,2},{2,0},{1,3},{3,1},{4,6},{6,4},{5,7},{7,5},{8,10},{10,8},{9,1... | collective-permute-start | bytes 688136 | tf_op jit(solution)/shard_map/ppermute | solution.py:20
  62.5 73.1 %collective-permute-start.28 = (bf16[448,1024]{1,0:T(8,128)(2,1)}, bf16[448,1024]{1,0:T(8,128)(2,1)S(1)}, u32[]{:S(2)}, u32[]{:S(2)}) collective-permute-start(bf16[448,1024]{1,0:T(8,128)(2,1)} %collective-permute-done.27), channel_id=1, source_target_pairs={{4,0},{8,12},{5,1},{9,13},{6,2},{10,14},{7,3},{11,15},{20,16},{24,... | collective-permute-start | bytes 2752520 | tf_op jit(solution)/shard_map/ppermute | solution.py:25
  73.2 27.2 %collective-permute-start.9 = (bf16[256,1024]{1,0:T(8,128)(2,1)S(1)}, bf16[256,1024]{1,0:T(8,128)(2,1)S(1)}, u32[]{:S(2)}, u32[]{:S(2)}) collective-permute-start(bf16[256,1024]{1,0:T(8,128)(2,1)S(1)} %get-tuple-element.43), channel_id=1, source_target_pairs={{0,4},{12,8},{1,5},{13,9},{2,6},{14,10},{3,7},{15,11},{16,20},{28,... | collective-permute-start | bytes 1572872 | tf_op jit(solution)/shard_map/ppermute | solution.py:25
  76.0 23.5 %collective-permute-start.14 = (bf16[2,256,512]{2,1,0:T(8,128)(2,1)S(1)}, bf16[2,256,512]{2,1,0:T(8,128)(2,1)S(1)}, u32[]{:S(2)}, u32[]{:S(2)}) collective-permute-start(bf16[2,256,512]{2,1,0:T(8,128)(2,1)S(1)} %bitcast.52), channel_id=1, source_target_pairs={{0,4},{12,8},{1,5},{13,9},{2,6},{14,10},{3,7},{15,11},{16,20},{28,... | collective-permute-start | bytes 1572872 | tf_op jit(solution)/shard_map/ppermute | solution.py:25
  84.7 22.1 %collective-permute-start.12 = (bf16[256,1024]{1,0:T(8,128)(2,1)S(1)}, bf16[256,1024]{1,0:T(8,128)(2,1)S(1)}, u32[]{:S(2)}, u32[]{:S(2)}) collective-permute-start(bf16[256,1024]{1,0:T(8,128)(2,1)S(1)} %get-tuple-element.44), channel_id=1, source_target_pairs={{0,4},{12,8},{1,5},{13,9},{2,6},{14,10},{3,7},{15,11},{16,20},{28,... | collective-permute-start | bytes 1572872 | tf_op jit(solution)/shard_map/ppermute | solution.py:25
  86.2 53.3 %collective-permute-start.29 = (bf16[448,1024]{1,0:T(8,128)(2,1)}, bf16[448,1024]{1,0:T(8,128)(2,1)S(1)}, u32[]{:S(2)}, u32[]{:S(2)}) collective-permute-start(bf16[448,1024]{1,0:T(8,128)(2,1)} %collective-permute-done.26), channel_id=1, source_target_pairs={{4,0},{8,12},{5,1},{9,13},{6,2},{10,14},{7,3},{11,15},{20,16},{24,... | collective-permute-start | bytes 2752520 | tf_op jit(solution)/shard_map/ppermute | solution.py:25
  100.7 18.4 %collective-permute-start.10 = (bf16[256,1024]{1,0:T(8,128)(2,1)S(1)}, bf16[256,1024]{1,0:T(8,128)(2,1)S(1)}, u32[]{:S(2)}, u32[]{:S(2)}) collective-permute-start(bf16[256,1024]{1,0:T(8,128)(2,1)S(1)} %fusion.2), channel_id=1, source_target_pairs={{8,4},{4,8},{9,5},{5,9},{10,6},{6,10},{11,7},{7,11},{24,20},{20,24... | collective-permute-start | bytes 1572872 | tf_op jit(solution)/shard_map/ppermute | solution.py:25
  107.0 34.0 %collective-permute-start.13 = (bf16[256,1024]{1,0:T(8,128)(2,1)S(1)}, bf16[256,1024]{1,0:T(8,128)(2,1)S(1)}, u32[]{:S(2)}, u32[]{:S(2)}) collective-permute-start(bf16[256,1024]{1,0:T(8,128)(2,1)S(1)} %fusion.1), channel_id=1, source_target_pairs={{8,4},{4,8},{9,5},{5,9},{10,6},{6,10},{11,7},{7,11},{24,20},{20,24... | collective-permute-start | bytes 1572872 | tf_op jit(solution)/shard_map/ppermute | solution.py:25
  108.0 27.3 %collective-permute-start.16 = (bf16[256,512]{1,0:T(8,128)(2,1)S(1)}, bf16[256,512]{1,0:T(8,128)(2,1)S(1)}, u32[]{:S(2)}, u32[]{:S(2)}) collective-permute-start(bf16[256,512]{1,0:T(8,128)(2,1)S(1)} %fusion.4), channel_id=1, source_target_pairs={{4,0},{0,4},{12,8},{8,12},{5,1},{1,5},{13,9},{9,13},{6,2},{2,6},{1... | collective-permute-start | bytes 786440 | tf_op jit(solution)/shard_map/ppermute | solution.py:25
  119.3 36.2 %collective-permute-start.11 = (bf16[256,1024]{1,0:T(8,128)(2,1)S(1)}, bf16[256,1024]{1,0:T(8,128)(2,1)S(1)}, u32[]{:S(2)}, u32[]{:S(2)}) collective-permute-start(bf16[256,1024]{1,0:T(8,128)(2,1)S(1)} %add_convert_fusion.1), channel_id=1, source_target_pairs={{4,0},{0,4},{12,8},{8,12},{5,1},{1,5},{13,9},{9,13},{6,2},{2,6},{1... | collective-permute-start | bytes 1572872 | tf_op jit(solution)/shard_map/ppermute | solution.py:25
  135.4 12.7 %collective-permute-start.17 = (bf16[256,512]{1,0:T(8,128)(2,1)S(1)}, bf16[256,512]{1,0:T(8,128)(2,1)S(1)}, u32[]{:S(2)}, u32[]{:S(2)}) collective-permute-start(bf16[256,512]{1,0:T(8,128)(2,1)S(1)} %fusion.3.rest_3_), channel_id=1, source_target_pairs={{4,0},{0,4},{12,8},{8,12},{5,1},{1,5},{13,9},{9,13},{6,2},{2,6},{1... | collective-permute-start | bytes 786440 | tf_op jit(solution)/shard_map/ppermute | solution.py:25
  135.5 12.6 %collective-permute-start.18 = (bf16[256,512]{1,0:T(8,128)(2,1)S(1)}, bf16[256,512]{1,0:T(8,128)(2,1)S(1)}, u32[]{:S(2)}, u32[]{:S(2)}) collective-permute-start(bf16[256,512]{1,0:T(8,128)(2,1)S(1)} %fusion.3.rest_3_), channel_id=1, source_target_pairs={{8,0},{12,4},{0,8},{4,12},{9,1},{13,5},{1,9},{5,13},{10,2},{14,6},... | collective-permute-start | bytes 786440 | tf_op jit(solution)/shard_map/ppermute | solution.py:25
  139.5 14.9 %collective-permute-start.19 = (bf16[256,512]{1,0:T(8,128)(2,1)S(1)}, bf16[256,512]{1,0:T(8,128)(2,1)S(1)}, u32[]{:S(2)}, u32[]{:S(2)}) collective-permute-start(bf16[256,512]{1,0:T(8,128)(2,1)S(1)} %fusion.3.rest_3_), channel_id=1, source_target_pairs={{12,0},{8,4},{4,8},{0,12},{13,1},{9,5},{5,9},{1,13},{14,2},{10,6},... | collective-permute-start | bytes 786440 | tf_op jit(solution)/shard_map/ppermute | solution.py:25
  140.9 16.1 %collective-permute-start.20 = (bf16[256,512]{1,0:T(8,128)(2,1)S(1)}, bf16[256,512]{1,0:T(8,128)(2,1)S(1)}, u32[]{:S(2)}, u32[]{:S(2)}) collective-permute-start(bf16[256,512]{1,0:T(8,128)(2,1)S(1)} %fusion.3.rest_3_), channel_id=1, source_target_pairs={{0,1},{1,0},{2,3},{3,2},{4,5},{5,4},{6,7},{7,6},{8,9},{9,8},{10,11... | collective-permute-start | bytes 786440 | tf_op jit(solution)/shard_map/ppermute | solution.py:20
  148.1 9.5 %collective-permute-start.21 = (bf16[256,512]{1,0:T(8,128)(2,1)S(1)}, bf16[256,512]{1,0:T(8,128)(2,1)S(1)}, u32[]{:S(2)}, u32[]{:S(2)}) collective-permute-start(bf16[256,512]{1,0:T(8,128)(2,1)S(1)} %collective-permute-done.17.rest_4_), channel_id=1, source_target_pairs={{0,1},{1,0},{2,3},{3,2},{4,5},{5,4},{6,7},{7,6},{8,9},{9,8},{10,11... | collective-permute-start | bytes 786440 | tf_op jit(solution)/shard_map/ppermute | solution.py:20
  148.1 11.2 %collective-permute-start.22 = (bf16[256,512]{1,0:T(8,128)(2,1)S(1)}, bf16[256,512]{1,0:T(8,128)(2,1)}, u32[]{:S(2)}, u32[]{:S(2)}) collective-permute-start(bf16[256,512]{1,0:T(8,128)(2,1)S(1)} %collective-permute-done.18.rest_5_), channel_id=1, source_target_pairs={{0,1},{1,0},{2,3},{3,2},{4,5},{5,4},{6,7},{7,6},{8,9},{9,8},{10,11... | collective-permute-start | bytes 786440 | tf_op jit(solution)/shard_map/ppermute | solution.py:20
  155.4 23.6 %collective-permute-start.30 = (bf16[448,1024]{1,0:T(8,128)(2,1)}, bf16[448,1024]{1,0:T(8,128)(2,1)}, u32[]{:S(2)}, u32[]{:S(2)}) collective-permute-start(bf16[448,1024]{1,0:T(8,128)(2,1)} %collective-permute-done.25.rest_5_.rest_3_), channel_id=1, source_target_pairs={{0,16},{16,0},{1,17},{17,1},{2,18},{18,2},{3,19},{19,3},{4,20},{20... | collective-permute-start | bytes 2752520 | tf_op jit(solution)/shard_map/ppermute | solution.py:20
  157.0 41.7 %collective-permute-start.31 = (bf16[448,1024]{1,0:T(8,128)(2,1)}, bf16[448,1024]{1,0:T(8,128)(2,1)}, u32[]{:S(2)}, u32[]{:S(2)}) collective-permute-start(bf16[448,1024]{1,0:T(8,128)(2,1)} %broadcast_select_fusion.1.rest_6_.rest_4_), channel_id=1, source_target_pairs={{0,16},{16,0},{1,17},{17,1},{2,18},{18,2},{3,19},{19,3},{4,20},{20... | collective-permute-start | bytes 2752520 | tf_op jit(solution)/shard_map/ppermute | solution.py:20
  157.8 60.2 %collective-permute-start.32 = (bf16[448,1024]{1,0:T(8,128)(2,1)}, bf16[448,1024]{1,0:T(8,128)(2,1)}, u32[]{:S(2)}, u32[]{:S(2)}) collective-permute-start(bf16[448,1024]{1,0:T(8,128)(2,1)} %broadcast_select_fusion.rest_7_.rest_5_), channel_id=1, source_target_pairs={{0,16},{16,0},{1,17},{17,1},{2,18},{18,2},{3,19},{19,3},{4,20},{20... | collective-permute-start | bytes 2752520 | tf_op jit(solution)/shard_map/ppermute | solution.py:20
  164.4 53.5 %collective-permute-start.24 = (bf16[256,1024]{1,0:T(8,128)(2,1)S(1)}, bf16[256,1024]{1,0:T(8,128)(2,1)}, u32[]{:S(2)}, u32[]{:S(2)}) collective-permute-start(bf16[256,1024]{1,0:T(8,128)(2,1)S(1)} %attend.1.rest_0_), channel_id=1, source_target_pairs={{0,1},{1,0},{2,3},{3,2},{4,5},{5,4},{6,7},{7,6},{8,9},{9,8},{10,11... | collective-permute-start | bytes 1572872 | tf_op jit(solution)/shard_map/ppermute | solution.py:20
  221.2 9.5 %collective-permute-start.36 = (bf16[1,256,448]{2,1,0:T(8,128)(2,1)S(1)}, bf16[1,256,448]{2,1,0:T(8,128)(2,1)S(1)}, u32[]{:S(2)}, u32[]{:S(2)}) collective-permute-start(bf16[1,256,448]{2,1,0:T(8,128)(2,1)S(1)} %project.9), channel_id=1, source_target_pairs={{0,2},{2,0},{1,3},{3,1},{4,6},{6,4},{5,7},{7,5},{8,10},{10,8},{9,1... | collective-permute-start | bytes 688136 | tf_op jit(solution)/shard_map/ppermute | solution.py:20
  234.9 17.3 %collective-permute-start.37 = (bf16[2,256,448]{2,1,0:T(8,128)(2,1)S(1)}, bf16[2,256,448]{2,1,0:T(8,128)(2,1)S(1)}, u32[]{:S(2)}, u32[]{:S(2)}) collective-permute-start(bf16[2,256,448]{2,1,0:T(8,128)(2,1)S(1)} %add_convert_fusion), channel_id=1, source_target_pairs={{0,1},{1,0},{2,3},{3,2},{4,5},{5,4},{6,7},{7,6},{8,9},{9,8},{10,11... | collective-permute-start | bytes 1376264 | tf_op jit(solution)/shard_map/ppermute | solution.py:20
  237.8 9.2 %collective-permute-start.33 = (bf16[1,256,448]{2,1,0:T(8,128)(2,1)S(1)}, bf16[1,256,448]{2,1,0:T(8,128)(2,1)S(1)}, u32[]{:S(2)}, u32[]{:S(2)}) collective-permute-start(bf16[1,256,448]{2,1,0:T(8,128)(2,1)S(1)} %project.6), channel_id=1, source_target_pairs={{0,2},{2,0},{1,3},{3,1},{4,6},{6,4},{5,7},{7,5},{8,10},{10,8},{9,1... | collective-permute-start | bytes 688136 | tf_op jit(solution)/shard_map/ppermute | solution.py:20
  241.3 10.9 %collective-permute-start.34 = (bf16[1,256,448]{2,1,0:T(8,128)(2,1)S(1)}, bf16[1,256,448]{2,1,0:T(8,128)(2,1)S(1)}, u32[]{:S(2)}, u32[]{:S(2)}) collective-permute-start(bf16[1,256,448]{2,1,0:T(8,128)(2,1)S(1)} %project.7), channel_id=1, source_target_pairs={{0,2},{2,0},{1,3},{3,1},{4,6},{6,4},{5,7},{7,5},{8,10},{10,8},{9,1... | collective-permute-start | bytes 688136 | tf_op jit(solution)/shard_map/ppermute | solution.py:20
  (29 other events, 395.1 us)
